TPU v7x, 128 devices: a whole 4x4x4 slice. The times are simulated.
128 devices in a mesh: wide: 8 (over y, core), sixteen: 16 (over z, x).
Axes of the slice: x: 4, y: 4, z: 4, core: 2. Of those that a mesh axis runs over, the one named last changes fastest.
Arguments:
- observations: float32 [64, 512, 1024], P(None, 'sixteen', 'wide'), may hold values from -60 to 60
- huber_scale: float32 [64], replicated, may hold values from 0.5 to 2
- observed: int32 [512, 1024], P('sixteen', 'wide'), may hold values from 0 to 1, as said below
- jitter: float32 [2, 512, 1024], P(None, 'sixteen', 'wide'), may hold values from -0.4 to 0.4
- owner_map: int32 [8, 128], P('wide'), may hold values from 0 to 15, as said below
- neighbours: int32 [8, 128, 6], P('wide'), may hold values from 0 to 127, as said below
Outputs:
- solution: float32 [8, 16, 64, 8, 512], P('wide', 'sixteen')
- residual: float32 [8, 16, 64, 8, 512], P('wide', 'sixteen')
Inputs may be any that keep to these rules, and one draw needn't show every extreme that they name: At least one whole lattice row and at least one whole lattice column hold no observed point. `owner_map`: in each column group every device along sixteen holds 8 blocks (block g on device g // 8) and sends them to 8 different owners; every owner receives exactly 8 blocks, each from a different device. `neighbours`: block g of a column group lists g + d and g - d modulo 128 for each of half of 6 different offsets d between 1 and 4; all blocks of one group use the same offsets, so every list holds 6 different blocks and the relation is symmetric.
All inputs are finite; a program needn't handle non-finite values.
Results may differ from a plain program's by a relative error of at most 0.0003.
Values sent between devices are 32-bit elements; how exact they have to be, the bound alone decides.
No kernel may reach another device: no remote copies, remote signals or barrier semaphores. Data moves between devices by JAX's collectives and lax.ppermute only.
A program may use at most 192 MiB of HBM per device.

v0:
```python
import functools

import jax
import jax.numpy as jnp
from jax import lax
from jax.experimental import pallas as pl
from jax.experimental.pallas import tpu as pltpu
from jax.sharding import Mesh
from jax.sharding import PartitionSpec as P

BLOCK = 512
BLOCKS_DEV = 8
REACH = 4
NEIGHBOURS = 6
PAIRED = NEIGHBOURS // 2
SWEEPS = 2
STRIP = 4
COL_DEV = 128
WIDE = ("wide_0", "wide_1")
SIXTEEN = ("sixteen_0", "sixteen_1")

HUBER_EDGE = 1.345
SILL_TERM = 0.02
ROOT_THREE = 1.7320508075688772
SPREAD = 2.0 * STRIP
CUTOFF = 6.0 * STRIP
BAND = 24
GROUP = 16

OWN_TILES = BLOCKS_DEV + PAIRED * BLOCKS_DEV - 6
HALO_TILES = 2 * (2 + 3 + 4)
ROW_TILES, COL_TILES = 7, 15
TILE_SLOTS = 4
OP_SLOTS = 5


def sent_to_all(shard, axis):
    peers = lax.axis_size(axis)
    return lax.all_to_all(
        jnp.broadcast_to(shard[None], (peers, *shard.shape)), axis, 0, 0, tiled=True
    )


def over_copies(shard, axis):
    return jnp.sum(sent_to_all(shard, axis), axis=0)


def sum_direct(part, axis):
    peers = lax.axis_size(axis)
    moved = [
        lax.ppermute(part, axis, [(i, (i + k) % peers) for i in range(peers)])
        for k in range(1, peers)
    ]
    return functools.reduce(jnp.add, moved, part)


def beside(shard, width):
    peers, length = lax.axis_size(SIXTEEN), shard.shape[0]
    up = [(i, (i + 1) % peers) for i in range(peers)]
    down = [(j, i) for i, j in up]
    last = lax.slice_in_dim(shard, length - width, length, axis=0)
    initial = lax.slice_in_dim(shard, 0, width, axis=0)
    shard, last, initial = lax.optimization_barrier((shard, last, initial))
    return lax.ppermute(last, SIXTEEN, up), lax.ppermute(initial, SIXTEEN, down), shard


def owned_table(group_map, owners, per_owner):
    total_strips = group_map.shape[0]
    member = (group_map[None, :] == jnp.arange(owners, dtype=jnp.int32)[:, None]).astype(jnp.int32)
    ranked = jnp.cumsum(member, axis=1, dtype=jnp.int32) - 1
    slot_hit = (ranked[:, :, None] == jnp.arange(per_owner, dtype=jnp.int32)[None, None, :]).astype(
        jnp.int32
    ) * member[:, :, None]
    numbers = jnp.arange(total_strips, dtype=jnp.int32)
    return jnp.sum(slot_hit * numbers[None, :, None], axis=1, dtype=jnp.int32)


def tile_lists(first_list, total):
    steps = jnp.arange(1, REACH + 1, dtype=jnp.int32)
    held = jnp.any(first_list[None, :] == (steps % total)[:, None], axis=1)
    missing = jnp.min(jnp.where(held, REACH + 1, steps))
    d1, d2, d3 = (k + (missing <= k).astype(jnp.int32) for k in range(1, PAIRED + 1))
    reach = d1 + d2 + d3
    t = jnp.arange(OWN_TILES + HALO_TILES, dtype=jnp.int32)
    n1, n2 = BLOCKS_DEV - d1, 2 * BLOCKS_DEV - d1 - d2
    own_count = (PAIRED + 1) * BLOCKS_DEV - reach
    p = t - BLOCKS_DEV
    pair_a = jnp.where(p < n1, p, jnp.where(p < n2, p - n1, p - n2))
    pair_b = pair_a + jnp.where(p < n1, d1, jnp.where(p < n2, d2, d3))
    q = t - OWN_TILES
    right = q >= reach
    q = jnp.where(right, q - reach, q)
    step = jnp.where(q < d1, d1, jnp.where(q < d1 + d2, d2, d3))
    pos = jnp.where(q < d1, q, jnp.where(q < d1 + d2, q - d1, q - d1 - d2))
    halo_a = jnp.where(right, BLOCKS_DEV - 1 - pos, pos)
    halo_b = jnp.where(right, BLOCKS_DEV - 1 - pos + step, pos - step)
    live = jnp.where(t < OWN_TILES, t < own_count, t < OWN_TILES + 2 * reach)
    one = jnp.where(t < BLOCKS_DEV, t, jnp.where(t < OWN_TILES, pair_a, halo_a))
    other = jnp.where(t < BLOCKS_DEV, t, jnp.where(t < OWN_TILES, pair_b, halo_b))
    one = jnp.where(live, one, 0)
    other = jnp.where(live, other, 0)
    counts = jnp.stack([own_count, 2 * reach])
    return jnp.concatenate([one, other, live.astype(jnp.int32), counts])


LISTED = OWN_TILES + HALO_TILES


def tiles_kernel(first, count, held, table_ref, rows_ref, cols_ref, *refs):
    tiles_ref, buf, sem = refs[held:]
    a, b = ROOT_THREE * CUTOFF / SPREAD, 4.0

    def out_copy(t):
        slot = lax.rem(t - first, TILE_SLOTS)
        return pltpu.make_async_copy(buf.at[slot], tiles_ref.at[t], sem.at[slot])

    def live(t):
        return table_ref[2 * LISTED + t] == 1

    def one_tile(t, carry):
        slot = lax.rem(t - first, TILE_SLOTS)
        past = jnp.maximum(t - TILE_SLOTS, first)

        @pl.when((t >= first + TILE_SLOTS) & live(past))
        def _():
            out_copy(past).wait()

        @pl.when(live(t))
        def _():
            one, other = table_ref[t], table_ref[LISTED + t]
            sill = jnp.where(one == other, (NEIGHBOURS + 1.0) * SILL_TERM, SILL_TERM)
            lane = lax.broadcasted_iota(jnp.int32, (GROUP, COL_DEV), 1)
            to = rows_ref[one + REACH]
            frm = cols_ref[other + REACH]
            for rb in range(STRIP):
                row_b = jnp.broadcast_to(frm[:, rb : rb + 1], (COL_DEV, COL_DEV))
                col_b = jnp.broadcast_to(frm[:, STRIP + rb : STRIP + rb + 1], (COL_DEV, COL_DEV))
                for u in range(COL_DEV // 2 // GROUP):
                    lo_s = slice(GROUP * u, GROUP * (u + 1))
                    hi_s = slice(64 + GROUP * u, 64 + GROUP * (u + 1))
                    near = (lane >= GROUP * u - BAND) & (lane < GROUP * (u + 1) + BAND)
                    one_m = jnp.where(near, 1.0, 0.0).astype(jnp.bfloat16)
                    other_m = jnp.where(near, 0.0, 1.0).astype(jnp.bfloat16)
                    row_s = jnp.where(near, row_b[lo_s], row_b[hi_s])
                    col_s = jnp.where(near, col_b[lo_s], col_b[hi_s])
                    for ra in range(STRIP):
                        dr = row_s - to[ra : ra + 1]
                        dc = col_s - to[STRIP + ra : STRIP + ra + 1]
                        square = dr * dr + dc * dc
                        far = square * lax.rsqrt(jnp.maximum(square, 1e-30))
                        fading = jnp.maximum(1.0 - far, 0.0)
                        fading = fading * fading
                        fading = fading * fading
                        shape = (1.0 + a * far) * (sill + (sill * b) * far)
                        value = shape * fading * jnp.exp(-a * far)
                        hi = value.astype(jnp.bfloat16)
                        lo = (value - hi.astype(jnp.float32)).astype(jnp.bfloat16)
                        lanes = slice(COL_DEV * ra, COL_DEV * (ra + 1))
                        top = rb * COL_DEV + GROUP * u
                        for part, at in ((hi, top), (lo, BLOCK + top)):
                            buf[slot, at : at + GROUP, lanes] = part * one_m
                            buf[slot, at + 64 : at + 64 + GROUP, lanes] = part * other_m
            out_copy(t).start()

        return carry

    lax.fori_loop(first, first + count, one_tile, 0)
    for t in range(max(first, first + count - TILE_SLOTS), first + count):

        @pl.when(live(t))
        def _(t=t):
            out_copy(t).wait()


def covariance_tiles(first, count, table, rows, cols, held):
    vmem, hbm = pl.BlockSpec(memory_space=pltpu.VMEM), pl.BlockSpec(memory_space=pl.ANY)
    extra = [] if held is None else [held]
    return pl.pallas_call(
        functools.partial(tiles_kernel, first, count, len(extra)),
        in_specs=[pl.BlockSpec(memory_space=pltpu.SMEM), vmem, vmem] + [hbm] * len(extra),
        out_specs=hbm,
        scratch_shapes=[
            pltpu.VMEM((TILE_SLOTS, 2 * BLOCK, BLOCK), jnp.bfloat16),
            pltpu.SemaphoreType.DMA((TILE_SLOTS,)),
        ],
        out_shape=jax.ShapeDtypeStruct((LISTED, 2 * BLOCK, BLOCK), jnp.bfloat16),
        input_output_aliases={3: 0} if extra else {},
        compiler_params=pltpu.CompilerParams(vmem_limit_bytes=32 << 20),
        cost_estimate=pl.CostEstimate(
            flops=count * 12 * BLOCK * BLOCK,
            bytes_accessed=count * 4 * BLOCK * BLOCK,
            transcendentals=count * BLOCK * BLOCK,
        ),
        name="tiles",
    )(table, rows, cols, *extra)


def halves(v):
    hi = v.astype(jnp.bfloat16)
    lo = (v - hi.astype(jnp.float32)).astype(jnp.bfloat16)
    return hi, lo


NN = (((1,), (0,)), ((), ()))
NT = (((1,), (1,)), ((), ()))


def product(both, tile_ref, dims):
    fields = both.shape[0] // 2
    main = lax.dot_general(
        both, tile_ref[:BLOCK], dims, preferred_element_type=jnp.float32
    )
    rest = lax.dot_general(
        both[:fields], tile_ref[BLOCK:], dims, preferred_element_type=jnp.float32
    )
    return main[:fields] + (main[fields:] + rest)


def tile_stream(tiles_ref, base, buf, sem):
    def copy(t):
        slot = lax.rem(t, OP_SLOTS)
        return pltpu.make_async_copy(tiles_ref.at[base + t], buf.at[slot], sem.at[slot])

    return copy


def own_kernel(table_ref, v_ref, tiles_ref, out_ref, both_ref, buf, sem):
    fields = v_ref.shape[1]
    count = table_ref[3 * LISTED]
    copy = tile_stream(tiles_ref, 0, buf, sem)
    for t in range(OP_SLOTS - 1):
        copy(t).start()
    for g in range(BLOCKS_DEV):
        hi, lo = halves(v_ref[g])
        both_ref[g, :fields] = hi
        both_ref[g, fields:] = lo

    def arrive(t):
        @pl.when(t + OP_SLOTS - 1 < count)
        def _():
            copy(t + OP_SLOTS - 1).start()

        copy(t).wait()
        return buf.at[lax.rem(t, OP_SLOTS)]

    def with_itself(t, carry):
        tile = arrive(t)
        out_ref[t] = product(both_ref[t], tile, NN)
        return carry

    def with_another(t, carry):
        tile = arrive(t)
        one, other = table_ref[t], table_ref[LISTED + t]
        out_ref[one] += product(both_ref[other], tile, NN)
        out_ref[other] += product(both_ref[one], tile, NT)
        return carry

    lax.fori_loop(0, BLOCKS_DEV, with_itself, 0)
    lax.fori_loop(BLOCKS_DEV, count, with_another, 0)


def halo_kernel(
    table_ref, target_ref, before_ref, after_ref, part_ref, tiles_ref, out_ref, *refs
):
    *slots_ref, both_ref, buf, sem, out_sem = refs
    fields = before_ref.shape[1]
    count = table_ref[3 * LISTED + 1]
    copy = tile_stream(tiles_ref, OWN_TILES, buf, sem)
    for t in range(OP_SLOTS - 1):
        copy(t).start()
    for side, ref in enumerate((before_ref, after_ref)):
        for g in range(REACH):
            hi, lo = halves(ref[g])
            both_ref[side * REACH + g, :fields] = hi
            both_ref[side * REACH + g, fields:] = lo
    out_ref[...] = part_ref[...]

    def with_beside(t, carry):
        @pl.when(t + OP_SLOTS - 1 < count)
        def _():
            copy(t + OP_SLOTS - 1).start()

        copy(t).wait()
        one, other = table_ref[OWN_TILES + t], table_ref[LISTED + OWN_TILES + t]
        side = jnp.where(other < 0, other + REACH, other - BLOCKS_DEV + REACH)
        out_ref[one] += product(both_ref[side], buf.at[lax.rem(t, OP_SLOTS)], NN)
        return carry

    lax.fori_loop(0, count, with_beside, 0)
    if slots_ref:
        sent = out_copies(out_ref, slots_ref[0], target_ref, out_sem)
        for copy_out in sent:
            copy_out.start()
        for copy_out in sent:
            copy_out.wait()


def out_copies(values_ref, slots_ref, target_ref, sem):
    return [
        pltpu.make_async_copy(values_ref.at[g], slots_ref.at[target_ref[g]], sem.at[g])
        for g in range(BLOCKS_DEV)
    ]


SMEM_SPEC = pl.BlockSpec(memory_space=pltpu.SMEM)
VMEM_SPEC = pl.BlockSpec(memory_space=pltpu.VMEM)
HBM_SPEC = pl.BlockSpec(memory_space=pltpu.HBM)


def stream_scratch():
    return [
        pltpu.VMEM((OP_SLOTS, 2 * BLOCK, BLOCK), jnp.bfloat16),
        pltpu.SemaphoreType.DMA((OP_SLOTS,)),
    ]


def slot_shape(v):
    return pltpu.HBM((lax.axis_size(SIXTEEN), *v.shape[1:]), jnp.float32)


def product_cost(tiles, products, fields):
    return pl.CostEstimate(
        flops=products * 3 * 2 * fields * BLOCK * BLOCK,
        bytes_accessed=tiles * 4 * BLOCK * BLOCK,
        transcendentals=0,
    )


def own_product(table, v, tiles):
    blocks, fields, _ = v.shape
    return pl.pallas_call(
        own_kernel,
        in_specs=[SMEM_SPEC, VMEM_SPEC, HBM_SPEC],
        out_specs=VMEM_SPEC,
        scratch_shapes=[pltpu.VMEM((blocks, 2 * fields, BLOCK), jnp.bfloat16)] + stream_scratch(),
        out_shape=jax.ShapeDtypeStruct(v.shape, jnp.float32),
        compiler_params=pltpu.CompilerParams(vmem_limit_bytes=32 << 20),
        cost_estimate=product_cost(OWN_TILES, 42, fields),
        name="own",
    )(table, v, tiles)


def spread_kernel(target_ref, v_ref, *refs):
    slots_ref, sem = refs[-2:]
    sent = out_copies(v_ref, slots_ref, target_ref, sem)
    for copy_out in sent:
        copy_out.start()
    for copy_out in sent:
        copy_out.wait()


def spread(targets, v, *behind):
    return pl.pallas_call(
        spread_kernel,
        in_specs=[SMEM_SPEC] + [VMEM_SPEC] * (1 + len(behind)),
        out_specs=HBM_SPEC,
        scratch_shapes=[pltpu.SemaphoreType.DMA((BLOCKS_DEV,))],
        out_shape=slot_shape(v),
        name="spread",
    )(targets, v, *behind)


def halo_product(table, targets, before, after, part, tiles, send):
    blocks, fields, _ = part.shape
    out = pl.pallas_call(
        halo_kernel,
        in_specs=[SMEM_SPEC, SMEM_SPEC, VMEM_SPEC, VMEM_SPEC, VMEM_SPEC, HBM_SPEC],
        out_specs=[VMEM_SPEC] + [HBM_SPEC] * send,
        scratch_shapes=[pltpu.VMEM((2 * REACH, 2 * fields, BLOCK), jnp.bfloat16)]
        + stream_scratch()
        + [pltpu.SemaphoreType.DMA((BLOCKS_DEV,))],
        out_shape=[jax.ShapeDtypeStruct(part.shape, jnp.float32)] + [slot_shape(part)] * send,
        compiler_params=pltpu.CompilerParams(vmem_limit_bytes=32 << 20),
        cost_estimate=product_cost(HALO_TILES, HALO_TILES, fields),
        name="halo",
    )(table, targets, before, after, part, tiles)
    return out if send else out[0]


def residual_kernel(obs_ref, weight_ref, row_ref, col_ref, out_ref):
    col = col_ref[...]
    for g in range(BLOCKS_DEV):
        for ra in range(STRIP):
            r = STRIP * g + ra
            left = obs_ref[:, r, :] - row_ref[:, r : r + 1] - col
            out_ref[g, :, COL_DEV * ra : COL_DEV * (ra + 1)] = weight_ref[r : r + 1, :] * left


def residual_of(observations, weight, row_effect, col_effect):
    fields = observations.shape[0]
    return pl.pallas_call(
        residual_kernel,
        in_specs=[VMEM_SPEC] * 4,
        out_specs=VMEM_SPEC,
        out_shape=jax.ShapeDtypeStruct((BLOCKS_DEV, fields, BLOCK), jnp.float32),
        compiler_params=pltpu.CompilerParams(vmem_limit_bytes=32 << 20),
        name="residual",
    )(observations, weight, row_effect, col_effect)


def combine_kernel(src_ref, scale_ref, *refs):
    ins, (x_ref, r_ref) = refs[:-2], refs[-2:]
    scale = scale_ref[...]
    for j in range(BLOCKS_DEV):
        r0, m1, m2 = (ref[0] for ref in ins[3 * j : 3 * j + 3])
        x_ref[:, j, :] = scale[:, 0:1] * r0 + scale[:, 1:2] * m1
        r_ref[:, j, :] = scale[:, 2:3] * r0 + scale[:, 3:4] * m1 + scale[:, 4:5] * m2


def combined(sources, scale, r0, m1, m2):
    fields = r0.shape[1]
    part = 16
    ins, specs = [], []
    for j in range(BLOCKS_DEV):
        for v in (r0, m1, m2):
            ins.append(v)
            specs.append(
                pl.BlockSpec(
                    (1, part, BLOCK), functools.partial(lambda j, i, s: (s[j], i, 0), j)
                )
            )
    out = pl.BlockSpec((part, BLOCKS_DEV, BLOCK), lambda i, s: (i, 0, 0))
    shape = jax.ShapeDtypeStruct((fields, BLOCKS_DEV, BLOCK), jnp.float32)
    return pl.pallas_call(
        combine_kernel,
        grid_spec=pltpu.PrefetchScalarGridSpec(
            num_scalar_prefetch=1,
            grid=(fields // part,),
            in_specs=[pl.BlockSpec((part, 8), lambda i, s: (i, 0))] + specs,
            out_specs=[out, out],
        ),
        out_shape=[shape, shape],
        compiler_params=pltpu.CompilerParams(vmem_limit_bytes=32 << 20),
        name="combine",
    )(sources, scale, *ins)


def to_owners(slots):
    return lax.all_to_all(slots, SIXTEEN, 0, 0, tiled=True)


def step_scales(h00, h01, h11, h12):
    mu = h01 / h00
    var = (h11 - mu * h01) / h00
    a0 = 1.0 / (1.0 + mu)
    beta = var * a0 * a0
    skew = (h12 - mu * h11 - mu * (h11 - mu * h01)) / h00
    a1 = var / (var + skew - var * var * a0)
    x_r0 = a0 + a1 * beta + a1 * a0 * mu
    x_m1 = -a1 * a0
    r_r0 = a0 * mu * (1.0 - a1) - a1 * beta
    r_m1 = -a0 * (1.0 - a1) - a1 * a0 * mu - a1 * beta
    r_m2 = a1 * a0
    zero = jnp.zeros_like(mu)
    return jnp.stack([x_r0, x_m1, r_r0, r_m1, r_m2, zero, zero, zero], axis=1)


def on_device(observations, huber_scale, observed, jitter, owner_map, neighbours):
    fields, row_dev, col_dev = observations.shape
    sixteen_size = lax.axis_size(SIXTEEN)
    my_place = lax.axis_index(SIXTEEN)
    group_place = lax.axis_index(WIDE)
    total_strips = BLOCKS_DEV * sixteen_size
    weight = observed.astype(jnp.float32)
    spread_scale = huber_scale[:, None, None]

    def with_count(part, count):
        rows = jnp.zeros((8, count.shape[0]), jnp.float32).at[0].set(count)
        return jnp.concatenate([part, rows], axis=0)

    def terms(row_effect, col_effect):
        return weight[None] * jnp.clip(
            (observations - row_effect[:, :, None] - col_effect[:, None, :]) / spread_scale,
            -HUBER_EDGE,
            HUBER_EDGE,
        )

    row_effect = jnp.zeros((fields, row_dev), jnp.float32)
    col_effect = jnp.zeros((fields, col_dev), jnp.float32)
    part = with_count(jnp.sum(terms(row_effect, col_effect), axis=2), jnp.sum(weight, axis=1))
    part, jitter, owner_map, neighbours = lax.optimization_barrier(
        (part, jitter, owner_map, neighbours)
    )

    group_map = owner_map[0]
    group_lists = neighbours[0]
    owned = owned_table(group_map, sixteen_size, BLOCKS_DEV)
    my_ids = lax.dynamic_index_in_dim(owned, my_place, 0, keepdims=False)
    sources = my_ids // BLOCKS_DEV
    my_targets = lax.dynamic_slice_in_dim(group_map, my_place * BLOCKS_DEV, BLOCKS_DEV)
    table = tile_lists(group_lists[0], total_strips)
    row_place = (my_place * row_dev + jnp.arange(row_dev, dtype=jnp.int32)).astype(jnp.float32)
    col_place = (group_place * col_dev + jnp.arange(col_dev, dtype=jnp.int32)).astype(jnp.float32)
    location = jnp.stack(
        [row_place[:, None] + jitter[0], col_place[None, :] + jitter[1]], axis=0
    ).reshape(2, BLOCKS_DEV, STRIP, col_dev)
    location = location.transpose(1, 0, 2, 3).reshape(BLOCKS_DEV, 2 * STRIP, col_dev)
    location = location * (1.0 / CUTOFF)
    none = jnp.zeros((REACH, 2 * STRIP, col_dev), jnp.float32)
    here = jnp.concatenate([none, location, none], axis=0)
    here = (here, here.transpose(0, 2, 1))

    def beside_tiles(part, axis, places, count, tiles, first):
        if first:
            part, places, tiles = lax.optimization_barrier((part, places, tiles))
        total = over_copies(part, axis)
        tiles = covariance_tiles(first, count, table, *places, tiles)
        total, tiles = lax.optimization_barrier((total, tiles))
        return total, tiles, first + count

    total, tiles, first = beside_tiles(part, WIDE, here, ROW_TILES, None, 0)
    total, table, here = lax.optimization_barrier((total, table, here))
    row_count = jnp.maximum(total[fields], 1.0)
    row_effect = huber_scale[:, None] * total[:fields] / row_count[None, :]
    part = with_count(jnp.sum(terms(row_effect, col_effect), axis=1), jnp.sum(weight, axis=0))
    before, after, location = beside(location, REACH)
    total, tiles, first = beside_tiles(part, SIXTEEN, here, COL_TILES, tiles, first)
    total, before, after = lax.optimization_barrier((total, before, after))
    wider = jnp.concatenate([before, location, after], axis=0)
    wider = (wider, wider.transpose(0, 2, 1))
    col_count = jnp.maximum(total[fields], 1.0)
    col_effect = huber_scale[:, None] * total[:fields] / col_count[None, :]
    part = jnp.sum(terms(row_effect, col_effect), axis=2)
    total, tiles, first = beside_tiles(part, WIDE, wider, ROW_TILES, tiles, first)
    row_effect = row_effect + huber_scale[:, None] * total / row_count[None, :]
    part = jnp.sum(terms(row_effect, col_effect), axis=1)
    total, tiles, first = beside_tiles(part, SIXTEEN, wider, COL_TILES, tiles, first)
    col_effect = col_effect + huber_scale[:, None] * total / col_count[None, :]

    r0 = residual_of(observations, weight, row_effect, col_effect)
    before, after, r0 = beside(r0, REACH)
    part = own_product(table, r0, tiles)
    slots = spread(my_targets, r0, part, before, after)
    owned_r0 = to_owners(slots)
    m1 = halo_product(table, my_targets, before, after, part, tiles, False)
    before, after, m1 = beside(m1, REACH)
    part = own_product(table, m1, tiles)
    slots = spread(my_targets, m1, part, before, after)
    slots, owned_r0 = lax.optimization_barrier((slots, owned_r0))
    owned_m1 = to_owners(slots)
    m2, slots = halo_product(table, my_targets, before, after, part, tiles, True)
    dots = jnp.stack(
        [jnp.sum(p * q, axis=(0, 2)) for p, q in ((r0, r0), (r0, m1), (m1, m1), (m1, m2))]
    )
    slots, owned_m1 = lax.optimization_barrier((slots, owned_m1))
    owned_m2 = to_owners(slots)
    for axis in WIDE[::-1] + SIXTEEN[::-1]:
        dots = sum_direct(dots, axis)
    scale = step_scales(*dots)
    solution_now, residual_now = combined(sources, scale, owned_r0, owned_m1, owned_m2)
    return (solution_now[None, None], residual_now[None, None])


def solution(mesh):
    finer = Mesh(mesh.devices.reshape(4, 2, 4, 4), ("wide_0", "wide_1", "sixteen_0", "sixteen_1"))
    in_specs = (
        P(None, SIXTEEN, WIDE),
        P(),
        P(SIXTEEN, WIDE),
        P(None, SIXTEEN, WIDE),
        P(WIDE, None),
        P(WIDE, None, None),
    )
    out_specs = (P(WIDE, SIXTEEN, None, None, None), P(WIDE, SIXTEEN, None, None, None))
    return jax.shard_map(
        on_device, mesh=finer, in_specs=in_specs, out_specs=out_specs, check_vma=False
    )
```

profile of v0, /device:TPU:16, one launch (start us, length us, event | category | flops | bytes accessed | tf_op | source)
XLA Modules:
  0.0 244.8 jit_solution(6818412477681727152)
XLA Ops:
  4.8 4.8 %all-to-all-start = ((f32[8,72,32]{1,2,0:T(8,128)}), f32[8,72,32]{1,2,0:T(8,128)S(1)}, u32[]{:S(2)}, u32[]{:S(2)}) async-start(f32[8,72,32]{1,2,0:T(8,128)} %broadcast_in_dim.34), calls=%async_computation | async-start | bytes 262144 | tf_op jit(solution)/shard_map/all_to_all | solution.py:39
  15.0 6.1 %tiles.4.refs_0_ = bf16[44,1024,512]{2,1,0:T(8,128)(2,1)} custom-call(s32[134]{0:T(256)S(1)} %concatenate.21.table_ref, f32[16,8,128]{2,1,0:T(8,128)S(1)} %copy.104.rows_ref, f32[16,128,8]{2,1,0:T(8,128)S(1)} %get-tuple-element.86.cols_ref), custom_call_target="tpu_custom_call" | custom-call | flops 22020096 | bytes 7340032 | tf_op jit(solution)/shard_map/tiles/pallas_call | solution.py:178
  22.9 7.9 %all-to-all-start.1 = ((f32[16,72,128]{2,1,0:T(8,128)}), f32[16,72,128]{2,1,0:T(8,128)}, u32[]{:S(2)}, u32[]{:S(2)}) async-start(f32[16,72,128]{2,1,0:T(8,128)} %broadcast_in_dim.39), calls=%async_computation.1 | async-start | bytes 1179648 | tf_op jit(solution)/shard_map/all_to_all | solution.py:39
  32.8 3.5 %collective-permute-start.1 = (f32[4,8,128]{2,1,0:T(8,128)S(1)}, f32[4,8,128]{2,1,0:T(8,128)S(1)}, u32[]{:S(2)}, u32[]{:S(2)}) collective-permute-start(f32[4,8,128]{2,1,0:T(8,128)S(1)} %bitcast.86), channel_id=1, source_target_pairs={{1,0},{2,1},{3,2},{4,3},{5,4},{6,5},{7,6},{8,7},{9,8},{10,9},{11,1... | collective-permute-start | bytes 49160 | tf_op jit(solution)/shard_map/ppermute | solution.py:64
  36.6 11.2 %tiles.5.refs_0_ = bf16[44,1024,512]{2,1,0:T(8,128)(2,1)} custom-call(s32[134]{0:T(256)S(1)} %concatenate.21.table_ref, f32[16,8,128]{2,1,0:T(8,128)S(1)} %copy.106.rows_ref, f32[16,128,8]{2,1,0:T(8,128)S(1)} %get-tuple-element.86.cols_ref, bf16[44,1024,512]{2,1,0:T(8,128)(2,1)} %tiles.4.refs_0_), custom_call_target="tpu_custom_call", output_to_operand_aliasing={{}: (3, {})} | custom-call | flops 47185920 | bytes 15728640 | tf_op jit(solution)/shard_map/tiles/pallas_call | solution.py:178
  51.0 4.8 %all-to-all-start.2 = ((f32[8,1,2048]{2,1,0:T(1,128)}), f32[8,1,2048]{2,1,0:T(1,128)S(1)}, u32[]{:S(2)}, u32[]{:S(2)}) async-start(f32[8,1,2048]{2,1,0:T(1,128)} %reshape.449), calls=%async_computation.2 | async-start | bytes 131072 | tf_op jit(solution)/shard_map/all_to_all | solution.py:39
  55.8 5.2 %tiles.6.refs_0_ = bf16[44,1024,512]{2,1,0:T(8,128)(2,1)} custom-call(s32[134]{0:T(256)S(1)} %concatenate.21.table_ref, f32[16,8,128]{2,1,0:T(8,128)S(1)} %constant_dynamic-update-slice_fusion.rows_ref, f32[16,128,8]{2,1,0:T(8,128)S(1)} %bitcast.80, bf16[44,1024,512]{2,1,0:T(8,128)(2,1)} %tiles.5.refs_0_), custom_call_target="tpu_custom_call", output_to_operand_aliasing={{}: (3, {})} | custom-call | flops 22020096 | bytes 7340032 | tf_op jit(solution)/shard_map/tiles/pallas_call | solution.py:178
  64.0 3.8 %all-to-all-start.3 = ((f32[16,64,128]{2,1,0:T(8,128)}), f32[16,64,128]{2,1,0:T(8,128)S(1)}, u32[]{:S(2)}, u32[]{:S(2)}) async-start(f32[16,64,128]{2,1,0:T(8,128)} %broadcast_in_dim.41), calls=%async_computation.3 | async-start | bytes 1048576 | tf_op jit(solution)/shard_map/all_to_all | solution.py:39
  67.9 11.2 %tiles.7.tiles_ref = bf16[44,1024,512]{2,1,0:T(8,128)(2,1)} custom-call(s32[134]{0:T(256)S(1)} %concatenate.21.table_ref, f32[16,8,128]{2,1,0:T(8,128)S(1)} %constant_dynamic-update-slice_fusion.rows_ref, f32[16,128,8]{2,1,0:T(8,128)S(1)} %bitcast.81, bf16[44,1024,512]{2,1,0:T(8,128)(2,1)} %tiles.6.refs_0_), custom_call_target="tpu_custom_call", output_to_operand_aliasing={{}: (3, {})} | custom-call | flops 47185920 | bytes 15728640 | tf_op jit(solution)/shard_map/tiles/pallas_call | solution.py:178
  82.3 4.9 %collective-permute-start.3 = (f32[4,64,512]{2,1,0:T(8,128)S(1)}, f32[4,64,512]{2,1,0:T(8,128)S(1)}, u32[]{:S(2)}, u32[]{:S(2)}) collective-permute-start(f32[4,64,512]{2,1,0:T(8,128)S(1)} %get-tuple-element.109), channel_id=1, source_target_pairs={{1,0},{2,1},{3,2},{4,3},{5,4},{6,5},{7,6},{8,7},{9,8},{10,9},{11,1... | collective-permute-start | bytes 1572872 | tf_op jit(solution)/shard_map/ppermute | solution.py:64
  87.8 13.8 %own.2.part_ref.refs_0_ = f32[8,64,512]{2,1,0:T(8,128)S(1)} custom-call(s32[134]{0:T(256)S(1)} %concatenate.21.table_ref, f32[8,64,512]{2,1,0:T(8,128)S(1)} %residual.1.v_ref, bf16[44,1024,512]{2,1,0:T(8,128)(2,1)} %tiles.7.tiles_ref), custom_call_target="tpu_custom_call" | custom-call | flops 4227858432 | bytes 27262976 | tf_op jit(solution)/shard_map/own/pallas_call | solution.py:331
  104.3 2.9 %spread.3 = f32[16,64,512]{2,1,0:T(8,128)} custom-call(s32[8]{0:T(128)} %dynamic-slice_bitcast_fusion.target_ref, f32[8,64,512]{2,1,0:T(8,128)} %copy-done.3, f32[8,64,512]{2,1,0:T(8,128)} %copy-done.7, f32[4,64,512]{2,1,0:T(8,128)} %copy-done.9, f32[4,64,512]{2,1,0:T(8,128)} %copy-done.13), custom_call_target="tpu_custom_call" | custom-call | tf_op jit(solution)/shard_map/spread/pallas_call | solution.py:353
  107.2 3.7 %all-to-all-start.4 = ((f32[16,64,512]{2,1,0:T(8,128)}), f32[16,64,512]{2,1,0:T(8,128)S(1)}, u32[]{:S(2)}, u32[]{:S(2)}) async-start(f32[16,64,512]{2,1,0:T(8,128)} %spread.3), calls=%async_computation.4 | async-start | bytes 4194304 | tf_op jit(solution)/shard_map/all_to_all | solution.py:439
  114.2 8.0 %halo.2.v_ref = f32[8,64,512]{2,1,0:T(8,128)S(1)} custom-call(s32[134]{0:T(256)S(1)} %concatenate.21.table_ref, s32[8]{0:T(128)S(1)} %copy-done.15, f32[4,64,512]{2,1,0:T(8,128)S(1)} %copy-done.10, f32[4,64,512]{2,1,0:T(8,128)S(1)} %copy-done.14, f32[8,64,512]{2,1,0:T(8,128)S(1)} %copy-done.8, bf16[44,1024,512]{2,1,0:T(8,128)(2,1)} %tiles.7.tiles_ref), custom_call_target="tpu_custom_call" | custom-call | flops 1811939328 | bytes 18874368 | tf_op jit(solution)/shard_map/halo/pallas_call | solution.py:365
  124.3 3.7 %collective-permute-start.5 = (f32[4,64,512]{2,1,0:T(8,128)S(1)}, f32[4,64,512]{2,1,0:T(8,128)}, u32[]{:S(2)}, u32[]{:S(2)}) collective-permute-start(f32[4,64,512]{2,1,0:T(8,128)S(1)} %get-tuple-element.113), channel_id=1, source_target_pairs={{1,0},{2,1},{3,2},{4,3},{5,4},{6,5},{7,6},{8,7},{9,8},{10,9},{11,1... | collective-permute-start | bytes 1572872 | tf_op jit(solution)/shard_map/ppermute | solution.py:64
  127.9 13.8 %own.3.part_ref.refs_0_ = f32[8,64,512]{2,1,0:T(8,128)S(1)} custom-call(s32[134]{0:T(256)S(1)} %concatenate.21.table_ref, f32[8,64,512]{2,1,0:T(8,128)S(1)} %halo.2.v_ref, bf16[44,1024,512]{2,1,0:T(8,128)(2,1)} %tiles.7.tiles_ref), custom_call_target="tpu_custom_call" | custom-call | flops 4227858432 | bytes 27262976 | tf_op jit(solution)/shard_map/own/pallas_call | solution.py:331
  142.7 10.9 %collective-permute-done.4.before_ref.refs_1_ = f32[4,64,512]{2,1,0:T(8,128)S(1)} collective-permute-done((f32[4,64,512]{2,1,0:T(8,128)S(1)}, f32[4,64,512]{2,1,0:T(8,128)S(1)}, u32[]{:S(2)}, u32[]{:S(2)}) %collective-permute-start.4) | collective-permute-done | bytes 524320 | tf_op jit(solution)/shard_map/ppermute | solution.py:64
  157.4 9.3 %all-to-all-start.5 = ((f32[16,64,512]{2,1,0:T(8,128)}), f32[16,64,512]{2,1,0:T(8,128)}, u32[]{:S(2)}, u32[]{:S(2)}) async-start(f32[16,64,512]{2,1,0:T(8,128)} %spread.2), calls=%async_computation.5 | async-start | bytes 4194304 | tf_op jit(solution)/shard_map/all_to_all | solution.py:439
  167.8 9.6 %halo.3 = (f32[8,64,512]{2,1,0:T(8,128)S(1)}, f32[16,64,512]{2,1,0:T(8,128)}) custom-call(s32[134]{0:T(256)S(1)} %concatenate.21.table_ref, s32[8]{0:T(128)S(1)} %copy-done.16, f32[4,64,512]{2,1,0:T(8,128)S(1)} %copy-done.12, f32[4,64,512]{2,1,0:T(8,128)} %collective-permute-done.5.after_ref.refs_2_, f32[8,64,512]{2,1,0:T(8,128)S(1)} %copy-done.6, ...), custom_call_target="tpu_custom_call" | custom-call | flops 1811939328 | bytes 18874368 | tf_op jit(solution)/shard_map/halo/pallas_call | solution.py:365
  178.2 21.3 %all-to-all-done.5.refs_1_.refs_4_.refs_7_.refs_10_.refs_13_.refs_16_.refs_19_.refs_22_ = f32[16,64,512]{2,1,0:T(8,128)} async-done(((f32[16,64,512]{2,1,0:T(8,128)}), f32[16,64,512]{2,1,0:T(8,128)}, u32[]{:S(2)}, u32[]{:S(2)}) %all-to-all-start.5) | async-done | bytes 2097184 | tf_op jit(solution)/shard_map/all_to_all | solution.py:439
  199.5 4.4 %all-to-all-start.6 = ((f32[16,64,512]{2,1,0:T(8,128)}), f32[16,64,512]{2,1,0:T(8,128)}, u32[]{:S(2)}, u32[]{:S(2)}) async-start(f32[16,64,512]{2,1,0:T(8,128)} %get-tuple-element.119), calls=%async_computation.6 | async-start | bytes 4194304 | tf_op jit(solution)/shard_map/all_to_all | solution.py:439
  216.0 12.9 %collective-permute-done.10 = f32[4,64]{1,0:T(4,128)S(1)} collective-permute-done((f32[4,64]{1,0:T(4,128)S(1)}, f32[4,64]{1,0:T(4,128)S(1)}, u32[]{:S(2)}, u32[]{:S(2)}) %collective-permute-start.10) | collective-permute-done | bytes 1056 | tf_op jit(solution)/shard_map/ppermute | solution.py:51
  228.9 4.0 %collective-permute-done.11 = f32[4,64]{1,0:T(4,128)S(1)} collective-permute-done((f32[4,64]{1,0:T(4,128)S(1)}, f32[4,64]{1,0:T(4,128)S(1)}, u32[]{:S(2)}, u32[]{:S(2)}) %collective-permute-start.11) | collective-permute-done | bytes 1056 | tf_op jit(solution)/shard_map/ppermute | solution.py:51
  240.0 4.7 %combine.1 = (f32[64,8,512]{2,1,0:T(8,128)}, f32[64,8,512]{2,1,0:T(8,128)}) custom-call(s32[8]{0:T(128)S(1)} %and_select_fusion.1.src_ref, f32[64,8]{1,0:T(8,128)S(1)} %copy.113.scale_ref, f32[16,64,512]{2,1,0:T(8,128)S(1)} %all-to-all-done.4.refs_0_.refs_3_.refs_6_.refs_9_.refs_12_.refs_15_.refs_18_.refs_21_, ...), custom_call_target="tpu_custom_call" | custom-call | tf_op jit(solution)/shard_map/combine/pallas_call | solution.py:424
  (148 shorter events, 55.1 us)
Async XLA Ops:
  4.8 16.4 %all-to-all-start = ((f32[8,72,32]{1,2,0:T(8,128)}), f32[8,72,32]{1,2,0:T(8,128)S(1)}, u32[]{:S(2)}, u32[]{:S(2)}) async-start(f32[8,72,32]{1,2,0:T(8,128)} %broadcast_in_dim.34), calls=%async_computation | async-start | bytes 262144 | tf_op jit(solution)/shard_map/all_to_all | solution.py:39
  22.9 24.9 %all-to-all-start.1 = ((f32[16,72,128]{2,1,0:T(8,128)}), f32[16,72,128]{2,1,0:T(8,128)}, u32[]{:S(2)}, u32[]{:S(2)}) async-start(f32[16,72,128]{2,1,0:T(8,128)} %broadcast_in_dim.39), calls=%async_computation.1 | async-start | bytes 1179648 | tf_op jit(solution)/shard_map/all_to_all | solution.py:39
  30.8 18.1 %collective-permute-start = (f32[4,8,128]{2,1,0:T(8,128)S(1)}, f32[4,8,128]{2,1,0:T(8,128)S(1)}, u32[]{:S(2)}, u32[]{:S(2)}) collective-permute-start(f32[4,8,128]{2,1,0:T(8,128)S(1)} %bitcast.87), channel_id=1, source_target_pairs={{0,1},{1,2},{2,3},{3,4},{4,5},{5,6},{6,7},{7,8},{8,9},{9,10},{10,1... | collective-permute-start | bytes 49160 | tf_op jit(solution)/shard_map/ppermute | solution.py:64
  32.8 16.1 %collective-permute-start.1 = (f32[4,8,128]{2,1,0:T(8,128)S(1)}, f32[4,8,128]{2,1,0:T(8,128)S(1)}, u32[]{:S(2)}, u32[]{:S(2)}) collective-permute-start(f32[4,8,128]{2,1,0:T(8,128)S(1)} %bitcast.86), channel_id=1, source_target_pairs={{1,0},{2,1},{3,2},{4,3},{5,4},{6,5},{7,6},{8,7},{9,8},{10,9},{11,1... | collective-permute-start | bytes 49160 | tf_op jit(solution)/shard_map/ppermute | solution.py:64
  51.0 10.0 %all-to-all-start.2 = ((f32[8,1,2048]{2,1,0:T(1,128)}), f32[8,1,2048]{2,1,0:T(1,128)S(1)}, u32[]{:S(2)}, u32[]{:S(2)}) async-start(f32[8,1,2048]{2,1,0:T(1,128)} %reshape.449), calls=%async_computation.2 | async-start | bytes 131072 | tf_op jit(solution)/shard_map/all_to_all | solution.py:39
  64.0 16.9 %all-to-all-start.3 = ((f32[16,64,128]{2,1,0:T(8,128)}), f32[16,64,128]{2,1,0:T(8,128)S(1)}, u32[]{:S(2)}, u32[]{:S(2)}) async-start(f32[16,64,128]{2,1,0:T(8,128)} %broadcast_in_dim.41), calls=%async_computation.3 | async-start | bytes 1048576 | tf_op jit(solution)/shard_map/all_to_all | solution.py:39
  81.7 20.0 %copy-start.3 = (f32[8,64,512]{2,1,0:T(8,128)}, f32[8,64,512]{2,1,0:T(8,128)S(1)}, u32[]{:S(2)}) copy-start(f32[8,64,512]{2,1,0:T(8,128)S(1)} %residual.1.v_ref) | copy-start | bytes 3145732
  81.8 20.9 %collective-permute-start.2 = (f32[4,64,512]{2,1,0:T(8,128)S(1)}, f32[4,64,512]{2,1,0:T(8,128)S(1)}, u32[]{:S(2)}, u32[]{:S(2)}) collective-permute-start(f32[4,64,512]{2,1,0:T(8,128)S(1)} %get-tuple-element.108), channel_id=1, source_target_pairs={{0,1},{1,2},{2,3},{3,4},{4,5},{5,6},{6,7},{7,8},{8,9},{9,10},{10,1... | collective-permute-start | bytes 1572872 | tf_op jit(solution)/shard_map/ppermute | solution.py:64
  82.3 20.3 %collective-permute-start.3 = (f32[4,64,512]{2,1,0:T(8,128)S(1)}, f32[4,64,512]{2,1,0:T(8,128)S(1)}, u32[]{:S(2)}, u32[]{:S(2)}) collective-permute-start(f32[4,64,512]{2,1,0:T(8,128)S(1)} %get-tuple-element.109), channel_id=1, source_target_pairs={{1,0},{2,1},{3,2},{4,3},{5,4},{6,5},{7,6},{8,7},{9,8},{10,9},{11,1... | collective-permute-start | bytes 1572872 | tf_op jit(solution)/shard_map/ppermute | solution.py:64
  107.2 50.2 %all-to-all-start.4 = ((f32[16,64,512]{2,1,0:T(8,128)}), f32[16,64,512]{2,1,0:T(8,128)S(1)}, u32[]{:S(2)}, u32[]{:S(2)}) async-start(f32[16,64,512]{2,1,0:T(8,128)} %spread.3), calls=%async_computation.4 | async-start | bytes 4194304 | tf_op jit(solution)/shard_map/all_to_all | solution.py:439
  122.4 31.2 %collective-permute-start.4 = (f32[4,64,512]{2,1,0:T(8,128)S(1)}, f32[4,64,512]{2,1,0:T(8,128)S(1)}, u32[]{:S(2)}, u32[]{:S(2)}) collective-permute-start(f32[4,64,512]{2,1,0:T(8,128)S(1)} %get-tuple-element.112), channel_id=1, source_target_pairs={{0,1},{1,2},{2,3},{3,4},{4,5},{5,6},{6,7},{7,8},{8,9},{9,10},{10,1... | collective-permute-start | bytes 1572872 | tf_op jit(solution)/shard_map/ppermute | solution.py:64
  124.3 30.2 %collective-permute-start.5 = (f32[4,64,512]{2,1,0:T(8,128)S(1)}, f32[4,64,512]{2,1,0:T(8,128)}, u32[]{:S(2)}, u32[]{:S(2)}) collective-permute-start(f32[4,64,512]{2,1,0:T(8,128)S(1)} %get-tuple-element.113), channel_id=1, source_target_pairs={{1,0},{2,1},{3,2},{4,3},{5,4},{6,5},{7,6},{8,7},{9,8},{10,9},{11,1... | collective-permute-start | bytes 1572872 | tf_op jit(solution)/shard_map/ppermute | solution.py:64
  157.4 42.1 %all-to-all-start.5 = ((f32[16,64,512]{2,1,0:T(8,128)}), f32[16,64,512]{2,1,0:T(8,128)}, u32[]{:S(2)}, u32[]{:S(2)}) async-start(f32[16,64,512]{2,1,0:T(8,128)} %spread.2), calls=%async_computation.5 | async-start | bytes 4194304 | tf_op jit(solution)/shard_map/all_to_all | solution.py:439
  177.8 26.1 %collective-permute-start.6 = (f32[4,64]{1,0:T(4,128)S(1)}, f32[4,64]{1,0:T(4,128)S(1)}, u32[]{:S(2)}, u32[]{:S(2)}) collective-permute-start(f32[4,64]{1,0:T(4,128)S(1)} %pad_maximum_fusion.1), channel_id=1, source_target_pairs={{0,16},{16,0},{1,17},{17,1},{2,18},{18,2},{3,19},{19,3},{4,20},{20... | collective-permute-start | bytes 3080 | tf_op jit(solution)/shard_map/ppermute | solution.py:51
  199.5 40.6 %all-to-all-start.6 = ((f32[16,64,512]{2,1,0:T(8,128)}), f32[16,64,512]{2,1,0:T(8,128)}, u32[]{:S(2)}, u32[]{:S(2)}) async-start(f32[16,64,512]{2,1,0:T(8,128)} %get-tuple-element.119), calls=%async_computation.6 | async-start | bytes 4194304 | tf_op jit(solution)/shard_map/all_to_all | solution.py:439
  203.9 3.7 %collective-permute-start.7 = (f32[4,64]{1,0:T(4,128)S(1)}, f32[4,64]{1,0:T(4,128)S(1)}, u32[]{:S(2)}, u32[]{:S(2)}) collective-permute-start(f32[4,64]{1,0:T(4,128)S(1)} %fusion.13), channel_id=1, source_target_pairs={{0,32},{32,64},{64,96},{96,0},{1,33},{33,65},{65,97},{97,1},{2,34}... | collective-permute-start | bytes 3080 | tf_op jit(solution)/shard_map/ppermute | solution.py:51
  204.0 5.2 %collective-permute-start.8 = (f32[4,64]{1,0:T(4,128)S(1)}, f32[4,64]{1,0:T(4,128)S(1)}, u32[]{:S(2)}, u32[]{:S(2)}) collective-permute-start(f32[4,64]{1,0:T(4,128)S(1)} %fusion.13), channel_id=1, source_target_pairs={{0,64},{32,96},{64,0},{96,32},{1,65},{33,97},{65,1},{97,33},{2,66}... | collective-permute-start | bytes 3080 | tf_op jit(solution)/shard_map/ppermute | solution.py:51
  204.1 5.6 %collective-permute-start.9 = (f32[4,64]{1,0:T(4,128)S(1)}, f32[4,64]{1,0:T(4,128)S(1)}, u32[]{:S(2)}, u32[]{:S(2)}) collective-permute-start(f32[4,64]{1,0:T(4,128)S(1)} %fusion.13), channel_id=1, source_target_pairs={{0,96},{32,0},{64,32},{96,64},{1,97},{33,1},{65,33},{97,65},{2,98}... | collective-permute-start | bytes 3080 | tf_op jit(solution)/shard_map/ppermute | solution.py:51
  209.7 19.2 %collective-permute-start.10 = (f32[4,64]{1,0:T(4,128)S(1)}, f32[4,64]{1,0:T(4,128)S(1)}, u32[]{:S(2)}, u32[]{:S(2)}) collective-permute-start(f32[4,64]{1,0:T(4,128)S(1)} %add_add_fusion.2), channel_id=1, source_target_pairs={{0,1},{1,2},{2,3},{3,0},{4,5},{5,6},{6,7},{7,4},{8,9},{9,10},{10,1... | collective-permute-start | bytes 3080 | tf_op jit(solution)/shard_map/ppermute | solution.py:51
  211.5 21.4 %collective-permute-start.11 = (f32[4,64]{1,0:T(4,128)S(1)}, f32[4,64]{1,0:T(4,128)S(1)}, u32[]{:S(2)}, u32[]{:S(2)}) collective-permute-start(f32[4,64]{1,0:T(4,128)S(1)} %add_add_fusion.2), channel_id=1, source_target_pairs={{0,2},{1,3},{2,0},{3,1},{4,6},{5,7},{6,4},{7,5},{8,10},{9,11},{10,... | collective-permute-start | bytes 3080 | tf_op jit(solution)/shard_map/ppermute | solution.py:51
  214.2 18.7 %collective-permute-start.12 = (f32[4,64]{1,0:T(4,128)S(1)}, f32[4,64]{1,0:T(4,128)S(1)}, u32[]{:S(2)}, u32[]{:S(2)}) collective-permute-start(f32[4,64]{1,0:T(4,128)S(1)} %add_add_fusion.2), channel_id=1, source_target_pairs={{0,3},{1,0},{2,1},{3,2},{4,7},{5,4},{6,5},{7,6},{8,11},{9,8},{10,9... | collective-permute-start | bytes 3080 | tf_op jit(solution)/shard_map/ppermute | solution.py:51
  232.9 5.6 %collective-permute-start.13 = (f32[4,64]{1,0:T(4,128)S(1)}, f32[4,64]{1,0:T(4,128)S(1)}, u32[]{:S(2)}, u32[]{:S(2)}) collective-permute-start(f32[4,64]{1,0:T(4,128)S(1)} %add_add_fusion.1), channel_id=1, source_target_pairs={{0,4},{4,8},{8,12},{12,0},{1,5},{5,9},{9,13},{13,1},{2,6},{6,10},{... | collective-permute-start | bytes 3080 | tf_op jit(solution)/shard_map/ppermute | solution.py:51
  233.5 5.1 %collective-permute-start.14 = (f32[4,64]{1,0:T(4,128)S(1)}, f32[4,64]{1,0:T(4,128)S(1)}, u32[]{:S(2)}, u32[]{:S(2)}) collective-permute-start(f32[4,64]{1,0:T(4,128)S(1)} %add_add_fusion.1), channel_id=1, source_target_pairs={{0,8},{4,12},{8,0},{12,4},{1,9},{5,13},{9,1},{13,5},{2,10},{6,14},... | collective-permute-start | bytes 3080 | tf_op jit(solution)/shard_map/ppermute | solution.py:51
  236.3 3.6 %collective-permute-start.15 = (f32[4,64]{1,0:T(4,128)S(1)}, f32[4,64]{1,0:T(4,128)S(1)}, u32[]{:S(2)}, u32[]{:S(2)}) collective-permute-start(f32[4,64]{1,0:T(4,128)S(1)} %add_add_fusion.1), channel_id=1, source_target_pairs={{0,12},{4,0},{8,4},{12,8},{1,13},{5,1},{9,5},{13,9},{2,14},{6,2},{... | collective-permute-start | bytes 3080 | tf_op jit(solution)/shard_map/ppermute | solution.py:51
  (18 other events, 89.0 us)
where the time goes:
time: 242 us; the launch traced here: 245 us
  Pallas kernels  90.1 us (37%)
  starting transfers between devices  68.9 us (28%)
  waiting for transfers between devices  55.9 us (23%)
  local copies, waits for them, and re-layouts  15.9 us (7%)
  other arithmetic  10.6 us (4%)
  between operations  3.42 us (1%)
    pallas_call x4, Pallas kernels, covariance_tiles(): pl.pallas_call(functools.partial(tiles_kernel, first, count, len(extra)),...  33.7 us
    pallas_call x2, Pallas kernels, own_product(): pl.pallas_call(own_kernel, in_specs=[SMEM_SPEC, VMEM_SPEC, HBM_SPEC], out...  27.6 us
    ppermute x10, waiting for transfers between devices, sum_direct(): lax.ppermute(part, axis, [(i, (i + k) % peers) for i in range(peers)])  21.9 us
    all_to_all x4, starting transfers between devices, sent_to_all(): lax.all_to_all(jnp.broadcast_to(shard[None], (peers, *shard.shape)), axis...  21.4 us
    all_to_all x3, waiting for transfers between devices, to_owners(): return lax.all_to_all(slots, SIXTEEN, 0, 0, tiled=True)  21.3 us
    pallas_call x2, Pallas kernels, halo_product(): pl.pallas_call(halo_kernel, in_specs=[SMEM_SPEC, SMEM_SPEC, VMEM_SPEC, VM...  17.7 us
    all_to_all x3, starting transfers between devices, to_owners(): return lax.all_to_all(slots, SIXTEEN, 0, 0, tiled=True)  17.5 us
    ppermute x10, starting transfers between devices, sum_direct(): lax.ppermute(part, axis, [(i, (i + k) % peers) for i in range(peers)])  13.7 us
  transfers between devices with their start and end apart: 23, of which 11 were waited for; matrix products, arithmetic and copies ran while one was open for 3% of the time, Pallas kernels for 33%

commit v1 on v0

--- a/solution.py
+++ b/solution.py
@@ -29,7 +29,7 @@
 
 OWN_TILES = BLOCKS_DEV + PAIRED * BLOCKS_DEV - 6
 HALO_TILES = 2 * (2 + 3 + 4)
-ROW_TILES, COL_TILES = 7, 15
+ROW_TILES, COL_TILES = 13, 9
 TILE_SLOTS = 4
 OP_SLOTS = 5
 
@@ -185,7 +185,7 @@
         ],
         out_shape=jax.ShapeDtypeStruct((LISTED, 2 * BLOCK, BLOCK), jnp.bfloat16),
         input_output_aliases={3: 0} if extra else {},
-        compiler_params=pltpu.CompilerParams(vmem_limit_bytes=32 << 20),
+        compiler_params=pltpu.CompilerParams(vmem_limit_bytes=12 << 20),
         cost_estimate=pl.CostEstimate(
             flops=count * 12 * BLOCK * BLOCK,
             bytes_accessed=count * 4 * BLOCK * BLOCK,
@@ -334,7 +334,7 @@
         out_specs=VMEM_SPEC,
         scratch_shapes=[pltpu.VMEM((blocks, 2 * fields, BLOCK), jnp.bfloat16)] + stream_scratch(),
         out_shape=jax.ShapeDtypeStruct(v.shape, jnp.float32),
-        compiler_params=pltpu.CompilerParams(vmem_limit_bytes=32 << 20),
+        compiler_params=pltpu.CompilerParams(vmem_limit_bytes=12 << 20),
         cost_estimate=product_cost(OWN_TILES, 42, fields),
         name="own",
     )(table, v, tiles)
@@ -349,13 +349,15 @@
         copy_out.wait()
 
 
-def spread(targets, v, *behind):
+def spread(targets, v, *others):
+    behind = [functools.reduce(jnp.add, [other[0, :8, :COL_DEV] for other in others])]
     return pl.pallas_call(
         spread_kernel,
         in_specs=[SMEM_SPEC] + [VMEM_SPEC] * (1 + len(behind)),
         out_specs=HBM_SPEC,
         scratch_shapes=[pltpu.SemaphoreType.DMA((BLOCKS_DEV,))],
         out_shape=slot_shape(v),
+        compiler_params=pltpu.CompilerParams(vmem_limit_bytes=1 << 20),
         name="spread",
     )(targets, v, *behind)
 
@@ -370,7 +372,7 @@
         + stream_scratch()
         + [pltpu.SemaphoreType.DMA((BLOCKS_DEV,))],
         out_shape=[jax.ShapeDtypeStruct(part.shape, jnp.float32)] + [slot_shape(part)] * send,
-        compiler_params=pltpu.CompilerParams(vmem_limit_bytes=32 << 20),
+        compiler_params=pltpu.CompilerParams(vmem_limit_bytes=12 << 20),
         cost_estimate=product_cost(HALO_TILES, HALO_TILES, fields),
         name="halo",
     )(table, targets, before, after, part, tiles)
@@ -393,46 +395,97 @@
         in_specs=[VMEM_SPEC] * 4,
         out_specs=VMEM_SPEC,
         out_shape=jax.ShapeDtypeStruct((BLOCKS_DEV, fields, BLOCK), jnp.float32),
-        compiler_params=pltpu.CompilerParams(vmem_limit_bytes=32 << 20),
+        compiler_params=pltpu.CompilerParams(vmem_limit_bytes=8 << 20),
         name="residual",
     )(observations, weight, row_effect, col_effect)
 
 
-def combine_kernel(src_ref, scale_ref, *refs):
+def observed_kernel(target_ref, obs_ref, one_ref, two_ref, buf, sem):
+    half = obs_ref.shape[0] // 2
+    for g in range(BLOCKS_DEV):
+        for ra in range(STRIP):
+            lanes = slice(COL_DEV * ra, COL_DEV * (ra + 1))
+            buf[g, :, lanes] = obs_ref[:, STRIP * g + ra, :]
+        for side, slots_ref in enumerate((one_ref, two_ref)):
+            pltpu.make_async_copy(
+                buf.at[g, pl.ds(half * side, half)], slots_ref.at[target_ref[g]], sem.at[side, g]
+            ).start()
+    for g in range(BLOCKS_DEV):
+        for side, slots_ref in enumerate((one_ref, two_ref)):
+            pltpu.make_async_copy(
+                buf.at[g, pl.ds(half * side, half)], slots_ref.at[target_ref[g]], sem.at[side, g]
+            ).wait()
+
+
+def observed_slots(targets, observations):
+    fields = observations.shape[0]
+    shape = pltpu.HBM((lax.axis_size(SIXTEEN), fields // 2, BLOCK), jnp.float32)
+    return pl.pallas_call(
+        observed_kernel,
+        in_specs=[SMEM_SPEC, VMEM_SPEC],
+        out_specs=[HBM_SPEC] * 2,
+        scratch_shapes=[
+            pltpu.VMEM((BLOCKS_DEV, fields, BLOCK), jnp.float32),
+            pltpu.SemaphoreType.DMA((2, BLOCKS_DEV)),
+        ],
+        out_shape=[shape] * 2,
+        compiler_params=pltpu.CompilerParams(vmem_limit_bytes=12 << 20),
+        name="observed",
+    )(targets, observations)
+
+
+def combine_kernel(src_ref, scale_ref, col_ref, weight_ref, row_ref, *refs):
     ins, (x_ref, r_ref) = refs[:-2], refs[-2:]
-    scale = scale_ref[...]
+
+    def with_half(half):
+        for j in range(BLOCKS_DEV):
+            obs_ref, m1_ref, m2_ref = ins[4 * j + half], ins[4 * j + 2], ins[4 * j + 3]
+            for ra in range(STRIP):
+                lanes = slice(COL_DEV * ra, COL_DEV * (ra + 1))
+                left = obs_ref[0, :, lanes] - row_ref[j, :, ra : ra + 1] - col_ref[...]
+                r0 = weight_ref[j : j + 1, lanes] * left
+                m1, m2 = m1_ref[0, :, lanes], m2_ref[0, :, lanes]
+                x_ref[:, j, lanes] = scale_ref[:, 0:1] * r0 + scale_ref[:, 1:2] * m1
+                r_ref[:, j, lanes] = (
+                    scale_ref[:, 2:3] * r0 + scale_ref[:, 3:4] * m1 + scale_ref[:, 4:5] * m2
+                )
+
+    for half in range(2):
+        pl.when(pl.program_id(0) == half)(functools.partial(with_half, half))
+
+
+def combined(sources, scale, col_effect, weight, rows, obs_one, obs_two, m1, m2):
+    fields = m2.shape[1]
+    part = fields // 2
+    ins, specs = [], []
+
+    def chosen(j, at):
+        return pl.BlockSpec((1, part, BLOCK), lambda i, s: (s[j], at(i), 0))
+
     for j in range(BLOCKS_DEV):
-        r0, m1, m2 = (ref[0] for ref in ins[3 * j : 3 * j + 3])
-        x_ref[:, j, :] = scale[:, 0:1] * r0 + scale[:, 1:2] * m1
-        r_ref[:, j, :] = scale[:, 2:3] * r0 + scale[:, 3:4] * m1 + scale[:, 4:5] * m2
-
-
-def combined(sources, scale, r0, m1, m2):
-    fields = r0.shape[1]
-    part = 16
-    ins, specs = [], []
-    for j in range(BLOCKS_DEV):
-        for v in (r0, m1, m2):
-            ins.append(v)
-            specs.append(
-                pl.BlockSpec(
-                    (1, part, BLOCK), functools.partial(lambda j, i, s: (s[j], i, 0), j)
-                )
-            )
+        ins += [obs_one, obs_two, m1, m2]
+        specs += [chosen(j, lambda i: 0)] * 2 + [chosen(j, lambda i: i)] * 2
     out = pl.BlockSpec((part, BLOCKS_DEV, BLOCK), lambda i, s: (i, 0, 0))
     shape = jax.ShapeDtypeStruct((fields, BLOCKS_DEV, BLOCK), jnp.float32)
+    by_field = lambda lanes: pl.BlockSpec((part, lanes), lambda i, s: (i, 0))
     return pl.pallas_call(
         combine_kernel,
         grid_spec=pltpu.PrefetchScalarGridSpec(
             num_scalar_prefetch=1,
-            grid=(fields // part,),
-            in_specs=[pl.BlockSpec((part, 8), lambda i, s: (i, 0))] + specs,
+            grid=(2,),
+            in_specs=[
+                by_field(8),
+                by_field(COL_DEV),
+                pl.BlockSpec(weight.shape, lambda i, s: (0, 0)),
+                pl.BlockSpec((BLOCKS_DEV, part, STRIP), lambda i, s: (0, i, 0)),
+            ]
+            + specs,
             out_specs=[out, out],
         ),
         out_shape=[shape, shape],
-        compiler_params=pltpu.CompilerParams(vmem_limit_bytes=32 << 20),
+        compiler_params=pltpu.CompilerParams(vmem_limit_bytes=20 << 20),
         name="combine",
-    )(sources, scale, *ins)
+    )(sources, scale, col_effect, weight, rows, *ins)
 
 
 def to_owners(slots):
@@ -475,6 +528,11 @@
             HUBER_EDGE,
         )
 
+    def sum_wide(part):
+        for axis in WIDE[::-1]:
+            part = sum_direct(part, axis)
+        return part
+
     row_effect = jnp.zeros((fields, row_dev), jnp.float32)
     col_effect = jnp.zeros((fields, col_dev), jnp.float32)
     part = with_count(jnp.sum(terms(row_effect, col_effect), axis=2), jnp.sum(weight, axis=1))
@@ -484,10 +542,11 @@
 
     group_map = owner_map[0]
     group_lists = neighbours[0]
+    my_targets = lax.dynamic_slice_in_dim(group_map, my_place * BLOCKS_DEV, BLOCKS_DEV)
+    sent_one, sent_two = observed_slots(my_targets, observations)
     owned = owned_table(group_map, sixteen_size, BLOCKS_DEV)
     my_ids = lax.dynamic_index_in_dim(owned, my_place, 0, keepdims=False)
     sources = my_ids // BLOCKS_DEV
-    my_targets = lax.dynamic_slice_in_dim(group_map, my_place * BLOCKS_DEV, BLOCKS_DEV)
     table = tile_lists(group_lists[0], total_strips)
     row_place = (my_place * row_dev + jnp.arange(row_dev, dtype=jnp.int32)).astype(jnp.float32)
     col_place = (group_place * col_dev + jnp.arange(col_dev, dtype=jnp.int32)).astype(jnp.float32)
@@ -500,54 +559,63 @@
     here = jnp.concatenate([none, location, none], axis=0)
     here = (here, here.transpose(0, 2, 1))
 
-    def beside_tiles(part, axis, places, count, tiles, first):
-        if first:
-            part, places, tiles = lax.optimization_barrier((part, places, tiles))
-        total = over_copies(part, axis)
-        tiles = covariance_tiles(first, count, table, *places, tiles)
-        total, tiles = lax.optimization_barrier((total, tiles))
-        return total, tiles, first + count
-
-    total, tiles, first = beside_tiles(part, WIDE, here, ROW_TILES, None, 0)
-    total, table, here = lax.optimization_barrier((total, table, here))
+    owned_one = to_owners(sent_one)
+    total = sum_wide(part)
+    tiles = covariance_tiles(0, ROW_TILES, table, *here, None)
+    total, tiles, owned_one = lax.optimization_barrier((total, tiles, owned_one))
     row_count = jnp.maximum(total[fields], 1.0)
     row_effect = huber_scale[:, None] * total[:fields] / row_count[None, :]
     part = with_count(jnp.sum(terms(row_effect, col_effect), axis=1), jnp.sum(weight, axis=0))
     before, after, location = beside(location, REACH)
-    total, tiles, first = beside_tiles(part, SIXTEEN, here, COL_TILES, tiles, first)
-    total, before, after = lax.optimization_barrier((total, before, after))
+    part, here, tiles = lax.optimization_barrier((part, here, tiles))
+    total = over_copies(part, SIXTEEN)
+    tiles = covariance_tiles(ROW_TILES, COL_TILES, table, *here, tiles)
+    total, tiles, before, after = lax.optimization_barrier((total, tiles, before, after))
     wider = jnp.concatenate([before, location, after], axis=0)
     wider = (wider, wider.transpose(0, 2, 1))
     col_count = jnp.maximum(total[fields], 1.0)
     col_effect = huber_scale[:, None] * total[:fields] / col_count[None, :]
     part = jnp.sum(terms(row_effect, col_effect), axis=2)
-    total, tiles, first = beside_tiles(part, WIDE, wider, ROW_TILES, tiles, first)
+    part, wider, tiles, sent_two = lax.optimization_barrier((part, wider, tiles, sent_two))
+    owned_two = to_owners(sent_two)
+    total = sum_wide(part)
+    tiles = covariance_tiles(ROW_TILES + COL_TILES, ROW_TILES, table, *wider, tiles)
+    total, tiles, owned_two = lax.optimization_barrier((total, tiles, owned_two))
     row_effect = row_effect + huber_scale[:, None] * total / row_count[None, :]
     part = jnp.sum(terms(row_effect, col_effect), axis=1)
-    total, tiles, first = beside_tiles(part, SIXTEEN, wider, COL_TILES, tiles, first)
+    part, tiles = lax.optimization_barrier((part, tiles))
+    total = over_copies(part, SIXTEEN)
+    tiles = covariance_tiles(2 * ROW_TILES + COL_TILES, COL_TILES, table, *wider, tiles)
+    total, tiles = lax.optimization_barrier((total, tiles))
     col_effect = col_effect + huber_scale[:, None] * total / col_count[None, :]
+    all_rows = lax.all_gather(
+        row_effect.T.reshape(BLOCKS_DEV, STRIP, fields), SIXTEEN, axis=0, tiled=True
+    )
+    all_weights = lax.all_gather(weight.reshape(BLOCKS_DEV, BLOCK), SIXTEEN, axis=0, tiled=True)
 
     r0 = residual_of(observations, weight, row_effect, col_effect)
     before, after, r0 = beside(r0, REACH)
     part = own_product(table, r0, tiles)
-    slots = spread(my_targets, r0, part, before, after)
-    owned_r0 = to_owners(slots)
     m1 = halo_product(table, my_targets, before, after, part, tiles, False)
     before, after, m1 = beside(m1, REACH)
     part = own_product(table, m1, tiles)
     slots = spread(my_targets, m1, part, before, after)
-    slots, owned_r0 = lax.optimization_barrier((slots, owned_r0))
     owned_m1 = to_owners(slots)
     m2, slots = halo_product(table, my_targets, before, after, part, tiles, True)
     dots = jnp.stack(
         [jnp.sum(p * q, axis=(0, 2)) for p, q in ((r0, r0), (r0, m1), (m1, m1), (m1, m2))]
     )
-    slots, owned_m1 = lax.optimization_barrier((slots, owned_m1))
+    dots = sum_wide(dots)
+    slots, owned_m1, dots = lax.optimization_barrier((slots, owned_m1, dots))
     owned_m2 = to_owners(slots)
-    for axis in WIDE[::-1] + SIXTEEN[::-1]:
+    for axis in SIXTEEN[::-1]:
         dots = sum_direct(dots, axis)
     scale = step_scales(*dots)
-    solution_now, residual_now = combined(sources, scale, owned_r0, owned_m1, owned_m2)
+    rows = jnp.take(all_rows, my_ids, axis=0).transpose(0, 2, 1)
+    weights = jnp.take(all_weights, my_ids, axis=0)
+    solution_now, residual_now = combined(
+        sources, scale, col_effect, weights, rows, owned_one, owned_two, owned_m1, owned_m2
+    )
     return (solution_now[None, None], residual_now[None, None])
 
 

time: 242 us -> 285 us (1.18)
  the two profiles are of different devices: /device:TPU:16 before, /device:TPU:0 now
where the time goes in v1:
time: 285 us; the launch traced here: 280 us
  Pallas kernels  85 us (30%)
  starting transfers between devices  74.2 us (26%)
  blocking collectives  64.4 us (23%)
  local copies, waits for them, and re-layouts  22.6 us (8%)
  waiting for transfers between devices  17.5 us (6%)
  other arithmetic  12.9 us (5%)
  between operations  3.33 us (1%)
    all_gather x1, blocking collectives, on_device(): lax.all_gather(weight.reshape(BLOCKS_DEV, BLOCK), SIXTEEN, axis=0, tiled=...  41.2 us
    pallas_call x2, Pallas kernels, own_product(): pl.pallas_call(own_kernel, in_specs=[SMEM_SPEC, VMEM_SPEC, HBM_SPEC], out...  31.3 us
    pallas_call x4, Pallas kernels, covariance_tiles(): pl.pallas_call(functools.partial(tiles_kernel, first, count, len(extra)),...  30.7 us
    ppermute x18, starting transfers between devices, sum_direct(): lax.ppermute(part, axis, [(i, (i + k) % peers) for i in range(peers)])  23.6 us
    all_gather x1, blocking collectives, on_device(): lax.all_gather(row_effect.T.reshape(BLOCKS_DEV, STRIP, fields), SIXTEEN,...  23.2 us
    all_to_all x4, starting transfers between devices, to_owners(): return lax.all_to_all(slots, SIXTEEN, 0, 0, tiled=True)  20 us
    all_to_all x2, starting transfers between devices, sent_to_all(): lax.all_to_all(jnp.broadcast_to(shard[None], (peers, *shard.shape)), axis...  14.4 us
    ppermute x3, starting transfers between devices, beside(): lax.ppermute(initial, SIXTEEN, down)  13.6 us
  transfers between devices with their start and end apart: 30, of which 10 were waited for; matrix products, arithmetic and copies ran while one was open for 5% of the time, Pallas kernels for 25%

profile of v1, /device:TPU:0, one launch (start us, length us, event | category | flops | bytes accessed | tf_op | source)
XLA Modules:
  0.0 280.0 jit_solution(17909816838343362750)
XLA Ops:
  8.4 8.0 %all-to-all-start = ((f32[16,32,512]{2,1,0:T(8,128)}), f32[16,32,512]{2,1,0:T(8,128)S(1)}, u32[]{:S(2)}, u32[]{:S(2)}) async-start(f32[16,32,512]{2,1,0:T(8,128)} %get-tuple-element.75), calls=%async_computation | async-start | bytes 2097152 | tf_op jit(solution)/shard_map/all_to_all | solution.py:492
  25.8 2.9 %collective-permute-start.2 = (f32[72,32]{1,0:T(8,128)S(1)}, f32[72,32]{1,0:T(8,128)S(1)}, u32[]{:S(2)}, u32[]{:S(2)}) collective-permute-start(f32[72,32]{1,0:T(8,128)S(1)} %add.283), channel_id=1, source_target_pairs={{0,64},{32,96},{64,0},{96,32},{1,65},{33,97},{65,1},{97,33},{2,66}... | collective-permute-start | bytes 27656 | tf_op jit(solution)/shard_map/ppermute | solution.py:51
  31.7 10.0 %tiles.4.refs_0_ = bf16[44,1024,512]{2,1,0:T(8,128)(2,1)} custom-call(s32[134]{0:T(256)S(1)} %concatenate.21.table_ref, f32[16,8,128]{2,1,0:T(8,128)S(1)} %copy.127.rows_ref, f32[16,128,8]{2,1,0:T(8,128)S(1)} %get-tuple-element.80.cols_ref), custom_call_target="tpu_custom_call" | custom-call | flops 40894464 | bytes 13631488 | tf_op jit(solution)/shard_map/tiles/pallas_call | solution.py:178
  43.2 7.3 %all-to-all-start.1 = ((f32[16,72,128]{2,1,0:T(8,128)}), f32[16,72,128]{2,1,0:T(8,128)}, u32[]{:S(2)}, u32[]{:S(2)}) async-start(f32[16,72,128]{2,1,0:T(8,128)} %broadcast_in_dim.48), calls=%async_computation.1 | async-start | bytes 1179648 | tf_op jit(solution)/shard_map/all_to_all | solution.py:39
  52.5 3.4 %collective-permute-start.5 = (f32[4,8,128]{2,1,0:T(8,128)S(1)}, f32[4,8,128]{2,1,0:T(8,128)S(1)}, u32[]{:S(2)}, u32[]{:S(2)}) collective-permute-start(f32[4,8,128]{2,1,0:T(8,128)S(1)} %bitcast.97), channel_id=1, source_target_pairs={{1,0},{2,1},{3,2},{4,3},{5,4},{6,5},{7,6},{8,7},{9,8},{10,9},{11,1... | collective-permute-start | bytes 49160 | tf_op jit(solution)/shard_map/ppermute | solution.py:64
  57.4 7.4 %tiles.5.refs_0_ = bf16[44,1024,512]{2,1,0:T(8,128)(2,1)} custom-call(s32[134]{0:T(256)S(1)} %concatenate.21.table_ref, f32[16,8,128]{2,1,0:T(8,128)S(1)} %copy.128.rows_ref, f32[16,128,8]{2,1,0:T(8,128)S(1)} %get-tuple-element.80.cols_ref, bf16[44,1024,512]{2,1,0:T(8,128)(2,1)} %tiles.4.refs_0_), custom_call_target="tpu_custom_call", output_to_operand_aliasing={{}: (3, {})} | custom-call | flops 28311552 | bytes 9437184 | tf_op jit(solution)/shard_map/tiles/pallas_call | solution.py:178
  68.2 3.9 %all-to-all-start.2 = ((f32[16,32,512]{2,1,0:T(8,128)}), f32[16,32,512]{2,1,0:T(8,128)S(1)}, u32[]{:S(2)}, u32[]{:S(2)}) async-start(f32[16,32,512]{2,1,0:T(8,128)} %get-tuple-element.94), calls=%async_computation.2 | async-start | bytes 2097152 | tf_op jit(solution)/shard_map/all_to_all | solution.py:492
  78.0 9.9 %tiles.6.refs_0_ = bf16[44,1024,512]{2,1,0:T(8,128)(2,1)} custom-call(s32[134]{0:T(256)S(1)} %concatenate.21.table_ref, f32[16,8,128]{2,1,0:T(8,128)S(1)} %constant_dynamic-update-slice_fusion.rows_ref, f32[16,128,8]{2,1,0:T(8,128)S(1)} %bitcast.88, bf16[44,1024,512]{2,1,0:T(8,128)(2,1)} %tiles.5.refs_0_), custom_call_target="tpu_custom_call", output_to_operand_aliasing={{}: (3, {})} | custom-call | flops 40894464 | bytes 13631488 | tf_op jit(solution)/shard_map/tiles/pallas_call | solution.py:178
  89.5 7.1 %all-to-all-start.3 = ((f32[16,64,128]{2,1,0:T(8,128)}), f32[16,64,128]{2,1,0:T(8,128)}, u32[]{:S(2)}, u32[]{:S(2)}) async-start(f32[16,64,128]{2,1,0:T(8,128)} %broadcast_in_dim.49), calls=%async_computation.3 | async-start | bytes 1048576 | tf_op jit(solution)/shard_map/all_to_all | solution.py:39
  97.8 3.5 %tiles.7.tiles_ref = bf16[44,1024,512]{2,1,0:T(8,128)(2,1)} custom-call(s32[134]{0:T(256)S(1)} %concatenate.21.table_ref, f32[16,8,128]{2,1,0:T(8,128)S(1)} %constant_dynamic-update-slice_fusion.rows_ref, f32[16,128,8]{2,1,0:T(8,128)S(1)} %bitcast.89, bf16[44,1024,512]{2,1,0:T(8,128)(2,1)} %tiles.6.refs_0_), custom_call_target="tpu_custom_call", output_to_operand_aliasing={{}: (3, {})} | custom-call | flops 28311552 | bytes 9437184 | tf_op jit(solution)/shard_map/tiles/pallas_call | solution.py:178
  101.3 5.7 %all-to-all-done.3 = f32[16,64,128]{2,1,0:T(8,128)} async-done(((f32[16,64,128]{2,1,0:T(8,128)}), f32[16,64,128]{2,1,0:T(8,128)}, u32[]{:S(2)}, u32[]{:S(2)}) %all-to-all-start.3) | async-done | bytes 524320 | tf_op jit(solution)/shard_map/all_to_all | solution.py:39
  109.6 4.8 %collective-permute-start.11 = (f32[4,64,512]{2,1,0:T(8,128)S(1)}, f32[4,64,512]{2,1,0:T(8,128)S(1)}, u32[]{:S(2)}, u32[]{:S(2)}) collective-permute-start(f32[4,64,512]{2,1,0:T(8,128)S(1)} %get-tuple-element.101), channel_id=1, source_target_pairs={{1,0},{2,1},{3,2},{4,3},{5,4},{6,5},{7,6},{8,7},{9,8},{10,9},{11,1... | collective-permute-start | bytes 1572872 | tf_op jit(solution)/shard_map/ppermute | solution.py:64
  114.4 15.6 %own.2.part_ref = f32[8,64,512]{2,1,0:T(8,128)S(1)} custom-call(s32[134]{0:T(256)S(1)} %concatenate.21.table_ref, f32[8,64,512]{2,1,0:T(8,128)S(1)} %residual.1.v_ref, bf16[44,1024,512]{2,1,0:T(8,128)(2,1)} %tiles.7.tiles_ref), custom_call_target="tpu_custom_call" | custom-call | flops 4227858432 | bytes 27262976 | tf_op jit(solution)/shard_map/own/pallas_call | solution.py:331
  130.1 6.0 %halo.2.v_ref = f32[8,64,512]{2,1,0:T(8,128)S(1)} custom-call(s32[134]{0:T(256)S(1)} %concatenate.21.table_ref, s32[8]{0:T(128)S(1)} %dynamic-slice_bitcast_fusion.target_ref, f32[4,64,512]{2,1,0:T(8,128)S(1)} %collective-permute-done.10.before_ref, f32[4,64,512]{2,1,0:T(8,128)S(1)} %collective-permute-done.11.after_ref, f32[8,64,512]{2,1,0:T(8,128)S(1)} %own.2.part_ref, ...), custom_call_target="tpu_custom_call" | custom-call | flops 1811939328 | bytes 18874368 | tf_op jit(solution)/shard_map/halo/pallas_call | solution.py:367
  136.3 5.3 %collective-permute-start.13 = (f32[4,64,512]{2,1,0:T(8,128)S(1)}, f32[4,64,512]{2,1,0:T(8,128)S(1)}, u32[]{:S(2)}, u32[]{:S(2)}) collective-permute-start(f32[4,64,512]{2,1,0:T(8,128)S(1)} %get-tuple-element.105), channel_id=1, source_target_pairs={{1,0},{2,1},{3,2},{4,3},{5,4},{6,5},{7,6},{8,7},{9,8},{10,9},{11,1... | collective-permute-start | bytes 1572872 | tf_op jit(solution)/shard_map/ppermute | solution.py:64
  141.6 15.6 %own.3.part_ref = f32[8,64,512]{2,1,0:T(8,128)S(1)} custom-call(s32[134]{0:T(256)S(1)} %concatenate.21.table_ref, f32[8,64,512]{2,1,0:T(8,128)S(1)} %halo.2.v_ref, bf16[44,1024,512]{2,1,0:T(8,128)(2,1)} %tiles.7.tiles_ref), custom_call_target="tpu_custom_call" | custom-call | flops 4227858432 | bytes 27262976 | tf_op jit(solution)/shard_map/own/pallas_call | solution.py:331
  161.5 3.7 %all-to-all-start.4 = ((f32[16,64,512]{2,1,0:T(8,128)}), f32[16,64,512]{2,1,0:T(8,128)S(1)}, u32[]{:S(2)}, u32[]{:S(2)}) async-start(f32[16,64,512]{2,1,0:T(8,128)} %spread.1), calls=%async_computation.4 | async-start | bytes 4194304 | tf_op jit(solution)/shard_map/all_to_all | solution.py:492
  169.0 7.0 %halo.3 = (f32[8,64,512]{2,1,0:T(8,128)S(1)}, f32[16,64,512]{2,1,0:T(8,128)}) custom-call(s32[134]{0:T(256)S(1)} %concatenate.21.table_ref, s32[8]{0:T(128)S(1)} %dynamic-slice_bitcast_fusion.target_ref, f32[4,64,512]{2,1,0:T(8,128)S(1)} %copy-done.13, f32[4,64,512]{2,1,0:T(8,128)S(1)} %copy-done.15, f32[8,64,512]{2,1,0:T(8,128)S(1)} %copy-done.11, ...), custom_call_target="tpu_custom_call" | custom-call | flops 1811939328 | bytes 18874368 | tf_op jit(solution)/shard_map/halo/pallas_call | solution.py:367
  180.4 2.5 collective-permute-start.17
  184.2 6.9 %all-to-all-done.4.refs_2_.refs_6_.refs_10_.refs_14_.refs_18_.refs_22_.refs_26_.refs_30_ = f32[16,64,512]{2,1,0:T(8,128)S(1)} async-done(((f32[16,64,512]{2,1,0:T(8,128)}), f32[16,64,512]{2,1,0:T(8,128)S(1)}, u32[]{:S(2)}, u32[]{:S(2)}) %all-to-all-start.4) | async-done | bytes 2097184 | tf_op jit(solution)/shard_map/all_to_all | solution.py:492
  191.1 4.4 %all-to-all-start.5 = ((f32[16,64,512]{2,1,0:T(8,128)}), f32[16,64,512]{2,1,0:T(8,128)}, u32[]{:S(2)}, u32[]{:S(2)}) async-start(f32[16,64,512]{2,1,0:T(8,128)} %get-tuple-element.113), calls=%async_computation.5 | async-start | bytes 4194304 | tf_op jit(solution)/shard_map/all_to_all | solution.py:492
  195.6 41.2 %all_gather.6 = f32[128,512]{1,0:T(8,128)} all-gather(f32[8,512]{1,0:T(8,128)S(1)} %reshape.487), channel_id=1, replica_groups=mesh['wide_0'=4,'wide_1'=2,'sixteen_0'=4,'sixteen_1'=4] {'sixteen_0','si..., dimensions={0}, use_global_device_ids=true | all-gather | bytes 278528 | tf_op jit(solution)/shard_map/all_gather | solution.py:594
  243.2 23.2 %all_gather.7 = f32[128,4,64]{2,1,0:T(4,128)S(1)} all-gather(f32[8,4,64]{2,1,0:T(4,128)S(1)} %bitcast.94), channel_id=1, replica_groups=mesh['wide_0'=4,'wide_1'=2,'sixteen_0'=4,'sixteen_1'=4] {'sixteen_0','si..., dimensions={0}, use_global_device_ids=true | all-gather | bytes 139264 | tf_op jit(solution)/shard_map/all_gather | solution.py:591
  274.2 5.8 %combine.1 = (f32[64,8,512]{2,1,0:T(8,128)}, f32[64,8,512]{2,1,0:T(8,128)}) custom-call(s32[8]{0:T(128)S(1)} %and_select_fusion.1.src_ref, f32[64,8]{1,0:T(8,128)S(1)} %copy.137.scale_ref, f32[64,128]{1,0:T(8,128)S(1)} %divide_add_fusion.col_ref, f32[8,512]{1,0:T(8,128)S(1)} %broadcast_select_fusion.1.weight_ref, f32[8,64,4]{2,1,0:T(8,128)S(1)} %bitcast.90, ...), custom_call_target="tpu_custom_call" | custom-call | tf_op jit(solution)/shard_map/combine/pallas_call | solution.py:471
  (167 shorter events, 65.5 us)
Async XLA Ops:
  4.3 19.9 %collective-permute-start = (f32[72,32]{1,0:T(8,128)S(1)}, f32[72,32]{1,0:T(8,128)S(1)}, u32[]{:S(2)}, u32[]{:S(2)}) collective-permute-start(f32[72,32]{1,0:T(8,128)S(1)} %copy.124), channel_id=1, source_target_pairs={{0,16},{16,0},{1,17},{17,1},{2,18},{18,2},{3,19},{19,3},{4,20},{20... | collective-permute-start | bytes 27656 | tf_op jit(solution)/shard_map/ppermute | solution.py:51
  8.4 33.4 %all-to-all-start = ((f32[16,32,512]{2,1,0:T(8,128)}), f32[16,32,512]{2,1,0:T(8,128)S(1)}, u32[]{:S(2)}, u32[]{:S(2)}) async-start(f32[16,32,512]{2,1,0:T(8,128)} %get-tuple-element.75), calls=%async_computation | async-start | bytes 2097152 | tf_op jit(solution)/shard_map/all_to_all | solution.py:492
  24.2 17.5 %collective-permute-start.1 = (f32[72,32]{1,0:T(8,128)S(1)}, f32[72,32]{1,0:T(8,128)S(1)}, u32[]{:S(2)}, u32[]{:S(2)}) collective-permute-start(f32[72,32]{1,0:T(8,128)S(1)} %add.283), channel_id=1, source_target_pairs={{0,32},{32,64},{64,96},{96,0},{1,33},{33,65},{65,97},{97,1},{2,34}... | collective-permute-start | bytes 27656 | tf_op jit(solution)/shard_map/ppermute | solution.py:51
  25.8 15.9 %collective-permute-start.2 = (f32[72,32]{1,0:T(8,128)S(1)}, f32[72,32]{1,0:T(8,128)S(1)}, u32[]{:S(2)}, u32[]{:S(2)}) collective-permute-start(f32[72,32]{1,0:T(8,128)S(1)} %add.283), channel_id=1, source_target_pairs={{0,64},{32,96},{64,0},{96,32},{1,65},{33,97},{65,1},{97,33},{2,66}... | collective-permute-start | bytes 27656 | tf_op jit(solution)/shard_map/ppermute | solution.py:51
  28.7 13.0 %collective-permute-start.3 = (f32[72,32]{1,0:T(8,128)S(1)}, f32[72,32]{1,0:T(8,128)S(1)}, u32[]{:S(2)}, u32[]{:S(2)}) collective-permute-start(f32[72,32]{1,0:T(8,128)S(1)} %add.283), channel_id=1, source_target_pairs={{0,96},{32,0},{64,32},{96,64},{1,97},{33,1},{65,33},{97,65},{2,98}... | collective-permute-start | bytes 27656 | tf_op jit(solution)/shard_map/ppermute | solution.py:51
  43.2 21.6 %all-to-all-start.1 = ((f32[16,72,128]{2,1,0:T(8,128)}), f32[16,72,128]{2,1,0:T(8,128)}, u32[]{:S(2)}, u32[]{:S(2)}) async-start(f32[16,72,128]{2,1,0:T(8,128)} %broadcast_in_dim.48), calls=%async_computation.1 | async-start | bytes 1179648 | tf_op jit(solution)/shard_map/all_to_all | solution.py:39
  50.5 15.4 %collective-permute-start.4 = (f32[4,8,128]{2,1,0:T(8,128)S(1)}, f32[4,8,128]{2,1,0:T(8,128)S(1)}, u32[]{:S(2)}, u32[]{:S(2)}) collective-permute-start(f32[4,8,128]{2,1,0:T(8,128)S(1)} %bitcast.98), channel_id=1, source_target_pairs={{0,1},{1,2},{2,3},{3,4},{4,5},{5,6},{6,7},{7,8},{8,9},{9,10},{10,1... | collective-permute-start | bytes 49160 | tf_op jit(solution)/shard_map/ppermute | solution.py:64
  52.5 13.5 %collective-permute-start.5 = (f32[4,8,128]{2,1,0:T(8,128)S(1)}, f32[4,8,128]{2,1,0:T(8,128)S(1)}, u32[]{:S(2)}, u32[]{:S(2)}) collective-permute-start(f32[4,8,128]{2,1,0:T(8,128)S(1)} %bitcast.97), channel_id=1, source_target_pairs={{1,0},{2,1},{3,2},{4,3},{5,4},{6,5},{7,6},{8,7},{9,8},{10,9},{11,1... | collective-permute-start | bytes 49160 | tf_op jit(solution)/shard_map/ppermute | solution.py:64
  68.2 19.9 %all-to-all-start.2 = ((f32[16,32,512]{2,1,0:T(8,128)}), f32[16,32,512]{2,1,0:T(8,128)S(1)}, u32[]{:S(2)}, u32[]{:S(2)}) async-start(f32[16,32,512]{2,1,0:T(8,128)} %get-tuple-element.94), calls=%async_computation.2 | async-start | bytes 2097152 | tf_op jit(solution)/shard_map/all_to_all | solution.py:492
  73.3 14.6 %collective-permute-start.7 = (f32[64,32]{1,0:T(8,128)S(1)}, f32[64,32]{1,0:T(8,128)S(1)}, u32[]{:S(2)}, u32[]{:S(2)}) collective-permute-start(f32[64,32]{1,0:T(8,128)S(1)} %add.296), channel_id=1, source_target_pairs={{0,32},{32,64},{64,96},{96,0},{1,33},{33,65},{65,97},{97,1},{2,34}... | collective-permute-start | bytes 24584 | tf_op jit(solution)/shard_map/ppermute | solution.py:51
  74.0 13.9 %collective-permute-start.8 = (f32[64,32]{1,0:T(8,128)S(1)}, f32[64,32]{1,0:T(8,128)S(1)}, u32[]{:S(2)}, u32[]{:S(2)}) collective-permute-start(f32[64,32]{1,0:T(8,128)S(1)} %add.296), channel_id=1, source_target_pairs={{0,64},{32,96},{64,0},{96,32},{1,65},{33,97},{65,1},{97,33},{2,66}... | collective-permute-start | bytes 24584 | tf_op jit(solution)/shard_map/ppermute | solution.py:51
  74.8 13.1 %collective-permute-start.9 = (f32[64,32]{1,0:T(8,128)S(1)}, f32[64,32]{1,0:T(8,128)S(1)}, u32[]{:S(2)}, u32[]{:S(2)}) collective-permute-start(f32[64,32]{1,0:T(8,128)S(1)} %add.296), channel_id=1, source_target_pairs={{0,96},{32,0},{64,32},{96,64},{1,97},{33,1},{65,33},{97,65},{2,98}... | collective-permute-start | bytes 24584 | tf_op jit(solution)/shard_map/ppermute | solution.py:51
  89.5 17.6 %all-to-all-start.3 = ((f32[16,64,128]{2,1,0:T(8,128)}), f32[16,64,128]{2,1,0:T(8,128)}, u32[]{:S(2)}, u32[]{:S(2)}) async-start(f32[16,64,128]{2,1,0:T(8,128)} %broadcast_in_dim.49), calls=%async_computation.3 | async-start | bytes 1048576 | tf_op jit(solution)/shard_map/all_to_all | solution.py:39
  109.0 21.1 %collective-permute-start.10 = (f32[4,64,512]{2,1,0:T(8,128)S(1)}, f32[4,64,512]{2,1,0:T(8,128)S(1)}, u32[]{:S(2)}, u32[]{:S(2)}) collective-permute-start(f32[4,64,512]{2,1,0:T(8,128)S(1)} %get-tuple-element.100), channel_id=1, source_target_pairs={{0,1},{1,2},{2,3},{3,4},{4,5},{5,6},{6,7},{7,8},{8,9},{9,10},{10,1... | collective-permute-start | bytes 1572872 | tf_op jit(solution)/shard_map/ppermute | solution.py:64
  109.6 20.5 %collective-permute-start.11 = (f32[4,64,512]{2,1,0:T(8,128)S(1)}, f32[4,64,512]{2,1,0:T(8,128)S(1)}, u32[]{:S(2)}, u32[]{:S(2)}) collective-permute-start(f32[4,64,512]{2,1,0:T(8,128)S(1)} %get-tuple-element.101), channel_id=1, source_target_pairs={{1,0},{2,1},{3,2},{4,3},{5,4},{6,5},{7,6},{8,7},{9,8},{10,9},{11,1... | collective-permute-start | bytes 1572872 | tf_op jit(solution)/shard_map/ppermute | solution.py:64
  136.2 21.1 %collective-permute-start.12 = (f32[4,64,512]{2,1,0:T(8,128)S(1)}, f32[4,64,512]{2,1,0:T(8,128)S(1)}, u32[]{:S(2)}, u32[]{:S(2)}) collective-permute-start(f32[4,64,512]{2,1,0:T(8,128)S(1)} %get-tuple-element.104), channel_id=1, source_target_pairs={{0,1},{1,2},{2,3},{3,4},{4,5},{5,6},{6,7},{7,8},{8,9},{9,10},{10,1... | collective-permute-start | bytes 1572872 | tf_op jit(solution)/shard_map/ppermute | solution.py:64
  136.3 21.0 %collective-permute-start.13 = (f32[4,64,512]{2,1,0:T(8,128)S(1)}, f32[4,64,512]{2,1,0:T(8,128)S(1)}, u32[]{:S(2)}, u32[]{:S(2)}) collective-permute-start(f32[4,64,512]{2,1,0:T(8,128)S(1)} %get-tuple-element.105), channel_id=1, source_target_pairs={{1,0},{2,1},{3,2},{4,3},{5,4},{6,5},{7,6},{8,7},{9,8},{10,9},{11,1... | collective-permute-start | bytes 1572872 | tf_op jit(solution)/shard_map/ppermute | solution.py:64
  161.5 29.6 %all-to-all-start.4 = ((f32[16,64,512]{2,1,0:T(8,128)}), f32[16,64,512]{2,1,0:T(8,128)S(1)}, u32[]{:S(2)}, u32[]{:S(2)}) async-start(f32[16,64,512]{2,1,0:T(8,128)} %spread.1), calls=%async_computation.4 | async-start | bytes 4194304 | tf_op jit(solution)/shard_map/all_to_all | solution.py:492
  177.7 5.2 %collective-permute-start.15 = (f32[4,64]{1,0:T(4,128)S(1)}, f32[4,64]{1,0:T(4,128)S(1)}, u32[]{:S(2)}, u32[]{:S(2)}) collective-permute-start(f32[4,64]{1,0:T(4,128)S(1)} %fusion.14), channel_id=1, source_target_pairs={{0,32},{32,64},{64,96},{96,0},{1,33},{33,65},{65,97},{97,1},{2,34}... | collective-permute-start | bytes 3080 | tf_op jit(solution)/shard_map/ppermute | solution.py:51
  191.1 81.9 %all-to-all-start.5 = ((f32[16,64,512]{2,1,0:T(8,128)}), f32[16,64,512]{2,1,0:T(8,128)}, u32[]{:S(2)}, u32[]{:S(2)}) async-start(f32[16,64,512]{2,1,0:T(8,128)} %get-tuple-element.113), calls=%async_computation.5 | async-start | bytes 4194304 | tf_op jit(solution)/shard_map/all_to_all | solution.py:492
  238.5 28.4 %collective-permute-start.18 = (f32[4,64]{1,0:T(4,128)S(1)}, f32[4,64]{1,0:T(4,128)S(1)}, u32[]{:S(2)}, u32[]{:S(2)}) collective-permute-start(f32[4,64]{1,0:T(4,128)S(1)} %add_add_fusion.4), channel_id=1, source_target_pairs={{0,1},{1,2},{2,3},{3,0},{4,5},{5,6},{6,7},{7,4},{8,9},{9,10},{10,1... | collective-permute-start | bytes 3080 | tf_op jit(solution)/shard_map/ppermute | solution.py:51
  239.8 27.1 %collective-permute-start.19 = (f32[4,64]{1,0:T(4,128)S(1)}, f32[4,64]{1,0:T(4,128)S(1)}, u32[]{:S(2)}, u32[]{:S(2)}) collective-permute-start(f32[4,64]{1,0:T(4,128)S(1)} %add_add_fusion.4), channel_id=1, source_target_pairs={{0,2},{1,3},{2,0},{3,1},{4,6},{5,7},{6,4},{7,5},{8,10},{9,11},{10,... | collective-permute-start | bytes 3080 | tf_op jit(solution)/shard_map/ppermute | solution.py:51
  241.9 25.0 %collective-permute-start.20 = (f32[4,64]{1,0:T(4,128)S(1)}, f32[4,64]{1,0:T(4,128)S(1)}, u32[]{:S(2)}, u32[]{:S(2)}) collective-permute-start(f32[4,64]{1,0:T(4,128)S(1)} %add_add_fusion.4), channel_id=1, source_target_pairs={{0,3},{1,0},{2,1},{3,2},{4,7},{5,4},{6,5},{7,6},{8,11},{9,8},{10,9... | collective-permute-start | bytes 3080 | tf_op jit(solution)/shard_map/ppermute | solution.py:51
  267.1 5.2 %collective-permute-start.22 = (f32[4,64]{1,0:T(4,128)S(1)}, f32[4,64]{1,0:T(4,128)S(1)}, u32[]{:S(2)}, u32[]{:S(2)}) collective-permute-start(f32[4,64]{1,0:T(4,128)S(1)} %add_add_fusion.3), channel_id=1, source_target_pairs={{0,8},{4,12},{8,0},{12,4},{1,9},{5,13},{9,1},{13,5},{2,10},{6,14},... | collective-permute-start | bytes 3080 | tf_op jit(solution)/shard_map/ppermute | solution.py:51
  (24 other events, 225.0 us)

commit v2 on v0

v2 whole, which is shorter than its diff:
```python
import functools

import jax
import jax.numpy as jnp
from jax import lax
from jax.experimental import pallas as pl
from jax.experimental.pallas import tpu as pltpu
from jax.sharding import Mesh
from jax.sharding import PartitionSpec as P

BLOCK = 512
BLOCKS_DEV = 8
REACH = 4
NEIGHBOURS = 6
PAIRED = NEIGHBOURS // 2
SWEEPS = 2
STRIP = 4
COL_DEV = 128
WIDE = ("wide_0", "wide_1")
SIXTEEN = ("sixteen_0", "sixteen_1")

HUBER_EDGE = 1.345
SILL_TERM = 0.02
ROOT_THREE = 1.7320508075688772
SPREAD = 2.0 * STRIP
CUTOFF = 6.0 * STRIP
BAND = 24
GROUP = 16

OWN_TILES = BLOCKS_DEV + PAIRED * BLOCKS_DEV - 6
HALO_TILES = 2 * (2 + 3 + 4)
ROW_TILES, COL_TILES = 7, 15
TILE_SLOTS = 4
OP_SLOTS = 5


def sent_to_all(shard, axis):
    peers = lax.axis_size(axis)
    return lax.all_to_all(
        jnp.broadcast_to(shard[None], (peers, *shard.shape)), axis, 0, 0, tiled=True
    )


def over_copies(shard, axis):
    return jnp.sum(sent_to_all(shard, axis), axis=0)


def sum_direct(part, axis):
    peers = lax.axis_size(axis)
    moved = [
        lax.ppermute(part, axis, [(i, (i + k) % peers) for i in range(peers)])
        for k in range(1, peers)
    ]
    return functools.reduce(jnp.add, moved, part)


def beside(shard, width, dim=0):
    peers, length = lax.axis_size(SIXTEEN), shard.shape[dim]
    up = [(i, (i + 1) % peers) for i in range(peers)]
    down = [(j, i) for i, j in up]
    last = lax.slice_in_dim(shard, length - width, length, axis=dim)
    initial = lax.slice_in_dim(shard, 0, width, axis=dim)
    shard, last, initial = lax.optimization_barrier((shard, last, initial))
    return lax.ppermute(last, SIXTEEN, up), lax.ppermute(initial, SIXTEEN, down), shard


def owned_table(group_map, owners, per_owner):
    total_strips = group_map.shape[0]
    member = (group_map[None, :] == jnp.arange(owners, dtype=jnp.int32)[:, None]).astype(jnp.int32)
    ranked = jnp.cumsum(member, axis=1, dtype=jnp.int32) - 1
    slot_hit = (ranked[:, :, None] == jnp.arange(per_owner, dtype=jnp.int32)[None, None, :]).astype(
        jnp.int32
    ) * member[:, :, None]
    numbers = jnp.arange(total_strips, dtype=jnp.int32)
    return jnp.sum(slot_hit * numbers[None, :, None], axis=1, dtype=jnp.int32)


def offsets_of(list_ref):
    held = [
        functools.reduce(jnp.logical_or, [list_ref[n] == d for n in range(NEIGHBOURS)])
        for d in range(1, REACH)
    ]
    missing = jnp.where(held[0], jnp.where(held[1], jnp.where(held[2], 4, 3), 2), 1)
    return [k + jnp.where(missing <= k, 1, 0) for k in range(1, PAIRED + 1)]


def own_count(offsets):
    return (PAIRED + 1) * BLOCKS_DEV - (offsets[0] + offsets[1] + offsets[2])


def halo_count(offsets):
    return 2 * (offsets[0] + offsets[1] + offsets[2])


def own_pair(t, offsets):
    d1, d2, d3 = offsets
    p = t - BLOCKS_DEV
    n1, n2 = BLOCKS_DEV - d1, 2 * BLOCKS_DEV - d1 - d2
    one = jnp.where(p < n1, p, jnp.where(p < n2, p - n1, p - n2))
    return one, one + jnp.where(p < n1, d1, jnp.where(p < n2, d2, d3))


def halo_pair(q, offsets):
    d1, d2, d3 = offsets
    reach = d1 + d2 + d3
    right = q >= reach
    q = jnp.where(right, q - reach, q)
    step = jnp.where(q < d1, d1, jnp.where(q < d1 + d2, d2, d3))
    pos = jnp.where(q < d1, q, jnp.where(q < d1 + d2, q - d1, q - d1 - d2))
    one = jnp.where(right, BLOCKS_DEV - 1 - pos, pos)
    return one, jnp.where(right, one + step, one - step)


LISTED = OWN_TILES + HALO_TILES


def tiles_kernel(first, count, beside, held, scalar_ref, jitter_ref, *refs):
    beside_refs, refs = refs[:beside], refs[beside + held :]
    tiles_ref, buf, sem = refs
    a, b = ROOT_THREE * CUTOFF / SPREAD, 4.0
    offsets = offsets_of(scalar_ref)
    place, group = scalar_ref[NEIGHBOURS], scalar_ref[NEIGHBOURS + 1]
    total_rows = scalar_ref[NEIGHBOURS + 2]
    row_dev = STRIP * BLOCKS_DEV
    lane = lax.broadcasted_iota(jnp.int32, (GROUP, COL_DEV), 1)
    within = lax.broadcasted_iota(jnp.int32, (STRIP, COL_DEV), 0)
    across = lax.broadcasted_iota(jnp.int32, (STRIP, COL_DEV), 1)
    col_place = (group * COL_DEV + across).astype(jnp.float32)

    def out_copy(t):
        slot = lax.rem(t - first, TILE_SLOTS)
        return pltpu.make_async_copy(buf.at[slot], tiles_ref.at[t], sem.at[slot])

    def live(t):
        mine = (t < OWN_TILES) & (t < own_count(offsets))
        return mine | ((t >= OWN_TILES) & (t < OWN_TILES + halo_count(offsets)))

    def places(block, ref, at):
        row = lax.rem(place * row_dev + STRIP * block + total_rows, total_rows)
        rows = (row + within).astype(jnp.float32) + ref[0, pl.ds(at, STRIP), :]
        cols = col_place + ref[1, pl.ds(at, STRIP), :]
        return jnp.concatenate([rows, cols], axis=0) * (1.0 / CUTOFF)

    def pair_of(t):
        q = t - OWN_TILES
        one, other = own_pair(t, offsets)
        one_q, other_q = halo_pair(q, offsets)
        same = t < BLOCKS_DEV
        mine = t < OWN_TILES
        one = jnp.where(same, t, jnp.where(mine, one, one_q))
        return one, jnp.where(same, t, jnp.where(mine, other, other_q))

    def evaluate(slot, to, frm, sill):
        for rb in range(STRIP):
            row_b = jnp.broadcast_to(frm[:, rb : rb + 1], (COL_DEV, COL_DEV))
            col_b = jnp.broadcast_to(frm[:, STRIP + rb : STRIP + rb + 1], (COL_DEV, COL_DEV))
            for u in range(COL_DEV // 2 // GROUP):
                lo_s = slice(GROUP * u, GROUP * (u + 1))
                hi_s = slice(64 + GROUP * u, 64 + GROUP * (u + 1))
                near = (lane >= GROUP * u - BAND) & (lane < GROUP * (u + 1) + BAND)
                one_m = jnp.where(near, 1.0, 0.0).astype(jnp.bfloat16)
                other_m = jnp.where(near, 0.0, 1.0).astype(jnp.bfloat16)
                row_s = jnp.where(near, row_b[lo_s], row_b[hi_s])
                col_s = jnp.where(near, col_b[lo_s], col_b[hi_s])
                for ra in range(STRIP):
                    dr = row_s - to[ra : ra + 1]
                    dc = col_s - to[STRIP + ra : STRIP + ra + 1]
                    square = dr * dr + dc * dc
                    far = square * lax.rsqrt(jnp.maximum(square, 1e-30))
                    fading = jnp.maximum(1.0 - far, 0.0)
                    fading = fading * fading
                    fading = fading * fading
                    shape = (1.0 + a * far) * (sill + (sill * b) * far)
                    value = shape * fading * jnp.exp(-a * far)
                    hi = value.astype(jnp.bfloat16)
                    lo = (value - hi.astype(jnp.float32)).astype(jnp.bfloat16)
                    lanes = slice(COL_DEV * ra, COL_DEV * (ra + 1))
                    top = rb * COL_DEV + GROUP * u
                    for part, at in ((hi, top), (lo, BLOCK + top)):
                        buf[slot, at : at + GROUP, lanes] = part * one_m
                        buf[slot, at + 64 : at + 64 + GROUP, lanes] = part * other_m

    def one_tile(t, carry):
        slot = lax.rem(t - first, TILE_SLOTS)
        past = jnp.maximum(t - TILE_SLOTS, first)

        @pl.when((t >= first + TILE_SLOTS) & live(past))
        def _():
            out_copy(past).wait()

        @pl.when(live(t))
        def _():
            one, other = pair_of(t)
            sill = jnp.where(one == other, (NEIGHBOURS + 1.0) * SILL_TERM, SILL_TERM)
            inside = jnp.clip(other, 0, BLOCKS_DEV - 1)
            to = places(one, jitter_ref, STRIP * one)
            frm = places(other, jitter_ref, STRIP * inside)
            if beside_refs:
                left = places(other, beside_refs[0], STRIP * jnp.clip(other + REACH, 0, REACH - 1))
                right = places(
                    other, beside_refs[1], STRIP * jnp.clip(other - BLOCKS_DEV, 0, REACH - 1)
                )
                frm = jnp.where(other < 0, left, jnp.where(other < BLOCKS_DEV, frm, right))
            evaluate(slot, to, frm.T, sill)
            out_copy(t).start()

        return carry

    lax.fori_loop(first, first + count, one_tile, 0)
    for t in range(max(first, first + count - TILE_SLOTS), first + count):

        @pl.when(live(t))
        def _(t=t):
            out_copy(t).wait()


def covariance_tiles(first, count, scalars, jitter, beside_jitter, held):
    extra = [] if held is None else [held]
    ins = [scalars, jitter, *beside_jitter, *extra]
    return pl.pallas_call(
        functools.partial(tiles_kernel, first, count, len(beside_jitter), len(extra)),
        in_specs=[SMEM_SPEC] + [VMEM_SPEC] * (1 + len(beside_jitter)) + [HBM_SPEC] * len(extra),
        out_specs=HBM_SPEC,
        scratch_shapes=[
            pltpu.VMEM((TILE_SLOTS, 2 * BLOCK, BLOCK), jnp.bfloat16),
            pltpu.SemaphoreType.DMA((TILE_SLOTS,)),
        ],
        out_shape=jax.ShapeDtypeStruct((LISTED, 2 * BLOCK, BLOCK), jnp.bfloat16),
        input_output_aliases={len(ins) - 1: 0} if extra else {},
        compiler_params=pltpu.CompilerParams(vmem_limit_bytes=12 << 20),
        cost_estimate=pl.CostEstimate(
            flops=count * 12 * BLOCK * BLOCK,
            bytes_accessed=count * 4 * BLOCK * BLOCK,
            transcendentals=count * BLOCK * BLOCK,
        ),
        name="tiles",
    )(*ins)


def halves(v):
    hi = v.astype(jnp.bfloat16)
    lo = (v - hi.astype(jnp.float32)).astype(jnp.bfloat16)
    return hi, lo


NN = (((1,), (0,)), ((), ()))
NT = (((1,), (1,)), ((), ()))


def product(both, tile_ref, dims):
    fields = both.shape[0] // 2
    main = lax.dot_general(
        both, tile_ref[:BLOCK], dims, preferred_element_type=jnp.float32
    )
    rest = lax.dot_general(
        both[:fields], tile_ref[BLOCK:], dims, preferred_element_type=jnp.float32
    )
    return main[:fields] + (main[fields:] + rest)


def op_kernel(own, halo, send, scalar_ref, target_ref, *refs):
    refs = list(refs)
    v_ref = refs.pop(0) if own else None
    beside_refs = [refs.pop(0), refs.pop(0)] if halo else []
    held_ref = None if own else refs.pop(0)
    tiles_ref, out_ref = refs.pop(0), refs.pop(0)
    slots_ref = refs.pop(0) if send else None
    values, both_ref, total, buf, sem, in_sem, out_sem = refs
    fields = total.shape[1]
    offsets = offsets_of(scalar_ref)
    mine = own_count(offsets) if own else 0
    base = 0 if own else OWN_TILES
    count = mine + (halo_count(offsets) if halo else 0)

    def copy(t):
        slot = lax.rem(t, OP_SLOTS)
        at = jnp.where(t < mine, t, t - mine + OWN_TILES) if own else t + OWN_TILES
        return pltpu.make_async_copy(tiles_ref.at[at], buf.at[slot], sem.at[slot])

    loads = []
    if own:
        loads.append((v_ref, 0, BLOCKS_DEV))
    for side, ref in enumerate(beside_refs):
        loads.append((ref, BLOCKS_DEV + REACH * side, REACH))
    arriving = [
        pltpu.make_async_copy(ref, values.at[pl.ds(at, size)], in_sem.at[i])
        for i, (ref, at, size) in enumerate(loads)
    ]
    if held_ref is not None:
        arriving.append(pltpu.make_async_copy(held_ref, total, in_sem.at[3]))
    for load in arriving:
        load.start()
    for t in range(OP_SLOTS - 1):
        copy(t).start()
    for load in arriving:
        load.wait()
    for _, at, size in loads:
        for g in range(at, at + size):
            hi, lo = halves(values[g])
            both_ref[g, :fields] = hi
            both_ref[g, fields:] = lo

    def arrive(t):
        @pl.when(t + OP_SLOTS - 1 < count)
        def _():
            copy(t + OP_SLOTS - 1).start()

        copy(t).wait()
        return buf.at[lax.rem(t, OP_SLOTS)]

    def with_itself(t, carry):
        tile = arrive(t)
        total[t] = product(both_ref[t], tile, NN)
        return carry

    def with_another(t, carry):
        tile = arrive(t)
        one, other = own_pair(t, offsets)
        total[one] += product(both_ref[other], tile, NN)
        total[other] += product(both_ref[one], tile, NT)
        return carry

    def with_beside(t, carry):
        tile = arrive(t)
        one, other = halo_pair(t - mine, offsets)
        side = BLOCKS_DEV + jnp.where(other < 0, other + REACH, other - BLOCKS_DEV + REACH)
        total[one] += product(both_ref[side], tile, NN)
        return carry

    if own:
        lax.fori_loop(0, BLOCKS_DEV, with_itself, 0)
        lax.fori_loop(BLOCKS_DEV, mine, with_another, 0)
    if halo:
        lax.fori_loop(mine, count, with_beside, 0)
    leaving = [pltpu.make_async_copy(total, out_ref, out_sem.at[BLOCKS_DEV])]
    if send:
        leaving += out_copies(total, slots_ref, target_ref, out_sem)
    for out in leaving:
        out.start()
    for out in leaving:
        out.wait()


def out_copies(values_ref, slots_ref, target_ref, sem):
    return [
        pltpu.make_async_copy(values_ref.at[g], slots_ref.at[target_ref[g]], sem.at[g])
        for g in range(BLOCKS_DEV)
    ]


SMEM_SPEC = pl.BlockSpec(memory_space=pltpu.SMEM)
VMEM_SPEC = pl.BlockSpec(memory_space=pltpu.VMEM)
HBM_SPEC = pl.BlockSpec(memory_space=pltpu.HBM)


def in_hbm(x):
    return pltpu.with_memory_space_constraint(x, pltpu.HBM)


def slot_shape(v):
    return pltpu.HBM((lax.axis_size(SIXTEEN), *v.shape[1:]), jnp.float32)


def applied(scalars, targets, tiles, v=None, beside=(), held=None, send=False):
    shape = (held if v is None else v).shape
    blocks, fields, _ = shape
    out = pltpu.HBM(shape, jnp.float32)
    ins = [in_hbm(x) for x in (v, *beside, held) if x is not None] + [tiles]
    number = OWN_TILES * (v is not None) + HALO_TILES * bool(beside)
    out = pl.pallas_call(
        functools.partial(op_kernel, v is not None, bool(beside), send),
        in_specs=[SMEM_SPEC] * 2 + [HBM_SPEC] * len(ins),
        out_specs=[HBM_SPEC] * (1 + send),
        scratch_shapes=[
            pltpu.VMEM((blocks + 2 * REACH, fields, BLOCK), jnp.float32),
            pltpu.VMEM((blocks + 2 * REACH, 2 * fields, BLOCK), jnp.bfloat16),
            pltpu.VMEM(shape, jnp.float32),
            pltpu.VMEM((OP_SLOTS, 2 * BLOCK, BLOCK), jnp.bfloat16),
            pltpu.SemaphoreType.DMA((OP_SLOTS,)),
            pltpu.SemaphoreType.DMA((4,)),
            pltpu.SemaphoreType.DMA((BLOCKS_DEV + 1,)),
        ],
        out_shape=[out] + [slot_shape(out)] * send,
        compiler_params=pltpu.CompilerParams(vmem_limit_bytes=24 << 20),
        cost_estimate=pl.CostEstimate(
            flops=3 * number * 3 * fields * BLOCK * BLOCK,
            bytes_accessed=number * 4 * BLOCK * BLOCK,
            transcendentals=0,
        ),
        name="applied",
    )(scalars, targets, *ins)
    return out if send else out[0]


def spread_kernel(target_ref, v_ref, *refs):
    slots_ref, sem = refs[-2:]
    sent = out_copies(v_ref, slots_ref, target_ref, sem)
    for copy_out in sent:
        copy_out.start()
    for copy_out in sent:
        copy_out.wait()


def spread(targets, v, *others):
    return pl.pallas_call(
        spread_kernel,
        in_specs=[SMEM_SPEC] + [HBM_SPEC] * (1 + len(others)),
        out_specs=HBM_SPEC,
        scratch_shapes=[pltpu.SemaphoreType.DMA((BLOCKS_DEV,))],
        out_shape=slot_shape(v),
        compiler_params=pltpu.CompilerParams(vmem_limit_bytes=1 << 20),
        name="spread",
    )(targets, *map(in_hbm, (v, *others)))


def residual_kernel(
    target_ref, obs_ref, weight_ref, row_ref, before_ref, before_row_ref, after_ref,
    after_row_ref, col_ref, out_ref, before_out_ref, after_out_ref, slots_ref, buf, sem,
):
    fields = obs_ref.shape[0]
    col = col_ref[...]

    def block(at, obs, weight, row, g):
        for ra in range(STRIP):
            r = STRIP * g + ra
            left = obs[:fields, r, :] - row[:, r : r + 1] - col
            weighted = weight[r : r + 1, :] * left
            buf[at, :, COL_DEV * ra : COL_DEV * (ra + 1)] = weighted

    copies = []
    for g in range(BLOCKS_DEV):
        block(g, obs_ref, weight_ref, row_ref, g)
        copies.append(
            pltpu.make_async_copy(buf.at[g], slots_ref.at[target_ref[g]], sem.at[g])
        )
        copies[-1].start()
    copies.append(
        pltpu.make_async_copy(buf.at[pl.ds(0, BLOCKS_DEV)], out_ref, sem.at[BLOCKS_DEV])
    )
    copies[-1].start()
    sides = ((before_ref, before_row_ref, before_out_ref), (after_ref, after_row_ref, after_out_ref))
    for side, (obs, row, out) in enumerate(sides):
        first = BLOCKS_DEV + REACH * side
        for g in range(REACH):
            block(first + g, obs, obs.at[fields], row, g)
        copies.append(
            pltpu.make_async_copy(
                buf.at[pl.ds(first, REACH)], out, sem.at[BLOCKS_DEV + 1 + side]
            )
        )
        copies[-1].start()
    for copy in copies:
        copy.wait()


def residual_of(targets, observations, weight, row_effect, before, before_row, after, after_row, col):
    fields = observations.shape[0]
    own = pltpu.HBM((BLOCKS_DEV, fields, BLOCK), jnp.float32)
    side = pltpu.HBM((REACH, fields, BLOCK), jnp.float32)
    return pl.pallas_call(
        residual_kernel,
        in_specs=[SMEM_SPEC] + [VMEM_SPEC] * 8,
        out_specs=[HBM_SPEC] * 4,
        scratch_shapes=[
            pltpu.VMEM((BLOCKS_DEV + 2 * REACH, fields, BLOCK), jnp.float32),
            pltpu.SemaphoreType.DMA((BLOCKS_DEV + 3,)),
        ],
        out_shape=[own, side, side, slot_shape(own)],
        compiler_params=pltpu.CompilerParams(vmem_limit_bytes=12 << 20),
        name="residual",
    )(targets, observations, weight, row_effect, before, before_row, after, after_row, col)


def combine_kernel(src_ref, scale_ref, *refs):
    ins, (x_ref, r_ref) = refs[:-2], refs[-2:]
    scale = scale_ref[...]
    for j in range(BLOCKS_DEV):
        r0, m1, m2 = (ref[0] for ref in ins[3 * j : 3 * j + 3])
        x_ref[:, j, :] = scale[:, 0:1] * r0 + scale[:, 1:2] * m1
        r_ref[:, j, :] = scale[:, 2:3] * r0 + scale[:, 3:4] * m1 + scale[:, 4:5] * m2


def combined(sources, scale, r0, m1, m2):
    fields = r0.shape[1]
    part = 16
    ins, specs = [], []
    for j in range(BLOCKS_DEV):
        for v in (r0, m1, m2):
            ins.append(v)
            specs.append(
                pl.BlockSpec(
                    (1, part, BLOCK), functools.partial(lambda j, i, s: (s[j], i, 0), j)
                )
            )
    out = pl.BlockSpec((part, BLOCKS_DEV, BLOCK), lambda i, s: (i, 0, 0))
    shape = jax.ShapeDtypeStruct((fields, BLOCKS_DEV, BLOCK), jnp.float32)
    return pl.pallas_call(
        combine_kernel,
        grid_spec=pltpu.PrefetchScalarGridSpec(
            num_scalar_prefetch=1,
            grid=(fields // part,),
            in_specs=[pl.BlockSpec((part, 8), lambda i, s: (i, 0))] + specs,
            out_specs=[out, out],
        ),
        out_shape=[shape, shape],
        compiler_params=pltpu.CompilerParams(vmem_limit_bytes=20 << 20),
        name="combine",
    )(sources, scale, *ins)


def to_owners(slots):
    return lax.all_to_all(slots, SIXTEEN, 0, 0, tiled=True)


def step_scales(h00, h01, h11, h12):
    mu = h01 / h00
    var = (h11 - mu * h01) / h00
    a0 = 1.0 / (1.0 + mu)
    beta = var * a0 * a0
    skew = (h12 - mu * h11 - mu * (h11 - mu * h01)) / h00
    a1 = var / (var + skew - var * var * a0)
    x_r0 = a0 + a1 * beta + a1 * a0 * mu
    x_m1 = -a1 * a0
    r_r0 = a0 * mu * (1.0 - a1) - a1 * beta
    r_m1 = -a0 * (1.0 - a1) - a1 * a0 * mu - a1 * beta
    r_m2 = a1 * a0
    zero = jnp.zeros_like(mu)
    return jnp.stack([x_r0, x_m1, r_r0, r_m1, r_m2, zero, zero, zero], axis=1)


def on_device(observations, huber_scale, observed, jitter, owner_map, neighbours):
    fields, row_dev, col_dev = observations.shape
    sixteen_size = lax.axis_size(SIXTEEN)
    my_place = lax.axis_index(SIXTEEN)
    group_place = lax.axis_index(WIDE)
    total_strips = BLOCKS_DEV * sixteen_size
    weight = observed.astype(jnp.float32)
    spread_scale = huber_scale[:, None, None]

    def with_count(part, count):
        rows = jnp.zeros((8, count.shape[0]), jnp.float32).at[0].set(count)
        return jnp.concatenate([part, rows], axis=0)

    def terms(row_effect, col_effect):
        return weight[None] * jnp.clip(
            (observations - row_effect[:, :, None] - col_effect[:, None, :]) / spread_scale,
            -HUBER_EDGE,
            HUBER_EDGE,
        )

    def sum_wide(part):
        for axis in WIDE[::-1]:
            part = sum_direct(part, axis)
        return part

    row_effect = jnp.zeros((fields, row_dev), jnp.float32)
    col_effect = jnp.zeros((fields, col_dev), jnp.float32)
    part = with_count(jnp.sum(terms(row_effect, col_effect), axis=2), jnp.sum(weight, axis=1))
    part, jitter, owner_map, neighbours = lax.optimization_barrier(
        (part, jitter, owner_map, neighbours)
    )
    group_map = owner_map[0]
    scalars = jnp.concatenate(
        [neighbours[0, 0], jnp.stack([my_place, group_place, total_strips * STRIP])]
    ).astype(jnp.int32)

    def beside_tiles(part, axis, count, tiles, first, near):
        if first:
            part, tiles = lax.optimization_barrier((part, tiles))
        total = over_copies(part, axis)
        tiles = covariance_tiles(first, count, scalars, jitter, near, tiles)
        total, tiles = lax.optimization_barrier((total, tiles))
        return total, tiles, first + count

    edges = jnp.concatenate([observations, weight[None], jitter], axis=0)
    before, after, _ = beside(edges, REACH * STRIP, 1)
    total, tiles, first = beside_tiles(part, WIDE, ROW_TILES, None, 0, ())
    row_count = jnp.maximum(total[fields], 1.0)
    row_effect = huber_scale[:, None] * total[:fields] / row_count[None, :]
    part = with_count(jnp.sum(terms(row_effect, col_effect), axis=1), jnp.sum(weight, axis=0))
    total, tiles, first = beside_tiles(part, SIXTEEN, COL_TILES, tiles, first, ())
    total, before, after = lax.optimization_barrier((total, before, after))
    near = (before[fields + 1 :], after[fields + 1 :])
    col_count = jnp.maximum(total[fields], 1.0)
    col_effect = huber_scale[:, None] * total[:fields] / col_count[None, :]
    part = jnp.sum(terms(row_effect, col_effect), axis=2)
    total, tiles, first = beside_tiles(part, WIDE, ROW_TILES, tiles, first, near)
    row_effect = row_effect + huber_scale[:, None] * total / row_count[None, :]
    part = jnp.sum(terms(row_effect, col_effect), axis=1)
    row_before, row_after, _ = beside(row_effect, REACH * STRIP, 1)
    total, tiles, first = beside_tiles(part, SIXTEEN, COL_TILES, tiles, first, near)
    col_effect = col_effect + huber_scale[:, None] * total / col_count[None, :]

    my_targets = lax.dynamic_slice_in_dim(group_map, my_place * BLOCKS_DEV, BLOCKS_DEV)
    r0, r0_before, r0_after, slots = residual_of(
        my_targets, observations, weight, row_effect, before, row_before, after, row_after, col_effect
    )
    owned_r0 = to_owners(slots)
    m1 = applied(scalars, my_targets, tiles, r0, (r0_before, r0_after))
    before, after, m1 = beside(m1, REACH)
    part = applied(scalars, my_targets, tiles, m1)
    slots = spread(my_targets, m1, part, before, after)
    slots, owned_r0 = lax.optimization_barrier((slots, owned_r0))
    owned_m1 = to_owners(slots)
    m2, slots = applied(scalars, my_targets, tiles, None, (before, after), part, True)
    dots = jnp.stack(
        [jnp.sum(p * q, axis=(0, 2)) for p, q in ((r0, r0), (r0, m1), (m1, m1), (m1, m2))]
    )
    dots = sum_wide(dots)
    slots, owned_m1, dots = lax.optimization_barrier((slots, owned_m1, dots))
    owned_m2 = to_owners(slots)
    for axis in SIXTEEN[::-1]:
        dots = sum_direct(dots, axis)
    scale = step_scales(*dots)
    owned = owned_table(group_map, sixteen_size, BLOCKS_DEV)
    my_ids = lax.dynamic_index_in_dim(owned, my_place, 0, keepdims=False)
    solution_now, residual_now = combined(
        my_ids // BLOCKS_DEV, scale, owned_r0, owned_m1, owned_m2
    )
    return (solution_now[None, None], residual_now[None, None])


def solution(mesh):
    finer = Mesh(mesh.devices.reshape(4, 2, 4, 4), ("wide_0", "wide_1", "sixteen_0", "sixteen_1"))
    in_specs = (
        P(None, SIXTEEN, WIDE),
        P(),
        P(SIXTEEN, WIDE),
        P(None, SIXTEEN, WIDE),
        P(WIDE, None),
        P(WIDE, None, None),
    )
    out_specs = (P(WIDE, SIXTEEN, None, None, None), P(WIDE, SIXTEEN, None, None, None))
    return jax.shard_map(
        on_device, mesh=finer, in_specs=in_specs, out_specs=out_specs, check_vma=False
    )
```

time: 242 us -> 263 us (1.087)
  the two profiles are of different devices: /device:TPU:16 before, /device:TPU:0 now
where the time goes in v2:
time: 263 us; the launch traced here: 261 us
  Pallas kernels  126 us (48%)
  starting transfers between devices  68.6 us (26%)
  waiting for transfers between devices  46.7 us (18%)
  other arithmetic  10 us (4%)
  local copies, waits for them, and re-layouts  9.06 us (3%)
    pallas_call x3, Pallas kernels, applied(): pl.pallas_call(functools.partial(op_kernel, v is not None, bool(beside),...  47.4 us
    pallas_call x4, Pallas kernels, covariance_tiles(): pl.pallas_call(functools.partial(tiles_kernel, first, count, len(beside_j...  36.8 us
    pallas_call x1, Pallas kernels, spread(): pl.pallas_call(spread_kernel, in_specs=[SMEM_SPEC] + [HBM_SPEC] * (1 + le...  33.5 us
    ppermute x10, waiting for transfers between devices, sum_direct(): lax.ppermute(part, axis, [(i, (i + k) % peers) for i in range(peers)])  29.1 us
    all_to_all x4, starting transfers between devices, sent_to_all(): lax.all_to_all(jnp.broadcast_to(shard[None], (peers, *shard.shape)), axis...  20.5 us
    ppermute x10, starting transfers between devices, sum_direct(): lax.ppermute(part, axis, [(i, (i + k) % peers) for i in range(peers)])  19.2 us
    all_to_all x3, waiting for transfers between devices, to_owners(): return lax.all_to_all(slots, SIXTEEN, 0, 0, tiled=True)  12.9 us
    all_to_all x3, starting transfers between devices, to_owners(): return lax.all_to_all(slots, SIXTEEN, 0, 0, tiled=True)  12.7 us
  transfers between devices with their start and end apart: 23, of which 8 were waited for; matrix products, arithmetic and copies ran while one was open for 3% of the time, Pallas kernels for 45%

profile of v2, /device:TPU:0, one launch (start us, length us, event | category | flops | bytes accessed | tf_op | source)
XLA Modules:
  0.0 261.3 jit_solution(14366450645269839231)
XLA Ops:
  4.9 4.6 %all-to-all-start = ((f32[8,72,32]{1,2,0:T(8,128)}), f32[8,72,32]{1,2,0:T(8,128)S(1)}, u32[]{:S(2)}, u32[]{:S(2)}) async-start(f32[8,72,32]{1,2,0:T(8,128)} %broadcast_in_dim.14), calls=%async_computation | async-start | bytes 262144 | tf_op jit(solution)/shard_map/all_to_all | solution.py:39
  11.3 7.0 %tiles.4.refs_0_ = bf16[44,1024,512]{2,1,0:T(8,128)(2,1)} custom-call(s32[9]{0:T(128)S(1)} %pad_add_fusion.scalar_ref, f32[2,32,128]{2,1,0:T(8,128)S(1)} %copy-done.1), custom_call_target="tpu_custom_call" | custom-call | flops 22020096 | bytes 7340032 | tf_op jit(solution)/shard_map/tiles/pallas_call | solution.py:220
  20.1 7.9 %all-to-all-start.1 = ((f32[16,72,128]{2,1,0:T(8,128)}), f32[16,72,128]{2,1,0:T(8,128)S(1)}, u32[]{:S(2)}, u32[]{:S(2)}) async-start(f32[16,72,128]{2,1,0:T(8,128)} %broadcast_in_dim.15), calls=%async_computation.1 | async-start | bytes 1179648 | tf_op jit(solution)/shard_map/all_to_all | solution.py:39
  30.7 3.4 %collective-permute-start.1 = (f32[67,16,128]{2,1,0:T(8,128)S(1)}, f32[67,16,128]{2,1,0:T(8,128)S(1)}, u32[]{:S(2)}, u32[]{:S(2)}) collective-permute-start(f32[67,16,128]{2,1,0:T(8,128)S(1)} %get-tuple-element.77), channel_id=1, source_target_pairs={{1,0},{2,1},{3,2},{4,3},{5,4},{6,5},{7,6},{8,7},{9,8},{10,9},{11,1... | collective-permute-start | bytes 1646600 | tf_op jit(solution)/shard_map/ppermute | solution.py:64
  34.2 13.3 %tiles.5.refs_2_ = bf16[44,1024,512]{2,1,0:T(8,128)(2,1)} custom-call(s32[9]{0:T(128)S(1)} %pad_add_fusion.scalar_ref, f32[2,32,128]{2,1,0:T(8,128)S(1)} %copy-done.1, bf16[44,1024,512]{2,1,0:T(8,128)(2,1)} %tiles.4.refs_0_), custom_call_target="tpu_custom_call", output_to_operand_aliasing={{}: (2, {})} | custom-call | flops 47185920 | bytes 15728640 | tf_op jit(solution)/shard_map/tiles/pallas_call | solution.py:220
  47.5 4.8 %collective-permute-done.before_ref = f32[67,16,128]{2,1,0:T(8,128)S(1)} collective-permute-done((f32[67,16,128]{2,1,0:T(8,128)}, f32[67,16,128]{2,1,0:T(8,128)S(1)}, u32[]{:S(2)}, u32[]{:S(2)}) %collective-permute-start) | collective-permute-done | bytes 548896 | tf_op jit(solution)/shard_map/ppermute | solution.py:64
  54.0 4.4 %all-to-all-start.2 = ((f32[8,1,2048]{2,1,0:T(1,128)}), f32[8,1,2048]{2,1,0:T(1,128)S(1)}, u32[]{:S(2)}, u32[]{:S(2)}) async-start(f32[8,1,2048]{2,1,0:T(1,128)} %reshape.401), calls=%async_computation.2 | async-start | bytes 131072 | tf_op jit(solution)/shard_map/all_to_all | solution.py:39
  58.5 6.4 %tiles.6.refs_2_ = bf16[44,1024,512]{2,1,0:T(8,128)(2,1)} custom-call(s32[9]{0:T(128)S(1)} %pad_add_fusion.scalar_ref, f32[2,32,128]{2,1,0:T(8,128)S(1)} %copy-done.1, f32[2,16,128]{2,1,0:T(8,128)S(1)} %slice.74.refs_0_, f32[2,16,128]{2,1,0:T(8,128)S(1)} %slice.75.refs_1_, bf16[44,1024,512]{2,1,0:T(8,128)(2,1)} %tiles.5.refs_2_), custom_call_target="tpu_custom_call", output_to_operand_aliasing={{}: (4, {})} | custom-call | flops 22020096 | bytes 7340032 | tf_op jit(solution)/shard_map/tiles/pallas_call | solution.py:220
  67.8 3.6 %all-to-all-start.3 = ((f32[16,64,128]{2,1,0:T(8,128)}), f32[16,64,128]{2,1,0:T(8,128)S(1)}, u32[]{:S(2)}, u32[]{:S(2)}) async-start(f32[16,64,128]{2,1,0:T(8,128)} %broadcast_in_dim.18), calls=%async_computation.3 | async-start | bytes 1048576 | tf_op jit(solution)/shard_map/all_to_all | solution.py:39
  73.4 3.5 %collective-permute-start.3 = (f32[64,16]{1,0:T(8,128)S(1)}, f32[64,16]{1,0:T(8,128)S(1)}, u32[]{:S(2)}, u32[]{:S(2)}) collective-permute-start(f32[64,16]{1,0:T(8,128)S(1)} %get-tuple-element.86), channel_id=1, source_target_pairs={{1,0},{2,1},{3,2},{4,3},{5,4},{6,5},{7,6},{8,7},{9,8},{10,9},{11,1... | collective-permute-start | bytes 12296 | tf_op jit(solution)/shard_map/ppermute | solution.py:64
  76.9 10.2 %tiles.7.refs_3_.refs_1_ = bf16[44,1024,512]{2,1,0:T(8,128)(2,1)} custom-call(s32[9]{0:T(128)S(1)} %pad_add_fusion.scalar_ref, f32[2,32,128]{2,1,0:T(8,128)S(1)} %copy-done.1, f32[2,16,128]{2,1,0:T(8,128)S(1)} %slice.74.refs_0_, f32[2,16,128]{2,1,0:T(8,128)S(1)} %slice.75.refs_1_, bf16[44,1024,512]{2,1,0:T(8,128)(2,1)} %tiles.6.refs_2_), custom_call_target="tpu_custom_call", output_to_operand_aliasing={{}: (4, {})} | custom-call | flops 47185920 | bytes 15728640 | tf_op jit(solution)/shard_map/tiles/pallas_call | solution.py:220
  87.2 3.3 %residual.1 = (f32[8,64,512]{2,1,0:T(8,128)}, f32[4,64,512]{2,1,0:T(8,128)}, f32[4,64,512]{2,1,0:T(8,128)}, f32[16,64,512]{2,1,0:T(8,128)}) custom-call(s32[8]{0:T(128)S(1)} %dynamic-slice_bitcast_fusion.target_ref, f32[64,32,128]{2,1,0:T(8,128)S(1)} %copy-done, f32[32,128]{1,0:T(8,128)S(1)} %get-tuple-element.128.weight_ref, ...), custom_call_target="tpu_custom_call" | custom-call | tf_op jit(solution)/shard_map/residual/pallas_call | solution.py:460
  90.6 3.8 %all-to-all-start.4 = ((f32[16,64,512]{2,1,0:T(8,128)}), f32[16,64,512]{2,1,0:T(8,128)S(1)}, u32[]{:S(2)}, u32[]{:S(2)}) async-start(f32[16,64,512]{2,1,0:T(8,128)} %get-tuple-element.99), calls=%async_computation.4 | async-start | bytes 4194304 | tf_op jit(solution)/shard_map/all_to_all | solution.py:512
  94.4 21.5 %applied.3.refs_0_.v_ref = f32[8,64,512]{2,1,0:T(8,128)} custom-call(s32[9]{0:T(128)S(1)} %pad_add_fusion.scalar_ref, s32[8]{0:T(128)S(1)} %dynamic-slice_bitcast_fusion.target_ref, f32[8,64,512]{2,1,0:T(8,128)} %get-tuple-element.91.refs_0_, f32[4,64,512]{2,1,0:T(8,128)} %get-tuple-element.92.refs_1_, f32[4,64,512]{2,1,0:T(8,128)} %get-tuple-element.93.refs_2_, ...), custom_call_target="tpu_custom_call" | custom-call | flops 6643777536 | bytes 46137344 | tf_op jit(solution)/shard_map/applied/pallas_call | solution.py:370
  119.2 3.6 %collective-permute-start.5 = (f32[4,64,512]{2,1,0:T(8,128)S(1)}, f32[4,64,512]{2,1,0:T(8,128)S(1)}, u32[]{:S(2)}, u32[]{:S(2)}) collective-permute-start(f32[4,64,512]{2,1,0:T(8,128)S(1)} %get-tuple-element.96), channel_id=1, source_target_pairs={{1,0},{2,1},{3,2},{4,3},{5,4},{6,5},{7,6},{8,7},{9,8},{10,9},{11,1... | collective-permute-start | bytes 1572872 | tf_op jit(solution)/shard_map/ppermute | solution.py:64
  122.8 16.5 %applied.4.refs_2_.refs_0_ = f32[8,64,512]{2,1,0:T(8,128)} custom-call(s32[9]{0:T(128)S(1)} %pad_add_fusion.scalar_ref, s32[8]{0:T(128)S(1)} %dynamic-slice_bitcast_fusion.target_ref, f32[8,64,512]{2,1,0:T(8,128)} %applied.3.refs_0_.v_ref, bf16[44,1024,512]{2,1,0:T(8,128)(2,1)} %tiles.7.refs_3_.refs_1_), custom_call_target="tpu_custom_call" | custom-call | flops 3925868544 | bytes 27262976 | tf_op jit(solution)/shard_map/applied/pallas_call | solution.py:370
  140.9 33.5 %spread.1 = f32[16,64,512]{2,1,0:T(8,128)} custom-call(s32[8]{0:T(128)S(1)} %dynamic-slice_bitcast_fusion.target_ref, f32[8,64,512]{2,1,0:T(8,128)} %applied.3.refs_0_.v_ref, f32[8,64,512]{2,1,0:T(8,128)} %applied.4.refs_2_.refs_0_, f32[4,64,512]{2,1,0:T(8,128)} %copy-done.4, f32[4,64,512]{2,1,0:T(8,128)} %copy-done.5), custom_call_target="tpu_custom_call" | custom-call | tf_op jit(solution)/shard_map/spread/pallas_call | solution.py:405
  174.4 4.4 %all-to-all-start.5 = ((f32[16,64,512]{2,1,0:T(8,128)}), f32[16,64,512]{2,1,0:T(8,128)}, u32[]{:S(2)}, u32[]{:S(2)}) async-start(f32[16,64,512]{2,1,0:T(8,128)} %spread.1), calls=%async_computation.5 | async-start | bytes 4194304 | tf_op jit(solution)/shard_map/all_to_all | solution.py:512
  178.9 9.4 %applied.5 = (f32[8,64,512]{2,1,0:T(8,128)}, f32[16,64,512]{2,1,0:T(8,128)}) custom-call(s32[9]{0:T(128)S(1)} %pad_add_fusion.scalar_ref, s32[8]{0:T(128)S(1)} %dynamic-slice_bitcast_fusion.target_ref, f32[4,64,512]{2,1,0:T(8,128)} %copy-done.4, f32[4,64,512]{2,1,0:T(8,128)} %copy-done.5, f32[8,64,512]{2,1,0:T(8,128)} %applied.4.refs_2_.refs_0_, ...), custom_call_target="tpu_custom_call" | custom-call | flops 2717908992 | bytes 18874368 | tf_op jit(solution)/shard_map/applied/pallas_call | solution.py:370
  200.9 12.9 %all-to-all-done.5.refs_1_.refs_4_.refs_7_.refs_10_.refs_13_.refs_16_.refs_19_.refs_22_ = f32[16,64,512]{2,1,0:T(8,128)} async-done(((f32[16,64,512]{2,1,0:T(8,128)}), f32[16,64,512]{2,1,0:T(8,128)}, u32[]{:S(2)}, u32[]{:S(2)}) %all-to-all-start.5) | async-done | bytes 2097184 | tf_op jit(solution)/shard_map/all_to_all | solution.py:512
  213.8 4.4 %all-to-all-start.6 = ((f32[16,64,512]{2,1,0:T(8,128)}), f32[16,64,512]{2,1,0:T(8,128)}, u32[]{:S(2)}, u32[]{:S(2)}) async-start(f32[16,64,512]{2,1,0:T(8,128)} %get-tuple-element.105), calls=%async_computation.6 | async-start | bytes 4194304 | tf_op jit(solution)/shard_map/all_to_all | solution.py:512
  224.8 20.7 %collective-permute-done.10 = f32[4,64]{1,0:T(4,128)S(1)} collective-permute-done((f32[4,64]{1,0:T(4,128)S(1)}, f32[4,64]{1,0:T(4,128)S(1)}, u32[]{:S(2)}, u32[]{:S(2)}) %collective-permute-start.10) | collective-permute-done | bytes 1056 | tf_op jit(solution)/shard_map/ppermute | solution.py:51
  245.5 4.1 %collective-permute-done.11 = f32[4,64]{1,0:T(4,128)S(1)} collective-permute-done((f32[4,64]{1,0:T(4,128)S(1)}, f32[4,64]{1,0:T(4,128)S(1)}, u32[]{:S(2)}, u32[]{:S(2)}) %collective-permute-start.11) | collective-permute-done | bytes 1056 | tf_op jit(solution)/shard_map/ppermute | solution.py:51
  256.5 4.7 %combine.1 = (f32[64,8,512]{2,1,0:T(8,128)}, f32[64,8,512]{2,1,0:T(8,128)}) custom-call(s32[8]{0:T(128)S(1)} %and_select_fusion.src_ref, f32[64,8]{1,0:T(8,128)S(1)} %copy.48.scale_ref, f32[16,64,512]{2,1,0:T(8,128)S(1)} %all-to-all-done.4.refs_0_.refs_3_.refs_6_.refs_9_.refs_12_.refs_15_.refs_18_.refs_21_, ...), custom_call_target="tpu_custom_call" | custom-call | tf_op jit(solution)/shard_map/combine/pallas_call | solution.py:497
  (106 shorter events, 48.2 us)
Async XLA Ops:
  0.6 10.6 %copy-start.1 = (f32[2,32,128]{2,1,0:T(8,128)S(1)}, f32[2,32,128]{2,1,0:T(8,128)}, u32[]{:S(2)}) copy-start(f32[2,32,128]{2,1,0:T(8,128)} %jitter_ref.3) | copy-start | bytes 98308
  4.9 13.4 %all-to-all-start = ((f32[8,72,32]{1,2,0:T(8,128)}), f32[8,72,32]{1,2,0:T(8,128)S(1)}, u32[]{:S(2)}, u32[]{:S(2)}) async-start(f32[8,72,32]{1,2,0:T(8,128)} %broadcast_in_dim.14), calls=%async_computation | async-start | bytes 262144 | tf_op jit(solution)/shard_map/all_to_all | solution.py:39
  20.1 27.4 %all-to-all-start.1 = ((f32[16,72,128]{2,1,0:T(8,128)}), f32[16,72,128]{2,1,0:T(8,128)S(1)}, u32[]{:S(2)}, u32[]{:S(2)}) async-start(f32[16,72,128]{2,1,0:T(8,128)} %broadcast_in_dim.15), calls=%async_computation.1 | async-start | bytes 1179648 | tf_op jit(solution)/shard_map/all_to_all | solution.py:39
  28.8 23.5 %collective-permute-start = (f32[67,16,128]{2,1,0:T(8,128)}, f32[67,16,128]{2,1,0:T(8,128)S(1)}, u32[]{:S(2)}, u32[]{:S(2)}) collective-permute-start(f32[67,16,128]{2,1,0:T(8,128)} %get-tuple-element.76), channel_id=1, source_target_pairs={{0,1},{1,2},{2,3},{3,4},{4,5},{5,6},{6,7},{7,8},{8,9},{9,10},{10,1... | collective-permute-start | bytes 1646600 | tf_op jit(solution)/shard_map/ppermute | solution.py:64
  30.7 21.5 %collective-permute-start.1 = (f32[67,16,128]{2,1,0:T(8,128)S(1)}, f32[67,16,128]{2,1,0:T(8,128)S(1)}, u32[]{:S(2)}, u32[]{:S(2)}) collective-permute-start(f32[67,16,128]{2,1,0:T(8,128)S(1)} %get-tuple-element.77), channel_id=1, source_target_pairs={{1,0},{2,1},{3,2},{4,3},{5,4},{6,5},{7,6},{8,7},{9,8},{10,9},{11,1... | collective-permute-start | bytes 1646600 | tf_op jit(solution)/shard_map/ppermute | solution.py:64
  54.0 10.8 %all-to-all-start.2 = ((f32[8,1,2048]{2,1,0:T(1,128)}), f32[8,1,2048]{2,1,0:T(1,128)S(1)}, u32[]{:S(2)}, u32[]{:S(2)}) async-start(f32[8,1,2048]{2,1,0:T(1,128)} %reshape.401), calls=%async_computation.2 | async-start | bytes 131072 | tf_op jit(solution)/shard_map/all_to_all | solution.py:39
  67.8 19.3 %all-to-all-start.3 = ((f32[16,64,128]{2,1,0:T(8,128)}), f32[16,64,128]{2,1,0:T(8,128)S(1)}, u32[]{:S(2)}, u32[]{:S(2)}) async-start(f32[16,64,128]{2,1,0:T(8,128)} %broadcast_in_dim.18), calls=%async_computation.3 | async-start | bytes 1048576 | tf_op jit(solution)/shard_map/all_to_all | solution.py:39
  71.6 15.7 %collective-permute-start.2 = (f32[64,16]{1,0:T(8,128)S(1)}, f32[64,16]{1,0:T(8,128)S(1)}, u32[]{:S(2)}, u32[]{:S(2)}) collective-permute-start(f32[64,16]{1,0:T(8,128)S(1)} %get-tuple-element.85), channel_id=1, source_target_pairs={{0,1},{1,2},{2,3},{3,4},{4,5},{5,6},{6,7},{7,8},{8,9},{9,10},{10,1... | collective-permute-start | bytes 12296 | tf_op jit(solution)/shard_map/ppermute | solution.py:64
  73.4 13.9 %collective-permute-start.3 = (f32[64,16]{1,0:T(8,128)S(1)}, f32[64,16]{1,0:T(8,128)S(1)}, u32[]{:S(2)}, u32[]{:S(2)}) collective-permute-start(f32[64,16]{1,0:T(8,128)S(1)} %get-tuple-element.86), channel_id=1, source_target_pairs={{1,0},{2,1},{3,2},{4,3},{5,4},{6,5},{7,6},{8,7},{9,8},{10,9},{11,1... | collective-permute-start | bytes 12296 | tf_op jit(solution)/shard_map/ppermute | solution.py:64
  90.6 83.8 %all-to-all-start.4 = ((f32[16,64,512]{2,1,0:T(8,128)}), f32[16,64,512]{2,1,0:T(8,128)S(1)}, u32[]{:S(2)}, u32[]{:S(2)}) async-start(f32[16,64,512]{2,1,0:T(8,128)} %get-tuple-element.99), calls=%async_computation.4 | async-start | bytes 4194304 | tf_op jit(solution)/shard_map/all_to_all | solution.py:512
  117.2 22.1 %collective-permute-start.4 = (f32[4,64,512]{2,1,0:T(8,128)S(1)}, f32[4,64,512]{2,1,0:T(8,128)S(1)}, u32[]{:S(2)}, u32[]{:S(2)}) collective-permute-start(f32[4,64,512]{2,1,0:T(8,128)S(1)} %get-tuple-element.95), channel_id=1, source_target_pairs={{0,1},{1,2},{2,3},{3,4},{4,5},{5,6},{6,7},{7,8},{8,9},{9,10},{10,1... | collective-permute-start | bytes 1572872 | tf_op jit(solution)/shard_map/ppermute | solution.py:64
  119.2 20.1 %collective-permute-start.5 = (f32[4,64,512]{2,1,0:T(8,128)S(1)}, f32[4,64,512]{2,1,0:T(8,128)S(1)}, u32[]{:S(2)}, u32[]{:S(2)}) collective-permute-start(f32[4,64,512]{2,1,0:T(8,128)S(1)} %get-tuple-element.96), channel_id=1, source_target_pairs={{1,0},{2,1},{3,2},{4,3},{5,4},{6,5},{7,6},{8,7},{9,8},{10,9},{11,1... | collective-permute-start | bytes 1572872 | tf_op jit(solution)/shard_map/ppermute | solution.py:64
  174.4 39.3 %all-to-all-start.5 = ((f32[16,64,512]{2,1,0:T(8,128)}), f32[16,64,512]{2,1,0:T(8,128)}, u32[]{:S(2)}, u32[]{:S(2)}) async-start(f32[16,64,512]{2,1,0:T(8,128)} %spread.1), calls=%async_computation.5 | async-start | bytes 4194304 | tf_op jit(solution)/shard_map/all_to_all | solution.py:512
  190.1 2.9 %collective-permute-start.6 = (f32[4,64]{1,0:T(4,128)S(1)}, f32[4,64]{1,0:T(4,128)S(1)}, u32[]{:S(2)}, u32[]{:S(2)}) collective-permute-start(f32[4,64]{1,0:T(4,128)S(1)} %pad_maximum_fusion.1), channel_id=1, source_target_pairs={{0,16},{16,0},{1,17},{17,1},{2,18},{18,2},{3,19},{19,3},{4,20},{20... | collective-permute-start | bytes 3080 | tf_op jit(solution)/shard_map/ppermute | solution.py:51
  193.0 5.7 %collective-permute-start.7 = (f32[4,64]{1,0:T(4,128)S(1)}, f32[4,64]{1,0:T(4,128)S(1)}, u32[]{:S(2)}, u32[]{:S(2)}) collective-permute-start(f32[4,64]{1,0:T(4,128)S(1)} %fusion.6), channel_id=1, source_target_pairs={{0,32},{32,64},{64,96},{96,0},{1,33},{33,65},{65,97},{97,1},{2,34}... | collective-permute-start | bytes 3080 | tf_op jit(solution)/shard_map/ppermute | solution.py:51
  194.8 5.1 %collective-permute-start.8 = (f32[4,64]{1,0:T(4,128)S(1)}, f32[4,64]{1,0:T(4,128)S(1)}, u32[]{:S(2)}, u32[]{:S(2)}) collective-permute-start(f32[4,64]{1,0:T(4,128)S(1)} %fusion.6), channel_id=1, source_target_pairs={{0,64},{32,96},{64,0},{96,32},{1,65},{33,97},{65,1},{97,33},{2,66}... | collective-permute-start | bytes 3080 | tf_op jit(solution)/shard_map/ppermute | solution.py:51
  197.3 3.6 %collective-permute-start.9 = (f32[4,64]{1,0:T(4,128)S(1)}, f32[4,64]{1,0:T(4,128)S(1)}, u32[]{:S(2)}, u32[]{:S(2)}) collective-permute-start(f32[4,64]{1,0:T(4,128)S(1)} %fusion.6), channel_id=1, source_target_pairs={{0,96},{32,0},{64,32},{96,64},{1,97},{33,1},{65,33},{97,65},{2,98}... | collective-permute-start | bytes 3080 | tf_op jit(solution)/shard_map/ppermute | solution.py:51
  213.8 42.8 %all-to-all-start.6 = ((f32[16,64,512]{2,1,0:T(8,128)}), f32[16,64,512]{2,1,0:T(8,128)}, u32[]{:S(2)}, u32[]{:S(2)}) async-start(f32[16,64,512]{2,1,0:T(8,128)} %get-tuple-element.105), calls=%async_computation.6 | async-start | bytes 4194304 | tf_op jit(solution)/shard_map/all_to_all | solution.py:512
  218.5 27.0 %collective-permute-start.10 = (f32[4,64]{1,0:T(4,128)S(1)}, f32[4,64]{1,0:T(4,128)S(1)}, u32[]{:S(2)}, u32[]{:S(2)}) collective-permute-start(f32[4,64]{1,0:T(4,128)S(1)} %add_add_fusion.2), channel_id=1, source_target_pairs={{0,1},{1,2},{2,3},{3,0},{4,5},{5,6},{6,7},{7,4},{8,9},{9,10},{10,1... | collective-permute-start | bytes 3080 | tf_op jit(solution)/shard_map/ppermute | solution.py:51
  220.3 29.3 %collective-permute-start.11 = (f32[4,64]{1,0:T(4,128)S(1)}, f32[4,64]{1,0:T(4,128)S(1)}, u32[]{:S(2)}, u32[]{:S(2)}) collective-permute-start(f32[4,64]{1,0:T(4,128)S(1)} %add_add_fusion.2), channel_id=1, source_target_pairs={{0,2},{1,3},{2,0},{3,1},{4,6},{5,7},{6,4},{7,5},{8,10},{9,11},{10,... | collective-permute-start | bytes 3080 | tf_op jit(solution)/shard_map/ppermute | solution.py:51
  223.0 26.6 %collective-permute-start.12 = (f32[4,64]{1,0:T(4,128)S(1)}, f32[4,64]{1,0:T(4,128)S(1)}, u32[]{:S(2)}, u32[]{:S(2)}) collective-permute-start(f32[4,64]{1,0:T(4,128)S(1)} %add_add_fusion.2), channel_id=1, source_target_pairs={{0,3},{1,0},{2,1},{3,2},{4,7},{5,4},{6,5},{7,6},{8,11},{9,8},{10,9... | collective-permute-start | bytes 3080 | tf_op jit(solution)/shard_map/ppermute | solution.py:51
  249.6 5.5 %collective-permute-start.13 = (f32[4,64]{1,0:T(4,128)S(1)}, f32[4,64]{1,0:T(4,128)S(1)}, u32[]{:S(2)}, u32[]{:S(2)}) collective-permute-start(f32[4,64]{1,0:T(4,128)S(1)} %add_add_fusion.1), channel_id=1, source_target_pairs={{0,4},{4,8},{8,12},{12,0},{1,5},{5,9},{9,13},{13,1},{2,6},{6,10},{... | collective-permute-start | bytes 3080 | tf_op jit(solution)/shard_map/ppermute | solution.py:51
  249.9 5.2 %collective-permute-start.14 = (f32[4,64]{1,0:T(4,128)S(1)}, f32[4,64]{1,0:T(4,128)S(1)}, u32[]{:S(2)}, u32[]{:S(2)}) collective-permute-start(f32[4,64]{1,0:T(4,128)S(1)} %add_add_fusion.1), channel_id=1, source_target_pairs={{0,8},{4,12},{8,0},{12,4},{1,9},{5,13},{9,1},{13,5},{2,10},{6,14},... | collective-permute-start | bytes 3080 | tf_op jit(solution)/shard_map/ppermute | solution.py:51
  252.6 3.7 %collective-permute-start.15 = (f32[4,64]{1,0:T(4,128)S(1)}, f32[4,64]{1,0:T(4,128)S(1)}, u32[]{:S(2)}, u32[]{:S(2)}) collective-permute-start(f32[4,64]{1,0:T(4,128)S(1)} %add_add_fusion.1), channel_id=1, source_target_pairs={{0,12},{4,0},{8,4},{12,8},{1,13},{5,1},{9,5},{13,9},{2,14},{6,2},{... | collective-permute-start | bytes 3080 | tf_op jit(solution)/shard_map/ppermute | solution.py:51
  (7 other events, 44.1 us)

commit v3 on v2

--- a/solution.py
+++ b/solution.py
@@ -32,6 +32,8 @@
 ROW_TILES, COL_TILES = 7, 15
 TILE_SLOTS = 4
 OP_SLOTS = 5
+EXTRA = 8
+EARLY_TILES = 12
 
 
 def sent_to_all(shard, axis):
@@ -258,28 +260,25 @@
     return main[:fields] + (main[fields:] + rest)
 
 
-def op_kernel(own, halo, send, scalar_ref, target_ref, *refs):
+def op_kernel(first, last, halo, held, send, scalar_ref, target_ref, *refs):
     refs = list(refs)
-    v_ref = refs.pop(0) if own else None
+    v_ref = refs.pop(0)
     beside_refs = [refs.pop(0), refs.pop(0)] if halo else []
-    held_ref = None if own else refs.pop(0)
+    held_ref = refs.pop(0) if held else None
     tiles_ref, out_ref = refs.pop(0), refs.pop(0)
     slots_ref = refs.pop(0) if send else None
     values, both_ref, total, buf, sem, in_sem, out_sem = refs
     fields = total.shape[1]
     offsets = offsets_of(scalar_ref)
-    mine = own_count(offsets) if own else 0
-    base = 0 if own else OWN_TILES
+    mine = (own_count(offsets) if last is None else last) - first
     count = mine + (halo_count(offsets) if halo else 0)
 
     def copy(t):
         slot = lax.rem(t, OP_SLOTS)
-        at = jnp.where(t < mine, t, t - mine + OWN_TILES) if own else t + OWN_TILES
+        at = jnp.where(t < mine, t + first, t - mine + OWN_TILES)
         return pltpu.make_async_copy(tiles_ref.at[at], buf.at[slot], sem.at[slot])
 
-    loads = []
-    if own:
-        loads.append((v_ref, 0, BLOCKS_DEV))
+    loads = [(v_ref, 0, BLOCKS_DEV)]
     for side, ref in enumerate(beside_refs):
         loads.append((ref, BLOCKS_DEV + REACH * side, REACH))
     arriving = [
@@ -315,7 +314,7 @@
 
     def with_another(t, carry):
         tile = arrive(t)
-        one, other = own_pair(t, offsets)
+        one, other = own_pair(t + first, offsets)
         total[one] += product(both_ref[other], tile, NN)
         total[other] += product(both_ref[one], tile, NT)
         return carry
@@ -327,9 +326,9 @@
         total[one] += product(both_ref[side], tile, NN)
         return carry
 
-    if own:
+    if first == 0:
         lax.fori_loop(0, BLOCKS_DEV, with_itself, 0)
-        lax.fori_loop(BLOCKS_DEV, mine, with_another, 0)
+    lax.fori_loop(max(BLOCKS_DEV - first, 0), mine, with_another, 0)
     if halo:
         lax.fori_loop(mine, count, with_beside, 0)
     leaving = [pltpu.make_async_copy(total, out_ref, out_sem.at[BLOCKS_DEV])]
@@ -342,8 +341,11 @@
 
 
 def out_copies(values_ref, slots_ref, target_ref, sem):
+    fields = values_ref.shape[1]
     return [
-        pltpu.make_async_copy(values_ref.at[g], slots_ref.at[target_ref[g]], sem.at[g])
+        pltpu.make_async_copy(
+            values_ref.at[g], slots_ref.at[target_ref[g], pl.ds(0, fields)], sem.at[g]
+        )
         for g in range(BLOCKS_DEV)
     ]
 
@@ -357,30 +359,31 @@
     return pltpu.with_memory_space_constraint(x, pltpu.HBM)
 
 
-def slot_shape(v):
-    return pltpu.HBM((lax.axis_size(SIXTEEN), *v.shape[1:]), jnp.float32)
-
-
-def applied(scalars, targets, tiles, v=None, beside=(), held=None, send=False):
-    shape = (held if v is None else v).shape
-    blocks, fields, _ = shape
-    out = pltpu.HBM(shape, jnp.float32)
+def slot_shape(v, extra=0):
+    _, fields, points = v.shape
+    return pltpu.HBM((lax.axis_size(SIXTEEN), fields + extra, points), jnp.float32)
+
+
+def applied(scalars, targets, tiles, v, tiles_of=(0, None), beside=(), held=None, extra=None):
+    blocks, fields, _ = v.shape
+    send = extra is not None
+    out = pltpu.HBM(v.shape, jnp.float32)
     ins = [in_hbm(x) for x in (v, *beside, held) if x is not None] + [tiles]
-    number = OWN_TILES * (v is not None) + HALO_TILES * bool(beside)
+    number = (tiles_of[1] or OWN_TILES) - tiles_of[0] + HALO_TILES * bool(beside)
     out = pl.pallas_call(
-        functools.partial(op_kernel, v is not None, bool(beside), send),
+        functools.partial(op_kernel, *tiles_of, bool(beside), held is not None, send),
         in_specs=[SMEM_SPEC] * 2 + [HBM_SPEC] * len(ins),
         out_specs=[HBM_SPEC] * (1 + send),
         scratch_shapes=[
             pltpu.VMEM((blocks + 2 * REACH, fields, BLOCK), jnp.float32),
             pltpu.VMEM((blocks + 2 * REACH, 2 * fields, BLOCK), jnp.bfloat16),
-            pltpu.VMEM(shape, jnp.float32),
+            pltpu.VMEM(v.shape, jnp.float32),
             pltpu.VMEM((OP_SLOTS, 2 * BLOCK, BLOCK), jnp.bfloat16),
             pltpu.SemaphoreType.DMA((OP_SLOTS,)),
             pltpu.SemaphoreType.DMA((4,)),
             pltpu.SemaphoreType.DMA((BLOCKS_DEV + 1,)),
         ],
-        out_shape=[out] + [slot_shape(out)] * send,
+        out_shape=[out] + [slot_shape(v, extra or 0)] * send,
         compiler_params=pltpu.CompilerParams(vmem_limit_bytes=24 << 20),
         cost_estimate=pl.CostEstimate(
             flops=3 * number * 3 * fields * BLOCK * BLOCK,
@@ -392,25 +395,47 @@
     return out if send else out[0]
 
 
-def spread_kernel(target_ref, v_ref, *refs):
-    slots_ref, sem = refs[-2:]
-    sent = out_copies(v_ref, slots_ref, target_ref, sem)
-    for copy_out in sent:
-        copy_out.start()
-    for copy_out in sent:
-        copy_out.wait()
-
-
-def spread(targets, v, *others):
+def gate_kernel(*refs):
+    pass
+
+
+def gate(slots, *others):
     return pl.pallas_call(
-        spread_kernel,
-        in_specs=[SMEM_SPEC] + [HBM_SPEC] * (1 + len(others)),
+        gate_kernel,
+        in_specs=[HBM_SPEC] + [VMEM_SPEC] * len(others),
         out_specs=HBM_SPEC,
-        scratch_shapes=[pltpu.SemaphoreType.DMA((BLOCKS_DEV,))],
-        out_shape=slot_shape(v),
+        out_shape=pltpu.HBM(slots.shape, jnp.float32),
+        input_output_aliases={0: 0},
         compiler_params=pltpu.CompilerParams(vmem_limit_bytes=1 << 20),
-        name="spread",
-    )(targets, *map(in_hbm, (v, *others)))
+        name="gate",
+    )(slots, *(other[0, :8, :COL_DEV] for other in others))
+
+
+def attach_kernel(rows_ref, slots_ref, out_ref, sem):
+    rows = rows_ref.shape[0]
+    copies = [
+        pltpu.make_async_copy(
+            rows_ref, out_ref.at[o, pl.ds(out_ref.shape[1] - rows, rows)], sem.at[o]
+        )
+        for o in range(out_ref.shape[0])
+    ]
+    for copy in copies:
+        copy.start()
+    for copy in copies:
+        copy.wait()
+
+
+def attach(slots, rows):
+    return pl.pallas_call(
+        attach_kernel,
+        in_specs=[VMEM_SPEC, HBM_SPEC],
+        out_specs=HBM_SPEC,
+        scratch_shapes=[pltpu.SemaphoreType.DMA((slots.shape[0],))],
+        out_shape=pltpu.HBM(slots.shape, jnp.float32),
+        input_output_aliases={1: 0},
+        compiler_params=pltpu.CompilerParams(vmem_limit_bytes=1 << 20),
+        name="attach",
+    )(rows, slots)
 
 
 def residual_kernel(
@@ -471,17 +496,26 @@
     )(targets, observations, weight, row_effect, before, before_row, after, after_row, col)
 
 
-def combine_kernel(src_ref, scale_ref, *refs):
-    ins, (x_ref, r_ref) = refs[:-2], refs[-2:]
-    scale = scale_ref[...]
+def combine_kernel(src_ref, sums_ref, *refs):
+    ins, (x_ref, r_ref, scale_ref) = refs[:-3], refs[-3:]
+    part = x_ref.shape[0]
+
+    @pl.when(pl.program_id(0) == 0)
+    def _():
+        sums = sums_ref[0, :, :COL_DEV]
+        for o in range(1, sums_ref.shape[0]):
+            sums = sums + sums_ref[o, :, :COL_DEV]
+        scale_ref[...] = step_scales(*(sums[k : k + 1] for k in range(4))).T
+
+    scale = scale_ref[pl.ds(pl.multiple_of(pl.program_id(0) * part, part), part), :]
     for j in range(BLOCKS_DEV):
         r0, m1, m2 = (ref[0] for ref in ins[3 * j : 3 * j + 3])
         x_ref[:, j, :] = scale[:, 0:1] * r0 + scale[:, 1:2] * m1
         r_ref[:, j, :] = scale[:, 2:3] * r0 + scale[:, 3:4] * m1 + scale[:, 4:5] * m2
 
 
-def combined(sources, scale, r0, m1, m2):
-    fields = r0.shape[1]
+def combined(sources, r0, m1, m2):
+    owners, fields, _ = r0.shape
     part = 16
     ins, specs = [], []
     for j in range(BLOCKS_DEV):
@@ -499,13 +533,15 @@
         grid_spec=pltpu.PrefetchScalarGridSpec(
             num_scalar_prefetch=1,
             grid=(fields // part,),
-            in_specs=[pl.BlockSpec((part, 8), lambda i, s: (i, 0))] + specs,
+            in_specs=[pl.BlockSpec((owners, EXTRA, COL_DEV), lambda i, s: (0, fields // EXTRA, 0))]
+            + specs,
             out_specs=[out, out],
+            scratch_shapes=[pltpu.VMEM((COL_DEV, 8), jnp.float32)],
         ),
         out_shape=[shape, shape],
         compiler_params=pltpu.CompilerParams(vmem_limit_bytes=20 << 20),
         name="combine",
-    )(sources, scale, *ins)
+    )(sources, m2, *ins)
 
 
 def to_owners(slots):
@@ -525,7 +561,7 @@
     r_m1 = -a0 * (1.0 - a1) - a1 * a0 * mu - a1 * beta
     r_m2 = a1 * a0
     zero = jnp.zeros_like(mu)
-    return jnp.stack([x_r0, x_m1, r_r0, r_m1, r_m2, zero, zero, zero], axis=1)
+    return jnp.concatenate([x_r0, x_m1, r_r0, r_m1, r_m2, zero, zero, zero], axis=0)
 
 
 def on_device(observations, huber_scale, observed, jitter, owner_map, neighbours):
@@ -596,27 +632,26 @@
         my_targets, observations, weight, row_effect, before, row_before, after, row_after, col_effect
     )
     owned_r0 = to_owners(slots)
-    m1 = applied(scalars, my_targets, tiles, r0, (r0_before, r0_after))
+    m1, slots = applied(
+        scalars, my_targets, tiles, r0, beside=(r0_before, r0_after), extra=0
+    )
     before, after, m1 = beside(m1, REACH)
-    part = applied(scalars, my_targets, tiles, m1)
-    slots = spread(my_targets, m1, part, before, after)
-    slots, owned_r0 = lax.optimization_barrier((slots, owned_r0))
+    part = applied(scalars, my_targets, tiles, m1, (0, EARLY_TILES))
+    slots = gate(slots, part, before, after, owned_r0)
     owned_m1 = to_owners(slots)
-    m2, slots = applied(scalars, my_targets, tiles, None, (before, after), part, True)
+    m2, slots = applied(
+        scalars, my_targets, tiles, m1, (EARLY_TILES, None), (before, after), part, EXTRA
+    )
     dots = jnp.stack(
         [jnp.sum(p * q, axis=(0, 2)) for p, q in ((r0, r0), (r0, m1), (m1, m1), (m1, m2))]
     )
-    dots = sum_wide(dots)
-    slots, owned_m1, dots = lax.optimization_barrier((slots, owned_m1, dots))
+    dots = sum_direct(dots, WIDE)
+    slots = attach(slots, jnp.pad(dots, ((0, EXTRA - 4), (0, BLOCK - fields))))
+    slots = gate(slots, owned_m1)
     owned_m2 = to_owners(slots)
-    for axis in SIXTEEN[::-1]:
-        dots = sum_direct(dots, axis)
-    scale = step_scales(*dots)
     owned = owned_table(group_map, sixteen_size, BLOCKS_DEV)
     my_ids = lax.dynamic_index_in_dim(owned, my_place, 0, keepdims=False)
-    solution_now, residual_now = combined(
-        my_ids // BLOCKS_DEV, scale, owned_r0, owned_m1, owned_m2
-    )
+    solution_now, residual_now = combined(my_ids // BLOCKS_DEV, owned_r0, owned_m1, owned_m2)
     return (solution_now[None, None], residual_now[None, None])
 
 

time: 263 us -> 230 us (0.87)
  Pallas kernels: 126 us -> 94 us
  local copies, waits for them, and re-layouts: 9.06 us -> 14 us
  starting transfers between devices: 68.6 us -> 64.2 us
    pallas_call x4 -> x6, Pallas kernels: 80.9 us -> 49.8 us  [the longest x3 49 us: applied(): pl.pallas_call(functools.partial(op_kernel, *tiles_of, bool(beside), held...]
    ppermute x10 -> x7, waiting for transfers between devices: 29.1 us -> 2.41 us  [sum_direct(): lax.ppermute(part, axis, [(i, (i + k) % peers) for i in range(peers)])]
    all_to_all x3, waiting for transfers between devices: 12.9 us -> 33.5 us  [to_owners(): return lax.all_to_all(slots, SIXTEEN, 0, 0, tiled=True)]
    ppermute x10 -> x7, starting transfers between devices: 19.2 us -> 13 us  [sum_direct(): lax.ppermute(part, axis, [(i, (i + k) % peers) for i in range(peers)])]
    ppermute x3, waiting for transfers between devices: 4.77 us -> 9.39 us  [beside(): lax.ppermute(last, SIXTEEN, up)]
    unnamed x20 -> x28, local copies, waits for them, and re-layouts: 2.58 us -> 6.91 us
  transfers between devices with their start and end apart: 23 -> 20, of which waited for: 8 -> 5; matrix products, arithmetic and copies ran while one was open for 3% -> 3% of each run, Pallas kernels for 45% -> 38%
where the time goes in v3:
time: 230 us; the launch traced here: 228 us
  Pallas kernels  94 us (41%)
  starting transfers between devices  64.2 us (28%)
  waiting for transfers between devices  45.3 us (20%)
  local copies, waits for them, and re-layouts  14 us (6%)
  other arithmetic  9.89 us (4%)
    pallas_call x3, Pallas kernels, applied(): pl.pallas_call(functools.partial(op_kernel, *tiles_of, bool(beside), held...  49 us
    pallas_call x4, Pallas kernels, covariance_tiles(): pl.pallas_call(functools.partial(tiles_kernel, first, count, len(beside_j...  37.8 us
    all_to_all x3, waiting for transfers between devices, to_owners(): return lax.all_to_all(slots, SIXTEEN, 0, 0, tiled=True)  33.5 us
    all_to_all x4, starting transfers between devices, sent_to_all(): lax.all_to_all(jnp.broadcast_to(shard[None], (peers, *shard.shape)), axis...  20.5 us
    all_to_all x3, starting transfers between devices, to_owners(): return lax.all_to_all(slots, SIXTEEN, 0, 0, tiled=True)  14.7 us
    ppermute x7, starting transfers between devices, sum_direct(): lax.ppermute(part, axis, [(i, (i + k) % peers) for i in range(peers)])  13 us
    ppermute x3, starting transfers between devices, beside(): lax.ppermute(initial, SIXTEEN, down)  12.3 us
    ppermute x3, waiting for transfers between devices, beside(): lax.ppermute(last, SIXTEEN, up)  9.39 us
  transfers between devices with their start and end apart: 20, of which 5 were waited for; matrix products, arithmetic and copies ran while one was open for 3% of the time, Pallas kernels for 38%

profile of v3, /device:TPU:0, one launch (start us, length us, event | category | flops | bytes accessed | tf_op | source)
XLA Modules:
  0.0 228.5 jit_solution(8743190852966080393)
XLA Ops:
  4.9 4.6 %all-to-all-start = ((f32[8,72,32]{1,2,0:T(8,128)}), f32[8,72,32]{1,2,0:T(8,128)S(1)}, u32[]{:S(2)}, u32[]{:S(2)}) async-start(f32[8,72,32]{1,2,0:T(8,128)} %broadcast_in_dim.14), calls=%async_computation | async-start | bytes 262144 | tf_op jit(solution)/shard_map/all_to_all | solution.py:41
  11.3 7.0 %tiles.4.refs_0_ = bf16[44,1024,512]{2,1,0:T(8,128)(2,1)} custom-call(s32[9]{0:T(128)S(1)} %pad_add_fusion.scalar_ref, f32[2,32,128]{2,1,0:T(8,128)S(1)} %copy-done.5), custom_call_target="tpu_custom_call" | custom-call | flops 22020096 | bytes 7340032 | tf_op jit(solution)/shard_map/tiles/pallas_call | solution.py:222
  20.0 7.9 %all-to-all-start.1 = ((f32[16,72,128]{2,1,0:T(8,128)}), f32[16,72,128]{2,1,0:T(8,128)S(1)}, u32[]{:S(2)}, u32[]{:S(2)}) async-start(f32[16,72,128]{2,1,0:T(8,128)} %broadcast_in_dim.15), calls=%async_computation.1 | async-start | bytes 1179648 | tf_op jit(solution)/shard_map/all_to_all | solution.py:41
  30.7 3.4 %collective-permute-start.1 = (f32[67,16,128]{2,1,0:T(8,128)S(1)}, f32[67,16,128]{2,1,0:T(8,128)S(1)}, u32[]{:S(2)}, u32[]{:S(2)}) collective-permute-start(f32[67,16,128]{2,1,0:T(8,128)S(1)} %get-tuple-element.74), channel_id=1, source_target_pairs={{1,0},{2,1},{3,2},{4,3},{5,4},{6,5},{7,6},{8,7},{9,8},{10,9},{11,1... | collective-permute-start | bytes 1646600 | tf_op jit(solution)/shard_map/ppermute | solution.py:66
  34.1 13.3 %tiles.5.refs_2_ = bf16[44,1024,512]{2,1,0:T(8,128)(2,1)} custom-call(s32[9]{0:T(128)S(1)} %pad_add_fusion.scalar_ref, f32[2,32,128]{2,1,0:T(8,128)S(1)} %copy-done.5, bf16[44,1024,512]{2,1,0:T(8,128)(2,1)} %tiles.4.refs_0_), custom_call_target="tpu_custom_call", output_to_operand_aliasing={{}: (2, {})} | custom-call | flops 47185920 | bytes 15728640 | tf_op jit(solution)/shard_map/tiles/pallas_call | solution.py:222
  47.5 4.8 %collective-permute-done.before_ref = f32[67,16,128]{2,1,0:T(8,128)S(1)} collective-permute-done((f32[67,16,128]{2,1,0:T(8,128)}, f32[67,16,128]{2,1,0:T(8,128)S(1)}, u32[]{:S(2)}, u32[]{:S(2)}) %collective-permute-start) | collective-permute-done | bytes 548896 | tf_op jit(solution)/shard_map/ppermute | solution.py:66
  54.0 4.4 %all-to-all-start.2 = ((f32[8,1,2048]{2,1,0:T(1,128)}), f32[8,1,2048]{2,1,0:T(1,128)S(1)}, u32[]{:S(2)}, u32[]{:S(2)}) async-start(f32[8,1,2048]{2,1,0:T(1,128)} %reshape.117), calls=%async_computation.2 | async-start | bytes 131072 | tf_op jit(solution)/shard_map/all_to_all | solution.py:41
  58.4 5.7 %tiles.6.refs_2_ = bf16[44,1024,512]{2,1,0:T(8,128)(2,1)} custom-call(s32[9]{0:T(128)S(1)} %pad_add_fusion.scalar_ref, f32[2,32,128]{2,1,0:T(8,128)S(1)} %copy-done.5, f32[2,16,128]{2,1,0:T(8,128)S(1)} %slice.89.refs_0_, f32[2,16,128]{2,1,0:T(8,128)S(1)} %slice.90.refs_1_, bf16[44,1024,512]{2,1,0:T(8,128)(2,1)} %tiles.5.refs_2_), custom_call_target="tpu_custom_call", output_to_operand_aliasing={{}: (4, {})} | custom-call | flops 22020096 | bytes 7340032 | tf_op jit(solution)/shard_map/tiles/pallas_call | solution.py:222
  67.1 3.6 %all-to-all-start.3 = ((f32[16,64,128]{2,1,0:T(8,128)}), f32[16,64,128]{2,1,0:T(8,128)S(1)}, u32[]{:S(2)}, u32[]{:S(2)}) async-start(f32[16,64,128]{2,1,0:T(8,128)} %broadcast_in_dim.18), calls=%async_computation.3 | async-start | bytes 1048576 | tf_op jit(solution)/shard_map/all_to_all | solution.py:41
  72.7 3.5 %collective-permute-start.3 = (f32[64,16]{1,0:T(8,128)S(1)}, f32[64,16]{1,0:T(8,128)S(1)}, u32[]{:S(2)}, u32[]{:S(2)}) collective-permute-start(f32[64,16]{1,0:T(8,128)S(1)} %get-tuple-element.83), channel_id=1, source_target_pairs={{1,0},{2,1},{3,2},{4,3},{5,4},{6,5},{7,6},{8,7},{9,8},{10,9},{11,1... | collective-permute-start | bytes 12296 | tf_op jit(solution)/shard_map/ppermute | solution.py:66
  76.2 11.8 %tiles.7.refs_3_.refs_1_.refs_4_ = bf16[44,1024,512]{2,1,0:T(8,128)(2,1)} custom-call(s32[9]{0:T(128)S(1)} %pad_add_fusion.scalar_ref, f32[2,32,128]{2,1,0:T(8,128)S(1)} %copy-done.5, f32[2,16,128]{2,1,0:T(8,128)S(1)} %slice.89.refs_0_, f32[2,16,128]{2,1,0:T(8,128)S(1)} %slice.90.refs_1_, ...), custom_call_target="tpu_custom_call", output_to_operand_aliasing={{}: (4, {})} | custom-call | flops 47185920 | bytes 15728640 | tf_op jit(solution)/shard_map/tiles/pallas_call | solution.py:222
  88.2 3.3 %residual.1 = (f32[8,64,512]{2,1,0:T(8,128)}, f32[4,64,512]{2,1,0:T(8,128)}, f32[4,64,512]{2,1,0:T(8,128)}, f32[16,64,512]{2,1,0:T(8,128)}) custom-call(s32[8]{0:T(128)S(1)} %dynamic-slice_bitcast_fusion.target_ref, f32[64,32,128]{2,1,0:T(8,128)S(1)} %copy-done.4, f32[32,128]{1,0:T(8,128)S(1)} %get-tuple-element.115.weight_ref, ...), custom_call_target="tpu_custom_call" | custom-call | tf_op jit(solution)/shard_map/residual/pallas_call | solution.py:485
  91.5 3.8 %all-to-all-start.4 = ((f32[16,64,512]{2,1,0:T(8,128)}), f32[16,64,512]{2,1,0:T(8,128)S(1)}, u32[]{:S(2)}, u32[]{:S(2)}) async-start(f32[16,64,512]{2,1,0:T(8,128)} %get-tuple-element.99), calls=%async_computation.4 | async-start | bytes 4194304 | tf_op jit(solution)/shard_map/all_to_all | solution.py:548
  95.3 21.9 %applied.3 = (f32[8,64,512]{2,1,0:T(8,128)}, f32[16,64,512]{2,1,0:T(8,128)}) custom-call(s32[9]{0:T(128)S(1)} %pad_add_fusion.scalar_ref, s32[8]{0:T(128)S(1)} %dynamic-slice_bitcast_fusion.target_ref, f32[8,64,512]{2,1,0:T(8,128)} %get-tuple-element.88.refs_0_, f32[4,64,512]{2,1,0:T(8,128)} %get-tuple-element.89.refs_1_, ...), custom_call_target="tpu_custom_call" | custom-call | flops 6643777536 | bytes 46137344 | tf_op jit(solution)/shard_map/applied/pallas_call | solution.py:373
  118.5 5.3 %collective-permute-start.5 = (f32[4,64,512]{2,1,0:T(8,128)S(1)}, f32[4,64,512]{2,1,0:T(8,128)S(1)}, u32[]{:S(2)}, u32[]{:S(2)}) collective-permute-start(f32[4,64,512]{2,1,0:T(8,128)S(1)} %get-tuple-element.95), channel_id=1, source_target_pairs={{1,0},{2,1},{3,2},{4,3},{5,4},{6,5},{7,6},{8,7},{9,8},{10,9},{11,1... | collective-permute-start | bytes 1572872 | tf_op jit(solution)/shard_map/ppermute | solution.py:66
  123.8 9.1 %applied.4.refs_3_ = f32[8,64,512]{2,1,0:T(8,128)} custom-call(s32[9]{0:T(128)S(1)} %pad_add_fusion.scalar_ref, s32[8]{0:T(128)S(1)} %dynamic-slice_bitcast_fusion.target_ref, f32[8,64,512]{2,1,0:T(8,128)} %get-tuple-element.93.refs_0_, bf16[44,1024,512]{2,1,0:T(8,128)(2,1)} %tiles.7.refs_3_.refs_1_.refs_4_), custom_call_target="tpu_custom_call" | custom-call | flops 1811939328 | bytes 12582912 | tf_op jit(solution)/shard_map/applied/pallas_call | solution.py:373
  133.6 4.6 %collective-permute-done.4.refs_1_ = f32[4,64,512]{2,1,0:T(8,128)S(1)} collective-permute-done((f32[4,64,512]{2,1,0:T(8,128)S(1)}, f32[4,64,512]{2,1,0:T(8,128)S(1)}, u32[]{:S(2)}, u32[]{:S(2)}) %collective-permute-start.4) | collective-permute-done | bytes 524320 | tf_op jit(solution)/shard_map/ppermute | solution.py:66
  139.7 3.7 %all-to-all-start.5 = ((f32[16,64,512]{2,1,0:T(8,128)}), f32[16,64,512]{2,1,0:T(8,128)S(1)}, u32[]{:S(2)}, u32[]{:S(2)}) async-start(f32[16,64,512]{2,1,0:T(8,128)} %gate.2), calls=%async_computation.5 | async-start | bytes 4194304 | tf_op jit(solution)/shard_map/all_to_all | solution.py:548
  143.5 18.0 %applied.5 = (f32[8,64,512]{2,1,0:T(8,128)}, f32[16,72,512]{2,1,0:T(8,128)}) custom-call(s32[9]{0:T(128)S(1)} %pad_add_fusion.scalar_ref, s32[8]{0:T(128)S(1)} %dynamic-slice_bitcast_fusion.target_ref, f32[8,64,512]{2,1,0:T(8,128)} %get-tuple-element.93.refs_0_, f32[4,64,512]{2,1,0:T(8,128)} %copy-done.9, f32[4,64,512]{2,1,0:T(8,128)} %copy-done.8, ...), custom_call_target="tpu_custom_call" | custom-call | flops 4831838208 | bytes 33554432 | tf_op jit(solution)/shard_map/applied/pallas_call | solution.py:373
  164.9 5.4 %collective-permute-start.11 = (f32[4,64]{1,0:T(4,128)S(1)}, f32[4,64]{1,0:T(4,128)S(1)}, u32[]{:S(2)}, u32[]{:S(2)}) collective-permute-start(f32[4,64]{1,0:T(4,128)S(1)} %pad_maximum_fusion.1), channel_id=1, source_target_pairs={{0,96},{16,112},{32,0},{48,16},{64,32},{80,48},{96,64},{112,80},{1... | collective-permute-start | bytes 3080 | tf_op jit(solution)/shard_map/ppermute | solution.py:53
  173.5 2.7 %collective-permute-start.9 = (f32[4,64]{1,0:T(4,128)S(1)}, f32[4,64]{1,0:T(4,128)S(1)}, u32[]{:S(2)}, u32[]{:S(2)}) collective-permute-start(f32[4,64]{1,0:T(4,128)S(1)} %pad_maximum_fusion.1), channel_id=1, source_target_pairs={{0,64},{16,80},{32,96},{48,112},{64,0},{80,16},{96,32},{112,48},{1... | collective-permute-start | bytes 3080 | tf_op jit(solution)/shard_map/ppermute | solution.py:53
  180.9 7.2 %all-to-all-start.6 = ((f32[16,72,512]{2,1,0:T(8,128)}), f32[16,72,512]{2,1,0:T(8,128)S(1)}, u32[]{:S(2)}, u32[]{:S(2)}) async-start(f32[16,72,512]{2,1,0:T(8,128)} %gate.3), calls=%async_computation.6 | async-start | bytes 4718592 | tf_op jit(solution)/shard_map/all_to_all | solution.py:548
  188.8 33.5 %all-to-all-done.6.sums_ref.refs_2_.refs_5_.refs_8_.refs_11_.refs_14_.refs_17_.refs_20_.refs_23_ = f32[16,72,512]{2,1,0:T(8,128)S(1)} async-done(((f32[16,72,512]{2,1,0:T(8,128)}), f32[16,72,512]{2,1,0:T(8,128)S(1)}, u32[]{:S(2)}, u32[]{:S(2)}) %all-to-all-start.6) | async-done | bytes 2359328 | tf_op jit(solution)/shard_map/all_to_all | solution.py:548
  225.4 3.1 %combine.1 = (f32[64,8,512]{2,1,0:T(8,128)}, f32[64,8,512]{2,1,0:T(8,128)}) custom-call(s32[8]{0:T(128)S(1)} %and_select_fusion.src_ref, f32[16,72,512]{2,1,0:T(8,128)S(1)} %all-to-all-done.6.sums_ref.refs_2_.refs_5_.refs_8_.refs_11_.refs_14_.refs_17_.refs_20_.refs_23_, f32[16,64,512]{2,1,0:T(8,128)S(1)} %copy-done.1, f32[16,64,512]{2,1,0:T(8,128)S(1)} %copy-done.3, ...), custom_call_target="tpu_custom_call" | custom-call | tf_op jit(solution)/shard_map/combine/pallas_call | solution.py:531
  (106 shorter events, 35.7 us)
Async XLA Ops:
  0.6 9.7 %copy-start.4 = (f32[64,32,128]{2,1,0:T(8,128)S(1)}, f32[64,32,128]{2,1,0:T(8,128)}, u32[]{:S(2)}) copy-start(f32[64,32,128]{2,1,0:T(8,128)} %obs_ref.1) | copy-start | bytes 3145732
  0.6 10.6 %copy-start.5 = (f32[2,32,128]{2,1,0:T(8,128)S(1)}, f32[2,32,128]{2,1,0:T(8,128)}, u32[]{:S(2)}) copy-start(f32[2,32,128]{2,1,0:T(8,128)} %jitter_ref.3) | copy-start | bytes 98308
  4.9 13.4 %all-to-all-start = ((f32[8,72,32]{1,2,0:T(8,128)}), f32[8,72,32]{1,2,0:T(8,128)S(1)}, u32[]{:S(2)}, u32[]{:S(2)}) async-start(f32[8,72,32]{1,2,0:T(8,128)} %broadcast_in_dim.14), calls=%async_computation | async-start | bytes 262144 | tf_op jit(solution)/shard_map/all_to_all | solution.py:41
  20.0 27.4 %all-to-all-start.1 = ((f32[16,72,128]{2,1,0:T(8,128)}), f32[16,72,128]{2,1,0:T(8,128)S(1)}, u32[]{:S(2)}, u32[]{:S(2)}) async-start(f32[16,72,128]{2,1,0:T(8,128)} %broadcast_in_dim.15), calls=%async_computation.1 | async-start | bytes 1179648 | tf_op jit(solution)/shard_map/all_to_all | solution.py:41
  28.8 23.5 %collective-permute-start = (f32[67,16,128]{2,1,0:T(8,128)}, f32[67,16,128]{2,1,0:T(8,128)S(1)}, u32[]{:S(2)}, u32[]{:S(2)}) collective-permute-start(f32[67,16,128]{2,1,0:T(8,128)} %get-tuple-element.73), channel_id=1, source_target_pairs={{0,1},{1,2},{2,3},{3,4},{4,5},{5,6},{6,7},{7,8},{8,9},{9,10},{10,1... | collective-permute-start | bytes 1646600 | tf_op jit(solution)/shard_map/ppermute | solution.py:66
  30.7 21.5 %collective-permute-start.1 = (f32[67,16,128]{2,1,0:T(8,128)S(1)}, f32[67,16,128]{2,1,0:T(8,128)S(1)}, u32[]{:S(2)}, u32[]{:S(2)}) collective-permute-start(f32[67,16,128]{2,1,0:T(8,128)S(1)} %get-tuple-element.74), channel_id=1, source_target_pairs={{1,0},{2,1},{3,2},{4,3},{5,4},{6,5},{7,6},{8,7},{9,8},{10,9},{11,1... | collective-permute-start | bytes 1646600 | tf_op jit(solution)/shard_map/ppermute | solution.py:66
  54.0 10.2 %all-to-all-start.2 = ((f32[8,1,2048]{2,1,0:T(1,128)}), f32[8,1,2048]{2,1,0:T(1,128)S(1)}, u32[]{:S(2)}, u32[]{:S(2)}) async-start(f32[8,1,2048]{2,1,0:T(1,128)} %reshape.117), calls=%async_computation.2 | async-start | bytes 131072 | tf_op jit(solution)/shard_map/all_to_all | solution.py:41
  67.1 20.9 %all-to-all-start.3 = ((f32[16,64,128]{2,1,0:T(8,128)}), f32[16,64,128]{2,1,0:T(8,128)S(1)}, u32[]{:S(2)}, u32[]{:S(2)}) async-start(f32[16,64,128]{2,1,0:T(8,128)} %broadcast_in_dim.18), calls=%async_computation.3 | async-start | bytes 1048576 | tf_op jit(solution)/shard_map/all_to_all | solution.py:41
  70.9 17.3 %collective-permute-start.2 = (f32[64,16]{1,0:T(8,128)S(1)}, f32[64,16]{1,0:T(8,128)S(1)}, u32[]{:S(2)}, u32[]{:S(2)}) collective-permute-start(f32[64,16]{1,0:T(8,128)S(1)} %get-tuple-element.82), channel_id=1, source_target_pairs={{0,1},{1,2},{2,3},{3,4},{4,5},{5,6},{6,7},{7,8},{8,9},{9,10},{10,1... | collective-permute-start | bytes 12296 | tf_op jit(solution)/shard_map/ppermute | solution.py:66
  72.7 15.5 %collective-permute-start.3 = (f32[64,16]{1,0:T(8,128)S(1)}, f32[64,16]{1,0:T(8,128)S(1)}, u32[]{:S(2)}, u32[]{:S(2)}) collective-permute-start(f32[64,16]{1,0:T(8,128)S(1)} %get-tuple-element.83), channel_id=1, source_target_pairs={{1,0},{2,1},{3,2},{4,3},{5,4},{6,5},{7,6},{8,7},{9,8},{10,9},{11,1... | collective-permute-start | bytes 12296 | tf_op jit(solution)/shard_map/ppermute | solution.py:66
  91.5 46.8 %all-to-all-start.4 = ((f32[16,64,512]{2,1,0:T(8,128)}), f32[16,64,512]{2,1,0:T(8,128)S(1)}, u32[]{:S(2)}, u32[]{:S(2)}) async-start(f32[16,64,512]{2,1,0:T(8,128)} %get-tuple-element.99), calls=%async_computation.4 | async-start | bytes 4194304 | tf_op jit(solution)/shard_map/all_to_all | solution.py:548
  118.5 15.1 %collective-permute-start.5 = (f32[4,64,512]{2,1,0:T(8,128)S(1)}, f32[4,64,512]{2,1,0:T(8,128)S(1)}, u32[]{:S(2)}, u32[]{:S(2)}) collective-permute-start(f32[4,64,512]{2,1,0:T(8,128)S(1)} %get-tuple-element.95), channel_id=1, source_target_pairs={{1,0},{2,1},{3,2},{4,3},{5,4},{6,5},{7,6},{8,7},{9,8},{10,9},{11,1... | collective-permute-start | bytes 1572872 | tf_op jit(solution)/shard_map/ppermute | solution.py:66
  123.8 14.4 %collective-permute-start.4 = (f32[4,64,512]{2,1,0:T(8,128)S(1)}, f32[4,64,512]{2,1,0:T(8,128)S(1)}, u32[]{:S(2)}, u32[]{:S(2)}) collective-permute-start(f32[4,64,512]{2,1,0:T(8,128)S(1)} %get-tuple-element.94), channel_id=1, source_target_pairs={{0,1},{1,2},{2,3},{3,4},{4,5},{5,6},{6,7},{7,8},{8,9},{9,10},{10,1... | collective-permute-start | bytes 1572872 | tf_op jit(solution)/shard_map/ppermute | solution.py:66
  139.7 39.8 %all-to-all-start.5 = ((f32[16,64,512]{2,1,0:T(8,128)}), f32[16,64,512]{2,1,0:T(8,128)S(1)}, u32[]{:S(2)}, u32[]{:S(2)}) async-start(f32[16,64,512]{2,1,0:T(8,128)} %gate.2), calls=%async_computation.5 | async-start | bytes 4194304 | tf_op jit(solution)/shard_map/all_to_all | solution.py:548
  143.4 18.0 %copy-start.6 = (f32[8,64,512]{2,1,0:T(8,128)S(1)}, f32[8,64,512]{2,1,0:T(8,128)}, u32[]{:S(2)}) copy-start(f32[8,64,512]{2,1,0:T(8,128)} %get-tuple-element.93.refs_0_) | copy-start | bytes 3145732
  143.4 18.0 %copy-start.7 = (f32[8,64,512]{2,1,0:T(8,128)S(1)}, f32[8,64,512]{2,1,0:T(8,128)}, u32[]{:S(2)}) copy-start(f32[8,64,512]{2,1,0:T(8,128)} %get-tuple-element.88.refs_0_) | copy-start | bytes 3145732
  163.2 8.9 %collective-permute-start.10 = (f32[4,64]{1,0:T(4,128)S(1)}, f32[4,64]{1,0:T(4,128)S(1)}, u32[]{:S(2)}, u32[]{:S(2)}) collective-permute-start(f32[4,64]{1,0:T(4,128)S(1)} %pad_maximum_fusion.1), channel_id=1, source_target_pairs={{0,80},{16,96},{32,112},{48,0},{64,16},{80,32},{96,48},{112,64},{1... | collective-permute-start | bytes 3080 | tf_op jit(solution)/shard_map/ppermute | solution.py:53
  164.9 8.6 %collective-permute-start.11 = (f32[4,64]{1,0:T(4,128)S(1)}, f32[4,64]{1,0:T(4,128)S(1)}, u32[]{:S(2)}, u32[]{:S(2)}) collective-permute-start(f32[4,64]{1,0:T(4,128)S(1)} %pad_maximum_fusion.1), channel_id=1, source_target_pairs={{0,96},{16,112},{32,0},{48,16},{64,32},{80,48},{96,64},{112,80},{1... | collective-permute-start | bytes 3080 | tf_op jit(solution)/shard_map/ppermute | solution.py:53
  170.4 5.8 %collective-permute-start.12 = (f32[4,64]{1,0:T(4,128)S(1)}, f32[4,64]{1,0:T(4,128)S(1)}, u32[]{:S(2)}, u32[]{:S(2)}) collective-permute-start(f32[4,64]{1,0:T(4,128)S(1)} %pad_maximum_fusion.1), channel_id=1, source_target_pairs={{0,112},{16,0},{32,16},{48,32},{64,48},{80,64},{96,80},{112,96},{1... | collective-permute-start | bytes 3080 | tf_op jit(solution)/shard_map/ppermute | solution.py:53
  170.4 5.8 %collective-permute-start.6 = (f32[4,64]{1,0:T(4,128)S(1)}, f32[4,64]{1,0:T(4,128)S(1)}, u32[]{:S(2)}, u32[]{:S(2)}) collective-permute-start(f32[4,64]{1,0:T(4,128)S(1)} %pad_maximum_fusion.1), channel_id=1, source_target_pairs={{0,16},{16,32},{32,48},{48,64},{64,80},{80,96},{96,112},{112,0},{1... | collective-permute-start | bytes 3080 | tf_op jit(solution)/shard_map/ppermute | solution.py:53
  170.9 5.3 %collective-permute-start.7 = (f32[4,64]{1,0:T(4,128)S(1)}, f32[4,64]{1,0:T(4,128)S(1)}, u32[]{:S(2)}, u32[]{:S(2)}) collective-permute-start(f32[4,64]{1,0:T(4,128)S(1)} %pad_maximum_fusion.1), channel_id=1, source_target_pairs={{0,32},{16,48},{32,64},{48,80},{64,96},{80,112},{96,0},{112,16},{1... | collective-permute-start | bytes 3080 | tf_op jit(solution)/shard_map/ppermute | solution.py:53
  172.2 4.5 %collective-permute-start.8 = (f32[4,64]{1,0:T(4,128)S(1)}, f32[4,64]{1,0:T(4,128)S(1)}, u32[]{:S(2)}, u32[]{:S(2)}) collective-permute-start(f32[4,64]{1,0:T(4,128)S(1)} %pad_maximum_fusion.1), channel_id=1, source_target_pairs={{0,48},{16,64},{32,80},{48,96},{64,112},{80,0},{96,16},{112,32},{1... | collective-permute-start | bytes 3080 | tf_op jit(solution)/shard_map/ppermute | solution.py:53
  173.5 5.1 %collective-permute-start.9 = (f32[4,64]{1,0:T(4,128)S(1)}, f32[4,64]{1,0:T(4,128)S(1)}, u32[]{:S(2)}, u32[]{:S(2)}) collective-permute-start(f32[4,64]{1,0:T(4,128)S(1)} %pad_maximum_fusion.1), channel_id=1, source_target_pairs={{0,64},{16,80},{32,96},{48,112},{64,0},{80,16},{96,32},{112,48},{1... | collective-permute-start | bytes 3080 | tf_op jit(solution)/shard_map/ppermute | solution.py:53
  180.9 41.3 %all-to-all-start.6 = ((f32[16,72,512]{2,1,0:T(8,128)}), f32[16,72,512]{2,1,0:T(8,128)S(1)}, u32[]{:S(2)}, u32[]{:S(2)}) async-start(f32[16,72,512]{2,1,0:T(8,128)} %gate.3), calls=%async_computation.6 | async-start | bytes 4718592 | tf_op jit(solution)/shard_map/all_to_all | solution.py:548
  (8 other events, 25.4 us)

commit v4 on v3

--- a/solution.py
+++ b/solution.py
@@ -22,6 +22,7 @@
 HUBER_EDGE = 1.345
 SILL_TERM = 0.02
 ROOT_THREE = 1.7320508075688772
+LOG2_E = 1.4426950408889634
 SPREAD = 2.0 * STRIP
 CUTOFF = 6.0 * STRIP
 BAND = 24
@@ -29,7 +30,7 @@
 
 OWN_TILES = BLOCKS_DEV + PAIRED * BLOCKS_DEV - 6
 HALO_TILES = 2 * (2 + 3 + 4)
-ROW_TILES, COL_TILES = 7, 15
+CHUNKS = (5, 9, 12, 18)
 TILE_SLOTS = 4
 OP_SLOTS = 5
 EXTRA = 8
@@ -154,8 +155,8 @@
 
     def evaluate(slot, to, frm, sill):
         for rb in range(STRIP):
-            row_b = jnp.broadcast_to(frm[:, rb : rb + 1], (COL_DEV, COL_DEV))
-            col_b = jnp.broadcast_to(frm[:, STRIP + rb : STRIP + rb + 1], (COL_DEV, COL_DEV))
+            row_b = jnp.broadcast_to(frm[rb : rb + 1], (COL_DEV, COL_DEV)).T
+            col_b = jnp.broadcast_to(frm[STRIP + rb : STRIP + rb + 1], (COL_DEV, COL_DEV)).T
             for u in range(COL_DEV // 2 // GROUP):
                 lo_s = slice(GROUP * u, GROUP * (u + 1))
                 hi_s = slice(64 + GROUP * u, 64 + GROUP * (u + 1))
@@ -172,8 +173,8 @@
                     fading = jnp.maximum(1.0 - far, 0.0)
                     fading = fading * fading
                     fading = fading * fading
-                    shape = (1.0 + a * far) * (sill + (sill * b) * far)
-                    value = shape * fading * jnp.exp(-a * far)
+                    shape = (sill + (sill * (a + b)) * far) + (sill * (a * b)) * square
+                    value = shape * fading * jnp.exp2((-a * LOG2_E) * far)
                     hi = value.astype(jnp.bfloat16)
                     lo = (value - hi.astype(jnp.float32)).astype(jnp.bfloat16)
                     lanes = slice(COL_DEV * ra, COL_DEV * (ra + 1))
@@ -203,7 +204,7 @@
                     other, beside_refs[1], STRIP * jnp.clip(other - BLOCKS_DEV, 0, REACH - 1)
                 )
                 frm = jnp.where(other < 0, left, jnp.where(other < BLOCKS_DEV, frm, right))
-            evaluate(slot, to, frm.T, sill)
+            evaluate(slot, to, frm, sill)
             out_copy(t).start()
 
         return carry
@@ -266,7 +267,7 @@
     beside_refs = [refs.pop(0), refs.pop(0)] if halo else []
     held_ref = refs.pop(0) if held else None
     tiles_ref, out_ref = refs.pop(0), refs.pop(0)
-    slots_ref = refs.pop(0) if send else None
+    slots_ref, dots_ref = (refs.pop(0), refs.pop(0)) if send else (None, None)
     values, both_ref, total, buf, sem, in_sem, out_sem = refs
     fields = total.shape[1]
     offsets = offsets_of(scalar_ref)
@@ -331,22 +332,44 @@
     lax.fori_loop(max(BLOCKS_DEV - first, 0), mine, with_another, 0)
     if halo:
         lax.fori_loop(mine, count, with_beside, 0)
-    leaving = [pltpu.make_async_copy(total, out_ref, out_sem.at[BLOCKS_DEV])]
+    leaving = [pltpu.make_async_copy(total, out_ref, out_sem.at[STRIP * BLOCKS_DEV])]
     if send:
         leaving += out_copies(total, slots_ref, target_ref, out_sem)
     for out in leaving:
         out.start()
+    if send:
+        lane = lax.broadcasted_iota(jnp.int32, (fields, COL_DEV), 1)
+        dots = jnp.zeros((fields, COL_DEV), jnp.float32)
+        for at, one, other in products_of(values, total, held):
+            summed = functools.reduce(jnp.add, [one[g] * other[g] for g in range(BLOCKS_DEV)])
+            dots = jnp.where(lane == at, jnp.sum(summed, axis=1, keepdims=True), dots)
+        dots = jnp.concatenate([dots, jnp.zeros((COL_DEV - fields, COL_DEV), jnp.float32)], axis=0)
+        dots_ref[...] = dots.T[:EXTRA]
     for out in leaving:
         out.wait()
 
 
+def products_of(v, image, second):
+    if second:
+        return [(3, v, image)]
+    return [(0, v, v), (1, v, image), (2, image, image)]
+
+
 def out_copies(values_ref, slots_ref, target_ref, sem):
     fields = values_ref.shape[1]
+    if slots_ref.shape[2] == BLOCK:
+        return [
+            pltpu.make_async_copy(values_ref.at[g], slots_ref.at[target_ref[g]], sem.at[g])
+            for g in range(BLOCKS_DEV)
+        ]
     return [
         pltpu.make_async_copy(
-            values_ref.at[g], slots_ref.at[target_ref[g], pl.ds(0, fields)], sem.at[g]
+            values_ref.at[g, :, pl.ds(COL_DEV * ra, COL_DEV)],
+            slots_ref.at[target_ref[g], pl.ds(fields * ra, fields)],
+            sem.at[STRIP * g + ra],
         )
         for g in range(BLOCKS_DEV)
+        for ra in range(STRIP)
     ]
 
 
@@ -361,7 +384,8 @@
 
 def slot_shape(v, extra=0):
     _, fields, points = v.shape
-    return pltpu.HBM((lax.axis_size(SIXTEEN), fields + extra, points), jnp.float32)
+    block = (STRIP * fields + extra, points // STRIP) if extra else (fields, points)
+    return pltpu.HBM((lax.axis_size(SIXTEEN), *block), jnp.float32)
 
 
 def applied(scalars, targets, tiles, v, tiles_of=(0, None), beside=(), held=None, extra=None):
@@ -373,7 +397,7 @@
     out = pl.pallas_call(
         functools.partial(op_kernel, *tiles_of, bool(beside), held is not None, send),
         in_specs=[SMEM_SPEC] * 2 + [HBM_SPEC] * len(ins),
-        out_specs=[HBM_SPEC] * (1 + send),
+        out_specs=[HBM_SPEC] + [HBM_SPEC, VMEM_SPEC] * send,
         scratch_shapes=[
             pltpu.VMEM((blocks + 2 * REACH, fields, BLOCK), jnp.float32),
             pltpu.VMEM((blocks + 2 * REACH, 2 * fields, BLOCK), jnp.bfloat16),
@@ -381,9 +405,10 @@
             pltpu.VMEM((OP_SLOTS, 2 * BLOCK, BLOCK), jnp.bfloat16),
             pltpu.SemaphoreType.DMA((OP_SLOTS,)),
             pltpu.SemaphoreType.DMA((4,)),
-            pltpu.SemaphoreType.DMA((BLOCKS_DEV + 1,)),
+            pltpu.SemaphoreType.DMA((STRIP * BLOCKS_DEV + 1,)),
         ],
-        out_shape=[out] + [slot_shape(v, extra or 0)] * send,
+        out_shape=[out]
+        + [slot_shape(v, extra or 0), jax.ShapeDtypeStruct((EXTRA, COL_DEV), jnp.float32)] * send,
         compiler_params=pltpu.CompilerParams(vmem_limit_bytes=24 << 20),
         cost_estimate=pl.CostEstimate(
             flops=3 * number * 3 * fields * BLOCK * BLOCK,
@@ -502,30 +527,32 @@
 
     @pl.when(pl.program_id(0) == 0)
     def _():
-        sums = sums_ref[0, :, :COL_DEV]
-        for o in range(1, sums_ref.shape[0]):
-            sums = sums + sums_ref[o, :, :COL_DEV]
+        sums = functools.reduce(jnp.add, [sums_ref[o] for o in range(sums_ref.shape[0])])
         scale_ref[...] = step_scales(*(sums[k : k + 1] for k in range(4))).T
 
     scale = scale_ref[pl.ds(pl.multiple_of(pl.program_id(0) * part, part), part), :]
     for j in range(BLOCKS_DEV):
-        r0, m1, m2 = (ref[0] for ref in ins[3 * j : 3 * j + 3])
-        x_ref[:, j, :] = scale[:, 0:1] * r0 + scale[:, 1:2] * m1
-        r_ref[:, j, :] = scale[:, 2:3] * r0 + scale[:, 3:4] * m1 + scale[:, 4:5] * m2
+        r0_ref, m1_ref, *m2_refs = ins[(2 + STRIP) * j : (2 + STRIP) * (j + 1)]
+        for ra in range(STRIP):
+            lanes = slice(COL_DEV * ra, COL_DEV * (ra + 1))
+            r0, m1, m2 = r0_ref[0, :, lanes], m1_ref[0, :, lanes], m2_refs[ra][0]
+            x_ref[:, j, lanes] = scale[:, 0:1] * r0 + scale[:, 1:2] * m1
+            r_ref[:, j, lanes] = scale[:, 2:3] * r0 + scale[:, 3:4] * m1 + scale[:, 4:5] * m2
 
 
 def combined(sources, r0, m1, m2):
     owners, fields, _ = r0.shape
     part = 16
     ins, specs = [], []
+    r0, m1 = in_hbm(r0), in_hbm(m1)
+
+    def chosen(j, points, at):
+        return pl.BlockSpec((1, part, points), lambda i, s: (s[j], at // part + i, 0))
+
     for j in range(BLOCKS_DEV):
-        for v in (r0, m1, m2):
-            ins.append(v)
-            specs.append(
-                pl.BlockSpec(
-                    (1, part, BLOCK), functools.partial(lambda j, i, s: (s[j], i, 0), j)
-                )
-            )
+        ins += [r0, m1] + [m2] * STRIP
+        specs += [chosen(j, BLOCK, 0)] * 2
+        specs += [chosen(j, COL_DEV, fields * ra) for ra in range(STRIP)]
     out = pl.BlockSpec((part, BLOCKS_DEV, BLOCK), lambda i, s: (i, 0, 0))
     shape = jax.ShapeDtypeStruct((fields, BLOCKS_DEV, BLOCK), jnp.float32)
     return pl.pallas_call(
@@ -533,7 +560,9 @@
         grid_spec=pltpu.PrefetchScalarGridSpec(
             num_scalar_prefetch=1,
             grid=(fields // part,),
-            in_specs=[pl.BlockSpec((owners, EXTRA, COL_DEV), lambda i, s: (0, fields // EXTRA, 0))]
+            in_specs=[
+                pl.BlockSpec((owners, EXTRA, COL_DEV), lambda i, s: (0, STRIP * fields // EXTRA, 0))
+            ]
             + specs,
             out_specs=[out, out],
             scratch_shapes=[pltpu.VMEM((COL_DEV, 8), jnp.float32)],
@@ -600,53 +629,59 @@
         [neighbours[0, 0], jnp.stack([my_place, group_place, total_strips * STRIP])]
     ).astype(jnp.int32)
 
-    def beside_tiles(part, axis, count, tiles, first, near):
-        if first:
+    def beside_tiles(part, axis, chunk, tiles, near=()):
+        first = sum(CHUNKS[:chunk])
+        if chunk:
             part, tiles = lax.optimization_barrier((part, tiles))
-        total = over_copies(part, axis)
-        tiles = covariance_tiles(first, count, scalars, jitter, near, tiles)
-        total, tiles = lax.optimization_barrier((total, tiles))
-        return total, tiles, first + count
+        received = sent_to_all(part, axis)
+        tiles = covariance_tiles(first, CHUNKS[chunk], scalars, jitter, near, tiles)
+        return lax.optimization_barrier((received, tiles))
 
     edges = jnp.concatenate([observations, weight[None], jitter], axis=0)
     before, after, _ = beside(edges, REACH * STRIP, 1)
-    total, tiles, first = beside_tiles(part, WIDE, ROW_TILES, None, 0, ())
+    received, tiles = beside_tiles(part, WIDE, 0, None)
+    total = jnp.sum(received, axis=0)
     row_count = jnp.maximum(total[fields], 1.0)
     row_effect = huber_scale[:, None] * total[:fields] / row_count[None, :]
     part = with_count(jnp.sum(terms(row_effect, col_effect), axis=1), jnp.sum(weight, axis=0))
-    total, tiles, first = beside_tiles(part, SIXTEEN, COL_TILES, tiles, first, ())
-    total, before, after = lax.optimization_barrier((total, before, after))
-    near = (before[fields + 1 :], after[fields + 1 :])
+    received, tiles = beside_tiles(part, SIXTEEN, 1, tiles)
+    total = jnp.sum(received, axis=0)
     col_count = jnp.maximum(total[fields], 1.0)
     col_effect = huber_scale[:, None] * total[:fields] / col_count[None, :]
     part = jnp.sum(terms(row_effect, col_effect), axis=2)
-    total, tiles, first = beside_tiles(part, WIDE, ROW_TILES, tiles, first, near)
-    row_effect = row_effect + huber_scale[:, None] * total / row_count[None, :]
+    received, tiles = beside_tiles(part, WIDE, 2, tiles)
+    received, before, after = lax.optimization_barrier((received, before, after))
+    near = (before[fields + 1 :], after[fields + 1 :])
+    row_effect = row_effect + huber_scale[:, None] * jnp.sum(received, axis=0) / row_count[None, :]
     part = jnp.sum(terms(row_effect, col_effect), axis=1)
-    row_before, row_after, _ = beside(row_effect, REACH * STRIP, 1)
-    total, tiles, first = beside_tiles(part, SIXTEEN, COL_TILES, tiles, first, near)
+    part = jnp.concatenate([part, row_effect.reshape(-1, col_dev)], axis=0)
+    received, tiles = beside_tiles(part, SIXTEEN, 3, tiles, near)
+    total = jnp.sum(received[:, :fields], axis=0)
     col_effect = col_effect + huber_scale[:, None] * total / col_count[None, :]
+
+    def rows_of(place, first):
+        rows = lax.dynamic_index_in_dim(received[:, fields:], place % sixteen_size, 0, False)
+        return rows.reshape(fields, row_dev)[:, first : first + REACH * STRIP]
+
+    row_before = rows_of(my_place + sixteen_size - 1, row_dev - REACH * STRIP)
+    row_after = rows_of(my_place + 1, 0)
 
     my_targets = lax.dynamic_slice_in_dim(group_map, my_place * BLOCKS_DEV, BLOCKS_DEV)
     r0, r0_before, r0_after, slots = residual_of(
         my_targets, observations, weight, row_effect, before, row_before, after, row_after, col_effect
     )
     owned_r0 = to_owners(slots)
-    m1, slots = applied(
+    m1, slots, dots = applied(
         scalars, my_targets, tiles, r0, beside=(r0_before, r0_after), extra=0
     )
     before, after, m1 = beside(m1, REACH)
     part = applied(scalars, my_targets, tiles, m1, (0, EARLY_TILES))
     slots = gate(slots, part, before, after, owned_r0)
     owned_m1 = to_owners(slots)
-    m2, slots = applied(
+    m2, slots, last = applied(
         scalars, my_targets, tiles, m1, (EARLY_TILES, None), (before, after), part, EXTRA
     )
-    dots = jnp.stack(
-        [jnp.sum(p * q, axis=(0, 2)) for p, q in ((r0, r0), (r0, m1), (m1, m1), (m1, m2))]
-    )
-    dots = sum_direct(dots, WIDE)
-    slots = attach(slots, jnp.pad(dots, ((0, EXTRA - 4), (0, BLOCK - fields))))
+    slots = attach(slots, sum_direct(dots + last, WIDE))
     slots = gate(slots, owned_m1)
     owned_m2 = to_owners(slots)
     owned = owned_table(group_map, sixteen_size, BLOCKS_DEV)

time: 230 us -> 213 us (0.926)
  starting transfers between devices: 64.2 us -> 53 us
  Pallas kernels: 94 us -> 91.2 us
  other arithmetic: 9.89 us -> 7.35 us
    ppermute x3 -> x2, waiting for transfers between devices: 9.39 us -> 2.6 us  [beside(): lax.ppermute(last, SIXTEEN, up)]
    pallas_call x4, Pallas kernels: 37.8 us -> 31.7 us  [covariance_tiles(): pl.pallas_call(functools.partial(tiles_kernel, first, count, len(beside_j...]
    ppermute x3 -> x2, waiting for transfers between devices: 0.01 us -> 5.35 us  [beside(): lax.ppermute(initial, SIXTEEN, down)]
    ppermute x7, starting transfers between devices: 13 us -> 8.04 us  [sum_direct(): lax.ppermute(part, axis, [(i, (i + k) % peers) for i in range(peers)])]
    ppermute x3 -> x2, starting transfers between devices: 12.3 us -> 8.74 us  [beside(): lax.ppermute(initial, SIXTEEN, down)]
    pallas_call x1, Pallas kernels: 3.06 us -> 5.91 us  [combined(): pl.pallas_call(combine_kernel, grid_spec=pltpu.PrefetchScalarGridSpec(num...]
    unnamed x28 -> x23, local copies, waits for them, and re-layouts: 6.91 us -> 4.59 us
  transfers between devices with their start and end apart: 20 -> 18, of which waited for: 5 -> 7; matrix products, arithmetic and copies ran while one was open for 3% -> 4% of each run, Pallas kernels for 38% -> 39%
where the time goes in v4:
time: 213 us; the launch traced here: 211 us
  Pallas kernels  91.2 us (43%)
  starting transfers between devices  53 us (25%)
  waiting for transfers between devices  46.6 us (22%)
  local copies, waits for them, and re-layouts  11.9 us (6%)
  other arithmetic  7.35 us (3%)
    pallas_call x3, Pallas kernels, applied(): pl.pallas_call(functools.partial(op_kernel, *tiles_of, bool(beside), held...  49.5 us
    all_to_all x3, waiting for transfers between devices, to_owners(): return lax.all_to_all(slots, SIXTEEN, 0, 0, tiled=True)  35.5 us
    pallas_call x4, Pallas kernels, covariance_tiles(): pl.pallas_call(functools.partial(tiles_kernel, first, count, len(beside_j...  31.7 us
    all_to_all x4, starting transfers between devices, sent_to_all(): lax.all_to_all(jnp.broadcast_to(shard[None], (peers, *shard.shape)), axis...  21.1 us
    all_to_all x3, starting transfers between devices, to_owners(): return lax.all_to_all(slots, SIXTEEN, 0, 0, tiled=True)  13.2 us
    ppermute x2, starting transfers between devices, beside(): lax.ppermute(initial, SIXTEEN, down)  8.74 us
    ppermute x7, starting transfers between devices, sum_direct(): lax.ppermute(part, axis, [(i, (i + k) % peers) for i in range(peers)])  8.04 us
    pallas_call x1, Pallas kernels, combined(): pl.pallas_call(combine_kernel, grid_spec=pltpu.PrefetchScalarGridSpec(num...  5.91 us
  transfers between devices with their start and end apart: 18, of which 7 were waited for; matrix products, arithmetic and copies ran while one was open for 4% of the time, Pallas kernels for 39%

profile of v4, /device:TPU:0, one launch (start us, length us, event | category | flops | bytes accessed | tf_op | source)
XLA Modules:
  0.0 211.3 jit_solution(9548302833324718456)
XLA Ops:
  4.8 4.6 %all-to-all-start = ((f32[8,72,32]{1,2,0:T(8,128)}), f32[8,72,32]{1,2,0:T(8,128)S(1)}, u32[]{:S(2)}, u32[]{:S(2)}) async-start(f32[8,72,32]{1,2,0:T(8,128)} %broadcast_in_dim.14), calls=%async_computation | async-start | bytes 262144 | tf_op jit(solution)/shard_map/all_to_all | solution.py:42
  11.1 4.8 %tiles.4.refs_0_ = bf16[44,1024,512]{2,1,0:T(8,128)(2,1)} custom-call(s32[9]{0:T(128)S(1)} %pad_add_fusion.scalar_ref, f32[2,32,128]{2,1,0:T(8,128)S(1)} %copy-done.1), custom_call_target="tpu_custom_call" | custom-call | flops 15728640 | bytes 5242880 | tf_op jit(solution)/shard_map/tiles/pallas_call | solution.py:223
  17.6 7.9 %all-to-all-start.1 = ((f32[16,72,128]{2,1,0:T(8,128)}), f32[16,72,128]{2,1,0:T(8,128)S(1)}, u32[]{:S(2)}, u32[]{:S(2)}) async-start(f32[16,72,128]{2,1,0:T(8,128)} %broadcast_in_dim.15), calls=%async_computation.1 | async-start | bytes 1179648 | tf_op jit(solution)/shard_map/all_to_all | solution.py:42
  26.5 1.9 collective-permute-start
  28.4 3.4 %collective-permute-start.1 = (f32[67,16,128]{2,1,0:T(8,128)S(1)}, f32[67,16,128]{2,1,0:T(8,128)S(1)}, u32[]{:S(2)}, u32[]{:S(2)}) collective-permute-start(f32[67,16,128]{2,1,0:T(8,128)S(1)} %get-tuple-element.77), channel_id=1, source_target_pairs={{1,0},{2,1},{3,2},{4,3},{5,4},{6,5},{7,6},{8,7},{9,8},{10,9},{11,1... | collective-permute-start | bytes 1646600 | tf_op jit(solution)/shard_map/ppermute | solution.py:67
  31.9 7.4 %tiles.5.refs_0_ = bf16[44,1024,512]{2,1,0:T(8,128)(2,1)} custom-call(s32[9]{0:T(128)S(1)} %pad_add_fusion.scalar_ref, f32[2,32,128]{2,1,0:T(8,128)S(1)} %copy-done.2, bf16[44,1024,512]{2,1,0:T(8,128)(2,1)} %tiles.4.refs_0_), custom_call_target="tpu_custom_call", output_to_operand_aliasing={{}: (2, {})} | custom-call | flops 28311552 | bytes 9437184 | tf_op jit(solution)/shard_map/tiles/pallas_call | solution.py:223
  41.0 4.8 %all-to-all-start.2 = ((f32[8,1,2048]{2,1,0:T(1,128)}), f32[8,1,2048]{2,1,0:T(1,128)S(1)}, u32[]{:S(2)}, u32[]{:S(2)}) async-start(f32[8,1,2048]{2,1,0:T(1,128)} %reshape.131), calls=%async_computation.2 | async-start | bytes 131072 | tf_op jit(solution)/shard_map/all_to_all | solution.py:42
  45.8 8.8 %tiles.6.refs_2_ = bf16[44,1024,512]{2,1,0:T(8,128)(2,1)} custom-call(s32[9]{0:T(128)S(1)} %pad_add_fusion.scalar_ref, f32[2,32,128]{2,1,0:T(8,128)S(1)} %copy-done.2, bf16[44,1024,512]{2,1,0:T(8,128)(2,1)} %tiles.5.refs_0_), custom_call_target="tpu_custom_call", output_to_operand_aliasing={{}: (2, {})} | custom-call | flops 37748736 | bytes 12582912 | tf_op jit(solution)/shard_map/tiles/pallas_call | solution.py:223
  57.8 3.9 %all-to-all-start.3 = ((f32[16,80,128]{2,1,0:T(8,128)}), f32[16,80,128]{2,1,0:T(8,128)S(1)}, u32[]{:S(2)}, u32[]{:S(2)}) async-start(f32[16,80,128]{2,1,0:T(8,128)} %broadcast_in_dim.18), calls=%async_computation.3 | async-start | bytes 1310720 | tf_op jit(solution)/shard_map/all_to_all | solution.py:42
  61.8 10.7 %tiles.7.refs_3_.refs_1_.refs_4_ = bf16[44,1024,512]{2,1,0:T(8,128)(2,1)} custom-call(s32[9]{0:T(128)S(1)} %pad_add_fusion.scalar_ref, f32[2,32,128]{2,1,0:T(8,128)S(1)} %copy-done.2, f32[2,16,128]{2,1,0:T(8,128)S(1)} %slice.96.refs_0_, f32[2,16,128]{2,1,0:T(8,128)S(1)} %slice.97.refs_1_, ...), custom_call_target="tpu_custom_call", output_to_operand_aliasing={{}: (4, {})} | custom-call | flops 56623104 | bytes 18874368 | tf_op jit(solution)/shard_map/tiles/pallas_call | solution.py:223
  74.3 3.3 %residual.1 = (f32[8,64,512]{2,1,0:T(8,128)}, f32[4,64,512]{2,1,0:T(8,128)}, f32[4,64,512]{2,1,0:T(8,128)}, f32[16,64,512]{2,1,0:T(8,128)}) custom-call(s32[8]{0:T(128)S(1)} %fusion.4.target_ref, f32[64,32,128]{2,1,0:T(8,128)S(1)} %copy-done, f32[32,128]{1,0:T(8,128)S(1)} %get-tuple-element.109.weight_ref, f32[64,32]{1,0:T(8,128)S(1)} %divide_add_fusion.1.row_ref, ...), custom_call_target="tpu_custom_call" | custom-call | tf_op jit(solution)/shard_map/residual/pallas_call | solution.py:510
  77.6 5.8 %all-to-all-start.4 = ((f32[16,64,512]{2,1,0:T(8,128)}), f32[16,64,512]{2,1,0:T(8,128)S(1)}, u32[]{:S(2)}, u32[]{:S(2)}) async-start(f32[16,64,512]{2,1,0:T(8,128)} %get-tuple-element.97), calls=%async_computation.4 | async-start | bytes 4194304 | tf_op jit(solution)/shard_map/all_to_all | solution.py:577
  83.4 22.0 %applied.3 = (f32[8,64,512]{2,1,0:T(8,128)}, f32[16,64,512]{2,1,0:T(8,128)}, f32[8,128]{1,0:T(8,128)S(1)}) custom-call(s32[9]{0:T(128)S(1)} %pad_add_fusion.scalar_ref, s32[8]{0:T(128)S(1)} %fusion.4.target_ref, f32[8,64,512]{2,1,0:T(8,128)} %get-tuple-element.85.refs_0_, f32[4,64,512]{2,1,0:T(8,128)} %get-tuple-element.86.refs_1_, ...), custom_call_target="tpu_custom_call" | custom-call | flops 6643777536 | bytes 46137344 | tf_op jit(solution)/shard_map/applied/pallas_call | solution.py:397
  106.7 5.3 %collective-permute-start.3 = (f32[4,64,512]{2,1,0:T(8,128)S(1)}, f32[4,64,512]{2,1,0:T(8,128)S(1)}, u32[]{:S(2)}, u32[]{:S(2)}) collective-permute-start(f32[4,64,512]{2,1,0:T(8,128)S(1)} %get-tuple-element.93), channel_id=1, source_target_pairs={{1,0},{2,1},{3,2},{4,3},{5,4},{6,5},{7,6},{8,7},{9,8},{10,9},{11,1... | collective-permute-start | bytes 1572872 | tf_op jit(solution)/shard_map/ppermute | solution.py:67
  112.1 9.3 %applied.4.refs_3_ = f32[8,64,512]{2,1,0:T(8,128)} custom-call(s32[9]{0:T(128)S(1)} %pad_add_fusion.scalar_ref, s32[8]{0:T(128)S(1)} %fusion.4.target_ref, f32[8,64,512]{2,1,0:T(8,128)} %get-tuple-element.91.refs_0_, bf16[44,1024,512]{2,1,0:T(8,128)(2,1)} %tiles.7.refs_3_.refs_1_.refs_4_), custom_call_target="tpu_custom_call" | custom-call | flops 1811939328 | bytes 12582912 | tf_op jit(solution)/shard_map/applied/pallas_call | solution.py:397
  122.1 5.3 %collective-permute-done.3.refs_2_ = f32[4,64,512]{2,1,0:T(8,128)S(1)} collective-permute-done((f32[4,64,512]{2,1,0:T(8,128)S(1)}, f32[4,64,512]{2,1,0:T(8,128)S(1)}, u32[]{:S(2)}, u32[]{:S(2)}) %collective-permute-start.3) | collective-permute-done | bytes 524320 | tf_op jit(solution)/shard_map/ppermute | solution.py:67
  127.4 2.6 %collective-permute-done.2.refs_1_ = f32[4,64,512]{2,1,0:T(8,128)S(1)} collective-permute-done((f32[4,64,512]{2,1,0:T(8,128)S(1)}, f32[4,64,512]{2,1,0:T(8,128)S(1)}, u32[]{:S(2)}, u32[]{:S(2)}) %collective-permute-start.2) | collective-permute-done | bytes 524320 | tf_op jit(solution)/shard_map/ppermute | solution.py:67
  131.5 3.7 %all-to-all-start.5 = ((f32[16,64,512]{2,1,0:T(8,128)}), f32[16,64,512]{2,1,0:T(8,128)S(1)}, u32[]{:S(2)}, u32[]{:S(2)}) async-start(f32[16,64,512]{2,1,0:T(8,128)} %gate.2), calls=%async_computation.5 | async-start | bytes 4194304 | tf_op jit(solution)/shard_map/all_to_all | solution.py:577
  135.2 18.1 %applied.5 = (f32[8,64,512]{2,1,0:T(8,128)}, f32[16,264,128]{2,1,0:T(8,128)}, f32[8,128]{1,0:T(8,128)S(1)}) custom-call(s32[9]{0:T(128)S(1)} %pad_add_fusion.scalar_ref, s32[8]{0:T(128)S(1)} %fusion.4.target_ref, f32[8,64,512]{2,1,0:T(8,128)} %get-tuple-element.91.refs_0_, f32[4,64,512]{2,1,0:T(8,128)} %copy-done.6, f32[4,64,512]{2,1,0:T(8,128)} %copy-done.5, ...), custom_call_target="tpu_custom_call" | custom-call | flops 4831838208 | bytes 33554432 | tf_op jit(solution)/shard_map/applied/pallas_call | solution.py:397
  155.5 3.8 %collective-permute-start.7 = (f32[8,128]{1,0:T(8,128)S(1)}, f32[8,128]{1,0:T(8,128)S(1)}, u32[]{:S(2)}, u32[]{:S(2)}) collective-permute-start(f32[8,128]{1,0:T(8,128)S(1)} %add.89), channel_id=1, source_target_pairs={{0,64},{16,80},{32,96},{48,112},{64,0},{80,16},{96,32},{112,48},{1... | collective-permute-start | bytes 12296 | tf_op jit(solution)/shard_map/ppermute | solution.py:54
  163.9 4.7 %all-to-all-done.5.refs_1_.refs_7_.refs_13_.refs_19_.refs_25_.refs_31_.refs_37_.refs_43_ = f32[16,64,512]{2,1,0:T(8,128)S(1)} async-done(((f32[16,64,512]{2,1,0:T(8,128)}), f32[16,64,512]{2,1,0:T(8,128)S(1)}, u32[]{:S(2)}, u32[]{:S(2)}) %all-to-all-start.5) | async-done | bytes 2097184 | tf_op jit(solution)/shard_map/all_to_all | solution.py:577
  170.0 3.7 %all-to-all-start.6 = ((f32[16,264,128]{2,1,0:T(8,128)}), f32[16,264,128]{2,1,0:T(8,128)S(1)}, u32[]{:S(2)}, u32[]{:S(2)}) async-start(f32[16,264,128]{2,1,0:T(8,128)} %gate.3), calls=%async_computation.6 | async-start | bytes 4325376 | tf_op jit(solution)/shard_map/all_to_all | solution.py:577
  174.4 30.8 %all-to-all-done.6.sums_ref.refs_2_.refs_3_.refs_4_.refs_5_.refs_8_.refs_9_.refs_10_.refs_11_.refs_14_.refs_15_.refs_16_.refs_17_.refs_20_.refs_21_.refs_22_.refs_23_.refs_26_.refs_27_.refs_28_.refs_29_.refs_32_.refs_33_.refs_34_.refs_35_.refs_38_.refs_39_.refs_40_.refs_41_.refs_44_.refs_45_.refs_46_.refs_47_ = f32[16,264,128]{2,1,0:T(8,128)S(1)} async-done(((f32[16,264,128]{2,1,0:T(8,128)}), ...) | async-done | bytes 2162720 | tf_op jit(solution)/shard_map/all_to_all | solution.py:577
  205.2 5.9 %combine.1 = (f32[64,8,512]{2,1,0:T(8,128)}, f32[64,8,512]{2,1,0:T(8,128)}) custom-call(s32[8]{0:T(128)S(1)} %and_select_fusion.src_ref, ...), custom_call_target="tpu_custom_call" | custom-call | tf_op jit(solution)/shard_map/combine/pallas_call | solution.py:558
  (100 shorter events, 27.5 us)
Async XLA Ops:
  4.8 11.1 %all-to-all-start = ((f32[8,72,32]{1,2,0:T(8,128)}), f32[8,72,32]{1,2,0:T(8,128)S(1)}, u32[]{:S(2)}, u32[]{:S(2)}) async-start(f32[8,72,32]{1,2,0:T(8,128)} %broadcast_in_dim.14), calls=%async_computation | async-start | bytes 262144 | tf_op jit(solution)/shard_map/all_to_all | solution.py:42
  11.1 5.1 %copy-start.7 = (f32[64]{0:T(128)S(1)}, f32[64]{0:T(128)}, u32[]{:S(2)}) copy-start(f32[64]{0:T(128)} %param.11) | copy-start | bytes 772
  11.1 5.2 %copy-start = (f32[64,32,128]{2,1,0:T(8,128)S(1)}, f32[64,32,128]{2,1,0:T(8,128)}, u32[]{:S(2)}) copy-start(f32[64,32,128]{2,1,0:T(8,128)} %obs_ref.1) | copy-start | bytes 3145732
  15.9 9.7 %copy-start.2 = (f32[2,32,128]{2,1,0:T(8,128)S(1)}, f32[2,32,128]{2,1,0:T(8,128)}, u32[]{:S(2)}) copy-start(f32[2,32,128]{2,1,0:T(8,128)} %jitter_ref.3) | copy-start | bytes 98308
  17.6 21.6 %all-to-all-start.1 = ((f32[16,72,128]{2,1,0:T(8,128)}), f32[16,72,128]{2,1,0:T(8,128)S(1)}, u32[]{:S(2)}, u32[]{:S(2)}) async-start(f32[16,72,128]{2,1,0:T(8,128)} %broadcast_in_dim.15), calls=%async_computation.1 | async-start | bytes 1179648 | tf_op jit(solution)/shard_map/all_to_all | solution.py:42
  26.5 29.6 %collective-permute-start = (f32[67,16,128]{2,1,0:T(8,128)}, f32[67,16,128]{2,1,0:T(8,128)S(1)}, u32[]{:S(2)}, u32[]{:S(2)}) collective-permute-start(f32[67,16,128]{2,1,0:T(8,128)} %get-tuple-element.76), channel_id=1, source_target_pairs={{0,1},{1,2},{2,3},{3,4},{4,5},{5,6},{6,7},{7,8},{8,9},{9,10},{10,1... | collective-permute-start | bytes 1646600 | tf_op jit(solution)/shard_map/ppermute | solution.py:67
  28.4 27.6 %collective-permute-start.1 = (f32[67,16,128]{2,1,0:T(8,128)S(1)}, f32[67,16,128]{2,1,0:T(8,128)S(1)}, u32[]{:S(2)}, u32[]{:S(2)}) collective-permute-start(f32[67,16,128]{2,1,0:T(8,128)S(1)} %get-tuple-element.77), channel_id=1, source_target_pairs={{1,0},{2,1},{3,2},{4,3},{5,4},{6,5},{7,6},{8,7},{9,8},{10,9},{11,1... | collective-permute-start | bytes 1646600 | tf_op jit(solution)/shard_map/ppermute | solution.py:67
  41.0 13.6 %all-to-all-start.2 = ((f32[8,1,2048]{2,1,0:T(1,128)}), f32[8,1,2048]{2,1,0:T(1,128)S(1)}, u32[]{:S(2)}, u32[]{:S(2)}) async-start(f32[8,1,2048]{2,1,0:T(1,128)} %reshape.131), calls=%async_computation.2 | async-start | bytes 131072 | tf_op jit(solution)/shard_map/all_to_all | solution.py:42
  54.6 7.1 %copy-start.8 = (s32[1,128]{1,0:T(1,128)S(1)}, s32[1,128]{1,0:T(1,128)}, u32[]{:S(2)}) copy-start(s32[1,128]{1,0:T(1,128)} %param.14) | copy-start | bytes 1540
  57.8 16.1 %all-to-all-start.3 = ((f32[16,80,128]{2,1,0:T(8,128)}), f32[16,80,128]{2,1,0:T(8,128)S(1)}, u32[]{:S(2)}, u32[]{:S(2)}) async-start(f32[16,80,128]{2,1,0:T(8,128)} %broadcast_in_dim.18), calls=%async_computation.3 | async-start | bytes 1310720 | tf_op jit(solution)/shard_map/all_to_all | solution.py:42
  77.6 52.4 %all-to-all-start.4 = ((f32[16,64,512]{2,1,0:T(8,128)}), f32[16,64,512]{2,1,0:T(8,128)S(1)}, u32[]{:S(2)}, u32[]{:S(2)}) async-start(f32[16,64,512]{2,1,0:T(8,128)} %get-tuple-element.97), calls=%async_computation.4 | async-start | bytes 4194304 | tf_op jit(solution)/shard_map/all_to_all | solution.py:577
  106.7 20.7 %collective-permute-start.3 = (f32[4,64,512]{2,1,0:T(8,128)S(1)}, f32[4,64,512]{2,1,0:T(8,128)S(1)}, u32[]{:S(2)}, u32[]{:S(2)}) collective-permute-start(f32[4,64,512]{2,1,0:T(8,128)S(1)} %get-tuple-element.93), channel_id=1, source_target_pairs={{1,0},{2,1},{3,2},{4,3},{5,4},{6,5},{7,6},{8,7},{9,8},{10,9},{11,1... | collective-permute-start | bytes 1572872 | tf_op jit(solution)/shard_map/ppermute | solution.py:67
  112.1 18.0 %collective-permute-start.2 = (f32[4,64,512]{2,1,0:T(8,128)S(1)}, f32[4,64,512]{2,1,0:T(8,128)S(1)}, u32[]{:S(2)}, u32[]{:S(2)}) collective-permute-start(f32[4,64,512]{2,1,0:T(8,128)S(1)} %get-tuple-element.92), channel_id=1, source_target_pairs={{0,1},{1,2},{2,3},{3,4},{4,5},{5,6},{6,7},{7,8},{8,9},{9,10},{10,1... | collective-permute-start | bytes 1572872 | tf_op jit(solution)/shard_map/ppermute | solution.py:67
  127.4 2.6 %copy-start.5 = (f32[4,64,512]{2,1,0:T(8,128)}, f32[4,64,512]{2,1,0:T(8,128)S(1)}, u32[]{:S(2)}) copy-start(f32[4,64,512]{2,1,0:T(8,128)S(1)} %collective-permute-done.3.refs_2_) | copy-start | bytes 1572868
  130.1 1.5 copy-start.3
  131.5 37.1 %all-to-all-start.5 = ((f32[16,64,512]{2,1,0:T(8,128)}), f32[16,64,512]{2,1,0:T(8,128)S(1)}, u32[]{:S(2)}, u32[]{:S(2)}) async-start(f32[16,64,512]{2,1,0:T(8,128)} %gate.2), calls=%async_computation.5 | async-start | bytes 4194304 | tf_op jit(solution)/shard_map/all_to_all | solution.py:577
  153.3 5.9 %collective-permute-start.10 = (f32[8,128]{1,0:T(8,128)S(1)}, f32[8,128]{1,0:T(8,128)S(1)}, u32[]{:S(2)}, u32[]{:S(2)}) collective-permute-start(f32[8,128]{1,0:T(8,128)S(1)} %add.89), channel_id=1, source_target_pairs={{0,112},{16,0},{32,16},{48,32},{64,48},{80,64},{96,80},{112,96},{1... | collective-permute-start | bytes 12296 | tf_op jit(solution)/shard_map/ppermute | solution.py:54
  153.4 6.1 %collective-permute-start.4 = (f32[8,128]{1,0:T(8,128)S(1)}, f32[8,128]{1,0:T(8,128)S(1)}, u32[]{:S(2)}, u32[]{:S(2)}) collective-permute-start(f32[8,128]{1,0:T(8,128)S(1)} %add.89), channel_id=1, source_target_pairs={{0,16},{16,32},{32,48},{48,64},{64,80},{80,96},{96,112},{112,0},{1... | collective-permute-start | bytes 12296 | tf_op jit(solution)/shard_map/ppermute | solution.py:54
  153.9 7.5 %collective-permute-start.5 = (f32[8,128]{1,0:T(8,128)S(1)}, f32[8,128]{1,0:T(8,128)S(1)}, u32[]{:S(2)}, u32[]{:S(2)}) collective-permute-start(f32[8,128]{1,0:T(8,128)S(1)} %add.89), channel_id=1, source_target_pairs={{0,32},{16,48},{32,64},{48,80},{64,96},{80,112},{96,0},{112,16},{1... | collective-permute-start | bytes 12296 | tf_op jit(solution)/shard_map/ppermute | solution.py:54
  155.1 6.3 %collective-permute-start.6 = (f32[8,128]{1,0:T(8,128)S(1)}, f32[8,128]{1,0:T(8,128)S(1)}, u32[]{:S(2)}, u32[]{:S(2)}) collective-permute-start(f32[8,128]{1,0:T(8,128)S(1)} %add.89), channel_id=1, source_target_pairs={{0,48},{16,64},{32,80},{48,96},{64,112},{80,0},{96,16},{112,32},{1... | collective-permute-start | bytes 12296 | tf_op jit(solution)/shard_map/ppermute | solution.py:54
  155.5 5.9 %collective-permute-start.7 = (f32[8,128]{1,0:T(8,128)S(1)}, f32[8,128]{1,0:T(8,128)S(1)}, u32[]{:S(2)}, u32[]{:S(2)}) collective-permute-start(f32[8,128]{1,0:T(8,128)S(1)} %add.89), channel_id=1, source_target_pairs={{0,64},{16,80},{32,96},{48,112},{64,0},{80,16},{96,32},{112,48},{1... | collective-permute-start | bytes 12296 | tf_op jit(solution)/shard_map/ppermute | solution.py:54
  159.2 3.0 %collective-permute-start.8 = (f32[8,128]{1,0:T(8,128)S(1)}, f32[8,128]{1,0:T(8,128)S(1)}, u32[]{:S(2)}, u32[]{:S(2)}) collective-permute-start(f32[8,128]{1,0:T(8,128)S(1)} %add.89), channel_id=1, source_target_pairs={{0,80},{16,96},{32,112},{48,0},{64,16},{80,32},{96,48},{112,64},{1... | collective-permute-start | bytes 12296 | tf_op jit(solution)/shard_map/ppermute | solution.py:54
  159.5 3.6 %collective-permute-start.9 = (f32[8,128]{1,0:T(8,128)S(1)}, f32[8,128]{1,0:T(8,128)S(1)}, u32[]{:S(2)}, u32[]{:S(2)}) collective-permute-start(f32[8,128]{1,0:T(8,128)S(1)} %add.89), channel_id=1, source_target_pairs={{0,96},{16,112},{32,0},{48,16},{64,32},{80,48},{96,64},{112,80},{1... | collective-permute-start | bytes 12296 | tf_op jit(solution)/shard_map/ppermute | solution.py:54
  170.0 35.2 %all-to-all-start.6 = ((f32[16,264,128]{2,1,0:T(8,128)}), f32[16,264,128]{2,1,0:T(8,128)S(1)}, u32[]{:S(2)}, u32[]{:S(2)}) async-start(f32[16,264,128]{2,1,0:T(8,128)} %gate.3), calls=%async_computation.6 | async-start | bytes 4325376 | tf_op jit(solution)/shard_map/all_to_all | solution.py:577
  (3 other events, 2.9 us)

commit v5 on v4

--- a/solution.py
+++ b/solution.py
@@ -34,7 +34,7 @@
 TILE_SLOTS = 4
 OP_SLOTS = 5
 EXTRA = 8
-EARLY_TILES = 12
+EARLY_TILES = 18
 
 
 def sent_to_all(shard, axis):
@@ -332,7 +332,7 @@
     lax.fori_loop(max(BLOCKS_DEV - first, 0), mine, with_another, 0)
     if halo:
         lax.fori_loop(mine, count, with_beside, 0)
-    leaving = [pltpu.make_async_copy(total, out_ref, out_sem.at[STRIP * BLOCKS_DEV])]
+    leaving = [pltpu.make_async_copy(total, out_ref, out_sem.at[BLOCKS_DEV])]
     if send:
         leaving += out_copies(total, slots_ref, target_ref, out_sem)
     for out in leaving:
@@ -356,20 +356,9 @@
 
 
 def out_copies(values_ref, slots_ref, target_ref, sem):
-    fields = values_ref.shape[1]
-    if slots_ref.shape[2] == BLOCK:
-        return [
-            pltpu.make_async_copy(values_ref.at[g], slots_ref.at[target_ref[g]], sem.at[g])
-            for g in range(BLOCKS_DEV)
-        ]
     return [
-        pltpu.make_async_copy(
-            values_ref.at[g, :, pl.ds(COL_DEV * ra, COL_DEV)],
-            slots_ref.at[target_ref[g], pl.ds(fields * ra, fields)],
-            sem.at[STRIP * g + ra],
-        )
+        pltpu.make_async_copy(values_ref.at[g], slots_ref.at[target_ref[g]], sem.at[g])
         for g in range(BLOCKS_DEV)
-        for ra in range(STRIP)
     ]
 
 
@@ -382,15 +371,12 @@
     return pltpu.with_memory_space_constraint(x, pltpu.HBM)
 
 
-def slot_shape(v, extra=0):
-    _, fields, points = v.shape
-    block = (STRIP * fields + extra, points // STRIP) if extra else (fields, points)
-    return pltpu.HBM((lax.axis_size(SIXTEEN), *block), jnp.float32)
-
-
-def applied(scalars, targets, tiles, v, tiles_of=(0, None), beside=(), held=None, extra=None):
+def slot_shape(v):
+    return pltpu.HBM((lax.axis_size(SIXTEEN), *v.shape[1:]), jnp.float32)
+
+
+def applied(scalars, targets, tiles, v, tiles_of=(0, None), beside=(), held=None, send=False):
     blocks, fields, _ = v.shape
-    send = extra is not None
     out = pltpu.HBM(v.shape, jnp.float32)
     ins = [in_hbm(x) for x in (v, *beside, held) if x is not None] + [tiles]
     number = (tiles_of[1] or OWN_TILES) - tiles_of[0] + HALO_TILES * bool(beside)
@@ -405,10 +391,10 @@
             pltpu.VMEM((OP_SLOTS, 2 * BLOCK, BLOCK), jnp.bfloat16),
             pltpu.SemaphoreType.DMA((OP_SLOTS,)),
             pltpu.SemaphoreType.DMA((4,)),
-            pltpu.SemaphoreType.DMA((STRIP * BLOCKS_DEV + 1,)),
+            pltpu.SemaphoreType.DMA((BLOCKS_DEV + 1,)),
         ],
         out_shape=[out]
-        + [slot_shape(v, extra or 0), jax.ShapeDtypeStruct((EXTRA, COL_DEV), jnp.float32)] * send,
+        + [slot_shape(v), jax.ShapeDtypeStruct((EXTRA, COL_DEV), jnp.float32)] * send,
         compiler_params=pltpu.CompilerParams(vmem_limit_bytes=24 << 20),
         cost_estimate=pl.CostEstimate(
             flops=3 * number * 3 * fields * BLOCK * BLOCK,
@@ -434,33 +420,6 @@
         compiler_params=pltpu.CompilerParams(vmem_limit_bytes=1 << 20),
         name="gate",
     )(slots, *(other[0, :8, :COL_DEV] for other in others))
-
-
-def attach_kernel(rows_ref, slots_ref, out_ref, sem):
-    rows = rows_ref.shape[0]
-    copies = [
-        pltpu.make_async_copy(
-            rows_ref, out_ref.at[o, pl.ds(out_ref.shape[1] - rows, rows)], sem.at[o]
-        )
-        for o in range(out_ref.shape[0])
-    ]
-    for copy in copies:
-        copy.start()
-    for copy in copies:
-        copy.wait()
-
-
-def attach(slots, rows):
-    return pl.pallas_call(
-        attach_kernel,
-        in_specs=[VMEM_SPEC, HBM_SPEC],
-        out_specs=HBM_SPEC,
-        scratch_shapes=[pltpu.SemaphoreType.DMA((slots.shape[0],))],
-        out_shape=pltpu.HBM(slots.shape, jnp.float32),
-        input_output_aliases={1: 0},
-        compiler_params=pltpu.CompilerParams(vmem_limit_bytes=1 << 20),
-        name="attach",
-    )(rows, slots)
 
 
 def residual_kernel(
@@ -521,56 +480,57 @@
     )(targets, observations, weight, row_effect, before, before_row, after, after_row, col)
 
 
-def combine_kernel(src_ref, sums_ref, *refs):
-    ins, (x_ref, r_ref, scale_ref) = refs[:-3], refs[-3:]
-    part = x_ref.shape[0]
-
+def scales_of(dots_ref, scale_ref, part):
     @pl.when(pl.program_id(0) == 0)
     def _():
-        sums = functools.reduce(jnp.add, [sums_ref[o] for o in range(sums_ref.shape[0])])
-        scale_ref[...] = step_scales(*(sums[k : k + 1] for k in range(4))).T
-
-    scale = scale_ref[pl.ds(pl.multiple_of(pl.program_id(0) * part, part), part), :]
+        scale_ref[...] = step_scales(*(dots_ref[k : k + 1] for k in range(4))).T
+
+    return scale_ref[pl.ds(pl.multiple_of(pl.program_id(0) * part, part), part), :]
+
+
+def first_kernel(src_ref, dots_ref, *refs):
+    ins, (x_ref, r_ref, scale_ref) = refs[:-3], refs[-3:]
+    scale = scales_of(dots_ref, scale_ref, x_ref.shape[0])
     for j in range(BLOCKS_DEV):
-        r0_ref, m1_ref, *m2_refs = ins[(2 + STRIP) * j : (2 + STRIP) * (j + 1)]
-        for ra in range(STRIP):
-            lanes = slice(COL_DEV * ra, COL_DEV * (ra + 1))
-            r0, m1, m2 = r0_ref[0, :, lanes], m1_ref[0, :, lanes], m2_refs[ra][0]
-            x_ref[:, j, lanes] = scale[:, 0:1] * r0 + scale[:, 1:2] * m1
-            r_ref[:, j, lanes] = scale[:, 2:3] * r0 + scale[:, 3:4] * m1 + scale[:, 4:5] * m2
-
-
-def combined(sources, r0, m1, m2):
-    owners, fields, _ = r0.shape
+        r0, m1 = (ref[0] for ref in ins[2 * j : 2 * j + 2])
+        x_ref[:, j, :] = scale[:, 0:1] * r0 + scale[:, 1:2] * m1
+        r_ref[:, j, :] = scale[:, 2:3] * r0 + scale[:, 3:4] * m1
+
+
+def second_kernel(src_ref, dots_ref, part_ref, *refs):
+    ins, (r_ref, scale_ref) = refs[:-2], refs[-2:]
+    scale = scales_of(dots_ref, scale_ref, r_ref.shape[0])
+    for j in range(BLOCKS_DEV):
+        r_ref[:, j, :] = part_ref[:, j, :] + scale[:, 4:5] * ins[j][0]
+
+
+def combined(kernel, name, outs, sources, dots, held, *owned):
+    _, fields, _ = owned[0].shape
     part = 16
-    ins, specs = [], []
-    r0, m1 = in_hbm(r0), in_hbm(m1)
-
-    def chosen(j, points, at):
-        return pl.BlockSpec((1, part, points), lambda i, s: (s[j], at // part + i, 0))
-
+    by_field = pl.BlockSpec((part, BLOCKS_DEV, BLOCK), lambda i, s: (i, 0, 0))
+    ins, specs = list(held), [by_field] * len(held)
     for j in range(BLOCKS_DEV):
-        ins += [r0, m1] + [m2] * STRIP
-        specs += [chosen(j, BLOCK, 0)] * 2
-        specs += [chosen(j, COL_DEV, fields * ra) for ra in range(STRIP)]
-    out = pl.BlockSpec((part, BLOCKS_DEV, BLOCK), lambda i, s: (i, 0, 0))
+        for v in owned:
+            ins.append(v)
+            specs.append(
+                pl.BlockSpec(
+                    (1, part, BLOCK), functools.partial(lambda j, i, s: (s[j], i, 0), j)
+                )
+            )
     shape = jax.ShapeDtypeStruct((fields, BLOCKS_DEV, BLOCK), jnp.float32)
     return pl.pallas_call(
-        combine_kernel,
+        kernel,
         grid_spec=pltpu.PrefetchScalarGridSpec(
             num_scalar_prefetch=1,
             grid=(fields // part,),
-            in_specs=[
-                pl.BlockSpec((owners, EXTRA, COL_DEV), lambda i, s: (0, STRIP * fields // EXTRA, 0))
-            ]
-            + specs,
-            out_specs=[out, out],
+            in_specs=[pl.BlockSpec(dots.shape, lambda i, s: (0, 0))] + specs,
+            out_specs=[by_field] * outs,
             scratch_shapes=[pltpu.VMEM((COL_DEV, 8), jnp.float32)],
         ),
-        out_shape=[shape, shape],
+        out_shape=[shape] * outs,
         compiler_params=pltpu.CompilerParams(vmem_limit_bytes=20 << 20),
-        name="combine",
-    )(sources, m2, *ins)
+        name=name,
+    )(sources, dots, *ins)
 
 
 def to_owners(slots):
@@ -672,21 +632,26 @@
     )
     owned_r0 = to_owners(slots)
     m1, slots, dots = applied(
-        scalars, my_targets, tiles, r0, beside=(r0_before, r0_after), extra=0
+        scalars, my_targets, tiles, r0, beside=(r0_before, r0_after), send=True
     )
     before, after, m1 = beside(m1, REACH)
     part = applied(scalars, my_targets, tiles, m1, (0, EARLY_TILES))
     slots = gate(slots, part, before, after, owned_r0)
     owned_m1 = to_owners(slots)
     m2, slots, last = applied(
-        scalars, my_targets, tiles, m1, (EARLY_TILES, None), (before, after), part, EXTRA
-    )
-    slots = attach(slots, sum_direct(dots + last, WIDE))
-    slots = gate(slots, owned_m1)
+        scalars, my_targets, tiles, m1, (EARLY_TILES, None), (before, after), part, True
+    )
+    dots = sum_direct(sum_direct(dots + last, WIDE), SIXTEEN[1])
+    slots = gate(slots, owned_m1, dots[None])
     owned_m2 = to_owners(slots)
+    dots = sum_direct(dots, SIXTEEN[0])
     owned = owned_table(group_map, sixteen_size, BLOCKS_DEV)
     my_ids = lax.dynamic_index_in_dim(owned, my_place, 0, keepdims=False)
-    solution_now, residual_now = combined(my_ids // BLOCKS_DEV, owned_r0, owned_m1, owned_m2)
+    sources = my_ids // BLOCKS_DEV
+    solution_now, part = combined(
+        first_kernel, "first", 2, sources, dots, (), in_hbm(owned_r0), in_hbm(owned_m1)
+    )
+    (residual_now,) = combined(second_kernel, "second", 1, sources, dots, (part,), owned_m2)
     return (solution_now[None, None], residual_now[None, None])
 
 

time: 213 us -> 209 us (0.981)
  waiting for transfers between devices: 46.6 us -> 27.6 us
  starting transfers between devices: 53 us -> 69.6 us
    all_to_all x3, waiting for transfers between devices: 35.5 us -> 0.61 us  [to_owners(): return lax.all_to_all(slots, SIXTEEN, 0, 0, tiled=True)]
    ppermute x7 -> x13, waiting for transfers between devices: 1.71 us -> 20.6 us  [sum_direct(): lax.ppermute(part, axis, [(i, (i + k) % peers) for i in range(peers)])]
    ppermute x7 -> x13, starting transfers between devices: 8.04 us -> 22.9 us  [sum_direct(): lax.ppermute(part, axis, [(i, (i + k) % peers) for i in range(peers)])]
    ppermute x2, waiting for transfers between devices: 5.35 us -> 0.01 us  [beside(): lax.ppermute(initial, SIXTEEN, down)]
    all_to_all x4, waiting for transfers between devices: 1.46 us -> 4.14 us  [sent_to_all(): lax.all_to_all(jnp.broadcast_to(shard[None], (peers, *shard.shape)), axis...]
    unnamed x23 -> x21, local copies, waits for them, and re-layouts: 4.59 us -> 3.29 us
  transfers between devices with their start and end apart: 18 -> 24, of which waited for: 7 -> 10; matrix products, arithmetic and copies ran while one was open for 4% -> 4% of each run, Pallas kernels for 39% -> 41%
where the time goes in v5:
time: 209 us; the launch traced here: 207 us
  Pallas kernels  90.2 us (43%)
  starting transfers between devices  69.6 us (33%)
  waiting for transfers between devices  27.6 us (13%)
  local copies, waits for them, and re-layouts  11.2 us (5%)
  other arithmetic  7.36 us (4%)
    pallas_call x3, Pallas kernels, applied(): pl.pallas_call(functools.partial(op_kernel, *tiles_of, bool(beside), held...  48.7 us
    pallas_call x4, Pallas kernels, covariance_tiles(): pl.pallas_call(functools.partial(tiles_kernel, first, count, len(beside_j...  30.9 us
    ppermute x13, starting transfers between devices, sum_direct(): lax.ppermute(part, axis, [(i, (i + k) % peers) for i in range(peers)])  22.9 us
    all_to_all x4, starting transfers between devices, sent_to_all(): lax.all_to_all(jnp.broadcast_to(shard[None], (peers, *shard.shape)), axis...  21.1 us
    ppermute x13, waiting for transfers between devices, sum_direct(): lax.ppermute(part, axis, [(i, (i + k) % peers) for i in range(peers)])  20.6 us
    all_to_all x3, starting transfers between devices, to_owners(): return lax.all_to_all(slots, SIXTEEN, 0, 0, tiled=True)  15 us
    ppermute x2, starting transfers between devices, beside(): lax.ppermute(initial, SIXTEEN, down)  8.71 us
    pallas_call x2, Pallas kernels, combined(): pl.pallas_call(kernel, grid_spec=pltpu.PrefetchScalarGridSpec(num_scalar_...  7.33 us
  transfers between devices with their start and end apart: 24, of which 10 were waited for; matrix products, arithmetic and copies ran while one was open for 4% of the time, Pallas kernels for 41%

profile of v5, /device:TPU:0, one launch (start us, length us, event | category | flops | bytes accessed | tf_op | source)
XLA Modules:
  0.0 207.1 jit_solution(8966703036736917580)
XLA Ops:
  4.8 4.6 %all-to-all-start = ((f32[8,72,32]{1,2,0:T(8,128)}), f32[8,72,32]{1,2,0:T(8,128)S(1)}, u32[]{:S(2)}, u32[]{:S(2)}) async-start(f32[8,72,32]{1,2,0:T(8,128)} %broadcast_in_dim.14), calls=%async_computation | async-start | bytes 262144 | tf_op jit(solution)/shard_map/all_to_all | solution.py:42
  11.1 4.8 %tiles.4.refs_0_ = bf16[44,1024,512]{2,1,0:T(8,128)(2,1)} custom-call(s32[9]{0:T(128)S(1)} %pad_add_fusion.scalar_ref, f32[2,32,128]{2,1,0:T(8,128)S(1)} %copy-done.1), custom_call_target="tpu_custom_call" | custom-call | flops 15728640 | bytes 5242880 | tf_op jit(solution)/shard_map/tiles/pallas_call | solution.py:223
  17.6 7.9 %all-to-all-start.1 = ((f32[16,72,128]{2,1,0:T(8,128)}), f32[16,72,128]{2,1,0:T(8,128)S(1)}, u32[]{:S(2)}, u32[]{:S(2)}) async-start(f32[16,72,128]{2,1,0:T(8,128)} %broadcast_in_dim.15), calls=%async_computation.1 | async-start | bytes 1179648 | tf_op jit(solution)/shard_map/all_to_all | solution.py:42
  28.4 3.4 %collective-permute-start.1 = (f32[67,16,128]{2,1,0:T(8,128)S(1)}, f32[67,16,128]{2,1,0:T(8,128)S(1)}, u32[]{:S(2)}, u32[]{:S(2)}) collective-permute-start(f32[67,16,128]{2,1,0:T(8,128)S(1)} %get-tuple-element.77), channel_id=1, source_target_pairs={{1,0},{2,1},{3,2},{4,3},{5,4},{6,5},{7,6},{8,7},{9,8},{10,9},{11,1... | collective-permute-start | bytes 1646600 | tf_op jit(solution)/shard_map/ppermute | solution.py:67
  31.9 7.4 %tiles.5.refs_0_ = bf16[44,1024,512]{2,1,0:T(8,128)(2,1)} custom-call(s32[9]{0:T(128)S(1)} %pad_add_fusion.scalar_ref, f32[2,32,128]{2,1,0:T(8,128)S(1)} %copy-done.2, bf16[44,1024,512]{2,1,0:T(8,128)(2,1)} %tiles.4.refs_0_), custom_call_target="tpu_custom_call", output_to_operand_aliasing={{}: (2, {})} | custom-call | flops 28311552 | bytes 9437184 | tf_op jit(solution)/shard_map/tiles/pallas_call | solution.py:223
  41.0 4.8 %all-to-all-start.2 = ((f32[8,1,2048]{2,1,0:T(1,128)}), f32[8,1,2048]{2,1,0:T(1,128)S(1)}, u32[]{:S(2)}, u32[]{:S(2)}) async-start(f32[8,1,2048]{2,1,0:T(1,128)} %reshape.131), calls=%async_computation.2 | async-start | bytes 131072 | tf_op jit(solution)/shard_map/all_to_all | solution.py:42
  45.8 9.3 %tiles.6.refs_2_ = bf16[44,1024,512]{2,1,0:T(8,128)(2,1)} custom-call(s32[9]{0:T(128)S(1)} %pad_add_fusion.scalar_ref, f32[2,32,128]{2,1,0:T(8,128)S(1)} %copy-done.2, bf16[44,1024,512]{2,1,0:T(8,128)(2,1)} %tiles.5.refs_0_), custom_call_target="tpu_custom_call", output_to_operand_aliasing={{}: (2, {})} | custom-call | flops 37748736 | bytes 12582912 | tf_op jit(solution)/shard_map/tiles/pallas_call | solution.py:223
  58.3 3.9 %all-to-all-start.3 = ((f32[16,80,128]{2,1,0:T(8,128)}), f32[16,80,128]{2,1,0:T(8,128)S(1)}, u32[]{:S(2)}, u32[]{:S(2)}) async-start(f32[16,80,128]{2,1,0:T(8,128)} %broadcast_in_dim.18), calls=%async_computation.3 | async-start | bytes 1310720 | tf_op jit(solution)/shard_map/all_to_all | solution.py:42
  62.3 9.3 %tiles.7.refs_3_.refs_1_.refs_4_ = bf16[44,1024,512]{2,1,0:T(8,128)(2,1)} custom-call(s32[9]{0:T(128)S(1)} %pad_add_fusion.scalar_ref, f32[2,32,128]{2,1,0:T(8,128)S(1)} %copy-done.2, f32[2,16,128]{2,1,0:T(8,128)S(1)} %slice.96.refs_0_, f32[2,16,128]{2,1,0:T(8,128)S(1)} %slice.97.refs_1_, ...), custom_call_target="tpu_custom_call", output_to_operand_aliasing={{}: (4, {})} | custom-call | flops 56623104 | bytes 18874368 | tf_op jit(solution)/shard_map/tiles/pallas_call | solution.py:223
  71.7 4.1 %all-to-all-done.3 = f32[16,80,128]{2,1,0:T(8,128)S(1)} async-done(((f32[16,80,128]{2,1,0:T(8,128)}), f32[16,80,128]{2,1,0:T(8,128)S(1)}, u32[]{:S(2)}, u32[]{:S(2)}) %all-to-all-start.3) | async-done | bytes 655392 | tf_op jit(solution)/shard_map/all_to_all | solution.py:42
  76.2 3.4 %residual.1 = (f32[8,64,512]{2,1,0:T(8,128)}, f32[4,64,512]{2,1,0:T(8,128)}, f32[4,64,512]{2,1,0:T(8,128)}, f32[16,64,512]{2,1,0:T(8,128)}) custom-call(s32[8]{0:T(128)S(1)} %fusion.4.target_ref, f32[64,32,128]{2,1,0:T(8,128)S(1)} %copy-done, f32[32,128]{1,0:T(8,128)S(1)} %get-tuple-element.109.weight_ref, f32[64,32]{1,0:T(8,128)S(1)} %divide_add_fusion.1.row_ref, ...), custom_call_target="tpu_custom_call" | custom-call | tf_op jit(solution)/shard_map/residual/pallas_call | solution.py:469
  79.6 3.7 %all-to-all-start.4 = ((f32[16,64,512]{2,1,0:T(8,128)}), f32[16,64,512]{2,1,0:T(8,128)S(1)}, u32[]{:S(2)}, u32[]{:S(2)}) async-start(f32[16,64,512]{2,1,0:T(8,128)} %get-tuple-element.95), calls=%async_computation.4 | async-start | bytes 4194304 | tf_op jit(solution)/shard_map/all_to_all | solution.py:537
  83.3 21.8 %applied.3 = (f32[8,64,512]{2,1,0:T(8,128)}, f32[16,64,512]{2,1,0:T(8,128)}, f32[8,128]{1,0:T(8,128)S(1)}) custom-call(s32[9]{0:T(128)S(1)} %pad_add_fusion.scalar_ref, s32[8]{0:T(128)S(1)} %fusion.4.target_ref, f32[8,64,512]{2,1,0:T(8,128)} %get-tuple-element.85.refs_0_, f32[4,64,512]{2,1,0:T(8,128)} %get-tuple-element.86.refs_1_, ...), custom_call_target="tpu_custom_call" | custom-call | flops 6643777536 | bytes 46137344 | tf_op jit(solution)/shard_map/applied/pallas_call | solution.py:383
  106.3 5.3 %collective-permute-start.3 = (f32[4,64,512]{2,1,0:T(8,128)S(1)}, f32[4,64,512]{2,1,0:T(8,128)S(1)}, u32[]{:S(2)}, u32[]{:S(2)}) collective-permute-start(f32[4,64,512]{2,1,0:T(8,128)S(1)} %get-tuple-element.93), channel_id=1, source_target_pairs={{1,0},{2,1},{3,2},{4,3},{5,4},{6,5},{7,6},{8,7},{9,8},{10,9},{11,1... | collective-permute-start | bytes 1572872 | tf_op jit(solution)/shard_map/ppermute | solution.py:67
  111.6 12.8 %applied.4.refs_3_ = f32[8,64,512]{2,1,0:T(8,128)} custom-call(s32[9]{0:T(128)S(1)} %pad_add_fusion.scalar_ref, s32[8]{0:T(128)S(1)} %fusion.4.target_ref, f32[8,64,512]{2,1,0:T(8,128)} %get-tuple-element.91.refs_0_, bf16[44,1024,512]{2,1,0:T(8,128)(2,1)} %tiles.7.refs_3_.refs_1_.refs_4_), custom_call_target="tpu_custom_call" | custom-call | flops 2717908992 | bytes 18874368 | tf_op jit(solution)/shard_map/applied/pallas_call | solution.py:383
  128.8 4.8 %all-to-all-start.5 = ((f32[16,64,512]{2,1,0:T(8,128)}), f32[16,64,512]{2,1,0:T(8,128)}, u32[]{:S(2)}, u32[]{:S(2)}) async-start(f32[16,64,512]{2,1,0:T(8,128)} %gate.2), calls=%async_computation.5 | async-start | bytes 4194304 | tf_op jit(solution)/shard_map/all_to_all | solution.py:537
  133.6 14.1 %applied.5 = (f32[8,64,512]{2,1,0:T(8,128)}, f32[16,64,512]{2,1,0:T(8,128)}, f32[8,128]{1,0:T(8,128)S(1)}) custom-call(s32[9]{0:T(128)S(1)} %pad_add_fusion.scalar_ref, s32[8]{0:T(128)S(1)} %fusion.4.target_ref, f32[8,64,512]{2,1,0:T(8,128)} %get-tuple-element.91.refs_0_, f32[4,64,512]{2,1,0:T(8,128)} %copy-done.5, f32[4,64,512]{2,1,0:T(8,128)} %copy-done.4, ...), custom_call_target="tpu_custom_call" | custom-call | flops 3925868544 | bytes 27262976 | tf_op jit(solution)/shard_map/applied/pallas_call | solution.py:383
  149.0 3.0 %collective-permute-start.5 = (f32[8,128]{1,0:T(8,128)S(1)}, f32[8,128]{1,0:T(8,128)S(1)}, u32[]{:S(2)}, u32[]{:S(2)}) collective-permute-start(f32[8,128]{1,0:T(8,128)S(1)} %add.107), channel_id=1, source_target_pairs={{0,32},{16,48},{32,64},{48,80},{64,96},{80,112},{96,0},{112,16},{1... | collective-permute-start | bytes 12296 | tf_op jit(solution)/shard_map/ppermute | solution.py:54
  152.9 2.9 %collective-permute-start.7 = (f32[8,128]{1,0:T(8,128)S(1)}, f32[8,128]{1,0:T(8,128)S(1)}, u32[]{:S(2)}, u32[]{:S(2)}) collective-permute-start(f32[8,128]{1,0:T(8,128)S(1)} %add.107), channel_id=1, source_target_pairs={{0,64},{16,80},{32,96},{48,112},{64,0},{80,16},{96,32},{112,48},{1... | collective-permute-start | bytes 12296 | tf_op jit(solution)/shard_map/ppermute | solution.py:54
  169.5 6.5 %all-to-all-start.6 = ((f32[16,64,512]{2,1,0:T(8,128)}), f32[16,64,512]{2,1,0:T(8,128)S(1)}, u32[]{:S(2)}, u32[]{:S(2)}) async-start(f32[16,64,512]{2,1,0:T(8,128)} %gate.3), calls=%async_computation.6 | async-start | bytes 4194304 | tf_op jit(solution)/shard_map/all_to_all | solution.py:537
  182.8 11.9 %collective-permute-done.14 = f32[8,128]{1,0:T(8,128)S(1)} collective-permute-done((f32[8,128]{1,0:T(8,128)S(1)}, f32[8,128]{1,0:T(8,128)S(1)}, u32[]{:S(2)}, u32[]{:S(2)}) %collective-permute-start.14) | collective-permute-done | bytes 4128 | tf_op jit(solution)/shard_map/ppermute | solution.py:54
  194.7 4.1 %collective-permute-done.15 = f32[8,128]{1,0:T(8,128)S(1)} collective-permute-done((f32[8,128]{1,0:T(8,128)S(1)}, f32[8,128]{1,0:T(8,128)S(1)}, u32[]{:S(2)}, u32[]{:S(2)}) %collective-permute-start.15) | collective-permute-done | bytes 4128 | tf_op jit(solution)/shard_map/ppermute | solution.py:54
  199.1 4.6 %first.1 = (f32[64,8,512]{2,1,0:T(8,128)}, f32[64,8,512]{2,1,0:T(8,128)S(1)}) custom-call(s32[8]{0:T(128)S(1)} %and_select_fusion.src_ref, f32[8,128]{1,0:T(8,128)S(1)} %add_add_fusion.dots_ref, f32[16,64,512]{2,1,0:T(8,128)} %copy-done.3, f32[16,64,512]{2,1,0:T(8,128)} %all-to-all-done.5.refs_1_.refs_3_.refs_5_.refs_7_.refs_9_.refs_11_.refs_13_.refs_15_, ...), custom_call_target="tpu_custom_call" | custom-call | tf_op jit(solution)/shard_map/first/pallas_call | solution.py:521
  204.4 2.7 %second.1 = f32[64,8,512]{2,1,0:T(8,128)} custom-call(s32[8]{0:T(128)S(1)} %and_select_fusion.src_ref, f32[8,128]{1,0:T(8,128)S(1)} %add_add_fusion.dots_ref, f32[64,8,512]{2,1,0:T(8,128)S(1)} %get-tuple-element.98.part_ref, f32[16,64,512]{2,1,0:T(8,128)S(1)} %all-to-all-done.6.refs_0_.refs_1_.refs_2_.refs_3_.refs_4_.refs_5_.refs_6_.refs_7_, ...), custom_call_target="tpu_custom_call" | custom-call | tf_op jit(solution)/shard_map/second/pallas_call | solution.py:521
  (112 shorter events, 44.9 us)
Async XLA Ops:
  4.8 11.1 %all-to-all-start = ((f32[8,72,32]{1,2,0:T(8,128)}), f32[8,72,32]{1,2,0:T(8,128)S(1)}, u32[]{:S(2)}, u32[]{:S(2)}) async-start(f32[8,72,32]{1,2,0:T(8,128)} %broadcast_in_dim.14), calls=%async_computation | async-start | bytes 262144 | tf_op jit(solution)/shard_map/all_to_all | solution.py:42
  17.6 21.6 %all-to-all-start.1 = ((f32[16,72,128]{2,1,0:T(8,128)}), f32[16,72,128]{2,1,0:T(8,128)S(1)}, u32[]{:S(2)}, u32[]{:S(2)}) async-start(f32[16,72,128]{2,1,0:T(8,128)} %broadcast_in_dim.15), calls=%async_computation.1 | async-start | bytes 1179648 | tf_op jit(solution)/shard_map/all_to_all | solution.py:42
  26.5 30.1 %collective-permute-start = (f32[67,16,128]{2,1,0:T(8,128)}, f32[67,16,128]{2,1,0:T(8,128)S(1)}, u32[]{:S(2)}, u32[]{:S(2)}) collective-permute-start(f32[67,16,128]{2,1,0:T(8,128)} %get-tuple-element.76), channel_id=1, source_target_pairs={{0,1},{1,2},{2,3},{3,4},{4,5},{5,6},{6,7},{7,8},{8,9},{9,10},{10,1... | collective-permute-start | bytes 1646600 | tf_op jit(solution)/shard_map/ppermute | solution.py:67
  28.4 28.2 %collective-permute-start.1 = (f32[67,16,128]{2,1,0:T(8,128)S(1)}, f32[67,16,128]{2,1,0:T(8,128)S(1)}, u32[]{:S(2)}, u32[]{:S(2)}) collective-permute-start(f32[67,16,128]{2,1,0:T(8,128)S(1)} %get-tuple-element.77), channel_id=1, source_target_pairs={{1,0},{2,1},{3,2},{4,3},{5,4},{6,5},{7,6},{8,7},{9,8},{10,9},{11,1... | collective-permute-start | bytes 1646600 | tf_op jit(solution)/shard_map/ppermute | solution.py:67
  41.0 14.2 %all-to-all-start.2 = ((f32[8,1,2048]{2,1,0:T(1,128)}), f32[8,1,2048]{2,1,0:T(1,128)S(1)}, u32[]{:S(2)}, u32[]{:S(2)}) async-start(f32[8,1,2048]{2,1,0:T(1,128)} %reshape.131), calls=%async_computation.2 | async-start | bytes 131072 | tf_op jit(solution)/shard_map/all_to_all | solution.py:42
  58.3 17.5 %all-to-all-start.3 = ((f32[16,80,128]{2,1,0:T(8,128)}), f32[16,80,128]{2,1,0:T(8,128)S(1)}, u32[]{:S(2)}, u32[]{:S(2)}) async-start(f32[16,80,128]{2,1,0:T(8,128)} %broadcast_in_dim.18), calls=%async_computation.3 | async-start | bytes 1310720 | tf_op jit(solution)/shard_map/all_to_all | solution.py:42
  79.6 47.8 %all-to-all-start.4 = ((f32[16,64,512]{2,1,0:T(8,128)}), f32[16,64,512]{2,1,0:T(8,128)S(1)}, u32[]{:S(2)}, u32[]{:S(2)}) async-start(f32[16,64,512]{2,1,0:T(8,128)} %get-tuple-element.95), calls=%async_computation.4 | async-start | bytes 4194304 | tf_op jit(solution)/shard_map/all_to_all | solution.py:537
  106.3 18.8 %collective-permute-start.3 = (f32[4,64,512]{2,1,0:T(8,128)S(1)}, f32[4,64,512]{2,1,0:T(8,128)S(1)}, u32[]{:S(2)}, u32[]{:S(2)}) collective-permute-start(f32[4,64,512]{2,1,0:T(8,128)S(1)} %get-tuple-element.93), channel_id=1, source_target_pairs={{1,0},{2,1},{3,2},{4,3},{5,4},{6,5},{7,6},{8,7},{9,8},{10,9},{11,1... | collective-permute-start | bytes 1572872 | tf_op jit(solution)/shard_map/ppermute | solution.py:67
  111.6 15.7 %collective-permute-start.2 = (f32[4,64,512]{2,1,0:T(8,128)S(1)}, f32[4,64,512]{2,1,0:T(8,128)S(1)}, u32[]{:S(2)}, u32[]{:S(2)}) collective-permute-start(f32[4,64,512]{2,1,0:T(8,128)S(1)} %get-tuple-element.92), channel_id=1, source_target_pairs={{0,1},{1,2},{2,3},{3,4},{4,5},{5,6},{6,7},{7,8},{8,9},{9,10},{10,1... | collective-permute-start | bytes 1572872 | tf_op jit(solution)/shard_map/ppermute | solution.py:67
  128.8 40.0 %all-to-all-start.5 = ((f32[16,64,512]{2,1,0:T(8,128)}), f32[16,64,512]{2,1,0:T(8,128)}, u32[]{:S(2)}, u32[]{:S(2)}) async-start(f32[16,64,512]{2,1,0:T(8,128)} %gate.2), calls=%async_computation.5 | async-start | bytes 4194304 | tf_op jit(solution)/shard_map/all_to_all | solution.py:537
  147.7 8.0 %collective-permute-start.10 = (f32[8,128]{1,0:T(8,128)S(1)}, f32[8,128]{1,0:T(8,128)S(1)}, u32[]{:S(2)}, u32[]{:S(2)}) collective-permute-start(f32[8,128]{1,0:T(8,128)S(1)} %add.107), channel_id=1, source_target_pairs={{0,112},{16,0},{32,16},{48,32},{64,48},{80,64},{96,80},{112,96},{1... | collective-permute-start | bytes 12296 | tf_op jit(solution)/shard_map/ppermute | solution.py:54
  149.0 7.9 %collective-permute-start.4 = (f32[8,128]{1,0:T(8,128)S(1)}, f32[8,128]{1,0:T(8,128)S(1)}, u32[]{:S(2)}, u32[]{:S(2)}) collective-permute-start(f32[8,128]{1,0:T(8,128)S(1)} %add.107), channel_id=1, source_target_pairs={{0,16},{16,32},{32,48},{48,64},{64,80},{80,96},{96,112},{112,0},{1... | collective-permute-start | bytes 12296 | tf_op jit(solution)/shard_map/ppermute | solution.py:54
  149.0 9.3 %collective-permute-start.5 = (f32[8,128]{1,0:T(8,128)S(1)}, f32[8,128]{1,0:T(8,128)S(1)}, u32[]{:S(2)}, u32[]{:S(2)}) collective-permute-start(f32[8,128]{1,0:T(8,128)S(1)} %add.107), channel_id=1, source_target_pairs={{0,32},{16,48},{32,64},{48,80},{64,96},{80,112},{96,0},{112,16},{1... | collective-permute-start | bytes 12296 | tf_op jit(solution)/shard_map/ppermute | solution.py:54
  152.1 6.3 %collective-permute-start.6 = (f32[8,128]{1,0:T(8,128)S(1)}, f32[8,128]{1,0:T(8,128)S(1)}, u32[]{:S(2)}, u32[]{:S(2)}) collective-permute-start(f32[8,128]{1,0:T(8,128)S(1)} %add.107), channel_id=1, source_target_pairs={{0,48},{16,64},{32,80},{48,96},{64,112},{80,0},{96,16},{112,32},{1... | collective-permute-start | bytes 12296 | tf_op jit(solution)/shard_map/ppermute | solution.py:54
  152.9 5.5 %collective-permute-start.7 = (f32[8,128]{1,0:T(8,128)S(1)}, f32[8,128]{1,0:T(8,128)S(1)}, u32[]{:S(2)}, u32[]{:S(2)}) collective-permute-start(f32[8,128]{1,0:T(8,128)S(1)} %add.107), channel_id=1, source_target_pairs={{0,64},{16,80},{32,96},{48,112},{64,0},{80,16},{96,32},{112,48},{1... | collective-permute-start | bytes 12296 | tf_op jit(solution)/shard_map/ppermute | solution.py:54
  155.7 3.0 %collective-permute-start.8 = (f32[8,128]{1,0:T(8,128)S(1)}, f32[8,128]{1,0:T(8,128)S(1)}, u32[]{:S(2)}, u32[]{:S(2)}) collective-permute-start(f32[8,128]{1,0:T(8,128)S(1)} %add.107), channel_id=1, source_target_pairs={{0,80},{16,96},{32,112},{48,0},{64,16},{80,32},{96,48},{112,64},{1... | collective-permute-start | bytes 12296 | tf_op jit(solution)/shard_map/ppermute | solution.py:54
  156.9 3.6 %collective-permute-start.9 = (f32[8,128]{1,0:T(8,128)S(1)}, f32[8,128]{1,0:T(8,128)S(1)}, u32[]{:S(2)}, u32[]{:S(2)}) collective-permute-start(f32[8,128]{1,0:T(8,128)S(1)} %add.107), channel_id=1, source_target_pairs={{0,96},{16,112},{32,0},{48,16},{64,32},{80,48},{96,64},{112,80},{1... | collective-permute-start | bytes 12296 | tf_op jit(solution)/shard_map/ppermute | solution.py:54
  160.6 6.1 %collective-permute-start.11 = (f32[8,128]{1,0:T(8,128)S(1)}, f32[8,128]{1,0:T(8,128)S(1)}, u32[]{:S(2)}, u32[]{:S(2)}) collective-permute-start(f32[8,128]{1,0:T(8,128)S(1)} %add_add_fusion.2), channel_id=1, source_target_pairs={{0,1},{1,2},{2,3},{3,0},{4,5},{5,6},{6,7},{7,4},{8,9},{9,10},{10,1... | collective-permute-start | bytes 12296 | tf_op jit(solution)/shard_map/ppermute | solution.py:54
  162.5 5.1 %collective-permute-start.12 = (f32[8,128]{1,0:T(8,128)S(1)}, f32[8,128]{1,0:T(8,128)S(1)}, u32[]{:S(2)}, u32[]{:S(2)}) collective-permute-start(f32[8,128]{1,0:T(8,128)S(1)} %add_add_fusion.2), channel_id=1, source_target_pairs={{0,2},{1,3},{2,0},{3,1},{4,6},{5,7},{6,4},{7,5},{8,10},{9,11},{10,... | collective-permute-start | bytes 12296 | tf_op jit(solution)/shard_map/ppermute | solution.py:54
  165.2 3.6 %collective-permute-start.13 = (f32[8,128]{1,0:T(8,128)S(1)}, f32[8,128]{1,0:T(8,128)S(1)}, u32[]{:S(2)}, u32[]{:S(2)}) collective-permute-start(f32[8,128]{1,0:T(8,128)S(1)} %add_add_fusion.2), channel_id=1, source_target_pairs={{0,3},{1,0},{2,1},{3,2},{4,7},{5,4},{6,5},{7,6},{8,11},{9,8},{10,9... | collective-permute-start | bytes 12296 | tf_op jit(solution)/shard_map/ppermute | solution.py:54
  169.5 34.9 %all-to-all-start.6 = ((f32[16,64,512]{2,1,0:T(8,128)}), f32[16,64,512]{2,1,0:T(8,128)S(1)}, u32[]{:S(2)}, u32[]{:S(2)}) async-start(f32[16,64,512]{2,1,0:T(8,128)} %gate.3), calls=%async_computation.6 | async-start | bytes 4194304 | tf_op jit(solution)/shard_map/all_to_all | solution.py:537
  176.6 18.1 %collective-permute-start.14 = (f32[8,128]{1,0:T(8,128)S(1)}, f32[8,128]{1,0:T(8,128)S(1)}, u32[]{:S(2)}, u32[]{:S(2)}) collective-permute-start(f32[8,128]{1,0:T(8,128)S(1)} %add_add_fusion.1.refs_2_), channel_id=1, source_target_pairs={{0,4},{4,8},{8,12},{12,0},{1,5},{5,9},{9,13},{13,1},{2,6},{6,10},{... | collective-permute-start | bytes 12296 | tf_op jit(solution)/shard_map/ppermute | solution.py:54
  178.6 20.2 %collective-permute-start.15 = (f32[8,128]{1,0:T(8,128)S(1)}, f32[8,128]{1,0:T(8,128)S(1)}, u32[]{:S(2)}, u32[]{:S(2)}) collective-permute-start(f32[8,128]{1,0:T(8,128)S(1)} %add_add_fusion.1.refs_2_), channel_id=1, source_target_pairs={{0,8},{4,12},{8,0},{12,4},{1,9},{5,13},{9,1},{13,5},{2,10},{6,14},... | collective-permute-start | bytes 12296 | tf_op jit(solution)/shard_map/ppermute | solution.py:54
  181.3 17.8 %collective-permute-start.16 = (f32[8,128]{1,0:T(8,128)S(1)}, f32[8,128]{1,0:T(8,128)S(1)}, u32[]{:S(2)}, u32[]{:S(2)}) collective-permute-start(f32[8,128]{1,0:T(8,128)S(1)} %add_add_fusion.1.refs_2_), channel_id=1, source_target_pairs={{0,12},{4,0},{8,4},{12,8},{1,13},{5,1},{9,5},{13,9},{2,14},{6,2},{... | collective-permute-start | bytes 12296 | tf_op jit(solution)/shard_map/ppermute | solution.py:54
  (8 other events, 32.3 us)

commit v6 on v5

--- a/solution.py
+++ b/solution.py
@@ -30,9 +30,10 @@
 
 OWN_TILES = BLOCKS_DEV + PAIRED * BLOCKS_DEV - 6
 HALO_TILES = 2 * (2 + 3 + 4)
-CHUNKS = (5, 9, 12, 18)
+CHUNKS = (5, 9, 9, 21)
 TILE_SLOTS = 4
-OP_SLOTS = 5
+OP_SLOTS = 12
+OP_FIRST = 4
 EXTRA = 8
 EARLY_TILES = 18
 
@@ -57,14 +58,18 @@
     return functools.reduce(jnp.add, moved, part)
 
 
-def beside(shard, width, dim=0):
-    peers, length = lax.axis_size(SIXTEEN), shard.shape[dim]
+def swapped(initial, last):
+    peers = lax.axis_size(SIXTEEN)
     up = [(i, (i + 1) % peers) for i in range(peers)]
     down = [(j, i) for i, j in up]
+    return lax.ppermute(last, SIXTEEN, up), lax.ppermute(initial, SIXTEEN, down)
+
+
+def beside(shard, width, dim=0):
+    length = shard.shape[dim]
     last = lax.slice_in_dim(shard, length - width, length, axis=dim)
     initial = lax.slice_in_dim(shard, 0, width, axis=dim)
-    shard, last, initial = lax.optimization_barrier((shard, last, initial))
-    return lax.ppermute(last, SIXTEEN, up), lax.ppermute(initial, SIXTEEN, down), shard
+    return swapped(*lax.optimization_barrier((initial, last)))
 
 
 def owned_table(group_map, owners, per_owner):
@@ -267,6 +272,7 @@
     beside_refs = [refs.pop(0), refs.pop(0)] if halo else []
     held_ref = refs.pop(0) if held else None
     tiles_ref, out_ref = refs.pop(0), refs.pop(0)
+    edge_refs = [refs.pop(0), refs.pop(0)] if send and not held else []
     slots_ref, dots_ref = (refs.pop(0), refs.pop(0)) if send else (None, None)
     values, both_ref, total, buf, sem, in_sem, out_sem = refs
     fields = total.shape[1]
@@ -290,7 +296,7 @@
         arriving.append(pltpu.make_async_copy(held_ref, total, in_sem.at[3]))
     for load in arriving:
         load.start()
-    for t in range(OP_SLOTS - 1):
+    for t in range(OP_FIRST):
         copy(t).start()
     for load in arriving:
         load.wait()
@@ -300,10 +306,16 @@
             both_ref[g, :fields] = hi
             both_ref[g, fields:] = lo
 
+    def started(t):
+        return jnp.minimum(jnp.minimum(OP_FIRST + 2 * t, t + OP_SLOTS - 1), count)
+
     def arrive(t):
-        @pl.when(t + OP_SLOTS - 1 < count)
-        def _():
-            copy(t + OP_SLOTS - 1).start()
+        following, end = started(t), started(t + 1)
+        for more in range(2):
+
+            @pl.when(following + more < end)
+            def _(more=more):
+                copy(following + more).start()
 
         copy(t).wait()
         return buf.at[lax.rem(t, OP_SLOTS)]
@@ -332,7 +344,13 @@
     lax.fori_loop(max(BLOCKS_DEV - first, 0), mine, with_another, 0)
     if halo:
         lax.fori_loop(mine, count, with_beside, 0)
-    leaving = [pltpu.make_async_copy(total, out_ref, out_sem.at[BLOCKS_DEV])]
+    leaving = [
+        pltpu.make_async_copy(
+            total.at[pl.ds(REACH * side, REACH)], ref, out_sem.at[BLOCKS_DEV + 1 + side]
+        )
+        for side, ref in enumerate(edge_refs)
+    ]
+    leaving.append(pltpu.make_async_copy(total, out_ref, out_sem.at[BLOCKS_DEV]))
     if send:
         leaving += out_copies(total, slots_ref, target_ref, out_sem)
     for out in leaving:
@@ -377,13 +395,14 @@
 
 def applied(scalars, targets, tiles, v, tiles_of=(0, None), beside=(), held=None, send=False):
     blocks, fields, _ = v.shape
+    edges = send and held is None
     out = pltpu.HBM(v.shape, jnp.float32)
     ins = [in_hbm(x) for x in (v, *beside, held) if x is not None] + [tiles]
     number = (tiles_of[1] or OWN_TILES) - tiles_of[0] + HALO_TILES * bool(beside)
     out = pl.pallas_call(
         functools.partial(op_kernel, *tiles_of, bool(beside), held is not None, send),
         in_specs=[SMEM_SPEC] * 2 + [HBM_SPEC] * len(ins),
-        out_specs=[HBM_SPEC] + [HBM_SPEC, VMEM_SPEC] * send,
+        out_specs=[HBM_SPEC] + [HBM_SPEC] * (2 * edges) + [HBM_SPEC, VMEM_SPEC] * send,
         scratch_shapes=[
             pltpu.VMEM((blocks + 2 * REACH, fields, BLOCK), jnp.float32),
             pltpu.VMEM((blocks + 2 * REACH, 2 * fields, BLOCK), jnp.bfloat16),
@@ -391,11 +410,12 @@
             pltpu.VMEM((OP_SLOTS, 2 * BLOCK, BLOCK), jnp.bfloat16),
             pltpu.SemaphoreType.DMA((OP_SLOTS,)),
             pltpu.SemaphoreType.DMA((4,)),
-            pltpu.SemaphoreType.DMA((BLOCKS_DEV + 1,)),
+            pltpu.SemaphoreType.DMA((BLOCKS_DEV + 3,)),
         ],
         out_shape=[out]
+        + [pltpu.HBM((REACH, fields, BLOCK), jnp.float32)] * (2 * edges)
         + [slot_shape(v), jax.ShapeDtypeStruct((EXTRA, COL_DEV), jnp.float32)] * send,
-        compiler_params=pltpu.CompilerParams(vmem_limit_bytes=24 << 20),
+        compiler_params=pltpu.CompilerParams(vmem_limit_bytes=28 << 20),
         cost_estimate=pl.CostEstimate(
             flops=3 * number * 3 * fields * BLOCK * BLOCK,
             bytes_accessed=number * 4 * BLOCK * BLOCK,
@@ -598,7 +618,7 @@
         return lax.optimization_barrier((received, tiles))
 
     edges = jnp.concatenate([observations, weight[None], jitter], axis=0)
-    before, after, _ = beside(edges, REACH * STRIP, 1)
+    before, after = beside(edges, REACH * STRIP, 1)
     received, tiles = beside_tiles(part, WIDE, 0, None)
     total = jnp.sum(received, axis=0)
     row_count = jnp.maximum(total[fields], 1.0)
@@ -608,11 +628,12 @@
     total = jnp.sum(received, axis=0)
     col_count = jnp.maximum(total[fields], 1.0)
     col_effect = huber_scale[:, None] * total[:fields] / col_count[None, :]
-    part = jnp.sum(terms(row_effect, col_effect), axis=2)
+    part = with_count(jnp.sum(terms(row_effect, col_effect), axis=2), jnp.zeros_like(row_count))
     received, tiles = beside_tiles(part, WIDE, 2, tiles)
     received, before, after = lax.optimization_barrier((received, before, after))
     near = (before[fields + 1 :], after[fields + 1 :])
-    row_effect = row_effect + huber_scale[:, None] * jnp.sum(received, axis=0) / row_count[None, :]
+    total = jnp.sum(received, axis=0)
+    row_effect = row_effect + huber_scale[:, None] * total[:fields] / row_count[None, :]
     part = jnp.sum(terms(row_effect, col_effect), axis=1)
     part = jnp.concatenate([part, row_effect.reshape(-1, col_dev)], axis=0)
     received, tiles = beside_tiles(part, SIXTEEN, 3, tiles, near)
@@ -631,10 +652,10 @@
         my_targets, observations, weight, row_effect, before, row_before, after, row_after, col_effect
     )
     owned_r0 = to_owners(slots)
-    m1, slots, dots = applied(
+    m1, initial, last, slots, dots = applied(
         scalars, my_targets, tiles, r0, beside=(r0_before, r0_after), send=True
     )
-    before, after, m1 = beside(m1, REACH)
+    before, after = swapped(initial, last)
     part = applied(scalars, my_targets, tiles, m1, (0, EARLY_TILES))
     slots = gate(slots, part, before, after, owned_r0)
     owned_m1 = to_owners(slots)

time: 209 us -> 207 us (level)
  starting transfers between devices: 69.6 us -> 73.3 us
  waiting for transfers between devices: 27.6 us -> 25.2 us
    all_to_all x4, waiting for transfers between devices: 4.14 us -> 1.44 us  [sent_to_all(): lax.all_to_all(jnp.broadcast_to(shard[None], (peers, *shard.shape)), axis...]
    all_to_all x3, starting transfers between devices: 15 us -> 17.1 us  [to_owners(): return lax.all_to_all(slots, SIXTEEN, 0, 0, tiled=True)]
  transfers between devices with their start and end apart: 24 -> 24, of which waited for: 10 -> 10; matrix products, arithmetic and copies ran while one was open for 4% -> 2% of each run, Pallas kernels for 41% -> 41%
where the time goes in v6:
time: 207 us; the launch traced here: 206 us
  Pallas kernels  91 us (44%)
  starting transfers between devices  73.3 us (35%)
  waiting for transfers between devices  25.2 us (12%)
  local copies, waits for them, and re-layouts  9.25 us (4%)
  other arithmetic  6.55 us (3%)
    pallas_call x3, Pallas kernels, applied(): pl.pallas_call(functools.partial(op_kernel, *tiles_of, bool(beside), held...  48.6 us
    pallas_call x4, Pallas kernels, covariance_tiles(): pl.pallas_call(functools.partial(tiles_kernel, first, count, len(beside_j...  31.7 us
    ppermute x13, starting transfers between devices, sum_direct(): lax.ppermute(part, axis, [(i, (i + k) % peers) for i in range(peers)])  24.4 us
    all_to_all x4, starting transfers between devices, sent_to_all(): lax.all_to_all(jnp.broadcast_to(shard[None], (peers, *shard.shape)), axis...  21.1 us
    ppermute x13, waiting for transfers between devices, sum_direct(): lax.ppermute(part, axis, [(i, (i + k) % peers) for i in range(peers)])  20.8 us
    all_to_all x3, starting transfers between devices, to_owners(): return lax.all_to_all(slots, SIXTEEN, 0, 0, tiled=True)  17.1 us
    ppermute x2, starting transfers between devices, swapped(): lax.ppermute(initial, SIXTEEN, down)  8.74 us
    pallas_call x2, Pallas kernels, combined(): pl.pallas_call(kernel, grid_spec=pltpu.PrefetchScalarGridSpec(num_scalar_...  7.33 us
  transfers between devices with their start and end apart: 24, of which 10 were waited for; matrix products, arithmetic and copies ran while one was open for 2% of the time, Pallas kernels for 41%

profile of v6, /device:TPU:0, one launch (start us, length us, event | category | flops | bytes accessed | tf_op | source)
XLA Modules:
  0.0 206.3 jit_solution(5981556381794011483)
XLA Ops:
  4.8 4.6 %all-to-all-start = ((f32[8,72,32]{1,2,0:T(8,128)}), f32[8,72,32]{1,2,0:T(8,128)S(1)}, u32[]{:S(2)}, u32[]{:S(2)}) async-start(f32[8,72,32]{1,2,0:T(8,128)} %broadcast_in_dim.14), calls=%async_computation | async-start | bytes 262144 | tf_op jit(solution)/shard_map/all_to_all | solution.py:43
  11.1 4.8 %tiles.4.refs_0_ = bf16[44,1024,512]{2,1,0:T(8,128)(2,1)} custom-call(s32[9]{0:T(128)S(1)} %pad_add_fusion.scalar_ref, f32[2,32,128]{2,1,0:T(8,128)S(1)} %copy-done.1), custom_call_target="tpu_custom_call" | custom-call | flops 15728640 | bytes 5242880 | tf_op jit(solution)/shard_map/tiles/pallas_call | solution.py:228
  17.6 7.9 %all-to-all-start.1 = ((f32[16,72,128]{2,1,0:T(8,128)}), f32[16,72,128]{2,1,0:T(8,128)S(1)}, u32[]{:S(2)}, u32[]{:S(2)}) async-start(f32[16,72,128]{2,1,0:T(8,128)} %broadcast_in_dim.15), calls=%async_computation.1 | async-start | bytes 1179648 | tf_op jit(solution)/shard_map/all_to_all | solution.py:43
  28.4 3.4 %collective-permute-start.1 = (f32[67,16,128]{2,1,0:T(8,128)S(1)}, f32[67,16,128]{2,1,0:T(8,128)S(1)}, u32[]{:S(2)}, u32[]{:S(2)}) collective-permute-start(f32[67,16,128]{2,1,0:T(8,128)S(1)} %get-tuple-element.88), channel_id=1, source_target_pairs={{1,0},{2,1},{3,2},{4,3},{5,4},{6,5},{7,6},{8,7},{9,8},{10,9},{11,1... | collective-permute-start | bytes 1646600 | tf_op jit(solution)/shard_map/ppermute | solution.py:65
  31.9 7.4 %tiles.5.refs_0_ = bf16[44,1024,512]{2,1,0:T(8,128)(2,1)} custom-call(s32[9]{0:T(128)S(1)} %pad_add_fusion.scalar_ref, f32[2,32,128]{2,1,0:T(8,128)S(1)} %copy-done.2, bf16[44,1024,512]{2,1,0:T(8,128)(2,1)} %tiles.4.refs_0_), custom_call_target="tpu_custom_call", output_to_operand_aliasing={{}: (2, {})} | custom-call | flops 28311552 | bytes 9437184 | tf_op jit(solution)/shard_map/tiles/pallas_call | solution.py:228
  41.0 4.8 %all-to-all-start.2 = ((f32[8,72,32]{1,2,0:T(8,128)}), f32[8,72,32]{1,2,0:T(8,128)S(1)}, u32[]{:S(2)}, u32[]{:S(2)}) async-start(f32[8,72,32]{1,2,0:T(8,128)} %broadcast_in_dim.16), calls=%async_computation.2 | async-start | bytes 262144 | tf_op jit(solution)/shard_map/all_to_all | solution.py:43
  45.8 7.4 %tiles.6.refs_2_ = bf16[44,1024,512]{2,1,0:T(8,128)(2,1)} custom-call(s32[9]{0:T(128)S(1)} %pad_add_fusion.scalar_ref, f32[2,32,128]{2,1,0:T(8,128)S(1)} %copy-done.2, bf16[44,1024,512]{2,1,0:T(8,128)(2,1)} %tiles.5.refs_0_), custom_call_target="tpu_custom_call", output_to_operand_aliasing={{}: (2, {})} | custom-call | flops 28311552 | bytes 9437184 | tf_op jit(solution)/shard_map/tiles/pallas_call | solution.py:228
  54.9 3.9 %all-to-all-start.3 = ((f32[16,80,128]{2,1,0:T(8,128)}), f32[16,80,128]{2,1,0:T(8,128)S(1)}, u32[]{:S(2)}, u32[]{:S(2)}) async-start(f32[16,80,128]{2,1,0:T(8,128)} %broadcast_in_dim.18), calls=%async_computation.3 | async-start | bytes 1310720 | tf_op jit(solution)/shard_map/all_to_all | solution.py:43
  58.9 12.0 %tiles.7.refs_3_.refs_1_.refs_4_ = bf16[44,1024,512]{2,1,0:T(8,128)(2,1)} custom-call(s32[9]{0:T(128)S(1)} %pad_add_fusion.scalar_ref, f32[2,32,128]{2,1,0:T(8,128)S(1)} %copy-done.2, f32[2,16,128]{2,1,0:T(8,128)S(1)} %slice.108.refs_0_, f32[2,16,128]{2,1,0:T(8,128)S(1)} %slice.109.refs_1_, ...), custom_call_target="tpu_custom_call", output_to_operand_aliasing={{}: (4, {})} | custom-call | flops 66060288 | bytes 22020096 | tf_op jit(solution)/shard_map/tiles/pallas_call | solution.py:228
  72.8 3.3 %residual.1 = (f32[8,64,512]{2,1,0:T(8,128)}, f32[4,64,512]{2,1,0:T(8,128)}, f32[4,64,512]{2,1,0:T(8,128)}, f32[16,64,512]{2,1,0:T(8,128)}) custom-call(s32[8]{0:T(128)S(1)} %fusion.4.target_ref, f32[64,32,128]{2,1,0:T(8,128)S(1)} %copy-done, f32[32,128]{1,0:T(8,128)S(1)} %get-tuple-element.117.weight_ref, f32[64,32]{1,0:T(8,128)S(1)} %divide_add_fusion.1.row_ref, ...), custom_call_target="tpu_custom_call" | custom-call | tf_op jit(solution)/shard_map/residual/pallas_call | solution.py:489
  76.2 5.8 %all-to-all-start.4 = ((f32[16,64,512]{2,1,0:T(8,128)}), f32[16,64,512]{2,1,0:T(8,128)S(1)}, u32[]{:S(2)}, u32[]{:S(2)}) async-start(f32[16,64,512]{2,1,0:T(8,128)} %get-tuple-element.105), calls=%async_computation.4 | async-start | bytes 4194304 | tf_op jit(solution)/shard_map/all_to_all | solution.py:557
  81.9 21.9 %applied.3 = (f32[8,64,512]{2,1,0:T(8,128)}, f32[4,64,512]{2,1,0:T(8,128)}, f32[4,64,512]{2,1,0:T(8,128)}, f32[16,64,512]{2,1,0:T(8,128)}, f32[8,128]{1,0:T(8,128)S(1)}) custom-call(s32[9]{0:T(128)S(1)} %pad_add_fusion.scalar_ref, s32[8]{0:T(128)S(1)} %fusion.4.target_ref, f32[8,64,512]{2,1,0:T(8,128)} %get-tuple-element.96.refs_0_, ...), custom_call_target="tpu_custom_call" | custom-call | flops 6643777536 | bytes 46137344 | tf_op jit(solution)/shard_map/applied/pallas_call | solution.py:402
  103.8 5.3 %collective-permute-start.3 = (f32[4,64,512]{2,1,0:T(8,128)}, f32[4,64,512]{2,1,0:T(8,128)S(1)}, u32[]{:S(2)}, u32[]{:S(2)}) collective-permute-start(f32[4,64,512]{2,1,0:T(8,128)} %get-tuple-element.103), channel_id=1, source_target_pairs={{1,0},{2,1},{3,2},{4,3},{5,4},{6,5},{7,6},{8,7},{9,8},{10,9},{11,1... | collective-permute-start | bytes 1572872 | tf_op jit(solution)/shard_map/ppermute | solution.py:65
  109.1 12.9 %applied.4.refs_3_ = f32[8,64,512]{2,1,0:T(8,128)} custom-call(s32[9]{0:T(128)S(1)} %pad_add_fusion.scalar_ref, s32[8]{0:T(128)S(1)} %fusion.4.target_ref, f32[8,64,512]{2,1,0:T(8,128)} %get-tuple-element.101.refs_0_, bf16[44,1024,512]{2,1,0:T(8,128)(2,1)} %tiles.7.refs_3_.refs_1_.refs_4_), custom_call_target="tpu_custom_call" | custom-call | flops 2717908992 | bytes 18874368 | tf_op jit(solution)/shard_map/applied/pallas_call | solution.py:402
  126.4 4.8 %all-to-all-start.5 = ((f32[16,64,512]{2,1,0:T(8,128)}), f32[16,64,512]{2,1,0:T(8,128)}, u32[]{:S(2)}, u32[]{:S(2)}) async-start(f32[16,64,512]{2,1,0:T(8,128)} %gate.2), calls=%async_computation.5 | async-start | bytes 4194304 | tf_op jit(solution)/shard_map/all_to_all | solution.py:557
  131.2 13.8 %applied.5 = (f32[8,64,512]{2,1,0:T(8,128)}, f32[16,64,512]{2,1,0:T(8,128)}, f32[8,128]{1,0:T(8,128)S(1)}) custom-call(s32[9]{0:T(128)S(1)} %pad_add_fusion.scalar_ref, s32[8]{0:T(128)S(1)} %fusion.4.target_ref, f32[8,64,512]{2,1,0:T(8,128)} %get-tuple-element.101.refs_0_, f32[4,64,512]{2,1,0:T(8,128)} %copy-done.5, f32[4,64,512]{2,1,0:T(8,128)} %copy-done.4, ...), custom_call_target="tpu_custom_call" | custom-call | flops 3925868544 | bytes 27262976 | tf_op jit(solution)/shard_map/applied/pallas_call | solution.py:402
  145.1 5.1 %collective-permute-start.10 = (f32[8,128]{1,0:T(8,128)S(1)}, f32[8,128]{1,0:T(8,128)S(1)}, u32[]{:S(2)}, u32[]{:S(2)}) collective-permute-start(f32[8,128]{1,0:T(8,128)S(1)} %add.111), channel_id=1, source_target_pairs={{0,112},{16,0},{32,16},{48,32},{64,48},{80,64},{96,80},{112,96},{1... | collective-permute-start | bytes 12296 | tf_op jit(solution)/shard_map/ppermute | solution.py:55
  151.8 2.9 %collective-permute-start.7 = (f32[8,128]{1,0:T(8,128)S(1)}, f32[8,128]{1,0:T(8,128)S(1)}, u32[]{:S(2)}, u32[]{:S(2)}) collective-permute-start(f32[8,128]{1,0:T(8,128)S(1)} %add.111), channel_id=1, source_target_pairs={{0,64},{16,80},{32,96},{48,112},{64,0},{80,16},{96,32},{112,48},{1... | collective-permute-start | bytes 12296 | tf_op jit(solution)/shard_map/ppermute | solution.py:55
  161.2 2.7 %collective-permute-start.12 = (f32[8,128]{1,0:T(8,128)S(1)}, f32[8,128]{1,0:T(8,128)S(1)}, u32[]{:S(2)}, u32[]{:S(2)}) collective-permute-start(f32[8,128]{1,0:T(8,128)S(1)} %add_add_fusion.2), channel_id=1, source_target_pairs={{0,2},{1,3},{2,0},{3,1},{4,6},{5,7},{6,4},{7,5},{8,10},{9,11},{10,... | collective-permute-start | bytes 12296 | tf_op jit(solution)/shard_map/ppermute | solution.py:55
  168.2 6.5 %all-to-all-start.6 = ((f32[16,64,512]{2,1,0:T(8,128)}), f32[16,64,512]{2,1,0:T(8,128)S(1)}, u32[]{:S(2)}, u32[]{:S(2)}) async-start(f32[16,64,512]{2,1,0:T(8,128)} %gate.3), calls=%async_computation.6 | async-start | bytes 4194304 | tf_op jit(solution)/shard_map/all_to_all | solution.py:557
  181.5 11.9 %collective-permute-done.14 = f32[8,128]{1,0:T(8,128)S(1)} collective-permute-done((f32[8,128]{1,0:T(8,128)S(1)}, f32[8,128]{1,0:T(8,128)S(1)}, u32[]{:S(2)}, u32[]{:S(2)}) %collective-permute-start.14) | collective-permute-done | bytes 4128 | tf_op jit(solution)/shard_map/ppermute | solution.py:55
  193.3 4.0 %collective-permute-done.15 = f32[8,128]{1,0:T(8,128)S(1)} collective-permute-done((f32[8,128]{1,0:T(8,128)S(1)}, f32[8,128]{1,0:T(8,128)S(1)}, u32[]{:S(2)}, u32[]{:S(2)}) %collective-permute-start.15) | collective-permute-done | bytes 4128 | tf_op jit(solution)/shard_map/ppermute | solution.py:55
  198.2 4.6 %first.1 = (f32[64,8,512]{2,1,0:T(8,128)}, f32[64,8,512]{2,1,0:T(8,128)S(1)}) custom-call(s32[8]{0:T(128)S(1)} %and_select_fusion.src_ref, f32[8,128]{1,0:T(8,128)S(1)} %add_add_fusion.dots_ref, f32[16,64,512]{2,1,0:T(8,128)} %copy-done.3, f32[16,64,512]{2,1,0:T(8,128)} %all-to-all-done.5.refs_1_.refs_3_.refs_5_.refs_7_.refs_9_.refs_11_.refs_13_.refs_15_, ...), custom_call_target="tpu_custom_call" | custom-call | tf_op jit(solution)/shard_map/first/pallas_call | solution.py:541
  203.7 2.7 %second.1 = f32[64,8,512]{2,1,0:T(8,128)} custom-call(s32[8]{0:T(128)S(1)} %and_select_fusion.src_ref, f32[8,128]{1,0:T(8,128)S(1)} %add_add_fusion.dots_ref, f32[64,8,512]{2,1,0:T(8,128)S(1)} %get-tuple-element.108.part_ref, f32[16,64,512]{2,1,0:T(8,128)S(1)} %all-to-all-done.6.refs_0_.refs_1_.refs_2_.refs_3_.refs_4_.refs_5_.refs_6_.refs_7_, ...), custom_call_target="tpu_custom_call" | custom-call | tf_op jit(solution)/shard_map/second/pallas_call | solution.py:541
  (108 shorter events, 40.8 us)
Async XLA Ops:
  4.8 11.1 %all-to-all-start = ((f32[8,72,32]{1,2,0:T(8,128)}), f32[8,72,32]{1,2,0:T(8,128)S(1)}, u32[]{:S(2)}, u32[]{:S(2)}) async-start(f32[8,72,32]{1,2,0:T(8,128)} %broadcast_in_dim.14), calls=%async_computation | async-start | bytes 262144 | tf_op jit(solution)/shard_map/all_to_all | solution.py:43
  17.6 21.6 %all-to-all-start.1 = ((f32[16,72,128]{2,1,0:T(8,128)}), f32[16,72,128]{2,1,0:T(8,128)S(1)}, u32[]{:S(2)}, u32[]{:S(2)}) async-start(f32[16,72,128]{2,1,0:T(8,128)} %broadcast_in_dim.15), calls=%async_computation.1 | async-start | bytes 1179648 | tf_op jit(solution)/shard_map/all_to_all | solution.py:43
  26.5 26.7 %collective-permute-start = (f32[67,16,128]{2,1,0:T(8,128)}, f32[67,16,128]{2,1,0:T(8,128)S(1)}, u32[]{:S(2)}, u32[]{:S(2)}) collective-permute-start(f32[67,16,128]{2,1,0:T(8,128)} %get-tuple-element.87), channel_id=1, source_target_pairs={{0,1},{1,2},{2,3},{3,4},{4,5},{5,6},{6,7},{7,8},{8,9},{9,10},{10,1... | collective-permute-start | bytes 1646600 | tf_op jit(solution)/shard_map/ppermute | solution.py:65
  28.4 24.8 %collective-permute-start.1 = (f32[67,16,128]{2,1,0:T(8,128)S(1)}, f32[67,16,128]{2,1,0:T(8,128)S(1)}, u32[]{:S(2)}, u32[]{:S(2)}) collective-permute-start(f32[67,16,128]{2,1,0:T(8,128)S(1)} %get-tuple-element.88), channel_id=1, source_target_pairs={{1,0},{2,1},{3,2},{4,3},{5,4},{6,5},{7,6},{8,7},{9,8},{10,9},{11,1... | collective-permute-start | bytes 1646600 | tf_op jit(solution)/shard_map/ppermute | solution.py:65
  41.0 12.2 %all-to-all-start.2 = ((f32[8,72,32]{1,2,0:T(8,128)}), f32[8,72,32]{1,2,0:T(8,128)S(1)}, u32[]{:S(2)}, u32[]{:S(2)}) async-start(f32[8,72,32]{1,2,0:T(8,128)} %broadcast_in_dim.16), calls=%async_computation.2 | async-start | bytes 262144 | tf_op jit(solution)/shard_map/all_to_all | solution.py:43
  54.9 17.5 %all-to-all-start.3 = ((f32[16,80,128]{2,1,0:T(8,128)}), f32[16,80,128]{2,1,0:T(8,128)S(1)}, u32[]{:S(2)}, u32[]{:S(2)}) async-start(f32[16,80,128]{2,1,0:T(8,128)} %broadcast_in_dim.18), calls=%async_computation.3 | async-start | bytes 1310720 | tf_op jit(solution)/shard_map/all_to_all | solution.py:43
  76.2 48.7 %all-to-all-start.4 = ((f32[16,64,512]{2,1,0:T(8,128)}), f32[16,64,512]{2,1,0:T(8,128)S(1)}, u32[]{:S(2)}, u32[]{:S(2)}) async-start(f32[16,64,512]{2,1,0:T(8,128)} %get-tuple-element.105), calls=%async_computation.4 | async-start | bytes 4194304 | tf_op jit(solution)/shard_map/all_to_all | solution.py:557
  103.8 19.0 %collective-permute-start.3 = (f32[4,64,512]{2,1,0:T(8,128)}, f32[4,64,512]{2,1,0:T(8,128)S(1)}, u32[]{:S(2)}, u32[]{:S(2)}) collective-permute-start(f32[4,64,512]{2,1,0:T(8,128)} %get-tuple-element.103), channel_id=1, source_target_pairs={{1,0},{2,1},{3,2},{4,3},{5,4},{6,5},{7,6},{8,7},{9,8},{10,9},{11,1... | collective-permute-start | bytes 1572872 | tf_op jit(solution)/shard_map/ppermute | solution.py:65
  109.1 15.8 %collective-permute-start.2 = (f32[4,64,512]{2,1,0:T(8,128)}, f32[4,64,512]{2,1,0:T(8,128)S(1)}, u32[]{:S(2)}, u32[]{:S(2)}) collective-permute-start(f32[4,64,512]{2,1,0:T(8,128)} %get-tuple-element.102), channel_id=1, source_target_pairs={{0,1},{1,2},{2,3},{3,4},{4,5},{5,6},{6,7},{7,8},{8,9},{9,10},{10,1... | collective-permute-start | bytes 1572872 | tf_op jit(solution)/shard_map/ppermute | solution.py:65
  126.4 41.1 %all-to-all-start.5 = ((f32[16,64,512]{2,1,0:T(8,128)}), f32[16,64,512]{2,1,0:T(8,128)}, u32[]{:S(2)}, u32[]{:S(2)}) async-start(f32[16,64,512]{2,1,0:T(8,128)} %gate.2), calls=%async_computation.5 | async-start | bytes 4194304 | tf_op jit(solution)/shard_map/all_to_all | solution.py:557
  145.1 9.6 %collective-permute-start.10 = (f32[8,128]{1,0:T(8,128)S(1)}, f32[8,128]{1,0:T(8,128)S(1)}, u32[]{:S(2)}, u32[]{:S(2)}) collective-permute-start(f32[8,128]{1,0:T(8,128)S(1)} %add.111), channel_id=1, source_target_pairs={{0,112},{16,0},{32,16},{48,32},{64,48},{80,64},{96,80},{112,96},{1... | collective-permute-start | bytes 12296 | tf_op jit(solution)/shard_map/ppermute | solution.py:55
  150.2 5.6 %collective-permute-start.4 = (f32[8,128]{1,0:T(8,128)S(1)}, f32[8,128]{1,0:T(8,128)S(1)}, u32[]{:S(2)}, u32[]{:S(2)}) collective-permute-start(f32[8,128]{1,0:T(8,128)S(1)} %add.111), channel_id=1, source_target_pairs={{0,16},{16,32},{32,48},{48,64},{64,80},{80,96},{96,112},{112,0},{1... | collective-permute-start | bytes 12296 | tf_op jit(solution)/shard_map/ppermute | solution.py:55
  150.2 7.3 %collective-permute-start.5 = (f32[8,128]{1,0:T(8,128)S(1)}, f32[8,128]{1,0:T(8,128)S(1)}, u32[]{:S(2)}, u32[]{:S(2)}) collective-permute-start(f32[8,128]{1,0:T(8,128)S(1)} %add.111), channel_id=1, source_target_pairs={{0,32},{16,48},{32,64},{48,80},{64,96},{80,112},{96,0},{112,16},{1... | collective-permute-start | bytes 12296 | tf_op jit(solution)/shard_map/ppermute | solution.py:55
  150.6 6.9 %collective-permute-start.6 = (f32[8,128]{1,0:T(8,128)S(1)}, f32[8,128]{1,0:T(8,128)S(1)}, u32[]{:S(2)}, u32[]{:S(2)}) collective-permute-start(f32[8,128]{1,0:T(8,128)S(1)} %add.111), channel_id=1, source_target_pairs={{0,48},{16,64},{32,80},{48,96},{64,112},{80,0},{96,16},{112,32},{1... | collective-permute-start | bytes 12296 | tf_op jit(solution)/shard_map/ppermute | solution.py:55
  151.8 5.7 %collective-permute-start.7 = (f32[8,128]{1,0:T(8,128)S(1)}, f32[8,128]{1,0:T(8,128)S(1)}, u32[]{:S(2)}, u32[]{:S(2)}) collective-permute-start(f32[8,128]{1,0:T(8,128)S(1)} %add.111), channel_id=1, source_target_pairs={{0,64},{16,80},{32,96},{48,112},{64,0},{80,16},{96,32},{112,48},{1... | collective-permute-start | bytes 12296 | tf_op jit(solution)/shard_map/ppermute | solution.py:55
  154.6 3.0 %collective-permute-start.8 = (f32[8,128]{1,0:T(8,128)S(1)}, f32[8,128]{1,0:T(8,128)S(1)}, u32[]{:S(2)}, u32[]{:S(2)}) collective-permute-start(f32[8,128]{1,0:T(8,128)S(1)} %add.111), channel_id=1, source_target_pairs={{0,80},{16,96},{32,112},{48,0},{64,16},{80,32},{96,48},{112,64},{1... | collective-permute-start | bytes 12296 | tf_op jit(solution)/shard_map/ppermute | solution.py:55
  155.8 3.6 %collective-permute-start.9 = (f32[8,128]{1,0:T(8,128)S(1)}, f32[8,128]{1,0:T(8,128)S(1)}, u32[]{:S(2)}, u32[]{:S(2)}) collective-permute-start(f32[8,128]{1,0:T(8,128)S(1)} %add.111), channel_id=1, source_target_pairs={{0,96},{16,112},{32,0},{48,16},{64,32},{80,48},{96,64},{112,80},{1... | collective-permute-start | bytes 12296 | tf_op jit(solution)/shard_map/ppermute | solution.py:55
  159.4 5.9 %collective-permute-start.11 = (f32[8,128]{1,0:T(8,128)S(1)}, f32[8,128]{1,0:T(8,128)S(1)}, u32[]{:S(2)}, u32[]{:S(2)}) collective-permute-start(f32[8,128]{1,0:T(8,128)S(1)} %add_add_fusion.2), channel_id=1, source_target_pairs={{0,1},{1,2},{2,3},{3,0},{4,5},{5,6},{6,7},{7,4},{8,9},{9,10},{10,1... | collective-permute-start | bytes 12296 | tf_op jit(solution)/shard_map/ppermute | solution.py:55
  161.2 5.1 %collective-permute-start.12 = (f32[8,128]{1,0:T(8,128)S(1)}, f32[8,128]{1,0:T(8,128)S(1)}, u32[]{:S(2)}, u32[]{:S(2)}) collective-permute-start(f32[8,128]{1,0:T(8,128)S(1)} %add_add_fusion.2), channel_id=1, source_target_pairs={{0,2},{1,3},{2,0},{3,1},{4,6},{5,7},{6,4},{7,5},{8,10},{9,11},{10,... | collective-permute-start | bytes 12296 | tf_op jit(solution)/shard_map/ppermute | solution.py:55
  163.9 3.6 %collective-permute-start.13 = (f32[8,128]{1,0:T(8,128)S(1)}, f32[8,128]{1,0:T(8,128)S(1)}, u32[]{:S(2)}, u32[]{:S(2)}) collective-permute-start(f32[8,128]{1,0:T(8,128)S(1)} %add_add_fusion.2), channel_id=1, source_target_pairs={{0,3},{1,0},{2,1},{3,2},{4,7},{5,4},{6,5},{7,6},{8,11},{9,8},{10,9... | collective-permute-start | bytes 12296 | tf_op jit(solution)/shard_map/ppermute | solution.py:55
  168.2 35.5 %all-to-all-start.6 = ((f32[16,64,512]{2,1,0:T(8,128)}), f32[16,64,512]{2,1,0:T(8,128)S(1)}, u32[]{:S(2)}, u32[]{:S(2)}) async-start(f32[16,64,512]{2,1,0:T(8,128)} %gate.3), calls=%async_computation.6 | async-start | bytes 4194304 | tf_op jit(solution)/shard_map/all_to_all | solution.py:557
  175.3 18.0 %collective-permute-start.14 = (f32[8,128]{1,0:T(8,128)S(1)}, f32[8,128]{1,0:T(8,128)S(1)}, u32[]{:S(2)}, u32[]{:S(2)}) collective-permute-start(f32[8,128]{1,0:T(8,128)S(1)} %add_add_fusion.1.refs_2_), channel_id=1, source_target_pairs={{0,4},{4,8},{8,12},{12,0},{1,5},{5,9},{9,13},{13,1},{2,6},{6,10},{... | collective-permute-start | bytes 12296 | tf_op jit(solution)/shard_map/ppermute | solution.py:55
  177.3 20.0 %collective-permute-start.15 = (f32[8,128]{1,0:T(8,128)S(1)}, f32[8,128]{1,0:T(8,128)S(1)}, u32[]{:S(2)}, u32[]{:S(2)}) collective-permute-start(f32[8,128]{1,0:T(8,128)S(1)} %add_add_fusion.1.refs_2_), channel_id=1, source_target_pairs={{0,8},{4,12},{8,0},{12,4},{1,9},{5,13},{9,1},{13,5},{2,10},{6,14},... | collective-permute-start | bytes 12296 | tf_op jit(solution)/shard_map/ppermute | solution.py:55
  180.0 18.2 %collective-permute-start.16 = (f32[8,128]{1,0:T(8,128)S(1)}, f32[8,128]{1,0:T(8,128)S(1)}, u32[]{:S(2)}, u32[]{:S(2)}) collective-permute-start(f32[8,128]{1,0:T(8,128)S(1)} %add_add_fusion.1.refs_2_), channel_id=1, source_target_pairs={{0,12},{4,0},{8,4},{12,8},{1,13},{5,1},{9,5},{13,9},{2,14},{6,2},{... | collective-permute-start | bytes 12296 | tf_op jit(solution)/shard_map/ppermute | solution.py:55
  (8 other events, 30.9 us)

commit v7 on v6

--- a/solution.py
+++ b/solution.py
@@ -35,7 +35,7 @@
 OP_SLOTS = 12
 OP_FIRST = 4
 EXTRA = 8
-EARLY_TILES = 18
+EARLY_TILES = 23
 
 
 def sent_to_all(shard, axis):
@@ -271,7 +271,8 @@
     v_ref = refs.pop(0)
     beside_refs = [refs.pop(0), refs.pop(0)] if halo else []
     held_ref = refs.pop(0) if held else None
-    tiles_ref, out_ref = refs.pop(0), refs.pop(0)
+    tiles_ref = refs.pop(0)
+    out_ref = None if send and held else refs.pop(0)
     edge_refs = [refs.pop(0), refs.pop(0)] if send and not held else []
     slots_ref, dots_ref = (refs.pop(0), refs.pop(0)) if send else (None, None)
     values, both_ref, total, buf, sem, in_sem, out_sem = refs
@@ -350,7 +351,8 @@
         )
         for side, ref in enumerate(edge_refs)
     ]
-    leaving.append(pltpu.make_async_copy(total, out_ref, out_sem.at[BLOCKS_DEV]))
+    if out_ref is not None:
+        leaving.append(pltpu.make_async_copy(total, out_ref, out_sem.at[BLOCKS_DEV]))
     if send:
         leaving += out_copies(total, slots_ref, target_ref, out_sem)
     for out in leaving:
@@ -396,13 +398,14 @@
 def applied(scalars, targets, tiles, v, tiles_of=(0, None), beside=(), held=None, send=False):
     blocks, fields, _ = v.shape
     edges = send and held is None
+    whole = not send or edges
     out = pltpu.HBM(v.shape, jnp.float32)
     ins = [in_hbm(x) for x in (v, *beside, held) if x is not None] + [tiles]
     number = (tiles_of[1] or OWN_TILES) - tiles_of[0] + HALO_TILES * bool(beside)
     out = pl.pallas_call(
         functools.partial(op_kernel, *tiles_of, bool(beside), held is not None, send),
         in_specs=[SMEM_SPEC] * 2 + [HBM_SPEC] * len(ins),
-        out_specs=[HBM_SPEC] + [HBM_SPEC] * (2 * edges) + [HBM_SPEC, VMEM_SPEC] * send,
+        out_specs=[HBM_SPEC] * whole + [HBM_SPEC] * (2 * edges) + [HBM_SPEC, VMEM_SPEC] * send,
         scratch_shapes=[
             pltpu.VMEM((blocks + 2 * REACH, fields, BLOCK), jnp.float32),
             pltpu.VMEM((blocks + 2 * REACH, 2 * fields, BLOCK), jnp.bfloat16),
@@ -412,7 +415,7 @@
             pltpu.SemaphoreType.DMA((4,)),
             pltpu.SemaphoreType.DMA((BLOCKS_DEV + 3,)),
         ],
-        out_shape=[out]
+        out_shape=[out] * whole
         + [pltpu.HBM((REACH, fields, BLOCK), jnp.float32)] * (2 * edges)
         + [slot_shape(v), jax.ShapeDtypeStruct((EXTRA, COL_DEV), jnp.float32)] * send,
         compiler_params=pltpu.CompilerParams(vmem_limit_bytes=28 << 20),
@@ -433,13 +436,13 @@
 def gate(slots, *others):
     return pl.pallas_call(
         gate_kernel,
-        in_specs=[HBM_SPEC] + [VMEM_SPEC] * len(others),
+        in_specs=[HBM_SPEC] + [HBM_SPEC if other.ndim == 3 else VMEM_SPEC for other in others],
         out_specs=HBM_SPEC,
         out_shape=pltpu.HBM(slots.shape, jnp.float32),
         input_output_aliases={0: 0},
         compiler_params=pltpu.CompilerParams(vmem_limit_bytes=1 << 20),
         name="gate",
-    )(slots, *(other[0, :8, :COL_DEV] for other in others))
+    )(slots, *(in_hbm(other) if other.ndim == 3 else other for other in others))
 
 
 def residual_kernel(
@@ -657,13 +660,13 @@
     )
     before, after = swapped(initial, last)
     part = applied(scalars, my_targets, tiles, m1, (0, EARLY_TILES))
-    slots = gate(slots, part, before, after, owned_r0)
+    slots = gate(slots, part, before, after)
     owned_m1 = to_owners(slots)
-    m2, slots, last = applied(
+    slots, last = applied(
         scalars, my_targets, tiles, m1, (EARLY_TILES, None), (before, after), part, True
     )
-    dots = sum_direct(sum_direct(dots + last, WIDE), SIXTEEN[1])
-    slots = gate(slots, owned_m1, dots[None])
+    dots = sum_direct(sum_wide(dots + last), SIXTEEN[1])
+    slots = gate(slots, dots)
     owned_m2 = to_owners(slots)
     dots = sum_direct(dots, SIXTEEN[0])
     owned = owned_table(group_map, sixteen_size, BLOCKS_DEV)

time: 207 us -> 205 us (level); the launches traced: 206 us -> 201 us
  starting transfers between devices: 73.3 us -> 65.3 us
    ppermute x13 -> x10, starting transfers between devices: 24.4 us -> 17.4 us  [sum_direct(): lax.ppermute(part, axis, [(i, (i + k) % peers) for i in range(peers)])]
    ppermute x13 -> x10, waiting for transfers between devices: 20.8 us -> 24.6 us  [sum_direct(): lax.ppermute(part, axis, [(i, (i + k) % peers) for i in range(peers)])]
    ppermute x2, waiting for transfers between devices: 2.11 us -> 0.01 us  [swapped(): lax.ppermute(last, SIXTEEN, up)]
  transfers between devices with their start and end apart: 24 -> 21, of which waited for: 10 -> 12; matrix products, arithmetic and copies ran while one was open for 2% -> 2% of each run, Pallas kernels for 41% -> 43%
where the time goes in v7:
time: 205 us; the launch traced here: 201 us
  Pallas kernels  92.2 us (45%)
  starting transfers between devices  65.3 us (32%)
  waiting for transfers between devices  26.9 us (13%)
  local copies, waits for them, and re-layouts  8.67 us (4%)
  other arithmetic  6.55 us (3%)
    pallas_call x3, Pallas kernels, applied(): pl.pallas_call(functools.partial(op_kernel, *tiles_of, bool(beside), held...  48.5 us
    pallas_call x4, Pallas kernels, covariance_tiles(): pl.pallas_call(functools.partial(tiles_kernel, first, count, len(beside_j...  33 us
    ppermute x10, waiting for transfers between devices, sum_direct(): lax.ppermute(part, axis, [(i, (i + k) % peers) for i in range(peers)])  24.6 us
    all_to_all x4, starting transfers between devices, sent_to_all(): lax.all_to_all(jnp.broadcast_to(shard[None], (peers, *shard.shape)), axis...  21.1 us
    ppermute x10, starting transfers between devices, sum_direct(): lax.ppermute(part, axis, [(i, (i + k) % peers) for i in range(peers)])  17.4 us
    all_to_all x3, starting transfers between devices, to_owners(): return lax.all_to_all(slots, SIXTEEN, 0, 0, tiled=True)  16 us
    pallas_call x2, Pallas kernels, combined(): pl.pallas_call(kernel, grid_spec=pltpu.PrefetchScalarGridSpec(num_scalar_...  7.33 us
    ppermute x2, starting transfers between devices, swapped(): lax.ppermute(initial, SIXTEEN, down)  6.88 us
  transfers between devices with their start and end apart: 21, of which 12 were waited for; matrix products, arithmetic and copies ran while one was open for 2% of the time, Pallas kernels for 43%

profile of v7, /device:TPU:0, one launch (start us, length us, event | category | flops | bytes accessed | tf_op | source)
XLA Modules:
  0.0 200.6 jit_solution(2604808999631984009)
XLA Ops:
  4.8 4.6 %all-to-all-start = ((f32[8,72,32]{1,2,0:T(8,128)}), f32[8,72,32]{1,2,0:T(8,128)S(1)}, u32[]{:S(2)}, u32[]{:S(2)}) async-start(f32[8,72,32]{1,2,0:T(8,128)} %broadcast_in_dim.14), calls=%async_computation | async-start | bytes 262144 | tf_op jit(solution)/shard_map/all_to_all | solution.py:43
  11.1 4.8 %tiles.4.refs_0_ = bf16[44,1024,512]{2,1,0:T(8,128)(2,1)} custom-call(s32[9]{0:T(128)S(1)} %pad_add_fusion.scalar_ref, f32[2,32,128]{2,1,0:T(8,128)S(1)} %copy-done.1), custom_call_target="tpu_custom_call" | custom-call | flops 15728640 | bytes 5242880 | tf_op jit(solution)/shard_map/tiles/pallas_call | solution.py:228
  17.7 7.9 %all-to-all-start.1 = ((f32[16,72,128]{2,1,0:T(8,128)}), f32[16,72,128]{2,1,0:T(8,128)S(1)}, u32[]{:S(2)}, u32[]{:S(2)}) async-start(f32[16,72,128]{2,1,0:T(8,128)} %broadcast_in_dim.15), calls=%async_computation.1 | async-start | bytes 1179648 | tf_op jit(solution)/shard_map/all_to_all | solution.py:43
  28.4 3.4 %collective-permute-start.1 = (f32[67,16,128]{2,1,0:T(8,128)S(1)}, f32[67,16,128]{2,1,0:T(8,128)S(1)}, u32[]{:S(2)}, u32[]{:S(2)}) collective-permute-start(f32[67,16,128]{2,1,0:T(8,128)S(1)} %get-tuple-element.88), channel_id=1, source_target_pairs={{1,0},{2,1},{3,2},{4,3},{5,4},{6,5},{7,6},{8,7},{9,8},{10,9},{11,1... | collective-permute-start | bytes 1646600 | tf_op jit(solution)/shard_map/ppermute | solution.py:65
  31.9 7.4 %tiles.5.refs_0_ = bf16[44,1024,512]{2,1,0:T(8,128)(2,1)} custom-call(s32[9]{0:T(128)S(1)} %pad_add_fusion.scalar_ref, f32[2,32,128]{2,1,0:T(8,128)S(1)} %copy-done.2, bf16[44,1024,512]{2,1,0:T(8,128)(2,1)} %tiles.4.refs_0_), custom_call_target="tpu_custom_call", output_to_operand_aliasing={{}: (2, {})} | custom-call | flops 28311552 | bytes 9437184 | tf_op jit(solution)/shard_map/tiles/pallas_call | solution.py:228
  41.0 4.8 %all-to-all-start.2 = ((f32[8,72,32]{1,2,0:T(8,128)}), f32[8,72,32]{1,2,0:T(8,128)S(1)}, u32[]{:S(2)}, u32[]{:S(2)}) async-start(f32[8,72,32]{1,2,0:T(8,128)} %broadcast_in_dim.16), calls=%async_computation.2 | async-start | bytes 262144 | tf_op jit(solution)/shard_map/all_to_all | solution.py:43
  45.8 7.4 %tiles.6.refs_2_ = bf16[44,1024,512]{2,1,0:T(8,128)(2,1)} custom-call(s32[9]{0:T(128)S(1)} %pad_add_fusion.scalar_ref, f32[2,32,128]{2,1,0:T(8,128)S(1)} %copy-done.2, bf16[44,1024,512]{2,1,0:T(8,128)(2,1)} %tiles.5.refs_0_), custom_call_target="tpu_custom_call", output_to_operand_aliasing={{}: (2, {})} | custom-call | flops 28311552 | bytes 9437184 | tf_op jit(solution)/shard_map/tiles/pallas_call | solution.py:228
  54.9 3.9 %all-to-all-start.3 = ((f32[16,80,128]{2,1,0:T(8,128)}), f32[16,80,128]{2,1,0:T(8,128)S(1)}, u32[]{:S(2)}, u32[]{:S(2)}) async-start(f32[16,80,128]{2,1,0:T(8,128)} %broadcast_in_dim.18), calls=%async_computation.3 | async-start | bytes 1310720 | tf_op jit(solution)/shard_map/all_to_all | solution.py:43
  59.0 13.4 %tiles.7.refs_3_.refs_1_.refs_4_ = bf16[44,1024,512]{2,1,0:T(8,128)(2,1)} custom-call(s32[9]{0:T(128)S(1)} %pad_add_fusion.scalar_ref, f32[2,32,128]{2,1,0:T(8,128)S(1)} %copy-done.2, f32[2,16,128]{2,1,0:T(8,128)S(1)} %slice.93.refs_0_, f32[2,16,128]{2,1,0:T(8,128)S(1)} %slice.94.refs_1_, ...), custom_call_target="tpu_custom_call", output_to_operand_aliasing={{}: (4, {})} | custom-call | flops 66060288 | bytes 22020096 | tf_op jit(solution)/shard_map/tiles/pallas_call | solution.py:228
  72.8 3.3 %residual.1 = (f32[8,64,512]{2,1,0:T(8,128)}, f32[4,64,512]{2,1,0:T(8,128)}, f32[4,64,512]{2,1,0:T(8,128)}, f32[16,64,512]{2,1,0:T(8,128)}) custom-call(s32[8]{0:T(128)S(1)} %fusion.4.target_ref, f32[64,32,128]{2,1,0:T(8,128)S(1)} %copy-done, f32[32,128]{1,0:T(8,128)S(1)} %get-tuple-element.117.weight_ref, f32[64,32]{1,0:T(8,128)S(1)} %divide_add_fusion.1.row_ref, ...), custom_call_target="tpu_custom_call" | custom-call | tf_op jit(solution)/shard_map/residual/pallas_call | solution.py:492
  76.1 7.1 %all-to-all-start.4 = ((f32[16,64,512]{2,1,0:T(8,128)}), f32[16,64,512]{2,1,0:T(8,128)S(1)}, u32[]{:S(2)}, u32[]{:S(2)}) async-start(f32[16,64,512]{2,1,0:T(8,128)} %get-tuple-element.105), calls=%async_computation.4 | async-start | bytes 4194304 | tf_op jit(solution)/shard_map/all_to_all | solution.py:560
  83.3 21.8 %applied.3 = (f32[8,64,512]{2,1,0:T(8,128)}, f32[4,64,512]{2,1,0:T(8,128)}, f32[4,64,512]{2,1,0:T(8,128)}, f32[16,64,512]{2,1,0:T(8,128)}, f32[8,128]{1,0:T(8,128)S(1)}) custom-call(s32[9]{0:T(128)S(1)} %pad_add_fusion.scalar_ref, s32[8]{0:T(128)S(1)} %fusion.4.target_ref, f32[8,64,512]{2,1,0:T(8,128)} %get-tuple-element.96.refs_0_, ...), custom_call_target="tpu_custom_call" | custom-call | flops 6643777536 | bytes 46137344 | tf_op jit(solution)/shard_map/applied/pallas_call | solution.py:405
  107.1 3.5 %collective-permute-start.3 = (f32[4,64,512]{2,1,0:T(8,128)}, f32[4,64,512]{2,1,0:T(8,128)S(1)}, u32[]{:S(2)}, u32[]{:S(2)}) collective-permute-start(f32[4,64,512]{2,1,0:T(8,128)} %get-tuple-element.103), channel_id=1, source_target_pairs={{1,0},{2,1},{3,2},{4,3},{5,4},{6,5},{7,6},{8,7},{9,8},{10,9},{11,1... | collective-permute-start | bytes 1572872 | tf_op jit(solution)/shard_map/ppermute | solution.py:65
  110.5 16.1 %applied.4.refs_3_.refs_1_ = f32[8,64,512]{2,1,0:T(8,128)} custom-call(s32[9]{0:T(128)S(1)} %pad_add_fusion.scalar_ref, s32[8]{0:T(128)S(1)} %fusion.4.target_ref, f32[8,64,512]{2,1,0:T(8,128)} %get-tuple-element.101.refs_0_, bf16[44,1024,512]{2,1,0:T(8,128)(2,1)} %tiles.7.refs_3_.refs_1_.refs_4_), custom_call_target="tpu_custom_call" | custom-call | flops 3472883712 | bytes 24117248 | tf_op jit(solution)/shard_map/applied/pallas_call | solution.py:405
  128.9 4.6 %all-to-all-start.5 = ((f32[16,64,512]{2,1,0:T(8,128)}), f32[16,64,512]{2,1,0:T(8,128)}, u32[]{:S(2)}, u32[]{:S(2)}) async-start(f32[16,64,512]{2,1,0:T(8,128)} %gate.2), calls=%async_computation.5 | async-start | bytes 4194304 | tf_op jit(solution)/shard_map/all_to_all | solution.py:560
  133.5 10.6 %applied.5 = (f32[16,64,512]{2,1,0:T(8,128)}, f32[8,128]{1,0:T(8,128)S(1)}) custom-call(s32[9]{0:T(128)S(1)} %pad_add_fusion.scalar_ref, s32[8]{0:T(128)S(1)} %fusion.4.target_ref, f32[8,64,512]{2,1,0:T(8,128)} %get-tuple-element.101.refs_0_, f32[4,64,512]{2,1,0:T(8,128)} %copy-done.4, f32[4,64,512]{2,1,0:T(8,128)} %copy-done.5, ...), custom_call_target="tpu_custom_call" | custom-call | flops 3170893824 | bytes 22020096 | tf_op jit(solution)/shard_map/applied/pallas_call | solution.py:405
  153.1 2.8 %collective-permute-start.10 = (f32[8,128]{1,0:T(8,128)S(1)}, f32[8,128]{1,0:T(8,128)S(1)}, u32[]{:S(2)}, u32[]{:S(2)}) collective-permute-start(f32[8,128]{1,0:T(8,128)S(1)} %add_add_fusion.2), channel_id=1, source_target_pairs={{0,3},{1,0},{2,1},{3,2},{4,7},{5,4},{6,5},{7,6},{8,11},{9,8},{10,9... | collective-permute-start | bytes 12296 | tf_op jit(solution)/shard_map/ppermute | solution.py:55
  155.9 2.3 %collective-permute-start.9 = (f32[8,128]{1,0:T(8,128)S(1)}, f32[8,128]{1,0:T(8,128)S(1)}, u32[]{:S(2)}, u32[]{:S(2)}) collective-permute-start(f32[8,128]{1,0:T(8,128)S(1)} %add_add_fusion.2), channel_id=1, source_target_pairs={{0,2},{1,3},{2,0},{3,1},{4,6},{5,7},{6,4},{7,5},{8,10},{9,11},{10,... | collective-permute-start | bytes 12296 | tf_op jit(solution)/shard_map/ppermute | solution.py:55
  163.8 4.3 %all-to-all-start.6 = ((f32[16,64,512]{2,1,0:T(8,128)}), f32[16,64,512]{2,1,0:T(8,128)S(1)}, u32[]{:S(2)}, u32[]{:S(2)}) async-start(f32[16,64,512]{2,1,0:T(8,128)} %gate.3), calls=%async_computation.6 | async-start | bytes 4194304 | tf_op jit(solution)/shard_map/all_to_all | solution.py:560
  170.8 2.7 %collective-permute-start.12 = (f32[8,128]{1,0:T(8,128)S(1)}, f32[8,128]{1,0:T(8,128)S(1)}, u32[]{:S(2)}, u32[]{:S(2)}) collective-permute-start(f32[8,128]{1,0:T(8,128)S(1)} %add_add_fusion.1.refs_1_), channel_id=1, source_target_pairs={{0,8},{4,12},{8,0},{12,4},{1,9},{5,13},{9,1},{13,5},{2,10},{6,14},... | collective-permute-start | bytes 12296 | tf_op jit(solution)/shard_map/ppermute | solution.py:55
  174.9 12.2 %collective-permute-done.11 = f32[8,128]{1,0:T(8,128)S(1)} collective-permute-done((f32[8,128]{1,0:T(8,128)S(1)}, f32[8,128]{1,0:T(8,128)S(1)}, u32[]{:S(2)}, u32[]{:S(2)}) %collective-permute-start.11) | collective-permute-done | bytes 4128 | tf_op jit(solution)/shard_map/ppermute | solution.py:55
  187.2 3.7 %collective-permute-done.12 = f32[8,128]{1,0:T(8,128)S(1)} collective-permute-done((f32[8,128]{1,0:T(8,128)S(1)}, f32[8,128]{1,0:T(8,128)S(1)}, u32[]{:S(2)}, u32[]{:S(2)}) %collective-permute-start.12) | collective-permute-done | bytes 4128 | tf_op jit(solution)/shard_map/ppermute | solution.py:55
  192.2 4.6 %first.1 = (f32[64,8,512]{2,1,0:T(8,128)}, f32[64,8,512]{2,1,0:T(8,128)S(1)}) custom-call(s32[8]{0:T(128)S(1)} %and_select_fusion.src_ref, f32[8,128]{1,0:T(8,128)S(1)} %add_add_fusion.dots_ref, f32[16,64,512]{2,1,0:T(8,128)} %copy-done.3, f32[16,64,512]{2,1,0:T(8,128)} %all-to-all-done.5.refs_1_.refs_3_.refs_5_.refs_7_.refs_9_.refs_11_.refs_13_.refs_15_, ...), custom_call_target="tpu_custom_call" | custom-call | tf_op jit(solution)/shard_map/first/pallas_call | solution.py:544
  198.0 2.7 %second.1 = f32[64,8,512]{2,1,0:T(8,128)} custom-call(s32[8]{0:T(128)S(1)} %and_select_fusion.src_ref, f32[8,128]{1,0:T(8,128)S(1)} %add_add_fusion.dots_ref, f32[64,8,512]{2,1,0:T(8,128)S(1)} %get-tuple-element.108.part_ref, f32[16,64,512]{2,1,0:T(8,128)S(1)} %all-to-all-done.6.refs_0_.refs_1_.refs_2_.refs_3_.refs_4_.refs_5_.refs_6_.refs_7_, ...), custom_call_target="tpu_custom_call" | custom-call | tf_op jit(solution)/shard_map/second/pallas_call | solution.py:544
  (98 shorter events, 39.7 us)
Async XLA Ops:
  4.8 11.1 %all-to-all-start = ((f32[8,72,32]{1,2,0:T(8,128)}), f32[8,72,32]{1,2,0:T(8,128)S(1)}, u32[]{:S(2)}, u32[]{:S(2)}) async-start(f32[8,72,32]{1,2,0:T(8,128)} %broadcast_in_dim.14), calls=%async_computation | async-start | bytes 262144 | tf_op jit(solution)/shard_map/all_to_all | solution.py:43
  11.1 5.2 %copy-start = (f32[64,32,128]{2,1,0:T(8,128)S(1)}, f32[64,32,128]{2,1,0:T(8,128)}, u32[]{:S(2)}) copy-start(f32[64,32,128]{2,1,0:T(8,128)} %obs_ref.1) | copy-start | bytes 3145732
  15.9 9.7 %copy-start.2 = (f32[2,32,128]{2,1,0:T(8,128)S(1)}, f32[2,32,128]{2,1,0:T(8,128)}, u32[]{:S(2)}) copy-start(f32[2,32,128]{2,1,0:T(8,128)} %jitter_ref.3) | copy-start | bytes 98308
  17.7 21.6 %all-to-all-start.1 = ((f32[16,72,128]{2,1,0:T(8,128)}), f32[16,72,128]{2,1,0:T(8,128)S(1)}, u32[]{:S(2)}, u32[]{:S(2)}) async-start(f32[16,72,128]{2,1,0:T(8,128)} %broadcast_in_dim.15), calls=%async_computation.1 | async-start | bytes 1179648 | tf_op jit(solution)/shard_map/all_to_all | solution.py:43
  26.5 26.7 %collective-permute-start = (f32[67,16,128]{2,1,0:T(8,128)}, f32[67,16,128]{2,1,0:T(8,128)S(1)}, u32[]{:S(2)}, u32[]{:S(2)}) collective-permute-start(f32[67,16,128]{2,1,0:T(8,128)} %get-tuple-element.87), channel_id=1, source_target_pairs={{0,1},{1,2},{2,3},{3,4},{4,5},{5,6},{6,7},{7,8},{8,9},{9,10},{10,1... | collective-permute-start | bytes 1646600 | tf_op jit(solution)/shard_map/ppermute | solution.py:65
  28.4 24.8 %collective-permute-start.1 = (f32[67,16,128]{2,1,0:T(8,128)S(1)}, f32[67,16,128]{2,1,0:T(8,128)S(1)}, u32[]{:S(2)}, u32[]{:S(2)}) collective-permute-start(f32[67,16,128]{2,1,0:T(8,128)S(1)} %get-tuple-element.88), channel_id=1, source_target_pairs={{1,0},{2,1},{3,2},{4,3},{5,4},{6,5},{7,6},{8,7},{9,8},{10,9},{11,1... | collective-permute-start | bytes 1646600 | tf_op jit(solution)/shard_map/ppermute | solution.py:65
  41.0 12.2 %all-to-all-start.2 = ((f32[8,72,32]{1,2,0:T(8,128)}), f32[8,72,32]{1,2,0:T(8,128)S(1)}, u32[]{:S(2)}, u32[]{:S(2)}) async-start(f32[8,72,32]{1,2,0:T(8,128)} %broadcast_in_dim.16), calls=%async_computation.2 | async-start | bytes 262144 | tf_op jit(solution)/shard_map/all_to_all | solution.py:43
  53.2 5.7 %copy-start.7 = (s32[1,128]{1,0:T(1,128)S(1)}, s32[1,128]{1,0:T(1,128)}, u32[]{:S(2)}) copy-start(s32[1,128]{1,0:T(1,128)} %param.16) | copy-start | bytes 1540
  54.9 17.5 %all-to-all-start.3 = ((f32[16,80,128]{2,1,0:T(8,128)}), f32[16,80,128]{2,1,0:T(8,128)S(1)}, u32[]{:S(2)}, u32[]{:S(2)}) async-start(f32[16,80,128]{2,1,0:T(8,128)} %broadcast_in_dim.18), calls=%async_computation.3 | async-start | bytes 1310720 | tf_op jit(solution)/shard_map/all_to_all | solution.py:43
  76.1 51.4 %all-to-all-start.4 = ((f32[16,64,512]{2,1,0:T(8,128)}), f32[16,64,512]{2,1,0:T(8,128)S(1)}, u32[]{:S(2)}, u32[]{:S(2)}) async-start(f32[16,64,512]{2,1,0:T(8,128)} %get-tuple-element.105), calls=%async_computation.4 | async-start | bytes 4194304 | tf_op jit(solution)/shard_map/all_to_all | solution.py:560
  105.1 21.5 %collective-permute-start.2 = (f32[4,64,512]{2,1,0:T(8,128)}, f32[4,64,512]{2,1,0:T(8,128)S(1)}, u32[]{:S(2)}, u32[]{:S(2)}) collective-permute-start(f32[4,64,512]{2,1,0:T(8,128)} %get-tuple-element.102), channel_id=1, source_target_pairs={{0,1},{1,2},{2,3},{3,4},{4,5},{5,6},{6,7},{7,8},{8,9},{9,10},{10,1... | collective-permute-start | bytes 1572872 | tf_op jit(solution)/shard_map/ppermute | solution.py:65
  107.1 19.6 %collective-permute-start.3 = (f32[4,64,512]{2,1,0:T(8,128)}, f32[4,64,512]{2,1,0:T(8,128)S(1)}, u32[]{:S(2)}, u32[]{:S(2)}) collective-permute-start(f32[4,64,512]{2,1,0:T(8,128)} %get-tuple-element.103), channel_id=1, source_target_pairs={{1,0},{2,1},{3,2},{4,3},{5,4},{6,5},{7,6},{8,7},{9,8},{10,9},{11,1... | collective-permute-start | bytes 1572872 | tf_op jit(solution)/shard_map/ppermute | solution.py:65
  128.9 34.9 %all-to-all-start.5 = ((f32[16,64,512]{2,1,0:T(8,128)}), f32[16,64,512]{2,1,0:T(8,128)}, u32[]{:S(2)}, u32[]{:S(2)}) async-start(f32[16,64,512]{2,1,0:T(8,128)} %gate.2), calls=%async_computation.5 | async-start | bytes 4194304 | tf_op jit(solution)/shard_map/all_to_all | solution.py:560
  144.1 1.2 collective-permute-start.4
  145.4 6.0 %collective-permute-start.5 = (f32[8,128]{1,0:T(8,128)S(1)}, f32[8,128]{1,0:T(8,128)S(1)}, u32[]{:S(2)}, u32[]{:S(2)}) collective-permute-start(f32[8,128]{1,0:T(8,128)S(1)} %add.103), channel_id=1, source_target_pairs={{0,32},{32,64},{64,96},{96,0},{1,33},{33,65},{65,97},{97,1},{2,34}... | collective-permute-start | bytes 12296 | tf_op jit(solution)/shard_map/ppermute | solution.py:55
  147.3 5.1 %collective-permute-start.6 = (f32[8,128]{1,0:T(8,128)S(1)}, f32[8,128]{1,0:T(8,128)S(1)}, u32[]{:S(2)}, u32[]{:S(2)}) collective-permute-start(f32[8,128]{1,0:T(8,128)S(1)} %add.103), channel_id=1, source_target_pairs={{0,64},{32,96},{64,0},{96,32},{1,65},{33,97},{65,1},{97,33},{2,66}... | collective-permute-start | bytes 12296 | tf_op jit(solution)/shard_map/ppermute | solution.py:55
  149.5 3.6 %collective-permute-start.7 = (f32[8,128]{1,0:T(8,128)S(1)}, f32[8,128]{1,0:T(8,128)S(1)}, u32[]{:S(2)}, u32[]{:S(2)}) collective-permute-start(f32[8,128]{1,0:T(8,128)S(1)} %add.103), channel_id=1, source_target_pairs={{0,96},{32,0},{64,32},{96,64},{1,97},{33,1},{65,33},{97,65},{2,98}... | collective-permute-start | bytes 12296 | tf_op jit(solution)/shard_map/ppermute | solution.py:55
  153.1 6.7 %collective-permute-start.10 = (f32[8,128]{1,0:T(8,128)S(1)}, f32[8,128]{1,0:T(8,128)S(1)}, u32[]{:S(2)}, u32[]{:S(2)}) collective-permute-start(f32[8,128]{1,0:T(8,128)S(1)} %add_add_fusion.2), channel_id=1, source_target_pairs={{0,3},{1,0},{2,1},{3,2},{4,7},{5,4},{6,5},{7,6},{8,11},{9,8},{10,9... | collective-permute-start | bytes 12296 | tf_op jit(solution)/shard_map/ppermute | solution.py:55
  155.9 4.8 %collective-permute-start.8 = (f32[8,128]{1,0:T(8,128)S(1)}, f32[8,128]{1,0:T(8,128)S(1)}, u32[]{:S(2)}, u32[]{:S(2)}) collective-permute-start(f32[8,128]{1,0:T(8,128)S(1)} %add_add_fusion.2), channel_id=1, source_target_pairs={{0,1},{1,2},{2,3},{3,0},{4,5},{5,6},{6,7},{7,4},{8,9},{9,10},{10,1... | collective-permute-start | bytes 12296 | tf_op jit(solution)/shard_map/ppermute | solution.py:55
  155.9 6.8 %collective-permute-start.9 = (f32[8,128]{1,0:T(8,128)S(1)}, f32[8,128]{1,0:T(8,128)S(1)}, u32[]{:S(2)}, u32[]{:S(2)}) collective-permute-start(f32[8,128]{1,0:T(8,128)S(1)} %add_add_fusion.2), channel_id=1, source_target_pairs={{0,2},{1,3},{2,0},{3,1},{4,6},{5,7},{6,4},{7,5},{8,10},{9,11},{10,... | collective-permute-start | bytes 12296 | tf_op jit(solution)/shard_map/ppermute | solution.py:55
  163.8 34.1 %all-to-all-start.6 = ((f32[16,64,512]{2,1,0:T(8,128)}), f32[16,64,512]{2,1,0:T(8,128)S(1)}, u32[]{:S(2)}, u32[]{:S(2)}) async-start(f32[16,64,512]{2,1,0:T(8,128)} %gate.3), calls=%async_computation.6 | async-start | bytes 4194304 | tf_op jit(solution)/shard_map/all_to_all | solution.py:560
  168.8 18.4 %collective-permute-start.11 = (f32[8,128]{1,0:T(8,128)S(1)}, f32[8,128]{1,0:T(8,128)S(1)}, u32[]{:S(2)}, u32[]{:S(2)}) collective-permute-start(f32[8,128]{1,0:T(8,128)S(1)} %add_add_fusion.1.refs_1_), channel_id=1, source_target_pairs={{0,4},{4,8},{8,12},{12,0},{1,5},{5,9},{9,13},{13,1},{2,6},{6,10},{... | collective-permute-start | bytes 12296 | tf_op jit(solution)/shard_map/ppermute | solution.py:55
  170.8 20.1 %collective-permute-start.12 = (f32[8,128]{1,0:T(8,128)S(1)}, f32[8,128]{1,0:T(8,128)S(1)}, u32[]{:S(2)}, u32[]{:S(2)}) collective-permute-start(f32[8,128]{1,0:T(8,128)S(1)} %add_add_fusion.1.refs_1_), channel_id=1, source_target_pairs={{0,8},{4,12},{8,0},{12,4},{1,9},{5,13},{9,1},{13,5},{2,10},{6,14},... | collective-permute-start | bytes 12296 | tf_op jit(solution)/shard_map/ppermute | solution.py:55
  173.5 18.8 %collective-permute-start.13 = (f32[8,128]{1,0:T(8,128)S(1)}, f32[8,128]{1,0:T(8,128)S(1)}, u32[]{:S(2)}, u32[]{:S(2)}) collective-permute-start(f32[8,128]{1,0:T(8,128)S(1)} %add_add_fusion.1.refs_1_), channel_id=1, source_target_pairs={{0,12},{4,0},{8,4},{12,8},{1,13},{5,1},{9,5},{13,9},{2,14},{6,2},{... | collective-permute-start | bytes 12296 | tf_op jit(solution)/shard_map/ppermute | solution.py:55
  (5 other events, 9.0 us)

commit v8 on v7

--- a/solution.py
+++ b/solution.py
@@ -30,12 +30,12 @@
 
 OWN_TILES = BLOCKS_DEV + PAIRED * BLOCKS_DEV - 6
 HALO_TILES = 2 * (2 + 3 + 4)
-CHUNKS = (5, 9, 9, 21)
+CHUNKS = (3, 9, 9, 23)
 TILE_SLOTS = 4
 OP_SLOTS = 12
 OP_FIRST = 4
 EXTRA = 8
-EARLY_TILES = 23
+EARLY_TILES = 21
 
 
 def sent_to_all(shard, axis):
@@ -266,13 +266,13 @@
     return main[:fields] + (main[fields:] + rest)
 
 
-def op_kernel(first, last, halo, held, send, scalar_ref, target_ref, *refs):
+def op_kernel(first, last, pieces, halo, held, send, scalar_ref, target_ref, *refs):
     refs = list(refs)
-    v_ref = refs.pop(0)
+    v_refs = [refs.pop(0) for _ in range(pieces)]
     beside_refs = [refs.pop(0), refs.pop(0)] if halo else []
     held_ref = refs.pop(0) if held else None
     tiles_ref = refs.pop(0)
-    out_ref = None if send and held else refs.pop(0)
+    out_ref = None if send else refs.pop(0)
     edge_refs = [refs.pop(0), refs.pop(0)] if send and not held else []
     slots_ref, dots_ref = (refs.pop(0), refs.pop(0)) if send else (None, None)
     values, both_ref, total, buf, sem, in_sem, out_sem = refs
@@ -286,7 +286,8 @@
         at = jnp.where(t < mine, t + first, t - mine + OWN_TILES)
         return pltpu.make_async_copy(tiles_ref.at[at], buf.at[slot], sem.at[slot])
 
-    loads = [(v_ref, 0, BLOCKS_DEV)]
+    size = BLOCKS_DEV // pieces
+    loads = [(ref, size * i, size) for i, ref in enumerate(v_refs)]
     for side, ref in enumerate(beside_refs):
         loads.append((ref, BLOCKS_DEV + REACH * side, REACH))
     arriving = [
@@ -294,7 +295,7 @@
         for i, (ref, at, size) in enumerate(loads)
     ]
     if held_ref is not None:
-        arriving.append(pltpu.make_async_copy(held_ref, total, in_sem.at[3]))
+        arriving.append(pltpu.make_async_copy(held_ref, total, in_sem.at[4]))
     for load in arriving:
         load.start()
     for t in range(OP_FIRST):
@@ -396,28 +397,29 @@
 
 
 def applied(scalars, targets, tiles, v, tiles_of=(0, None), beside=(), held=None, send=False):
-    blocks, fields, _ = v.shape
+    _, fields, _ = v[0].shape
+    blocks = BLOCKS_DEV
+    shape = (blocks, fields, BLOCK)
     edges = send and held is None
-    whole = not send or edges
-    out = pltpu.HBM(v.shape, jnp.float32)
-    ins = [in_hbm(x) for x in (v, *beside, held) if x is not None] + [tiles]
+    out = pltpu.HBM(shape, jnp.float32)
+    ins = [in_hbm(x) for x in (*v, *beside, held) if x is not None] + [tiles]
     number = (tiles_of[1] or OWN_TILES) - tiles_of[0] + HALO_TILES * bool(beside)
     out = pl.pallas_call(
-        functools.partial(op_kernel, *tiles_of, bool(beside), held is not None, send),
+        functools.partial(op_kernel, *tiles_of, len(v), bool(beside), held is not None, send),
         in_specs=[SMEM_SPEC] * 2 + [HBM_SPEC] * len(ins),
-        out_specs=[HBM_SPEC] * whole + [HBM_SPEC] * (2 * edges) + [HBM_SPEC, VMEM_SPEC] * send,
+        out_specs=[HBM_SPEC] * (not send) + [HBM_SPEC] * (2 * edges) + [HBM_SPEC, VMEM_SPEC] * send,
         scratch_shapes=[
             pltpu.VMEM((blocks + 2 * REACH, fields, BLOCK), jnp.float32),
             pltpu.VMEM((blocks + 2 * REACH, 2 * fields, BLOCK), jnp.bfloat16),
-            pltpu.VMEM(v.shape, jnp.float32),
+            pltpu.VMEM(shape, jnp.float32),
             pltpu.VMEM((OP_SLOTS, 2 * BLOCK, BLOCK), jnp.bfloat16),
             pltpu.SemaphoreType.DMA((OP_SLOTS,)),
-            pltpu.SemaphoreType.DMA((4,)),
+            pltpu.SemaphoreType.DMA((5,)),
             pltpu.SemaphoreType.DMA((BLOCKS_DEV + 3,)),
         ],
-        out_shape=[out] * whole
+        out_shape=[out] * (not send)
         + [pltpu.HBM((REACH, fields, BLOCK), jnp.float32)] * (2 * edges)
-        + [slot_shape(v), jax.ShapeDtypeStruct((EXTRA, COL_DEV), jnp.float32)] * send,
+        + [slot_shape(out), jax.ShapeDtypeStruct((EXTRA, COL_DEV), jnp.float32)] * send,
         compiler_params=pltpu.CompilerParams(vmem_limit_bytes=28 << 20),
         cost_estimate=pl.CostEstimate(
             flops=3 * number * 3 * fields * BLOCK * BLOCK,
@@ -655,10 +657,10 @@
         my_targets, observations, weight, row_effect, before, row_before, after, row_after, col_effect
     )
     owned_r0 = to_owners(slots)
-    m1, initial, last, slots, dots = applied(
-        scalars, my_targets, tiles, r0, beside=(r0_before, r0_after), send=True
-    )
-    before, after = swapped(initial, last)
+    *m1, slots, dots = applied(
+        scalars, my_targets, tiles, (r0,), beside=(r0_before, r0_after), send=True
+    )
+    before, after = swapped(*m1)
     part = applied(scalars, my_targets, tiles, m1, (0, EARLY_TILES))
     slots = gate(slots, part, before, after)
     owned_m1 = to_owners(slots)

time: 205 us -> 213 us (1.039)
  the two profiles are of different devices: /device:TPU:0 before, /device:TPU:14 now
where the time goes in v8:
time: 213 us; the launch traced here: 209 us
  Pallas kernels  89.4 us (42%)
  starting transfers between devices  71.8 us (34%)
  waiting for transfers between devices  31.7 us (15%)
  local copies, waits for them, and re-layouts  8.69 us (4%)
  other arithmetic  6.55 us (3%)
    pallas_call x3, Pallas kernels, applied(): pl.pallas_call(functools.partial(op_kernel, *tiles_of, len(v), bool(besid...  47.1 us
    all_to_all x4, starting transfers between devices, sent_to_all(): lax.all_to_all(jnp.broadcast_to(shard[None], (peers, *shard.shape)), axis...  33.1 us
    pallas_call x4, Pallas kernels, covariance_tiles(): pl.pallas_call(functools.partial(tiles_kernel, first, count, len(beside_j...  31.7 us
    ppermute x10, waiting for transfers between devices, sum_direct(): lax.ppermute(part, axis, [(i, (i + k) % peers) for i in range(peers)])  28.3 us
    all_to_all x3, starting transfers between devices, to_owners(): return lax.all_to_all(slots, SIXTEEN, 0, 0, tiled=True)  20.9 us
    ppermute x10, starting transfers between devices, sum_direct(): lax.ppermute(part, axis, [(i, (i + k) % peers) for i in range(peers)])  13.7 us
    pallas_call x2, Pallas kernels, combined(): pl.pallas_call(kernel, grid_spec=pltpu.PrefetchScalarGridSpec(num_scalar_...  7.36 us
  transfers between devices with their start and end apart: 21, of which 8 were waited for; matrix products, arithmetic and copies ran while one was open for 2% of the time, Pallas kernels for 40%

profile of v8, /device:TPU:14, one launch (start us, length us, event | category | flops | bytes accessed | tf_op | source)
XLA Modules:
  0.0 209.2 jit_solution(846078016863384017)
XLA Ops:
  4.8 4.9 %all-to-all-start = ((f32[8,72,32]{1,2,0:T(8,128)}), f32[8,72,32]{1,2,0:T(8,128)S(1)}, u32[]{:S(2)}, u32[]{:S(2)}) async-start(f32[8,72,32]{1,2,0:T(8,128)} %broadcast_in_dim.14), calls=%async_computation | async-start | bytes 262144 | tf_op jit(solution)/shard_map/all_to_all | solution.py:43
  11.4 3.5 %tiles.4.refs_0_ = bf16[44,1024,512]{2,1,0:T(8,128)(2,1)} custom-call(s32[9]{0:T(128)S(1)} %pad_add_fusion.scalar_ref, f32[2,32,128]{2,1,0:T(8,128)S(1)} %copy-done.1), custom_call_target="tpu_custom_call" | custom-call | flops 9437184 | bytes 3145728 | tf_op jit(solution)/shard_map/tiles/pallas_call | solution.py:228
  16.7 8.3 %all-to-all-start.1 = ((f32[16,72,128]{2,1,0:T(8,128)}), f32[16,72,128]{2,1,0:T(8,128)S(1)}, u32[]{:S(2)}, u32[]{:S(2)}) async-start(f32[16,72,128]{2,1,0:T(8,128)} %broadcast_in_dim.15), calls=%async_computation.1 | async-start | bytes 1179648 | tf_op jit(solution)/shard_map/all_to_all | solution.py:43
  28.0 7.4 %tiles.5.refs_0_ = bf16[44,1024,512]{2,1,0:T(8,128)(2,1)} custom-call(s32[9]{0:T(128)S(1)} %pad_add_fusion.scalar_ref, f32[2,32,128]{2,1,0:T(8,128)S(1)} %copy-done.2, bf16[44,1024,512]{2,1,0:T(8,128)(2,1)} %tiles.4.refs_0_), custom_call_target="tpu_custom_call", output_to_operand_aliasing={{}: (2, {})} | custom-call | flops 28311552 | bytes 9437184 | tf_op jit(solution)/shard_map/tiles/pallas_call | solution.py:228
  37.1 4.8 %all-to-all-start.2 = ((f32[8,72,32]{1,2,0:T(8,128)}), f32[8,72,32]{1,2,0:T(8,128)S(1)}, u32[]{:S(2)}, u32[]{:S(2)}) async-start(f32[8,72,32]{1,2,0:T(8,128)} %broadcast_in_dim.16), calls=%async_computation.2 | async-start | bytes 262144 | tf_op jit(solution)/shard_map/all_to_all | solution.py:43
  41.9 7.4 %tiles.6.refs_2_ = bf16[44,1024,512]{2,1,0:T(8,128)(2,1)} custom-call(s32[9]{0:T(128)S(1)} %pad_add_fusion.scalar_ref, f32[2,32,128]{2,1,0:T(8,128)S(1)} %copy-done.2, bf16[44,1024,512]{2,1,0:T(8,128)(2,1)} %tiles.5.refs_0_), custom_call_target="tpu_custom_call", output_to_operand_aliasing={{}: (2, {})} | custom-call | flops 28311552 | bytes 9437184 | tf_op jit(solution)/shard_map/tiles/pallas_call | solution.py:228
  51.0 15.1 %all-to-all-start.3 = ((f32[16,80,128]{2,1,0:T(8,128)}), f32[16,80,128]{2,1,0:T(8,128)S(1)}, u32[]{:S(2)}, u32[]{:S(2)}) async-start(f32[16,80,128]{2,1,0:T(8,128)} %broadcast_in_dim.18), calls=%async_computation.3 | async-start | bytes 1310720 | tf_op jit(solution)/shard_map/all_to_all | solution.py:43
  66.2 13.4 %tiles.7.refs_3_.refs_2_.refs_5_ = bf16[44,1024,512]{2,1,0:T(8,128)(2,1)} custom-call(s32[9]{0:T(128)S(1)} %pad_add_fusion.scalar_ref, f32[2,32,128]{2,1,0:T(8,128)S(1)} %copy-done.2, f32[2,16,128]{2,1,0:T(8,128)S(1)} %slice.93.refs_0_, f32[2,16,128]{2,1,0:T(8,128)S(1)} %slice.94.refs_1_, ...), custom_call_target="tpu_custom_call", output_to_operand_aliasing={{}: (4, {})} | custom-call | flops 72351744 | bytes 24117248 | tf_op jit(solution)/shard_map/tiles/pallas_call | solution.py:228
  80.0 3.3 %residual.1 = (f32[8,64,512]{2,1,0:T(8,128)}, f32[4,64,512]{2,1,0:T(8,128)}, f32[4,64,512]{2,1,0:T(8,128)}, f32[16,64,512]{2,1,0:T(8,128)}) custom-call(s32[8]{0:T(128)S(1)} %fusion.4.target_ref, f32[64,32,128]{2,1,0:T(8,128)S(1)} %copy-done, f32[32,128]{1,0:T(8,128)S(1)} %get-tuple-element.115.weight_ref, f32[64,32]{1,0:T(8,128)S(1)} %divide_add_fusion.1.row_ref, ...), custom_call_target="tpu_custom_call" | custom-call | tf_op jit(solution)/shard_map/residual/pallas_call | solution.py:494
  83.3 7.2 %all-to-all-start.4 = ((f32[16,64,512]{2,1,0:T(8,128)}), f32[16,64,512]{2,1,0:T(8,128)S(1)}, u32[]{:S(2)}, u32[]{:S(2)}) async-start(f32[16,64,512]{2,1,0:T(8,128)} %get-tuple-element.103), calls=%async_computation.4 | async-start | bytes 4194304 | tf_op jit(solution)/shard_map/all_to_all | solution.py:562
  90.5 21.5 %applied.3 = (f32[4,64,512]{2,1,0:T(8,128)}, f32[4,64,512]{2,1,0:T(8,128)}, f32[16,64,512]{2,1,0:T(8,128)}, f32[8,128]{1,0:T(8,128)S(1)}) custom-call(s32[9]{0:T(128)S(1)} %pad_add_fusion.scalar_ref, s32[8]{0:T(128)S(1)} %fusion.4.target_ref, f32[8,64,512]{2,1,0:T(8,128)} %get-tuple-element.95.refs_0_, f32[4,64,512]{2,1,0:T(8,128)} %get-tuple-element.96.refs_1_, ...), custom_call_target="tpu_custom_call" | custom-call | flops 6643777536 | bytes 46137344 | tf_op jit(solution)/shard_map/applied/pallas_call | solution.py:407
  114.2 14.8 %applied.4.refs_4_.refs_1_ = f32[8,64,512]{2,1,0:T(8,128)} custom-call(s32[9]{0:T(128)S(1)} %pad_add_fusion.scalar_ref, s32[8]{0:T(128)S(1)} %fusion.4.target_ref, f32[4,64,512]{2,1,0:T(8,128)} %get-tuple-element.100.refs_0_, f32[4,64,512]{2,1,0:T(8,128)} %get-tuple-element.101.refs_1_, bf16[44,1024,512]{2,1,0:T(8,128)(2,1)} %tiles.7.refs_3_.refs_2_.refs_5_), custom_call_target="tpu_custom_call" | custom-call | flops 3170893824 | bytes 22020096 | tf_op jit(solution)/shard_map/applied/pallas_call | solution.py:407
  128.9 3.4 %collective-permute-done.2.refs_2_ = f32[4,64,512]{2,1,0:T(8,128)S(1)} collective-permute-done((f32[4,64,512]{2,1,0:T(8,128)}, f32[4,64,512]{2,1,0:T(8,128)S(1)}, u32[]{:S(2)}, u32[]{:S(2)}) %collective-permute-start.2) | collective-permute-done | bytes 524320 | tf_op jit(solution)/shard_map/ppermute | solution.py:65
  134.6 6.8 %all-to-all-start.5 = ((f32[16,64,512]{2,1,0:T(8,128)}), f32[16,64,512]{2,1,0:T(8,128)}, u32[]{:S(2)}, u32[]{:S(2)}) async-start(f32[16,64,512]{2,1,0:T(8,128)} %gate.2), calls=%async_computation.5 | async-start | bytes 4194304 | tf_op jit(solution)/shard_map/all_to_all | solution.py:562
  141.4 10.8 %applied.5 = (f32[16,64,512]{2,1,0:T(8,128)}, f32[8,128]{1,0:T(8,128)S(1)}) custom-call(s32[9]{0:T(128)S(1)} %pad_add_fusion.scalar_ref, s32[8]{0:T(128)S(1)} %fusion.4.target_ref, f32[4,64,512]{2,1,0:T(8,128)} %get-tuple-element.100.refs_0_, f32[4,64,512]{2,1,0:T(8,128)} %get-tuple-element.101.refs_1_, f32[4,64,512]{2,1,0:T(8,128)} %copy-done.4, ...), custom_call_target="tpu_custom_call" | custom-call | flops 3472883712 | bytes 24117248 | tf_op jit(solution)/shard_map/applied/pallas_call | solution.py:407
  157.8 2.8 %collective-permute-done.6 = f32[8,128]{1,0:T(8,128)S(1)} collective-permute-done((f32[8,128]{1,0:T(8,128)S(1)}, f32[8,128]{1,0:T(8,128)S(1)}, u32[]{:S(2)}, u32[]{:S(2)}) %collective-permute-start.6) | collective-permute-done | bytes 4128 | tf_op jit(solution)/shard_map/ppermute | solution.py:55
  161.5 2.4 %collective-permute-start.8 = (f32[8,128]{1,0:T(8,128)S(1)}, f32[8,128]{1,0:T(8,128)S(1)}, u32[]{:S(2)}, u32[]{:S(2)}) collective-permute-start(f32[8,128]{1,0:T(8,128)S(1)} %add_add_fusion.2), channel_id=1, source_target_pairs={{0,1},{1,2},{2,3},{3,0},{4,5},{5,6},{6,7},{7,4},{8,9},{9,10},{10,1... | collective-permute-start | bytes 12296 | tf_op jit(solution)/shard_map/ppermute | solution.py:55
  165.5 2.7 %collective-permute-done.8 = f32[8,128]{1,0:T(8,128)S(1)} collective-permute-done((f32[8,128]{1,0:T(8,128)S(1)}, f32[8,128]{1,0:T(8,128)S(1)}, u32[]{:S(2)}, u32[]{:S(2)}) %collective-permute-start.8) | collective-permute-done | bytes 4128 | tf_op jit(solution)/shard_map/ppermute | solution.py:55
  169.0 7.0 %all-to-all-start.6 = ((f32[16,64,512]{2,1,0:T(8,128)}), f32[16,64,512]{2,1,0:T(8,128)S(1)}, u32[]{:S(2)}, u32[]{:S(2)}) async-start(f32[16,64,512]{2,1,0:T(8,128)} %gate.3), calls=%async_computation.6 | async-start | bytes 4194304 | tf_op jit(solution)/shard_map/all_to_all | solution.py:562
  178.2 2.7 %collective-permute-start.12 = (f32[8,128]{1,0:T(8,128)S(1)}, f32[8,128]{1,0:T(8,128)S(1)}, u32[]{:S(2)}, u32[]{:S(2)}) collective-permute-start(f32[8,128]{1,0:T(8,128)S(1)} %add_add_fusion.1.refs_1_), channel_id=1, source_target_pairs={{0,8},{4,12},{8,0},{12,4},{1,9},{5,13},{9,1},{13,5},{2,10},{6,14},... | collective-permute-start | bytes 12296 | tf_op jit(solution)/shard_map/ppermute | solution.py:55
  182.3 16.4 %collective-permute-done.11 = f32[8,128]{1,0:T(8,128)S(1)} collective-permute-done((f32[8,128]{1,0:T(8,128)S(1)}, f32[8,128]{1,0:T(8,128)S(1)}, u32[]{:S(2)}, u32[]{:S(2)}) %collective-permute-start.11) | collective-permute-done | bytes 4128 | tf_op jit(solution)/shard_map/ppermute | solution.py:55
  198.8 3.1 %collective-permute-done.12 = f32[8,128]{1,0:T(8,128)S(1)} collective-permute-done((f32[8,128]{1,0:T(8,128)S(1)}, f32[8,128]{1,0:T(8,128)S(1)}, u32[]{:S(2)}, u32[]{:S(2)}) %collective-permute-start.12) | collective-permute-done | bytes 4128 | tf_op jit(solution)/shard_map/ppermute | solution.py:55
  201.8 4.7 %first.1 = (f32[64,8,512]{2,1,0:T(8,128)}, f32[64,8,512]{2,1,0:T(8,128)S(1)}) custom-call(s32[8]{0:T(128)S(1)} %and_select_fusion.src_ref, f32[8,128]{1,0:T(8,128)S(1)} %add_add_fusion.dots_ref, f32[16,64,512]{2,1,0:T(8,128)} %copy-done.3, f32[16,64,512]{2,1,0:T(8,128)} %all-to-all-done.5.refs_1_.refs_3_.refs_5_.refs_7_.refs_9_.refs_11_.refs_13_.refs_15_, ...), custom_call_target="tpu_custom_call" | custom-call | tf_op jit(solution)/shard_map/first/pallas_call | solution.py:546
  206.5 2.7 %second.1 = f32[64,8,512]{2,1,0:T(8,128)} custom-call(s32[8]{0:T(128)S(1)} %and_select_fusion.src_ref, f32[8,128]{1,0:T(8,128)S(1)} %add_add_fusion.dots_ref, f32[64,8,512]{2,1,0:T(8,128)S(1)} %get-tuple-element.106.part_ref, f32[16,64,512]{2,1,0:T(8,128)S(1)} %all-to-all-done.6.refs_0_.refs_1_.refs_2_.refs_3_.refs_4_.refs_5_.refs_6_.refs_7_, ...), custom_call_target="tpu_custom_call" | custom-call | tf_op jit(solution)/shard_map/second/pallas_call | solution.py:546
  (98 shorter events, 31.3 us)
Async XLA Ops:
  4.8 10.2 %all-to-all-start = ((f32[8,72,32]{1,2,0:T(8,128)}), f32[8,72,32]{1,2,0:T(8,128)S(1)}, u32[]{:S(2)}, u32[]{:S(2)}) async-start(f32[8,72,32]{1,2,0:T(8,128)} %broadcast_in_dim.14), calls=%async_computation | async-start | bytes 262144 | tf_op jit(solution)/shard_map/all_to_all | solution.py:43
  11.4 3.9 %copy-start = (f32[64,32,128]{2,1,0:T(8,128)S(1)}, f32[64,32,128]{2,1,0:T(8,128)}, u32[]{:S(2)}) copy-start(f32[64,32,128]{2,1,0:T(8,128)} %obs_ref.1) | copy-start | bytes 3145732
  15.0 10.0 %copy-start.2 = (f32[2,32,128]{2,1,0:T(8,128)S(1)}, f32[2,32,128]{2,1,0:T(8,128)}, u32[]{:S(2)}) copy-start(f32[2,32,128]{2,1,0:T(8,128)} %jitter_ref.3) | copy-start | bytes 98308
  16.7 18.7 %all-to-all-start.1 = ((f32[16,72,128]{2,1,0:T(8,128)}), f32[16,72,128]{2,1,0:T(8,128)S(1)}, u32[]{:S(2)}, u32[]{:S(2)}) async-start(f32[16,72,128]{2,1,0:T(8,128)} %broadcast_in_dim.15), calls=%async_computation.1 | async-start | bytes 1179648 | tf_op jit(solution)/shard_map/all_to_all | solution.py:43
  26.0 23.4 %collective-permute-start = (f32[67,16,128]{2,1,0:T(8,128)}, f32[67,16,128]{2,1,0:T(8,128)S(1)}, u32[]{:S(2)}, u32[]{:S(2)}) collective-permute-start(f32[67,16,128]{2,1,0:T(8,128)} %get-tuple-element.86), channel_id=1, source_target_pairs={{0,1},{1,2},{2,3},{3,4},{4,5},{5,6},{6,7},{7,8},{8,9},{9,10},{10,1... | collective-permute-start | bytes 1646600 | tf_op jit(solution)/shard_map/ppermute | solution.py:65
  27.4 21.9 %collective-permute-start.1 = (f32[67,16,128]{2,1,0:T(8,128)S(1)}, f32[67,16,128]{2,1,0:T(8,128)S(1)}, u32[]{:S(2)}, u32[]{:S(2)}) collective-permute-start(f32[67,16,128]{2,1,0:T(8,128)S(1)} %get-tuple-element.87), channel_id=1, source_target_pairs={{1,0},{2,1},{3,2},{4,3},{5,4},{6,5},{7,6},{8,7},{9,8},{10,9},{11,1... | collective-permute-start | bytes 1646600 | tf_op jit(solution)/shard_map/ppermute | solution.py:65
  37.1 12.2 %all-to-all-start.2 = ((f32[8,72,32]{1,2,0:T(8,128)}), f32[8,72,32]{1,2,0:T(8,128)S(1)}, u32[]{:S(2)}, u32[]{:S(2)}) async-start(f32[8,72,32]{1,2,0:T(8,128)} %broadcast_in_dim.16), calls=%async_computation.2 | async-start | bytes 262144 | tf_op jit(solution)/shard_map/all_to_all | solution.py:43
  49.3 16.8 %copy-start.7 = (s32[1,128]{1,0:T(1,128)S(1)}, s32[1,128]{1,0:T(1,128)}, u32[]{:S(2)}) copy-start(s32[1,128]{1,0:T(1,128)} %param.16) | copy-start | bytes 1540
  51.0 28.5 %all-to-all-start.3 = ((f32[16,80,128]{2,1,0:T(8,128)}), f32[16,80,128]{2,1,0:T(8,128)S(1)}, u32[]{:S(2)}, u32[]{:S(2)}) async-start(f32[16,80,128]{2,1,0:T(8,128)} %broadcast_in_dim.18), calls=%async_computation.3 | async-start | bytes 1310720 | tf_op jit(solution)/shard_map/all_to_all | solution.py:43
  83.3 50.0 %all-to-all-start.4 = ((f32[16,64,512]{2,1,0:T(8,128)}), f32[16,64,512]{2,1,0:T(8,128)S(1)}, u32[]{:S(2)}, u32[]{:S(2)}) async-start(f32[16,64,512]{2,1,0:T(8,128)} %get-tuple-element.103), calls=%async_computation.4 | async-start | bytes 4194304 | tf_op jit(solution)/shard_map/all_to_all | solution.py:562
  112.1 20.3 %collective-permute-start.2 = (f32[4,64,512]{2,1,0:T(8,128)}, f32[4,64,512]{2,1,0:T(8,128)S(1)}, u32[]{:S(2)}, u32[]{:S(2)}) collective-permute-start(f32[4,64,512]{2,1,0:T(8,128)} %get-tuple-element.101.refs_1_), channel_id=1, source_target_pairs={{0,1},{1,2},{2,3},{3,4},{4,5},{5,6},{6,7},{7,8},{8,9},{9,10},{10,1... | collective-permute-start | bytes 1572872 | tf_op jit(solution)/shard_map/ppermute | solution.py:65
  113.6 18.8 %collective-permute-start.3 = (f32[4,64,512]{2,1,0:T(8,128)}, f32[4,64,512]{2,1,0:T(8,128)S(1)}, u32[]{:S(2)}, u32[]{:S(2)}) collective-permute-start(f32[4,64,512]{2,1,0:T(8,128)} %get-tuple-element.100.refs_0_), channel_id=1, source_target_pairs={{1,0},{2,1},{3,2},{4,3},{5,4},{6,5},{7,6},{8,7},{9,8},{10,9},{11,1... | collective-permute-start | bytes 1572872 | tf_op jit(solution)/shard_map/ppermute | solution.py:65
  134.6 34.4 %all-to-all-start.5 = ((f32[16,64,512]{2,1,0:T(8,128)}), f32[16,64,512]{2,1,0:T(8,128)}, u32[]{:S(2)}, u32[]{:S(2)}) async-start(f32[16,64,512]{2,1,0:T(8,128)} %gate.2), calls=%async_computation.5 | async-start | bytes 4194304 | tf_op jit(solution)/shard_map/all_to_all | solution.py:562
  152.2 1.2 collective-permute-start.4
  153.4 4.4 %collective-permute-start.5 = (f32[8,128]{1,0:T(8,128)S(1)}, f32[8,128]{1,0:T(8,128)S(1)}, u32[]{:S(2)}, u32[]{:S(2)}) collective-permute-start(f32[8,128]{1,0:T(8,128)S(1)} %add.103), channel_id=1, source_target_pairs={{0,32},{32,64},{64,96},{96,0},{1,33},{33,65},{65,97},{97,1},{2,34}... | collective-permute-start | bytes 12296 | tf_op jit(solution)/shard_map/ppermute | solution.py:55
  155.5 5.1 %collective-permute-start.6 = (f32[8,128]{1,0:T(8,128)S(1)}, f32[8,128]{1,0:T(8,128)S(1)}, u32[]{:S(2)}, u32[]{:S(2)}) collective-permute-start(f32[8,128]{1,0:T(8,128)S(1)} %add.103), channel_id=1, source_target_pairs={{0,64},{32,96},{64,0},{96,32},{1,65},{33,97},{65,1},{97,33},{2,66}... | collective-permute-start | bytes 12296 | tf_op jit(solution)/shard_map/ppermute | solution.py:55
  155.5 5.1 %collective-permute-start.7 = (f32[8,128]{1,0:T(8,128)S(1)}, f32[8,128]{1,0:T(8,128)S(1)}, u32[]{:S(2)}, u32[]{:S(2)}) collective-permute-start(f32[8,128]{1,0:T(8,128)S(1)} %add.103), channel_id=1, source_target_pairs={{0,96},{32,0},{64,32},{96,64},{1,97},{33,1},{65,33},{97,65},{2,98}... | collective-permute-start | bytes 12296 | tf_op jit(solution)/shard_map/ppermute | solution.py:55
  160.6 4.9 %collective-permute-start.10 = (f32[8,128]{1,0:T(8,128)S(1)}, f32[8,128]{1,0:T(8,128)S(1)}, u32[]{:S(2)}, u32[]{:S(2)}) collective-permute-start(f32[8,128]{1,0:T(8,128)S(1)} %add_add_fusion.2), channel_id=1, source_target_pairs={{0,3},{1,0},{2,1},{3,2},{4,7},{5,4},{6,5},{7,6},{8,11},{9,8},{10,9... | collective-permute-start | bytes 12296 | tf_op jit(solution)/shard_map/ppermute | solution.py:55
  161.5 6.7 %collective-permute-start.8 = (f32[8,128]{1,0:T(8,128)S(1)}, f32[8,128]{1,0:T(8,128)S(1)}, u32[]{:S(2)}, u32[]{:S(2)}) collective-permute-start(f32[8,128]{1,0:T(8,128)S(1)} %add_add_fusion.2), channel_id=1, source_target_pairs={{0,1},{1,2},{2,3},{3,0},{4,5},{5,6},{6,7},{7,4},{8,9},{9,10},{10,1... | collective-permute-start | bytes 12296 | tf_op jit(solution)/shard_map/ppermute | solution.py:55
  163.9 5.1 %collective-permute-start.9 = (f32[8,128]{1,0:T(8,128)S(1)}, f32[8,128]{1,0:T(8,128)S(1)}, u32[]{:S(2)}, u32[]{:S(2)}) collective-permute-start(f32[8,128]{1,0:T(8,128)S(1)} %add_add_fusion.2), channel_id=1, source_target_pairs={{0,2},{1,3},{2,0},{3,1},{4,6},{5,7},{6,4},{7,5},{8,10},{9,11},{10,... | collective-permute-start | bytes 12296 | tf_op jit(solution)/shard_map/ppermute | solution.py:55
  169.0 37.5 %all-to-all-start.6 = ((f32[16,64,512]{2,1,0:T(8,128)}), f32[16,64,512]{2,1,0:T(8,128)S(1)}, u32[]{:S(2)}, u32[]{:S(2)}) async-start(f32[16,64,512]{2,1,0:T(8,128)} %gate.3), calls=%async_computation.6 | async-start | bytes 4194304 | tf_op jit(solution)/shard_map/all_to_all | solution.py:562
  176.6 22.1 %collective-permute-start.11 = (f32[8,128]{1,0:T(8,128)S(1)}, f32[8,128]{1,0:T(8,128)S(1)}, u32[]{:S(2)}, u32[]{:S(2)}) collective-permute-start(f32[8,128]{1,0:T(8,128)S(1)} %add_add_fusion.1.refs_1_), channel_id=1, source_target_pairs={{0,4},{4,8},{8,12},{12,0},{1,5},{5,9},{9,13},{13,1},{2,6},{6,10},{... | collective-permute-start | bytes 12296 | tf_op jit(solution)/shard_map/ppermute | solution.py:55
  178.2 23.7 %collective-permute-start.12 = (f32[8,128]{1,0:T(8,128)S(1)}, f32[8,128]{1,0:T(8,128)S(1)}, u32[]{:S(2)}, u32[]{:S(2)}) collective-permute-start(f32[8,128]{1,0:T(8,128)S(1)} %add_add_fusion.1.refs_1_), channel_id=1, source_target_pairs={{0,8},{4,12},{8,0},{12,4},{1,9},{5,13},{9,1},{13,5},{2,10},{6,14},... | collective-permute-start | bytes 12296 | tf_op jit(solution)/shard_map/ppermute | solution.py:55
  180.9 21.0 %collective-permute-start.13 = (f32[8,128]{1,0:T(8,128)S(1)}, f32[8,128]{1,0:T(8,128)S(1)}, u32[]{:S(2)}, u32[]{:S(2)}) collective-permute-start(f32[8,128]{1,0:T(8,128)S(1)} %add_add_fusion.1.refs_1_), channel_id=1, source_target_pairs={{0,12},{4,0},{8,4},{12,8},{1,13},{5,1},{9,5},{13,9},{2,14},{6,2},{... | collective-permute-start | bytes 12296 | tf_op jit(solution)/shard_map/ppermute | solution.py:55
  (5 other events, 7.7 us)

commit v9 on v8

--- a/solution.py
+++ b/solution.py
@@ -30,7 +30,7 @@
 
 OWN_TILES = BLOCKS_DEV + PAIRED * BLOCKS_DEV - 6
 HALO_TILES = 2 * (2 + 3 + 4)
-CHUNKS = (3, 9, 9, 23)
+CHUNKS = (5, 9, 9, 21)
 TILE_SLOTS = 4
 OP_SLOTS = 12
 OP_FIRST = 4

time: 213 us -> 203 us (0.953)
  the two profiles are of different devices: /device:TPU:14 before, /device:TPU:0 now
where the time goes in v9:
time: 203 us; the launch traced here: 202 us
  Pallas kernels  88.8 us (44%)
  starting transfers between devices  63.5 us (31%)
  waiting for transfers between devices  33.6 us (17%)
  local copies, waits for them, and re-layouts  8.52 us (4%)
  other arithmetic  6.55 us (3%)
    pallas_call x3, Pallas kernels, applied(): pl.pallas_call(functools.partial(op_kernel, *tiles_of, len(v), bool(besid...  47.2 us
    pallas_call x4, Pallas kernels, covariance_tiles(): pl.pallas_call(functools.partial(tiles_kernel, first, count, len(beside_j...  31 us
    ppermute x10, waiting for transfers between devices, sum_direct(): lax.ppermute(part, axis, [(i, (i + k) % peers) for i in range(peers)])  26.5 us
    all_to_all x4, starting transfers between devices, sent_to_all(): lax.all_to_all(jnp.broadcast_to(shard[None], (peers, *shard.shape)), axis...  21.1 us
    ppermute x10, starting transfers between devices, sum_direct(): lax.ppermute(part, axis, [(i, (i + k) % peers) for i in range(peers)])  16.7 us
    all_to_all x3, starting transfers between devices, to_owners(): return lax.all_to_all(slots, SIXTEEN, 0, 0, tiled=True)  15 us
    pallas_call x2, Pallas kernels, combined(): pl.pallas_call(kernel, grid_spec=pltpu.PrefetchScalarGridSpec(num_scalar_...  7.35 us
    ppermute x2, starting transfers between devices, swapped(): lax.ppermute(initial, SIXTEEN, down)  6.89 us
  transfers between devices with their start and end apart: 21, of which 12 were waited for; matrix products, arithmetic and copies ran while one was open for 2% of the time, Pallas kernels for 41%

profile of v9, /device:TPU:0, one launch (start us, length us, event | category | flops | bytes accessed | tf_op | source)
XLA Modules:
  0.0 202.0 jit_solution(13217432907453185839)
XLA Ops:
  4.8 4.6 %all-to-all-start = ((f32[8,72,32]{1,2,0:T(8,128)}), f32[8,72,32]{1,2,0:T(8,128)S(1)}, u32[]{:S(2)}, u32[]{:S(2)}) async-start(f32[8,72,32]{1,2,0:T(8,128)} %broadcast_in_dim.14), calls=%async_computation | async-start | bytes 262144 | tf_op jit(solution)/shard_map/all_to_all | solution.py:43
  11.1 4.8 %tiles.4.refs_0_ = bf16[44,1024,512]{2,1,0:T(8,128)(2,1)} custom-call(s32[9]{0:T(128)S(1)} %pad_add_fusion.scalar_ref, f32[2,32,128]{2,1,0:T(8,128)S(1)} %copy-done.1), custom_call_target="tpu_custom_call" | custom-call | flops 15728640 | bytes 5242880 | tf_op jit(solution)/shard_map/tiles/pallas_call | solution.py:228
  17.7 7.9 %all-to-all-start.1 = ((f32[16,72,128]{2,1,0:T(8,128)}), f32[16,72,128]{2,1,0:T(8,128)S(1)}, u32[]{:S(2)}, u32[]{:S(2)}) async-start(f32[16,72,128]{2,1,0:T(8,128)} %broadcast_in_dim.15), calls=%async_computation.1 | async-start | bytes 1179648 | tf_op jit(solution)/shard_map/all_to_all | solution.py:43
  28.4 3.4 %collective-permute-start.1 = (f32[67,16,128]{2,1,0:T(8,128)S(1)}, f32[67,16,128]{2,1,0:T(8,128)S(1)}, u32[]{:S(2)}, u32[]{:S(2)}) collective-permute-start(f32[67,16,128]{2,1,0:T(8,128)S(1)} %get-tuple-element.87), channel_id=1, source_target_pairs={{1,0},{2,1},{3,2},{4,3},{5,4},{6,5},{7,6},{8,7},{9,8},{10,9},{11,1... | collective-permute-start | bytes 1646600 | tf_op jit(solution)/shard_map/ppermute | solution.py:65
  31.9 7.4 %tiles.5.refs_0_ = bf16[44,1024,512]{2,1,0:T(8,128)(2,1)} custom-call(s32[9]{0:T(128)S(1)} %pad_add_fusion.scalar_ref, f32[2,32,128]{2,1,0:T(8,128)S(1)} %copy-done.2, bf16[44,1024,512]{2,1,0:T(8,128)(2,1)} %tiles.4.refs_0_), custom_call_target="tpu_custom_call", output_to_operand_aliasing={{}: (2, {})} | custom-call | flops 28311552 | bytes 9437184 | tf_op jit(solution)/shard_map/tiles/pallas_call | solution.py:228
  41.0 4.8 %all-to-all-start.2 = ((f32[8,72,32]{1,2,0:T(8,128)}), f32[8,72,32]{1,2,0:T(8,128)S(1)}, u32[]{:S(2)}, u32[]{:S(2)}) async-start(f32[8,72,32]{1,2,0:T(8,128)} %broadcast_in_dim.16), calls=%async_computation.2 | async-start | bytes 262144 | tf_op jit(solution)/shard_map/all_to_all | solution.py:43
  45.8 7.4 %tiles.6.refs_2_ = bf16[44,1024,512]{2,1,0:T(8,128)(2,1)} custom-call(s32[9]{0:T(128)S(1)} %pad_add_fusion.scalar_ref, f32[2,32,128]{2,1,0:T(8,128)S(1)} %copy-done.2, bf16[44,1024,512]{2,1,0:T(8,128)(2,1)} %tiles.5.refs_0_), custom_call_target="tpu_custom_call", output_to_operand_aliasing={{}: (2, {})} | custom-call | flops 28311552 | bytes 9437184 | tf_op jit(solution)/shard_map/tiles/pallas_call | solution.py:228
  54.9 3.9 %all-to-all-start.3 = ((f32[16,80,128]{2,1,0:T(8,128)}), f32[16,80,128]{2,1,0:T(8,128)S(1)}, u32[]{:S(2)}, u32[]{:S(2)}) async-start(f32[16,80,128]{2,1,0:T(8,128)} %broadcast_in_dim.18), calls=%async_computation.3 | async-start | bytes 1310720 | tf_op jit(solution)/shard_map/all_to_all | solution.py:43
  59.0 11.3 %tiles.7.refs_3_.refs_2_.refs_5_ = bf16[44,1024,512]{2,1,0:T(8,128)(2,1)} custom-call(s32[9]{0:T(128)S(1)} %pad_add_fusion.scalar_ref, f32[2,32,128]{2,1,0:T(8,128)S(1)} %copy-done.2, f32[2,16,128]{2,1,0:T(8,128)S(1)} %slice.93.refs_0_, f32[2,16,128]{2,1,0:T(8,128)S(1)} %slice.94.refs_1_, ...), custom_call_target="tpu_custom_call", output_to_operand_aliasing={{}: (4, {})} | custom-call | flops 66060288 | bytes 22020096 | tf_op jit(solution)/shard_map/tiles/pallas_call | solution.py:228
  72.8 3.3 %residual.1 = (f32[8,64,512]{2,1,0:T(8,128)}, f32[4,64,512]{2,1,0:T(8,128)}, f32[4,64,512]{2,1,0:T(8,128)}, f32[16,64,512]{2,1,0:T(8,128)}) custom-call(s32[8]{0:T(128)S(1)} %fusion.4.target_ref, f32[64,32,128]{2,1,0:T(8,128)S(1)} %copy-done, f32[32,128]{1,0:T(8,128)S(1)} %get-tuple-element.115.weight_ref, f32[64,32]{1,0:T(8,128)S(1)} %divide_add_fusion.1.row_ref, ...), custom_call_target="tpu_custom_call" | custom-call | tf_op jit(solution)/shard_map/residual/pallas_call | solution.py:494
  76.1 5.1 %all-to-all-start.4 = ((f32[16,64,512]{2,1,0:T(8,128)}), f32[16,64,512]{2,1,0:T(8,128)S(1)}, u32[]{:S(2)}, u32[]{:S(2)}) async-start(f32[16,64,512]{2,1,0:T(8,128)} %get-tuple-element.103), calls=%async_computation.4 | async-start | bytes 4194304 | tf_op jit(solution)/shard_map/all_to_all | solution.py:562
  81.2 21.6 %applied.3 = (f32[4,64,512]{2,1,0:T(8,128)}, f32[4,64,512]{2,1,0:T(8,128)}, f32[16,64,512]{2,1,0:T(8,128)}, f32[8,128]{1,0:T(8,128)S(1)}) custom-call(s32[9]{0:T(128)S(1)} %pad_add_fusion.scalar_ref, s32[8]{0:T(128)S(1)} %fusion.4.target_ref, f32[8,64,512]{2,1,0:T(8,128)} %get-tuple-element.95.refs_0_, f32[4,64,512]{2,1,0:T(8,128)} %get-tuple-element.96.refs_1_, ...), custom_call_target="tpu_custom_call" | custom-call | flops 6643777536 | bytes 46137344 | tf_op jit(solution)/shard_map/applied/pallas_call | solution.py:407
  104.8 3.5 %collective-permute-start.3 = (f32[4,64,512]{2,1,0:T(8,128)}, f32[4,64,512]{2,1,0:T(8,128)S(1)}, u32[]{:S(2)}, u32[]{:S(2)}) collective-permute-start(f32[4,64,512]{2,1,0:T(8,128)} %get-tuple-element.100.refs_0_), channel_id=1, source_target_pairs={{1,0},{2,1},{3,2},{4,3},{5,4},{6,5},{7,6},{8,7},{9,8},{10,9},{11,1... | collective-permute-start | bytes 1572872 | tf_op jit(solution)/shard_map/ppermute | solution.py:65
  108.2 14.8 %applied.4.refs_4_.refs_1_ = f32[8,64,512]{2,1,0:T(8,128)} custom-call(s32[9]{0:T(128)S(1)} %pad_add_fusion.scalar_ref, s32[8]{0:T(128)S(1)} %fusion.4.target_ref, f32[4,64,512]{2,1,0:T(8,128)} %get-tuple-element.100.refs_0_, f32[4,64,512]{2,1,0:T(8,128)} %get-tuple-element.101.refs_1_, bf16[44,1024,512]{2,1,0:T(8,128)(2,1)} %tiles.7.refs_3_.refs_2_.refs_5_), custom_call_target="tpu_custom_call" | custom-call | flops 3170893824 | bytes 22020096 | tf_op jit(solution)/shard_map/applied/pallas_call | solution.py:407
  126.4 6.2 %all-to-all-start.5 = ((f32[16,64,512]{2,1,0:T(8,128)}), f32[16,64,512]{2,1,0:T(8,128)}, u32[]{:S(2)}, u32[]{:S(2)}) async-start(f32[16,64,512]{2,1,0:T(8,128)} %gate.2), calls=%async_computation.5 | async-start | bytes 4194304 | tf_op jit(solution)/shard_map/all_to_all | solution.py:562
  132.6 10.8 %applied.5 = (f32[16,64,512]{2,1,0:T(8,128)}, f32[8,128]{1,0:T(8,128)S(1)}) custom-call(s32[9]{0:T(128)S(1)} %pad_add_fusion.scalar_ref, s32[8]{0:T(128)S(1)} %fusion.4.target_ref, f32[4,64,512]{2,1,0:T(8,128)} %get-tuple-element.100.refs_0_, f32[4,64,512]{2,1,0:T(8,128)} %get-tuple-element.101.refs_1_, f32[4,64,512]{2,1,0:T(8,128)} %copy-done.4, ...), custom_call_target="tpu_custom_call" | custom-call | flops 3472883712 | bytes 24117248 | tf_op jit(solution)/shard_map/applied/pallas_call | solution.py:407
  145.9 2.7 %collective-permute-start.6 = (f32[8,128]{1,0:T(8,128)S(1)}, f32[8,128]{1,0:T(8,128)S(1)}, u32[]{:S(2)}, u32[]{:S(2)}) collective-permute-start(f32[8,128]{1,0:T(8,128)S(1)} %add.103), channel_id=1, source_target_pairs={{0,64},{32,96},{64,0},{96,32},{1,65},{33,97},{65,1},{97,33},{2,66}... | collective-permute-start | bytes 12296 | tf_op jit(solution)/shard_map/ppermute | solution.py:55
  152.2 2.8 %collective-permute-start.10 = (f32[8,128]{1,0:T(8,128)S(1)}, f32[8,128]{1,0:T(8,128)S(1)}, u32[]{:S(2)}, u32[]{:S(2)}) collective-permute-start(f32[8,128]{1,0:T(8,128)S(1)} %add_add_fusion.2), channel_id=1, source_target_pairs={{0,3},{1,0},{2,1},{3,2},{4,7},{5,4},{6,5},{7,6},{8,11},{9,8},{10,9... | collective-permute-start | bytes 12296 | tf_op jit(solution)/shard_map/ppermute | solution.py:55
  157.3 5.5 %collective-permute-done.10 = f32[8,128]{1,0:T(8,128)S(1)} collective-permute-done((f32[8,128]{1,0:T(8,128)S(1)}, f32[8,128]{1,0:T(8,128)S(1)}, u32[]{:S(2)}, u32[]{:S(2)}) %collective-permute-start.10) | collective-permute-done | bytes 4128 | tf_op jit(solution)/shard_map/ppermute | solution.py:55
  165.5 3.7 %all-to-all-start.6 = ((f32[16,64,512]{2,1,0:T(8,128)}), f32[16,64,512]{2,1,0:T(8,128)S(1)}, u32[]{:S(2)}, u32[]{:S(2)}) async-start(f32[16,64,512]{2,1,0:T(8,128)} %gate.3), calls=%async_computation.6 | async-start | bytes 4194304 | tf_op jit(solution)/shard_map/all_to_all | solution.py:562
  171.8 2.7 %collective-permute-start.12 = (f32[8,128]{1,0:T(8,128)S(1)}, f32[8,128]{1,0:T(8,128)S(1)}, u32[]{:S(2)}, u32[]{:S(2)}) collective-permute-start(f32[8,128]{1,0:T(8,128)S(1)} %add_add_fusion.1.refs_1_), channel_id=1, source_target_pairs={{0,8},{4,12},{8,0},{12,4},{1,9},{5,13},{9,1},{13,5},{2,10},{6,14},... | collective-permute-start | bytes 12296 | tf_op jit(solution)/shard_map/ppermute | solution.py:55
  175.9 12.6 %collective-permute-done.11 = f32[8,128]{1,0:T(8,128)S(1)} collective-permute-done((f32[8,128]{1,0:T(8,128)S(1)}, f32[8,128]{1,0:T(8,128)S(1)}, u32[]{:S(2)}, u32[]{:S(2)}) %collective-permute-start.11) | collective-permute-done | bytes 4128 | tf_op jit(solution)/shard_map/ppermute | solution.py:55
  188.5 3.6 %collective-permute-done.12 = f32[8,128]{1,0:T(8,128)S(1)} collective-permute-done((f32[8,128]{1,0:T(8,128)S(1)}, f32[8,128]{1,0:T(8,128)S(1)}, u32[]{:S(2)}, u32[]{:S(2)}) %collective-permute-start.12) | collective-permute-done | bytes 4128 | tf_op jit(solution)/shard_map/ppermute | solution.py:55
  192.1 4.7 %first.1 = (f32[64,8,512]{2,1,0:T(8,128)}, f32[64,8,512]{2,1,0:T(8,128)S(1)}) custom-call(s32[8]{0:T(128)S(1)} %and_select_fusion.src_ref, f32[8,128]{1,0:T(8,128)S(1)} %add_add_fusion.dots_ref, f32[16,64,512]{2,1,0:T(8,128)} %copy-done.3, f32[16,64,512]{2,1,0:T(8,128)} %all-to-all-done.5.refs_1_.refs_3_.refs_5_.refs_7_.refs_9_.refs_11_.refs_13_.refs_15_, ...), custom_call_target="tpu_custom_call" | custom-call | tf_op jit(solution)/shard_map/first/pallas_call | solution.py:546
  (98 shorter events, 42.1 us)
Async XLA Ops:
  4.8 11.1 %all-to-all-start = ((f32[8,72,32]{1,2,0:T(8,128)}), f32[8,72,32]{1,2,0:T(8,128)S(1)}, u32[]{:S(2)}, u32[]{:S(2)}) async-start(f32[8,72,32]{1,2,0:T(8,128)} %broadcast_in_dim.14), calls=%async_computation | async-start | bytes 262144 | tf_op jit(solution)/shard_map/all_to_all | solution.py:43
  11.1 5.2 %copy-start = (f32[64,32,128]{2,1,0:T(8,128)S(1)}, f32[64,32,128]{2,1,0:T(8,128)}, u32[]{:S(2)}) copy-start(f32[64,32,128]{2,1,0:T(8,128)} %obs_ref.1) | copy-start | bytes 3145732
  15.9 9.7 %copy-start.2 = (f32[2,32,128]{2,1,0:T(8,128)S(1)}, f32[2,32,128]{2,1,0:T(8,128)}, u32[]{:S(2)}) copy-start(f32[2,32,128]{2,1,0:T(8,128)} %jitter_ref.3) | copy-start | bytes 98308
  17.7 21.6 %all-to-all-start.1 = ((f32[16,72,128]{2,1,0:T(8,128)}), f32[16,72,128]{2,1,0:T(8,128)S(1)}, u32[]{:S(2)}, u32[]{:S(2)}) async-start(f32[16,72,128]{2,1,0:T(8,128)} %broadcast_in_dim.15), calls=%async_computation.1 | async-start | bytes 1179648 | tf_op jit(solution)/shard_map/all_to_all | solution.py:43
  26.5 26.7 %collective-permute-start = (f32[67,16,128]{2,1,0:T(8,128)}, f32[67,16,128]{2,1,0:T(8,128)S(1)}, u32[]{:S(2)}, u32[]{:S(2)}) collective-permute-start(f32[67,16,128]{2,1,0:T(8,128)} %get-tuple-element.86), channel_id=1, source_target_pairs={{0,1},{1,2},{2,3},{3,4},{4,5},{5,6},{6,7},{7,8},{8,9},{9,10},{10,1... | collective-permute-start | bytes 1646600 | tf_op jit(solution)/shard_map/ppermute | solution.py:65
  28.4 24.8 %collective-permute-start.1 = (f32[67,16,128]{2,1,0:T(8,128)S(1)}, f32[67,16,128]{2,1,0:T(8,128)S(1)}, u32[]{:S(2)}, u32[]{:S(2)}) collective-permute-start(f32[67,16,128]{2,1,0:T(8,128)S(1)} %get-tuple-element.87), channel_id=1, source_target_pairs={{1,0},{2,1},{3,2},{4,3},{5,4},{6,5},{7,6},{8,7},{9,8},{10,9},{11,1... | collective-permute-start | bytes 1646600 | tf_op jit(solution)/shard_map/ppermute | solution.py:65
  41.0 12.2 %all-to-all-start.2 = ((f32[8,72,32]{1,2,0:T(8,128)}), f32[8,72,32]{1,2,0:T(8,128)S(1)}, u32[]{:S(2)}, u32[]{:S(2)}) async-start(f32[8,72,32]{1,2,0:T(8,128)} %broadcast_in_dim.16), calls=%async_computation.2 | async-start | bytes 262144 | tf_op jit(solution)/shard_map/all_to_all | solution.py:43
  53.2 5.7 %copy-start.7 = (s32[1,128]{1,0:T(1,128)S(1)}, s32[1,128]{1,0:T(1,128)}, u32[]{:S(2)}) copy-start(s32[1,128]{1,0:T(1,128)} %param.16) | copy-start | bytes 1540
  54.9 17.5 %all-to-all-start.3 = ((f32[16,80,128]{2,1,0:T(8,128)}), f32[16,80,128]{2,1,0:T(8,128)S(1)}, u32[]{:S(2)}, u32[]{:S(2)}) async-start(f32[16,80,128]{2,1,0:T(8,128)} %broadcast_in_dim.18), calls=%async_computation.3 | async-start | bytes 1310720 | tf_op jit(solution)/shard_map/all_to_all | solution.py:43
  76.1 48.9 %all-to-all-start.4 = ((f32[16,64,512]{2,1,0:T(8,128)}), f32[16,64,512]{2,1,0:T(8,128)S(1)}, u32[]{:S(2)}, u32[]{:S(2)}) async-start(f32[16,64,512]{2,1,0:T(8,128)} %get-tuple-element.103), calls=%async_computation.4 | async-start | bytes 4194304 | tf_op jit(solution)/shard_map/all_to_all | solution.py:562
  102.8 20.9 %collective-permute-start.2 = (f32[4,64,512]{2,1,0:T(8,128)}, f32[4,64,512]{2,1,0:T(8,128)S(1)}, u32[]{:S(2)}, u32[]{:S(2)}) collective-permute-start(f32[4,64,512]{2,1,0:T(8,128)} %get-tuple-element.101.refs_1_), channel_id=1, source_target_pairs={{0,1},{1,2},{2,3},{3,4},{4,5},{5,6},{6,7},{7,8},{8,9},{9,10},{10,1... | collective-permute-start | bytes 1572872 | tf_op jit(solution)/shard_map/ppermute | solution.py:65
  104.8 19.5 %collective-permute-start.3 = (f32[4,64,512]{2,1,0:T(8,128)}, f32[4,64,512]{2,1,0:T(8,128)S(1)}, u32[]{:S(2)}, u32[]{:S(2)}) collective-permute-start(f32[4,64,512]{2,1,0:T(8,128)} %get-tuple-element.100.refs_0_), channel_id=1, source_target_pairs={{1,0},{2,1},{3,2},{4,3},{5,4},{6,5},{7,6},{8,7},{9,8},{10,9},{11,1... | collective-permute-start | bytes 1572872 | tf_op jit(solution)/shard_map/ppermute | solution.py:65
  126.4 39.1 %all-to-all-start.5 = ((f32[16,64,512]{2,1,0:T(8,128)}), f32[16,64,512]{2,1,0:T(8,128)}, u32[]{:S(2)}, u32[]{:S(2)}) async-start(f32[16,64,512]{2,1,0:T(8,128)} %gate.2), calls=%async_computation.5 | async-start | bytes 4194304 | tf_op jit(solution)/shard_map/all_to_all | solution.py:562
  143.4 1.2 collective-permute-start.4
  144.6 5.4 %collective-permute-start.5 = (f32[8,128]{1,0:T(8,128)S(1)}, f32[8,128]{1,0:T(8,128)S(1)}, u32[]{:S(2)}, u32[]{:S(2)}) collective-permute-start(f32[8,128]{1,0:T(8,128)S(1)} %add.103), channel_id=1, source_target_pairs={{0,32},{32,64},{64,96},{96,0},{1,33},{33,65},{65,97},{97,1},{2,34}... | collective-permute-start | bytes 12296 | tf_op jit(solution)/shard_map/ppermute | solution.py:55
  145.9 5.1 %collective-permute-start.6 = (f32[8,128]{1,0:T(8,128)S(1)}, f32[8,128]{1,0:T(8,128)S(1)}, u32[]{:S(2)}, u32[]{:S(2)}) collective-permute-start(f32[8,128]{1,0:T(8,128)S(1)} %add.103), channel_id=1, source_target_pairs={{0,64},{32,96},{64,0},{96,32},{1,65},{33,97},{65,1},{97,33},{2,66}... | collective-permute-start | bytes 12296 | tf_op jit(solution)/shard_map/ppermute | solution.py:55
  148.6 3.6 %collective-permute-start.7 = (f32[8,128]{1,0:T(8,128)S(1)}, f32[8,128]{1,0:T(8,128)S(1)}, u32[]{:S(2)}, u32[]{:S(2)}) collective-permute-start(f32[8,128]{1,0:T(8,128)S(1)} %add.103), channel_id=1, source_target_pairs={{0,96},{32,0},{64,32},{96,64},{1,97},{33,1},{65,33},{97,65},{2,98}... | collective-permute-start | bytes 12296 | tf_op jit(solution)/shard_map/ppermute | solution.py:55
  152.2 10.6 %collective-permute-start.10 = (f32[8,128]{1,0:T(8,128)S(1)}, f32[8,128]{1,0:T(8,128)S(1)}, u32[]{:S(2)}, u32[]{:S(2)}) collective-permute-start(f32[8,128]{1,0:T(8,128)S(1)} %add_add_fusion.2), channel_id=1, source_target_pairs={{0,3},{1,0},{2,1},{3,2},{4,7},{5,4},{6,5},{7,6},{8,11},{9,8},{10,9... | collective-permute-start | bytes 12296 | tf_op jit(solution)/shard_map/ppermute | solution.py:55
  155.0 7.8 %collective-permute-start.8 = (f32[8,128]{1,0:T(8,128)S(1)}, f32[8,128]{1,0:T(8,128)S(1)}, u32[]{:S(2)}, u32[]{:S(2)}) collective-permute-start(f32[8,128]{1,0:T(8,128)S(1)} %add_add_fusion.2), channel_id=1, source_target_pairs={{0,1},{1,2},{2,3},{3,0},{4,5},{5,6},{6,7},{7,4},{8,9},{9,10},{10,1... | collective-permute-start | bytes 12296 | tf_op jit(solution)/shard_map/ppermute | solution.py:55
  155.0 9.4 %collective-permute-start.9 = (f32[8,128]{1,0:T(8,128)S(1)}, f32[8,128]{1,0:T(8,128)S(1)}, u32[]{:S(2)}, u32[]{:S(2)}) collective-permute-start(f32[8,128]{1,0:T(8,128)S(1)} %add_add_fusion.2), channel_id=1, source_target_pairs={{0,2},{1,3},{2,0},{3,1},{4,6},{5,7},{6,4},{7,5},{8,10},{9,11},{10,... | collective-permute-start | bytes 12296 | tf_op jit(solution)/shard_map/ppermute | solution.py:55
  165.5 33.9 %all-to-all-start.6 = ((f32[16,64,512]{2,1,0:T(8,128)}), f32[16,64,512]{2,1,0:T(8,128)S(1)}, u32[]{:S(2)}, u32[]{:S(2)}) async-start(f32[16,64,512]{2,1,0:T(8,128)} %gate.3), calls=%async_computation.6 | async-start | bytes 4194304 | tf_op jit(solution)/shard_map/all_to_all | solution.py:562
  169.8 18.7 %collective-permute-start.11 = (f32[8,128]{1,0:T(8,128)S(1)}, f32[8,128]{1,0:T(8,128)S(1)}, u32[]{:S(2)}, u32[]{:S(2)}) collective-permute-start(f32[8,128]{1,0:T(8,128)S(1)} %add_add_fusion.1.refs_1_), channel_id=1, source_target_pairs={{0,4},{4,8},{8,12},{12,0},{1,5},{5,9},{9,13},{13,1},{2,6},{6,10},{... | collective-permute-start | bytes 12296 | tf_op jit(solution)/shard_map/ppermute | solution.py:55
  171.8 20.3 %collective-permute-start.12 = (f32[8,128]{1,0:T(8,128)S(1)}, f32[8,128]{1,0:T(8,128)S(1)}, u32[]{:S(2)}, u32[]{:S(2)}) collective-permute-start(f32[8,128]{1,0:T(8,128)S(1)} %add_add_fusion.1.refs_1_), channel_id=1, source_target_pairs={{0,8},{4,12},{8,0},{12,4},{1,9},{5,13},{9,1},{13,5},{2,10},{6,14},... | collective-permute-start | bytes 12296 | tf_op jit(solution)/shard_map/ppermute | solution.py:55
  174.5 17.6 %collective-permute-start.13 = (f32[8,128]{1,0:T(8,128)S(1)}, f32[8,128]{1,0:T(8,128)S(1)}, u32[]{:S(2)}, u32[]{:S(2)}) collective-permute-start(f32[8,128]{1,0:T(8,128)S(1)} %add_add_fusion.1.refs_1_), channel_id=1, source_target_pairs={{0,12},{4,0},{8,4},{12,8},{1,13},{5,1},{9,5},{13,9},{2,14},{6,2},{... | collective-permute-start | bytes 12296 | tf_op jit(solution)/shard_map/ppermute | solution.py:55
  (5 other events, 8.8 us)

commit v10 on v9

--- a/solution.py
+++ b/solution.py
@@ -49,13 +49,16 @@
     return jnp.sum(sent_to_all(shard, axis), axis=0)
 
 
-def sum_direct(part, axis):
+def sum_direct(part, axis, beside=None):
     peers = lax.axis_size(axis)
     moved = [
         lax.ppermute(part, axis, [(i, (i + k) % peers) for i in range(peers)])
         for k in range(1, peers)
     ]
-    return functools.reduce(jnp.add, moved, part)
+    if beside is not None:
+        part, beside = lax.optimization_barrier((part, beside))
+    total = functools.reduce(jnp.add, moved, part)
+    return total if beside is None else (total, beside)
 
 
 def swapped(initial, last):
@@ -513,27 +516,28 @@
     return scale_ref[pl.ds(pl.multiple_of(pl.program_id(0) * part, part), part), :]
 
 
-def first_kernel(src_ref, dots_ref, *refs):
+def gather_kernel(src_ref, *refs):
+    ins, outs = refs[:-2], refs[-2:]
+    for j in range(BLOCKS_DEV):
+        for k, out_ref in enumerate(outs):
+            out_ref[:, j, :] = ins[2 * j + k][0]
+
+
+def combine_kernel(src_ref, dots_ref, r0_ref, m1_ref, *refs):
     ins, (x_ref, r_ref, scale_ref) = refs[:-3], refs[-3:]
-    scale = scales_of(dots_ref, scale_ref, x_ref.shape[0])
-    for j in range(BLOCKS_DEV):
-        r0, m1 = (ref[0] for ref in ins[2 * j : 2 * j + 2])
-        x_ref[:, j, :] = scale[:, 0:1] * r0 + scale[:, 1:2] * m1
-        r_ref[:, j, :] = scale[:, 2:3] * r0 + scale[:, 3:4] * m1
-
-
-def second_kernel(src_ref, dots_ref, part_ref, *refs):
-    ins, (r_ref, scale_ref) = refs[:-2], refs[-2:]
     scale = scales_of(dots_ref, scale_ref, r_ref.shape[0])
     for j in range(BLOCKS_DEV):
-        r_ref[:, j, :] = part_ref[:, j, :] + scale[:, 4:5] * ins[j][0]
-
-
-def combined(kernel, name, outs, sources, dots, held, *owned):
+        r0, m1 = r0_ref[:, j, :], m1_ref[:, j, :]
+        x_ref[:, j, :] = scale[:, 0:1] * r0 + scale[:, 1:2] * m1
+        r_ref[:, j, :] = scale[:, 2:3] * r0 + scale[:, 3:4] * m1 + scale[:, 4:5] * ins[j][0]
+
+
+def combined(kernel, name, sources, dots, held, *owned):
     _, fields, _ = owned[0].shape
     part = 16
     by_field = pl.BlockSpec((part, BLOCKS_DEV, BLOCK), lambda i, s: (i, 0, 0))
-    ins, specs = list(held), [by_field] * len(held)
+    ins, specs = dots + held, [pl.BlockSpec(x.shape, lambda i, s: (0, 0)) for x in dots]
+    specs += [by_field] * len(held)
     for j in range(BLOCKS_DEV):
         for v in owned:
             ins.append(v)
@@ -542,20 +546,24 @@
                     (1, part, BLOCK), functools.partial(lambda j, i, s: (s[j], i, 0), j)
                 )
             )
-    shape = jax.ShapeDtypeStruct((fields, BLOCKS_DEV, BLOCK), jnp.float32)
+    form = jax.ShapeDtypeStruct if dots else pltpu.HBM
+    shape = form((fields, BLOCKS_DEV, BLOCK), jnp.float32)
     return pl.pallas_call(
         kernel,
         grid_spec=pltpu.PrefetchScalarGridSpec(
             num_scalar_prefetch=1,
             grid=(fields // part,),
-            in_specs=[pl.BlockSpec(dots.shape, lambda i, s: (0, 0))] + specs,
-            out_specs=[by_field] * outs,
-            scratch_shapes=[pltpu.VMEM((COL_DEV, 8), jnp.float32)],
+            in_specs=specs,
+            out_specs=[by_field] * 2,
+            scratch_shapes=[pltpu.VMEM((COL_DEV, 8), jnp.float32)] * len(dots),
         ),
-        out_shape=[shape] * outs,
+        out_shape=[shape] * 2,
         compiler_params=pltpu.CompilerParams(vmem_limit_bytes=20 << 20),
+        cost_estimate=pl.CostEstimate(
+            flops=0, bytes_accessed=16 * fields * BLOCKS_DEV * BLOCK, transcendentals=0
+        ),
         name=name,
-    )(sources, dots, *ins)
+    )(sources, *ins)
 
 
 def to_owners(slots):
@@ -670,14 +678,14 @@
     dots = sum_direct(sum_wide(dots + last), SIXTEEN[1])
     slots = gate(slots, dots)
     owned_m2 = to_owners(slots)
-    dots = sum_direct(dots, SIXTEEN[0])
     owned = owned_table(group_map, sixteen_size, BLOCKS_DEV)
     my_ids = lax.dynamic_index_in_dim(owned, my_place, 0, keepdims=False)
     sources = my_ids // BLOCKS_DEV
-    solution_now, part = combined(
-        first_kernel, "first", 2, sources, dots, (), in_hbm(owned_r0), in_hbm(owned_m1)
-    )
-    (residual_now,) = combined(second_kernel, "second", 1, sources, dots, (part,), owned_m2)
+    early = combined(gather_kernel, "gather", sources, [], [], in_hbm(owned_r0), in_hbm(owned_m1))
+    dots, early = sum_direct(dots, SIXTEEN[0], early)
+    solution_now, residual_now = combined(
+        combine_kernel, "combine", sources, [dots], list(map(in_hbm, early)), owned_m2
+    )
     return (solution_now[None, None], residual_now[None, None])
 
 

time: 203 us -> 205 us (level)
  the two profiles are of different devices: /device:TPU:0 before, /device:TPU:24 now
where the time goes in v10:
time: 205 us; the launch traced here: 201 us
  Pallas kernels  92.6 us (45%)
  starting transfers between devices  62.5 us (30%)
  waiting for transfers between devices  30.1 us (15%)
  local copies, waits for them, and re-layouts  8.66 us (4%)
  other arithmetic  6.55 us (3%)
    pallas_call x3, Pallas kernels, applied(): pl.pallas_call(functools.partial(op_kernel, *tiles_of, len(v), bool(besid...  47.1 us
    pallas_call x4, Pallas kernels, covariance_tiles(): pl.pallas_call(functools.partial(tiles_kernel, first, count, len(beside_j...  32.6 us
    ppermute x10, waiting for transfers between devices, sum_direct(): lax.ppermute(part, axis, [(i, (i + k) % peers) for i in range(peers)])  21.6 us
    all_to_all x4, starting transfers between devices, sent_to_all(): lax.all_to_all(jnp.broadcast_to(shard[None], (peers, *shard.shape)), axis...  21.3 us
    all_to_all x3, starting transfers between devices, to_owners(): return lax.all_to_all(slots, SIXTEEN, 0, 0, tiled=True)  16 us
    ppermute x10, starting transfers between devices, sum_direct(): lax.ppermute(part, axis, [(i, (i + k) % peers) for i in range(peers)])  14.5 us
    pallas_call x2, Pallas kernels, combined(): pl.pallas_call(kernel, grid_spec=pltpu.PrefetchScalarGridSpec(num_scalar_...  9.55 us
    all_to_all x3, waiting for transfers between devices, to_owners(): return lax.all_to_all(slots, SIXTEEN, 0, 0, tiled=True)  8.42 us
  transfers between devices with their start and end apart: 21, of which 12 were waited for; matrix products, arithmetic and copies ran while one was open for 2% of the time, Pallas kernels for 42%

profile of v10, /device:TPU:24, one launch (start us, length us, event | category | flops | bytes accessed | tf_op | source)
XLA Modules:
  0.0 201.5 jit_solution(3089845016276018599)
XLA Ops:
  4.8 4.7 %all-to-all-start = ((f32[8,72,32]{1,2,0:T(8,128)}), f32[8,72,32]{1,2,0:T(8,128)S(1)}, u32[]{:S(2)}, u32[]{:S(2)}) async-start(f32[8,72,32]{1,2,0:T(8,128)} %broadcast_in_dim.14), calls=%async_computation | async-start | bytes 262144 | tf_op jit(solution)/shard_map/all_to_all | solution.py:43
  11.2 4.8 %tiles.4.refs_0_ = bf16[44,1024,512]{2,1,0:T(8,128)(2,1)} custom-call(s32[9]{0:T(128)S(1)} %pad_add_fusion.scalar_ref, f32[2,32,128]{2,1,0:T(8,128)S(1)} %copy-done.1), custom_call_target="tpu_custom_call" | custom-call | flops 15728640 | bytes 5242880 | tf_op jit(solution)/shard_map/tiles/pallas_call | solution.py:231
  17.8 7.9 %all-to-all-start.1 = ((f32[16,72,128]{2,1,0:T(8,128)}), f32[16,72,128]{2,1,0:T(8,128)S(1)}, u32[]{:S(2)}, u32[]{:S(2)}) async-start(f32[16,72,128]{2,1,0:T(8,128)} %broadcast_in_dim.15), calls=%async_computation.1 | async-start | bytes 1179648 | tf_op jit(solution)/shard_map/all_to_all | solution.py:43
  28.6 3.4 %collective-permute-start.1 = (f32[67,16,128]{2,1,0:T(8,128)S(1)}, f32[67,16,128]{2,1,0:T(8,128)S(1)}, u32[]{:S(2)}, u32[]{:S(2)}) collective-permute-start(f32[67,16,128]{2,1,0:T(8,128)S(1)} %get-tuple-element.92), channel_id=1, source_target_pairs={{1,0},{2,1},{3,2},{4,3},{5,4},{6,5},{7,6},{8,7},{9,8},{10,9},{11,1... | collective-permute-start | bytes 1646600 | tf_op jit(solution)/shard_map/ppermute | solution.py:68
  32.0 7.4 %tiles.5.refs_0_ = bf16[44,1024,512]{2,1,0:T(8,128)(2,1)} custom-call(s32[9]{0:T(128)S(1)} %pad_add_fusion.scalar_ref, f32[2,32,128]{2,1,0:T(8,128)S(1)} %copy-done.2, bf16[44,1024,512]{2,1,0:T(8,128)(2,1)} %tiles.4.refs_0_), custom_call_target="tpu_custom_call", output_to_operand_aliasing={{}: (2, {})} | custom-call | flops 28311552 | bytes 9437184 | tf_op jit(solution)/shard_map/tiles/pallas_call | solution.py:231
  41.1 4.8 %all-to-all-start.2 = ((f32[8,72,32]{1,2,0:T(8,128)}), f32[8,72,32]{1,2,0:T(8,128)S(1)}, u32[]{:S(2)}, u32[]{:S(2)}) async-start(f32[8,72,32]{1,2,0:T(8,128)} %broadcast_in_dim.16), calls=%async_computation.2 | async-start | bytes 262144 | tf_op jit(solution)/shard_map/all_to_all | solution.py:43
  45.9 7.4 %tiles.6.refs_2_ = bf16[44,1024,512]{2,1,0:T(8,128)(2,1)} custom-call(s32[9]{0:T(128)S(1)} %pad_add_fusion.scalar_ref, f32[2,32,128]{2,1,0:T(8,128)S(1)} %copy-done.2, bf16[44,1024,512]{2,1,0:T(8,128)(2,1)} %tiles.5.refs_0_), custom_call_target="tpu_custom_call", output_to_operand_aliasing={{}: (2, {})} | custom-call | flops 28311552 | bytes 9437184 | tf_op jit(solution)/shard_map/tiles/pallas_call | solution.py:231
  55.1 3.9 %all-to-all-start.3 = ((f32[16,80,128]{2,1,0:T(8,128)}), f32[16,80,128]{2,1,0:T(8,128)S(1)}, u32[]{:S(2)}, u32[]{:S(2)}) async-start(f32[16,80,128]{2,1,0:T(8,128)} %broadcast_in_dim.18), calls=%async_computation.3 | async-start | bytes 1310720 | tf_op jit(solution)/shard_map/all_to_all | solution.py:43
  59.1 13.0 %tiles.7.refs_3_.refs_2_.refs_5_ = bf16[44,1024,512]{2,1,0:T(8,128)(2,1)} custom-call(s32[9]{0:T(128)S(1)} %pad_add_fusion.scalar_ref, f32[2,32,128]{2,1,0:T(8,128)S(1)} %copy-done.2, f32[2,16,128]{2,1,0:T(8,128)S(1)} %slice.93.refs_0_, f32[2,16,128]{2,1,0:T(8,128)S(1)} %slice.94.refs_1_, ...), custom_call_target="tpu_custom_call", output_to_operand_aliasing={{}: (4, {})} | custom-call | flops 66060288 | bytes 22020096 | tf_op jit(solution)/shard_map/tiles/pallas_call | solution.py:231
  72.6 3.3 %residual.1 = (f32[8,64,512]{2,1,0:T(8,128)}, f32[4,64,512]{2,1,0:T(8,128)}, f32[4,64,512]{2,1,0:T(8,128)}, f32[16,64,512]{2,1,0:T(8,128)}) custom-call(s32[8]{0:T(128)S(1)} %fusion.4.target_ref, f32[64,32,128]{2,1,0:T(8,128)S(1)} %copy-done, f32[32,128]{1,0:T(8,128)S(1)} %get-tuple-element.125.weight_ref, f32[64,32]{1,0:T(8,128)S(1)} %divide_add_fusion.1.row_ref, ...), custom_call_target="tpu_custom_call" | custom-call | tf_op jit(solution)/shard_map/residual/pallas_call | solution.py:497
  75.9 7.1 %all-to-all-start.4 = ((f32[16,64,512]{2,1,0:T(8,128)}), f32[16,64,512]{2,1,0:T(8,128)S(1)}, u32[]{:S(2)}, u32[]{:S(2)}) async-start(f32[16,64,512]{2,1,0:T(8,128)} %get-tuple-element.108), calls=%async_computation.4 | async-start | bytes 4194304 | tf_op jit(solution)/shard_map/all_to_all | solution.py:570
  83.0 21.5 %applied.3 = (f32[4,64,512]{2,1,0:T(8,128)}, f32[4,64,512]{2,1,0:T(8,128)}, f32[16,64,512]{2,1,0:T(8,128)}, f32[8,128]{1,0:T(8,128)S(1)}) custom-call(s32[9]{0:T(128)S(1)} %pad_add_fusion.scalar_ref, s32[8]{0:T(128)S(1)} %fusion.4.target_ref, f32[8,64,512]{2,1,0:T(8,128)} %get-tuple-element.100.refs_0_, f32[4,64,512]{2,1,0:T(8,128)} %get-tuple-element.101.refs_1_, ...), custom_call_target="tpu_custom_call" | custom-call | flops 6643777536 | bytes 46137344 | tf_op jit(solution)/shard_map/applied/pallas_call | solution.py:410
  106.5 3.4 %collective-permute-start.3 = (f32[4,64,512]{2,1,0:T(8,128)}, f32[4,64,512]{2,1,0:T(8,128)S(1)}, u32[]{:S(2)}, u32[]{:S(2)}) collective-permute-start(f32[4,64,512]{2,1,0:T(8,128)} %get-tuple-element.105.refs_0_), channel_id=1, source_target_pairs={{1,0},{2,1},{3,2},{4,3},{5,4},{6,5},{7,6},{8,7},{9,8},{10,9},{11,1... | collective-permute-start | bytes 1572872 | tf_op jit(solution)/shard_map/ppermute | solution.py:68
  110.0 14.8 %applied.4.refs_4_.refs_1_ = f32[8,64,512]{2,1,0:T(8,128)} custom-call(s32[9]{0:T(128)S(1)} %pad_add_fusion.scalar_ref, s32[8]{0:T(128)S(1)} %fusion.4.target_ref, f32[4,64,512]{2,1,0:T(8,128)} %get-tuple-element.105.refs_0_, f32[4,64,512]{2,1,0:T(8,128)} %get-tuple-element.106.refs_1_, bf16[44,1024,512]{2,1,0:T(8,128)(2,1)} %tiles.7.refs_3_.refs_2_.refs_5_), custom_call_target="tpu_custom_call" | custom-call | flops 3170893824 | bytes 22020096 | tf_op jit(solution)/shard_map/applied/pallas_call | solution.py:410
  127.1 4.7 %all-to-all-start.5 = ((f32[16,64,512]{2,1,0:T(8,128)}), f32[16,64,512]{2,1,0:T(8,128)}, u32[]{:S(2)}, u32[]{:S(2)}) async-start(f32[16,64,512]{2,1,0:T(8,128)} %gate.2), calls=%async_computation.5 | async-start | bytes 4194304 | tf_op jit(solution)/shard_map/all_to_all | solution.py:570
  131.8 10.7 %applied.5 = (f32[16,64,512]{2,1,0:T(8,128)}, f32[8,128]{1,0:T(8,128)S(1)}) custom-call(s32[9]{0:T(128)S(1)} %pad_add_fusion.scalar_ref, s32[8]{0:T(128)S(1)} %fusion.4.target_ref, f32[4,64,512]{2,1,0:T(8,128)} %get-tuple-element.105.refs_0_, f32[4,64,512]{2,1,0:T(8,128)} %get-tuple-element.106.refs_1_, f32[4,64,512]{2,1,0:T(8,128)} %copy-done.4, ...), custom_call_target="tpu_custom_call" | custom-call | flops 3472883712 | bytes 24117248 | tf_op jit(solution)/shard_map/applied/pallas_call | solution.py:410
  151.4 2.8 %collective-permute-start.10 = (f32[8,128]{1,0:T(8,128)S(1)}, f32[8,128]{1,0:T(8,128)S(1)}, u32[]{:S(2)}, u32[]{:S(2)}) collective-permute-start(f32[8,128]{1,0:T(8,128)S(1)} %add_add_fusion.2), channel_id=1, source_target_pairs={{0,3},{1,0},{2,1},{3,2},{4,7},{5,4},{6,5},{7,6},{8,11},{9,8},{10,9... | collective-permute-start | bytes 12296 | tf_op jit(solution)/shard_map/ppermute | solution.py:55
  162.3 4.2 %all-to-all-start.6 = ((f32[16,64,512]{2,1,0:T(8,128)}), f32[16,64,512]{2,1,0:T(8,128)S(1)}, u32[]{:S(2)}, u32[]{:S(2)}) async-start(f32[16,64,512]{2,1,0:T(8,128)} %gate.3), calls=%async_computation.6 | async-start | bytes 4194304 | tf_op jit(solution)/shard_map/all_to_all | solution.py:570
  169.1 2.7 %collective-permute-start.12 = (f32[8,128]{1,0:T(8,128)S(1)}, f32[8,128]{1,0:T(8,128)S(1)}, u32[]{:S(2)}, u32[]{:S(2)}) collective-permute-start(f32[8,128]{1,0:T(8,128)S(1)} %add_add_fusion.1.refs_1_), channel_id=1, source_target_pairs={{0,8},{4,12},{8,0},{12,4},{1,9},{5,13},{9,1},{13,5},{2,10},{6,14},... | collective-permute-start | bytes 12296 | tf_op jit(solution)/shard_map/ppermute | solution.py:55
  173.2 4.6 %gather.1 = (f32[64,8,512]{2,1,0:T(8,128)}, f32[64,8,512]{2,1,0:T(8,128)}) custom-call(s32[8]{0:T(128)S(1)} %and_select_fusion.src_ref, f32[16,64,512]{2,1,0:T(8,128)} %copy-done.3, f32[16,64,512]{2,1,0:T(8,128)} %all-to-all-done.5.refs_1_.refs_3_.refs_5_.refs_7_.refs_9_.refs_11_.refs_13_.refs_15_, f32[16,64,512]{2,1,0:T(8,128)} %copy-done.3, ...), custom_call_target="tpu_custom_call" | custom-call | bytes 4194304 | tf_op jit(solution)/shard_map/gather/pallas_call | solution.py:551
  177.8 7.9 %collective-permute-done.11 = f32[8,128]{1,0:T(8,128)S(1)} collective-permute-done((f32[8,128]{1,0:T(8,128)S(1)}, f32[8,128]{1,0:T(8,128)S(1)}, u32[]{:S(2)}, u32[]{:S(2)}) %collective-permute-start.11) | collective-permute-done | bytes 4128 | tf_op jit(solution)/shard_map/ppermute | solution.py:55
  185.7 3.7 %collective-permute-done.12 = f32[8,128]{1,0:T(8,128)S(1)} collective-permute-done((f32[8,128]{1,0:T(8,128)S(1)}, f32[8,128]{1,0:T(8,128)S(1)}, u32[]{:S(2)}, u32[]{:S(2)}) %collective-permute-start.12) | collective-permute-done | bytes 4128 | tf_op jit(solution)/shard_map/ppermute | solution.py:55
  189.4 7.1 %all-to-all-done.6.refs_0_.refs_1_.refs_2_.refs_3_.refs_4_.refs_5_.refs_6_.refs_7_ = f32[16,64,512]{2,1,0:T(8,128)S(1)} async-done(((f32[16,64,512]{2,1,0:T(8,128)}), f32[16,64,512]{2,1,0:T(8,128)S(1)}, u32[]{:S(2)}, u32[]{:S(2)}) %all-to-all-start.6) | async-done | bytes 2097184 | tf_op jit(solution)/shard_map/all_to_all | solution.py:570
  196.5 5.0 %combine.1 = (f32[64,8,512]{2,1,0:T(8,128)}, f32[64,8,512]{2,1,0:T(8,128)}) custom-call(s32[8]{0:T(128)S(1)} %and_select_fusion.src_ref, f32[8,128]{1,0:T(8,128)S(1)} %add_add_fusion.dots_ref, f32[64,8,512]{2,1,0:T(8,128)} %get-tuple-element.113.r0_ref, f32[64,8,512]{2,1,0:T(8,128)} %get-tuple-element.114.m1_ref, ...), custom_call_target="tpu_custom_call" | custom-call | bytes 4194304 | tf_op jit(solution)/shard_map/combine/pallas_call | solution.py:551
  (98 shorter events, 39.6 us)
Async XLA Ops:
  4.8 11.2 %all-to-all-start = ((f32[8,72,32]{1,2,0:T(8,128)}), f32[8,72,32]{1,2,0:T(8,128)S(1)}, u32[]{:S(2)}, u32[]{:S(2)}) async-start(f32[8,72,32]{1,2,0:T(8,128)} %broadcast_in_dim.14), calls=%async_computation | async-start | bytes 262144 | tf_op jit(solution)/shard_map/all_to_all | solution.py:43
  11.2 5.2 %copy-start = (f32[64,32,128]{2,1,0:T(8,128)S(1)}, f32[64,32,128]{2,1,0:T(8,128)}, u32[]{:S(2)}) copy-start(f32[64,32,128]{2,1,0:T(8,128)} %obs_ref.1) | copy-start | bytes 3145732
  16.0 9.7 %copy-start.2 = (f32[2,32,128]{2,1,0:T(8,128)S(1)}, f32[2,32,128]{2,1,0:T(8,128)}, u32[]{:S(2)}) copy-start(f32[2,32,128]{2,1,0:T(8,128)} %jitter_ref.3) | copy-start | bytes 98308
  17.8 21.6 %all-to-all-start.1 = ((f32[16,72,128]{2,1,0:T(8,128)}), f32[16,72,128]{2,1,0:T(8,128)S(1)}, u32[]{:S(2)}, u32[]{:S(2)}) async-start(f32[16,72,128]{2,1,0:T(8,128)} %broadcast_in_dim.15), calls=%async_computation.1 | async-start | bytes 1179648 | tf_op jit(solution)/shard_map/all_to_all | solution.py:43
  26.6 26.7 %collective-permute-start = (f32[67,16,128]{2,1,0:T(8,128)}, f32[67,16,128]{2,1,0:T(8,128)S(1)}, u32[]{:S(2)}, u32[]{:S(2)}) collective-permute-start(f32[67,16,128]{2,1,0:T(8,128)} %get-tuple-element.91), channel_id=1, source_target_pairs={{0,1},{1,2},{2,3},{3,4},{4,5},{5,6},{6,7},{7,8},{8,9},{9,10},{10,1... | collective-permute-start | bytes 1646600 | tf_op jit(solution)/shard_map/ppermute | solution.py:68
  28.6 24.8 %collective-permute-start.1 = (f32[67,16,128]{2,1,0:T(8,128)S(1)}, f32[67,16,128]{2,1,0:T(8,128)S(1)}, u32[]{:S(2)}, u32[]{:S(2)}) collective-permute-start(f32[67,16,128]{2,1,0:T(8,128)S(1)} %get-tuple-element.92), channel_id=1, source_target_pairs={{1,0},{2,1},{3,2},{4,3},{5,4},{6,5},{7,6},{8,7},{9,8},{10,9},{11,1... | collective-permute-start | bytes 1646600 | tf_op jit(solution)/shard_map/ppermute | solution.py:68
  41.1 12.2 %all-to-all-start.2 = ((f32[8,72,32]{1,2,0:T(8,128)}), f32[8,72,32]{1,2,0:T(8,128)S(1)}, u32[]{:S(2)}, u32[]{:S(2)}) async-start(f32[8,72,32]{1,2,0:T(8,128)} %broadcast_in_dim.16), calls=%async_computation.2 | async-start | bytes 262144 | tf_op jit(solution)/shard_map/all_to_all | solution.py:43
  53.3 5.7 %copy-start.7 = (s32[1,128]{1,0:T(1,128)S(1)}, s32[1,128]{1,0:T(1,128)}, u32[]{:S(2)}) copy-start(s32[1,128]{1,0:T(1,128)} %param.16) | copy-start | bytes 1540
  55.1 17.2 %all-to-all-start.3 = ((f32[16,80,128]{2,1,0:T(8,128)}), f32[16,80,128]{2,1,0:T(8,128)S(1)}, u32[]{:S(2)}, u32[]{:S(2)}) async-start(f32[16,80,128]{2,1,0:T(8,128)} %broadcast_in_dim.18), calls=%async_computation.3 | async-start | bytes 1310720 | tf_op jit(solution)/shard_map/all_to_all | solution.py:43
  75.9 49.9 %all-to-all-start.4 = ((f32[16,64,512]{2,1,0:T(8,128)}), f32[16,64,512]{2,1,0:T(8,128)S(1)}, u32[]{:S(2)}, u32[]{:S(2)}) async-start(f32[16,64,512]{2,1,0:T(8,128)} %get-tuple-element.108), calls=%async_computation.4 | async-start | bytes 4194304 | tf_op jit(solution)/shard_map/all_to_all | solution.py:570
  104.5 20.2 %collective-permute-start.2 = (f32[4,64,512]{2,1,0:T(8,128)}, f32[4,64,512]{2,1,0:T(8,128)S(1)}, u32[]{:S(2)}, u32[]{:S(2)}) collective-permute-start(f32[4,64,512]{2,1,0:T(8,128)} %get-tuple-element.106.refs_1_), channel_id=1, source_target_pairs={{0,1},{1,2},{2,3},{3,4},{4,5},{5,6},{6,7},{7,8},{8,9},{9,10},{10,1... | collective-permute-start | bytes 1572872 | tf_op jit(solution)/shard_map/ppermute | solution.py:68
  106.5 18.3 %collective-permute-start.3 = (f32[4,64,512]{2,1,0:T(8,128)}, f32[4,64,512]{2,1,0:T(8,128)S(1)}, u32[]{:S(2)}, u32[]{:S(2)}) collective-permute-start(f32[4,64,512]{2,1,0:T(8,128)} %get-tuple-element.105.refs_0_), channel_id=1, source_target_pairs={{1,0},{2,1},{3,2},{4,3},{5,4},{6,5},{7,6},{8,7},{9,8},{10,9},{11,1... | collective-permute-start | bytes 1572872 | tf_op jit(solution)/shard_map/ppermute | solution.py:68
  127.1 35.2 %all-to-all-start.5 = ((f32[16,64,512]{2,1,0:T(8,128)}), f32[16,64,512]{2,1,0:T(8,128)}, u32[]{:S(2)}, u32[]{:S(2)}) async-start(f32[16,64,512]{2,1,0:T(8,128)} %gate.2), calls=%async_computation.5 | async-start | bytes 4194304 | tf_op jit(solution)/shard_map/all_to_all | solution.py:570
  142.5 1.2 collective-permute-start.4
  143.8 3.6 %collective-permute-start.5 = (f32[8,128]{1,0:T(8,128)S(1)}, f32[8,128]{1,0:T(8,128)S(1)}, u32[]{:S(2)}, u32[]{:S(2)}) collective-permute-start(f32[8,128]{1,0:T(8,128)S(1)} %add.103), channel_id=1, source_target_pairs={{0,32},{32,64},{64,96},{96,0},{1,33},{33,65},{65,97},{97,1},{2,34}... | collective-permute-start | bytes 12296 | tf_op jit(solution)/shard_map/ppermute | solution.py:55
  143.9 5.1 %collective-permute-start.6 = (f32[8,128]{1,0:T(8,128)S(1)}, f32[8,128]{1,0:T(8,128)S(1)}, u32[]{:S(2)}, u32[]{:S(2)}) collective-permute-start(f32[8,128]{1,0:T(8,128)S(1)} %add.103), channel_id=1, source_target_pairs={{0,64},{32,96},{64,0},{96,32},{1,65},{33,97},{65,1},{97,33},{2,66}... | collective-permute-start | bytes 12296 | tf_op jit(solution)/shard_map/ppermute | solution.py:55
  146.6 4.8 %collective-permute-start.7 = (f32[8,128]{1,0:T(8,128)S(1)}, f32[8,128]{1,0:T(8,128)S(1)}, u32[]{:S(2)}, u32[]{:S(2)}) collective-permute-start(f32[8,128]{1,0:T(8,128)S(1)} %add.103), channel_id=1, source_target_pairs={{0,96},{32,0},{64,32},{96,64},{1,97},{33,1},{65,33},{97,65},{2,98}... | collective-permute-start | bytes 12296 | tf_op jit(solution)/shard_map/ppermute | solution.py:55
  151.4 6.9 %collective-permute-start.10 = (f32[8,128]{1,0:T(8,128)S(1)}, f32[8,128]{1,0:T(8,128)S(1)}, u32[]{:S(2)}, u32[]{:S(2)}) collective-permute-start(f32[8,128]{1,0:T(8,128)S(1)} %add_add_fusion.2), channel_id=1, source_target_pairs={{0,3},{1,0},{2,1},{3,2},{4,7},{5,4},{6,5},{7,6},{8,11},{9,8},{10,9... | collective-permute-start | bytes 12296 | tf_op jit(solution)/shard_map/ppermute | solution.py:55
  154.1 4.8 %collective-permute-start.8 = (f32[8,128]{1,0:T(8,128)S(1)}, f32[8,128]{1,0:T(8,128)S(1)}, u32[]{:S(2)}, u32[]{:S(2)}) collective-permute-start(f32[8,128]{1,0:T(8,128)S(1)} %add_add_fusion.2), channel_id=1, source_target_pairs={{0,1},{1,2},{2,3},{3,0},{4,5},{5,6},{6,7},{7,4},{8,9},{9,10},{10,1... | collective-permute-start | bytes 12296 | tf_op jit(solution)/shard_map/ppermute | solution.py:55
  154.2 6.8 %collective-permute-start.9 = (f32[8,128]{1,0:T(8,128)S(1)}, f32[8,128]{1,0:T(8,128)S(1)}, u32[]{:S(2)}, u32[]{:S(2)}) collective-permute-start(f32[8,128]{1,0:T(8,128)S(1)} %add_add_fusion.2), channel_id=1, source_target_pairs={{0,2},{1,3},{2,0},{3,1},{4,6},{5,7},{6,4},{7,5},{8,10},{9,11},{10,... | collective-permute-start | bytes 12296 | tf_op jit(solution)/shard_map/ppermute | solution.py:55
  162.3 34.2 %all-to-all-start.6 = ((f32[16,64,512]{2,1,0:T(8,128)}), f32[16,64,512]{2,1,0:T(8,128)S(1)}, u32[]{:S(2)}, u32[]{:S(2)}) async-start(f32[16,64,512]{2,1,0:T(8,128)} %gate.3), calls=%async_computation.6 | async-start | bytes 4194304 | tf_op jit(solution)/shard_map/all_to_all | solution.py:570
  167.1 18.6 %collective-permute-start.11 = (f32[8,128]{1,0:T(8,128)S(1)}, f32[8,128]{1,0:T(8,128)S(1)}, u32[]{:S(2)}, u32[]{:S(2)}) collective-permute-start(f32[8,128]{1,0:T(8,128)S(1)} %add_add_fusion.1.refs_1_), channel_id=1, source_target_pairs={{0,4},{4,8},{8,12},{12,0},{1,5},{5,9},{9,13},{13,1},{2,6},{6,10},{... | collective-permute-start | bytes 12296 | tf_op jit(solution)/shard_map/ppermute | solution.py:55
  169.1 20.3 %collective-permute-start.12 = (f32[8,128]{1,0:T(8,128)S(1)}, f32[8,128]{1,0:T(8,128)S(1)}, u32[]{:S(2)}, u32[]{:S(2)}) collective-permute-start(f32[8,128]{1,0:T(8,128)S(1)} %add_add_fusion.1.refs_1_), channel_id=1, source_target_pairs={{0,8},{4,12},{8,0},{12,4},{1,9},{5,13},{9,1},{13,5},{2,10},{6,14},... | collective-permute-start | bytes 12296 | tf_op jit(solution)/shard_map/ppermute | solution.py:55
  171.7 17.6 %collective-permute-start.13 = (f32[8,128]{1,0:T(8,128)S(1)}, f32[8,128]{1,0:T(8,128)S(1)}, u32[]{:S(2)}, u32[]{:S(2)}) collective-permute-start(f32[8,128]{1,0:T(8,128)S(1)} %add_add_fusion.1.refs_1_), channel_id=1, source_target_pairs={{0,12},{4,0},{8,4},{12,8},{1,13},{5,1},{9,5},{13,9},{2,14},{6,2},{... | collective-permute-start | bytes 12296 | tf_op jit(solution)/shard_map/ppermute | solution.py:55
  (5 other events, 8.9 us)
